TPU v7x, 512 devices: a whole 4x8x8 slice. The times are simulated.
512 devices in a mesh: row: 32 (over z, x_lo, core), col: 16 (over x_hi, y).
Axes of the slice: x: 4 (x_hi: 2, x_lo: 2; x = x_hi * 2 + x_lo), y: 8, z: 8, core: 2. Of those that a mesh axis runs over, the one named last changes fastest.
Arguments:
- slab_block: bfloat16 [65536, 2048], P('row', 'col'), may hold values from -6 to 6
- scale_first: bfloat16 [65536], P('row'), may hold values from 0.5 to 2
- scale_second: bfloat16 [65536], P('row'), may hold values from 0.5 to 2
- panel_lower: bfloat16 [65536, 4096], P('row', 'col'), may hold values from -0.09375 to 0.09375
Outputs:
- updated_slab: bfloat16 [65536, 2048], P('row', 'col')
All inputs are finite; a program needn't handle non-finite values.
Results may differ from a plain program's by a relative error of at most 0.015.
Values may be sent and summed in bfloat16 or wider, within the bound.
No kernel may reach another device: no remote copies, remote signals or barrier semaphores. Data moves between devices by JAX's collectives and lax.ppermute only.
A program may use at most 64 MiB of HBM per device.

v0:
```python
import jax
import jax.numpy as jnp
from jax import lax
from jax.sharding import PartitionSpec as P

PANEL_W = 4096


inv_root = 0.7071067811865476


def from_partner(block, axis, bit):
    count = lax.axis_size(axis)
    route = []
    for low in range(count):
        high = low | 1 << bit
        if high != low and high < count:
            route += [(low, high), (high, low)]
    return lax.ppermute(block, axis, route)


def per_device(slab_block, scale_first, scale_second, panel_lower):
    row_count, col_width = slab_block.shape
    groups = lax.axis_size("row")
    top_bit = groups.bit_length() - 1
    first = (scale_first.astype(jnp.float32)[:, None] * slab_block.astype(jnp.float32)).astype(
        jnp.bfloat16
    )
    my_index = lax.axis_index("row")
    partner = from_partner(first, "row", top_bit - 1)
    upper_one = my_index // (groups // 2) % 2 == 0
    own_vals = first.astype(jnp.float32)
    far_vals = partner.astype(jnp.float32)
    level_one = jnp.where(
        upper_one, (own_vals + far_vals) * inv_root, (far_vals - own_vals) * inv_root
    )
    second = (scale_second.astype(jnp.float32)[:, None] * level_one).astype(jnp.bfloat16)
    partner_two = from_partner(second, "row", top_bit - 2)
    upper_two = my_index // (groups // 4) % 2 == 0
    own_two = second.astype(jnp.float32)
    far_two = partner_two.astype(jnp.float32)
    level_two = jnp.where(upper_two, (own_two + far_two) * inv_root, (far_two - own_two) * inv_root)
    transformed = level_two.astype(jnp.bfloat16)
    moved = lax.all_to_all(
        transformed.reshape(row_count // groups, groups, col_width),
        "row",
        split_axis=1,
        concat_axis=0,
        tiled=True,
    )
    stored = moved.reshape(row_count, col_width)
    top_count = PANEL_W // groups
    top_local = stored[:top_count].reshape(top_count, 1, col_width)
    upper_rows = lax.all_gather(top_local, "row", axis=1, tiled=True).reshape(PANEL_W, col_width)
    block_width = panel_lower.shape[1]
    empty_sum = jnp.zeros((row_count, col_width), jnp.float32)
    shard_piece = lax.all_gather(panel_lower, "col", axis=1, tiled=True)
    blocks_in = shard_piece.shape[1] // block_width

    def one_block(blocknum, running):
        panel_part = lax.dynamic_slice_in_dim(shard_piece, blocknum * block_width, block_width, 1)
        rows_used = lax.dynamic_slice_in_dim(upper_rows, blocknum * block_width, block_width, 0)
        product = jnp.dot(panel_part, rows_used, preferred_element_type=jnp.float32)
        return running + product.astype(jnp.bfloat16).astype(jnp.float32)

    update_sum = lax.fori_loop(0, blocks_in, one_block, empty_sum)
    return (stored.astype(jnp.float32) - update_sum).astype(jnp.bfloat16)


def solution(mesh):
    placed = (P("row", "col"), P("row"), P("row"), P("row", "col"))
    return jax.shard_map(
        per_device, mesh=mesh, in_specs=placed, out_specs=P("row", "col"), check_vma=False
    )
```

profile of v0, /device:TPU:8, one launch (start us, length us, event | category | flops | bytes accessed | tf_op | source)
XLA Modules:
  0.0 444.3 jit_solution(17364804723847924911)
XLA Ops:
  6.5 0.7 convert_element_type.54
  7.2 1.4 multiply_convert_fusion
  8.6 10.9 %collective-permute-start = (bf16[2048,128]{1,0:T(8,128)(2,1)S(1)}, bf16[2048,128]{1,0:T(8,128)(2,1)S(1)}, u32[]{:S(2)}, u32[]{:S(2)}) collective-permute-start(bf16[2048,128]{1,0:T(8,128)(2,1)S(1)} %multiply_convert_fusion), channel_id=1, source_target_pairs={{0,256},{256,0},{16,272},{272,16},{32,288},{288,32},{48,304},{304,... | collective-permute-start | bytes 1572872 | tf_op jit(solution)/shard_map/ppermute | solution.py:19
  19.6 0.7 convert_element_type.53
  20.3 11.4 %collective-permute-done = bf16[2048,128]{1,0:T(8,128)(2,1)S(1)} collective-permute-done((bf16[2048,128]{1,0:T(8,128)(2,1)S(1)}, bf16[2048,128]{1,0:T(8,128)(2,1)S(1)}, u32[]{:S(2)}, u32[]{:S(2)}) %collective-permute-start) | collective-permute-done | bytes 524320 | tf_op jit(solution)/shard_map/ppermute | solution.py:19
  31.6 1.7 fusion.8
  33.3 15.4 %collective-permute-start.1 = (bf16[2048,128]{1,0:T(8,128)(2,1)S(1)}, bf16[2048,128]{1,0:T(8,128)(2,1)S(1)}, u32[]{:S(2)}, u32[]{:S(2)}) collective-permute-start(bf16[2048,128]{1,0:T(8,128)(2,1)S(1)} %fusion.8), channel_id=1, source_target_pairs={{0,128},{128,0},{16,144},{144,16},{32,160},{160,32},{48,176},{176,... | collective-permute-start | bytes 1572872 | tf_op jit(solution)/shard_map/ppermute | solution.py:19
  48.7 23.2 %collective-permute-done.1 = bf16[2048,128]{1,0:T(8,128)(2,1)S(1)} collective-permute-done((bf16[2048,128]{1,0:T(8,128)(2,1)S(1)}, bf16[2048,128]{1,0:T(8,128)(2,1)S(1)}, u32[]{:S(2)}, u32[]{:S(2)}) %collective-permute-start.1) | collective-permute-done | bytes 524320 | tf_op jit(solution)/shard_map/ppermute | solution.py:19
  72.4 25.9 %all_to_all.15 = bf16[64,32,128]{2,0,1:T(8,128)(2,1)S(1)} all-to-all(bf16[64,32,128]{2,0,1:T(8,128)(2,1)S(1)} %copy.8), channel_id=1, replica_groups=mesh['row'=32,'col'=16] {'row'}, dimensions={1} | all-to-all | bytes 1048576 | tf_op jit(solution)/shard_map/all_to_all | solution.py:44
  98.3 0.6 slice.5
  99.0 0.7 all-gather.3.cloned.1.call-update
  99.7 62.5 %all-gather.5.cloned.1.call-done = bf16[128,32,128]{2,0,1:T(8,128)(2,1)} async-done(((bf16[128,1,128]{2,0,1:T(8,128)(2,1)}), bf16[128,32,128]{2,0,1:T(8,128)(2,1)}) %all-gather.5.cloned.1.call-update) | async-done | bytes 1048592 | tf_op jit(solution)/shard_map/all_gather | solution.py:54
  162.2 1.9 copy.9
  164.1 243.9 %all-gather.3.cloned.1.call-done = bf16[2048,4096]{1,0:T(8,128)(2,1)} async-done(((bf16[2048,256]{1,0:T(8,128)(2,1)}), bf16[2048,4096]{1,0:T(8,128)(2,1)}) %all-gather.3.cloned.1.call-update) | async-done | bytes 16777232 | tf_op jit(solution)/shard_map/all_gather | solution.py:57
  408.0 28.6 %while.14 = (s32[]{:T(128)}, f32[2048,128]{1,0:T(8,128)S(1)}, bf16[2048,4096]{1,0:T(8,128)(2,1)}, bf16[4096,128]{1,0:T(8,128)(2,1)S(1)}, s32[]{:T(128)}, /*index=5*/s32[]{:T(128)}, s32[]{:T(128)}, s32[]{:T(128)}) while((s32[]{:T(128)}, f32[2048,128]{1,0:T(8,128)S(1)}, bf16[2048,4096]{1,0:T(8,128)(2,1)}, ...), condition=%wide.region_1.2_spmd.clone, body=%wide.region_0.1_spmd.clone.sunk | while | flops 135266304 | bytes 3212948 | solution.py:66
  408.0 1.8 fusion.20
  409.8 1.8 fusion.20
  411.6 1.8 fusion.20
  413.3 1.8 fusion.20
  415.1 1.8 fusion.20
  416.9 1.8 fusion.20
  418.7 1.8 fusion.20
  420.5 1.8 fusion.20
  422.3 1.8 fusion.20
  424.1 1.8 fusion.20
  425.9 1.8 fusion.20
  427.6 1.8 fusion.20
  429.4 1.8 fusion.20
  431.2 1.8 fusion.20
  433.0 1.8 fusion.20
  434.8 1.8 fusion.20
  436.6 0.9 fusion.14
  (6 shorter events, 0.5 us)
Async XLA Ops:
  6.5 155.7 %all-gather.5.cloned.1.call-start = ((), (), s32[]{:S(2)}) async-start(), calls=%async_computation.2 | async-start | bytes 1081344 | tf_op jit(solution)/shard_map/all_gather | solution.py:54
  8.6 23.0 %collective-permute-start = (bf16[2048,128]{1,0:T(8,128)(2,1)S(1)}, bf16[2048,128]{1,0:T(8,128)(2,1)S(1)}, u32[]{:S(2)}, u32[]{:S(2)}) collective-permute-start(bf16[2048,128]{1,0:T(8,128)(2,1)S(1)} %multiply_convert_fusion), channel_id=1, source_target_pairs={{0,256},{256,0},{16,272},{272,16},{32,288},{288,32},{48,304},{304,... | collective-permute-start | bytes 1572872 | tf_op jit(solution)/shard_map/ppermute | solution.py:19
  33.3 38.7 %collective-permute-start.1 = (bf16[2048,128]{1,0:T(8,128)(2,1)S(1)}, bf16[2048,128]{1,0:T(8,128)(2,1)S(1)}, u32[]{:S(2)}, u32[]{:S(2)}) collective-permute-start(bf16[2048,128]{1,0:T(8,128)(2,1)S(1)} %fusion.8), channel_id=1, source_target_pairs={{0,128},{128,0},{16,144},{144,16},{32,160},{160,32},{48,176},{176,... | collective-permute-start | bytes 1572872 | tf_op jit(solution)/shard_map/ppermute | solution.py:19
  99.0 309.0 %all-gather.3.cloned.1.call-start = ((), (), s32[]{:S(2)}) async-start(), calls=%async_computation.1 | async-start | bytes 17825792 | tf_op jit(solution)/shard_map/all_gather | solution.py:57
Sparse Core Ops, SparseCore 0:
  99.1 63.0 all-gather.4
  165.3 242.6 all-gather.2
where the time goes:
time: 445 us; the launch traced here: 444 us
  waiting for transfers between devices  342 us (77%)
  matrix products  28.1 us (6%)
  starting transfers between devices  26.4 us (6%)
  blocking collectives  25.9 us (6%)
  between operations  13.5 us (3%)
  other arithmetic  5.61 us (1%)
    all_gather x1, waiting for transfers between devices, per_device(): shard_piece = lax.all_gather(panel_lower, 'col', axis=1, tiled=True)  244 us
    all_gather x1, waiting for transfers between devices, per_device(): lax.all_gather(top_local, 'row', axis=1, tiled=True)  62.5 us
    ppermute x2, waiting for transfers between devices, from_partner(): return lax.ppermute(block, axis, route)  34.6 us
    dot_general x16, matrix products, one_block(): product = jnp.dot(panel_part, rows_used, preferred_element_type=jnp.float32)  28.1 us
    ppermute x2, starting transfers between devices, from_partner(): return lax.ppermute(block, axis, route)  26.4 us
    all_to_all x1, blocking collectives, per_device(): lax.all_to_all(transformed.reshape(row_count // groups, groups, col_width...  25.9 us
  transfers between devices with their start and end apart: 4, of which 4 were waited for; matrix products, arithmetic and copies ran while one was open for 1% of the time, Pallas kernels for 0%

commit v1 on v0

v1 whole, which is shorter than its diff:
```python
import jax
import jax.numpy as jnp
from jax import lax
from jax.sharding import Mesh, PartitionSpec as P

PANEL_W = 4096
X_HI = 2
CHUNKS = 4

inv_root = 0.7071067811865476


def butterfly(top, bottom):
    top = top.astype(jnp.float32)
    bottom = bottom.astype(jnp.float32)
    return jnp.concatenate([(top + bottom) * inv_root, (top - bottom) * inv_root], axis=0)


def per_device(slab_block, scale_first, scale_second, panel_lower):
    row_count, col_width = slab_block.shape
    groups = lax.axis_size("row")
    y_count = lax.axis_size("y")
    block_width = panel_lower.shape[1]
    chunk = row_count // CHUNKS

    gathered = [
        lax.all_gather(panel_lower[c * chunk : (c + 1) * chunk], "y", axis=1, tiled=True)
        for c in range(CHUNKS)
    ]

    first = (scale_first.astype(jnp.float32)[:, None] * slab_block.astype(jnp.float32)).astype(
        jnp.bfloat16
    )
    cyclic = lax.all_to_all(
        first.reshape(row_count // groups, groups, col_width), "row", split_axis=1, concat_axis=0, tiled=True
    ).reshape(row_count, col_width)
    scale_cyclic = lax.all_to_all(
        scale_second.reshape(row_count // groups, groups), "row", split_axis=1, concat_axis=0, tiled=True
    ).reshape(row_count)

    half = row_count // 2
    quarter = row_count // 4
    level_one = butterfly(cyclic[:half], cyclic[half:])
    second = (scale_cyclic.astype(jnp.float32)[:, None] * level_one).astype(jnp.bfloat16)
    stored = jnp.concatenate(
        [
            butterfly(second[:quarter], second[quarter:half]),
            butterfly(second[half : half + quarter], second[half + quarter :]),
        ],
        axis=0,
    ).astype(jnp.bfloat16)

    top_count = PANEL_W // groups // X_HI
    top = stored[: top_count * X_HI].reshape(1, X_HI, top_count, col_width)
    send = jnp.broadcast_to(top, (groups, X_HI, top_count, col_width)).reshape(
        groups * X_HI, top_count, col_width
    )
    got = lax.all_to_all(send, ("row", "x_hi"), split_axis=0, concat_axis=0)
    got = got.reshape(groups, X_HI, top_count, col_width)
    upper = jnp.transpose(got, (1, 2, 0, 3)).reshape(X_HI, top_count * groups, col_width)
    mine = lax.axis_index("x_hi")
    upper_own = lax.dynamic_index_in_dim(upper, mine, 0, keepdims=False)
    upper_far = lax.dynamic_index_in_dim(upper, 1 - mine, 0, keepdims=False)

    swap = [(i, X_HI - 1 - i) for i in range(X_HI)]
    out = []
    for c in range(CHUNKS):
        far = jnp.dot(gathered[c], upper_far, preferred_element_type=jnp.float32).astype(jnp.bfloat16)
        came = lax.ppermute(far, "x_hi", swap)
        own = jnp.dot(gathered[c], upper_own, preferred_element_type=jnp.float32)
        base = stored[c * chunk : (c + 1) * chunk].astype(jnp.float32)
        out.append((base - (own + came.astype(jnp.float32))).astype(jnp.bfloat16))
    return jnp.concatenate(out, axis=0)


def solution(mesh):
    rows, cols = mesh.devices.shape
    split = Mesh(mesh.devices.reshape(rows, X_HI, cols // X_HI), ("row", "x_hi", "y"))
    col = ("x_hi", "y")
    placed = (P("row", col), P("row"), P("row"), P("row", col))
    return jax.shard_map(
        per_device, mesh=split, in_specs=placed, out_specs=P("row", col), check_vma=False
    )
```

time: 445 us -> 238 us (0.53)
  the two profiles are of different devices: /device:TPU:8 before, /device:TPU:16 now
where the time goes in v1:
time: 238 us; the launch traced here: 237 us
  waiting for transfers between devices  165 us (69%)
  starting transfers between devices  33.6 us (14%)
  matrix products  15.9 us (7%)
  between operations  13.4 us (6%)
  local copies, waits for them, and re-layouts  9.13 us (4%)
    all_gather x4, waiting for transfers between devices, per_device(): lax.all_gather(panel_lower[c * chunk:(c + 1) * chunk], 'y', axis=1, tiled...  107 us
    all_to_all x1, waiting for transfers between devices, per_device(): got = lax.all_to_all(send, ('row', 'x_hi'), split_axis=0, concat_axis=0)  30.1 us
    all_to_all x1, waiting for transfers between devices, per_device(): lax.all_to_all(first.reshape(row_count // groups, groups, col_width), 'ro...  17.3 us
    ppermute x4, starting transfers between devices, per_device(): came = lax.ppermute(far, 'x_hi', swap)  12.3 us
    dot_general x4, matrix products, per_device(): jnp.dot(gathered[c], upper_far, preferred_element_type=jnp.float32)  11.7 us
    all_to_all x1, starting transfers between devices, per_device(): lax.all_to_all(scale_second.reshape(row_count // groups, groups), 'row',...  11.6 us
    all_to_all x1, waiting for transfers between devices, per_device(): lax.all_to_all(scale_second.reshape(row_count // groups, groups), 'row',...  6.85 us
    all_to_all x1, starting transfers between devices, per_device(): got = lax.all_to_all(send, ('row', 'x_hi'), split_axis=0, concat_axis=0)  5.65 us
  transfers between devices with their start and end apart: 11, of which 7 were waited for; matrix products, arithmetic and copies ran while one was open for 8% of the time, Pallas kernels for 0%

profile of v1, /device:TPU:16, one launch (start us, length us, event | category | flops | bytes accessed | tf_op | source)
XLA Modules:
  0.0 237.5 jit_solution(13325261711682254845)
XLA Ops:
  6.5 2.3 fusion.47
  8.9 0.7 all-gather.7.cloned.1.call-update
  9.7 0.7 all-gather.9.cloned.1.call-update
  10.4 0.7 copy.21
  11.1 11.6 %all-to-all-start = ((bf16[64,32,1]{0,2,1:T(2,128)(2,1)}), bf16[64,32,1]{0,2,1:T(2,128)(2,1)S(1)}, u32[]{:S(2)}, u32[]{:S(2)}) async-start(bf16[64,32,1]{0,2,1:T(2,128)(2,1)} %copy.21), calls=%async_computation | async-start | bytes 32768 | tf_op jit(solution)/shard_map/all_to_all | solution.py:37
  23.1 1.0 copy.22
  24.1 6.9 %all-to-all-done = bf16[64,32,1]{0,2,1:T(2,128)(2,1)S(1)} async-done(((bf16[64,32,1]{0,2,1:T(2,128)(2,1)}), bf16[64,32,1]{0,2,1:T(2,128)(2,1)S(1)}, u32[]{:S(2)}, u32[]{:S(2)}) %all-to-all-start) | async-done | bytes 4128 | tf_op jit(solution)/shard_map/all_to_all | solution.py:37
  31.0 3.9 %all-to-all-start.1 = ((bf16[64,32,128]{2,0,1:T(8,128)(2,1)}), bf16[64,32,128]{2,0,1:T(8,128)(2,1)S(1)}, u32[]{:S(2)}, u32[]{:S(2)}) async-start(bf16[64,32,128]{2,0,1:T(8,128)(2,1)} %copy.22), calls=%async_computation.1 | async-start | bytes 1048576 | tf_op jit(solution)/shard_map/all_to_all | solution.py:34
  35.6 17.3 %all-to-all-done.1 = bf16[64,32,128]{2,0,1:T(8,128)(2,1)S(1)} async-done(((bf16[64,32,128]{2,0,1:T(8,128)(2,1)}), bf16[64,32,128]{2,0,1:T(8,128)(2,1)S(1)}, u32[]{:S(2)}, u32[]{:S(2)}) %all-to-all-start.1) | async-done | bytes 524320 | tf_op jit(solution)/shard_map/all_to_all | solution.py:34
  53.6 0.8 copy-done.4
  54.5 1.3 broadcast_in_dim.10
  55.8 5.6 %all-to-all-start.2 = ((bf16[64,64,128]{2,1,0:T(8,128)(2,1)}), bf16[64,64,128]{2,1,0:T(8,128)(2,1)S(1)}, u32[]{:S(2)}, u32[]{:S(2)}) async-start(bf16[64,64,128]{2,1,0:T(8,128)(2,1)} %bitcast.8), calls=%async_computation.2 | async-start | bytes 2097152 | tf_op jit(solution)/shard_map/all_to_all | solution.py:58
  61.5 30.1 %all-to-all-done.2 = bf16[64,64,128]{2,1,0:T(8,128)(2,1)S(1)} async-done(((bf16[64,64,128]{2,1,0:T(8,128)(2,1)}), bf16[64,64,128]{2,1,0:T(8,128)(2,1)S(1)}, u32[]{:S(2)}, u32[]{:S(2)}) %all-to-all-start.2) | async-done | bytes 1048608 | tf_op jit(solution)/shard_map/all_to_all | solution.py:58
  91.6 0.7 copy.26
  92.3 3.1 %fusion = bf16[512,128]{0,1:T(8,128)(2,1)} fusion(bf16[512,2048]{1,0:T(8,128)(2,1)} %all-gather.5.cloned.1.call-done, bf16[2,2048,128]{2,1,0:T(8,128)(2,1)S(1)} %bitcast.72, s32[]{:T(128)S(6)} %select_n.8), kind=kOutput, calls=%fused_computation.8 | convolution fusion | flops 268500992 | bytes 2752516 | tf_op jit(solution)/shard_map/dot_general | solution.py:68
  95.4 3.7 %collective-permute-start = (bf16[512,128]{0,1:T(8,128)(2,1)}, bf16[512,128]{0,1:T(8,128)(2,1)S(1)}, u32[]{:S(2)}, u32[]{:S(2)}) collective-permute-start(bf16[512,128]{0,1:T(8,128)(2,1)} %fusion), channel_id=1, source_target_pairs={{0,8},{8,0},{1,9},{9,1},{2,10},{10,2},{3,11},{11,3},{4,12},{12,4},... | collective-permute-start | bytes 393224 | tf_op jit(solution)/shard_map/ppermute | solution.py:69
  99.1 16.7 %all-gather.7.cloned.1.call-done = bf16[512,2048]{1,0:T(8,128)(2,1)} async-done(((bf16[512,256]{1,0:T(8,128)(2,1)}), bf16[512,2048]{1,0:T(8,128)(2,1)}) %all-gather.7.cloned.1.call-update) | async-done | bytes 2097168 | tf_op jit(solution)/shard_map/all_gather | solution.py:27
  115.8 3.1 %fusion.1 = bf16[512,128]{0,1:T(8,128)(2,1)} fusion(bf16[512,2048]{1,0:T(8,128)(2,1)} %all-gather.7.cloned.1.call-done, bf16[2,2048,128]{2,1,0:T(8,128)(2,1)S(1)} %bitcast.73, s32[]{:T(128)S(6)} %select_n.8), kind=kOutput, calls=%fused_computation.9 | convolution fusion | flops 268500992 | bytes 2752516 | tf_op jit(solution)/shard_map/dot_general | solution.py:68
  118.8 3.0 %collective-permute-start.1 = (bf16[512,128]{0,1:T(8,128)(2,1)}, bf16[512,128]{0,1:T(8,128)(2,1)S(1)}, u32[]{:S(2)}, u32[]{:S(2)}) collective-permute-start(bf16[512,128]{0,1:T(8,128)(2,1)} %fusion.1), channel_id=1, source_target_pairs={{0,8},{8,0},{1,9},{9,1},{2,10},{10,2},{3,11},{11,3},{4,12},{12,4},... | collective-permute-start | bytes 393224 | tf_op jit(solution)/shard_map/ppermute | solution.py:69
  121.8 45.2 %all-gather.9.cloned.1.call-done = bf16[512,2048]{1,0:T(8,128)(2,1)} async-done(((bf16[512,256]{1,0:T(8,128)(2,1)}), bf16[512,2048]{1,0:T(8,128)(2,1)}) %all-gather.9.cloned.1.call-update) | async-done | bytes 2097168 | tf_op jit(solution)/shard_map/all_gather | solution.py:27
  167.0 3.1 %fusion.2 = bf16[512,128]{0,1:T(8,128)(2,1)} fusion(bf16[512,2048]{1,0:T(8,128)(2,1)} %all-gather.9.cloned.1.call-done, bf16[2,2048,128]{2,1,0:T(8,128)(2,1)S(1)} %bitcast.74, s32[]{:T(128)S(6)} %select_n.8), kind=kOutput, calls=%fused_computation.10 | convolution fusion | flops 268500992 | bytes 2752516 | tf_op jit(solution)/shard_map/dot_general | solution.py:68
  170.1 2.8 %collective-permute-start.2 = (bf16[512,128]{0,1:T(8,128)(2,1)}, bf16[512,128]{0,1:T(8,128)(2,1)}, u32[]{:S(2)}, u32[]{:S(2)}) collective-permute-start(bf16[512,128]{0,1:T(8,128)(2,1)} %fusion.2), channel_id=1, source_target_pairs={{0,8},{8,0},{1,9},{9,1},{2,10},{10,2},{3,11},{11,3},{4,12},{12,4},... | collective-permute-start | bytes 393224 | tf_op jit(solution)/shard_map/ppermute | solution.py:69
  172.9 45.2 %all-gather.11.cloned.1.call-done = bf16[512,2048]{1,0:T(8,128)(2,1)} async-done(((bf16[512,256]{1,0:T(8,128)(2,1)}), bf16[512,2048]{1,0:T(8,128)(2,1)}) %all-gather.11.cloned.1.call-update) | async-done | bytes 2097168 | tf_op jit(solution)/shard_map/all_gather | solution.py:27
  218.1 2.4 %fusion.3 = bf16[512,128]{0,1:T(8,128)(2,1)S(1)} fusion(bf16[512,2048]{1,0:T(8,128)(2,1)} %all-gather.11.cloned.1.call-done, bf16[2,2048,128]{2,1,0:T(8,128)(2,1)S(1)} %bitcast.75, s32[]{:T(128)S(6)} %select_n.8), kind=kOutput, calls=%fused_computation.11 | convolution fusion | flops 268500992 | bytes 2752516 | tf_op jit(solution)/shard_map/dot_general | solution.py:68
  220.5 2.9 %collective-permute-start.3 = (bf16[512,128]{0,1:T(8,128)(2,1)S(1)}, bf16[512,128]{0,1:T(8,128)(2,1)S(1)}, u32[]{:S(2)}, u32[]{:S(2)}) collective-permute-start(bf16[512,128]{0,1:T(8,128)(2,1)S(1)} %fusion.3), channel_id=1, source_target_pairs={{0,8},{8,0},{1,9},{9,1},{2,10},{10,2},{3,11},{11,3},{4,12},{12,4},... | collective-permute-start | bytes 393224 | tf_op jit(solution)/shard_map/ppermute | solution.py:69
  223.5 0.8 subtract_convert_fusion.3
  224.4 0.8 subtract_convert_fusion.2
  225.2 0.7 copy-done.2
  225.9 1.8 subtract_convert_fusion.1
  227.7 1.4 collective-permute-done.3
  229.0 0.9 subtract_convert_fusion
  230.0 1.0 copy.27
  (39 shorter events, 2.1 us)
Async XLA Ops:
  6.5 3.8 %copy-start.7 = (bf16[2048]{0:T(1024)(128)(2,1)S(1)}, bf16[2048]{0:T(1024)(128)(2,1)}, u32[]{:S(2)}) copy-start(bf16[2048]{0:T(1024)(128)(2,1)} %param.6) | copy-start | bytes 12292
  6.5 16.2 %copy-start.8 = (bf16[2048]{0:T(1024)(128)(2,1)S(1)}, bf16[2048]{0:T(1024)(128)(2,1)}, u32[]{:S(2)}) copy-start(bf16[2048]{0:T(1024)(128)(2,1)} %param.5) | copy-start | bytes 12292
  6.5 16.3 %copy-start.6 = (bf16[2048,128]{1,0:T(8,128)(2,1)S(1)}, bf16[2048,128]{1,0:T(8,128)(2,1)}, u32[]{:S(2)}) copy-start(bf16[2048,128]{1,0:T(8,128)(2,1)} %param.4) | copy-start | bytes 1572868
  6.5 85.8 %all-gather.5.cloned.1.call-start = ((), (), s32[]{:S(2)}) async-start(), calls=%async_computation.3 | async-start | bytes 2359296 | tf_op jit(solution)/shard_map/all_gather | solution.py:27
  8.9 106.9 %all-gather.7.cloned.1.call-start = ((), (), s32[]{:S(2)}) async-start(), calls=%async_computation.4 | async-start | bytes 2359296 | tf_op jit(solution)/shard_map/all_gather | solution.py:27
  9.6 157.4 %all-gather.9.cloned.1.call-start = ((), (), s32[]{:S(2)}) async-start(), calls=%async_computation.5 | async-start | bytes 2359296 | tf_op jit(solution)/shard_map/all_gather | solution.py:27
  11.1 19.9 %all-to-all-start = ((bf16[64,32,1]{0,2,1:T(2,128)(2,1)}), bf16[64,32,1]{0,2,1:T(2,128)(2,1)S(1)}, u32[]{:S(2)}, u32[]{:S(2)}) async-start(bf16[64,32,1]{0,2,1:T(2,128)(2,1)} %copy.21), calls=%async_computation | async-start | bytes 32768 | tf_op jit(solution)/shard_map/all_to_all | solution.py:37
  31.0 21.9 %all-to-all-start.1 = ((bf16[64,32,128]{2,0,1:T(8,128)(2,1)}), bf16[64,32,128]{2,0,1:T(8,128)(2,1)S(1)}, u32[]{:S(2)}, u32[]{:S(2)}) async-start(bf16[64,32,128]{2,0,1:T(8,128)(2,1)} %copy.22), calls=%async_computation.1 | async-start | bytes 1048576 | tf_op jit(solution)/shard_map/all_to_all | solution.py:34
  34.9 183.2 %all-gather.11.cloned.1.call-start = ((), (), s32[]{:S(2)}) async-start(), calls=%async_computation.6 | async-start | bytes 2359296 | tf_op jit(solution)/shard_map/all_gather | solution.py:27
  53.5 0.8 copy-start.4
  55.8 35.8 %all-to-all-start.2 = ((bf16[64,64,128]{2,1,0:T(8,128)(2,1)}), bf16[64,64,128]{2,1,0:T(8,128)(2,1)S(1)}, u32[]{:S(2)}, u32[]{:S(2)}) async-start(bf16[64,64,128]{2,1,0:T(8,128)(2,1)} %bitcast.8), calls=%async_computation.2 | async-start | bytes 2097152 | tf_op jit(solution)/shard_map/all_to_all | solution.py:58
  95.4 128.1 %collective-permute-start = (bf16[512,128]{0,1:T(8,128)(2,1)}, bf16[512,128]{0,1:T(8,128)(2,1)S(1)}, u32[]{:S(2)}, u32[]{:S(2)}) collective-permute-start(bf16[512,128]{0,1:T(8,128)(2,1)} %fusion), channel_id=1, source_target_pairs={{0,8},{8,0},{1,9},{9,1},{2,10},{10,2},{3,11},{11,3},{4,12},{12,4},... | collective-permute-start | bytes 393224 | tf_op jit(solution)/shard_map/ppermute | solution.py:69
  118.8 104.6 %copy-start = (bf16[512,2048]{1,0:T(8,128)(2,1)S(1)}, bf16[512,2048]{1,0:T(8,128)(2,1)}, u32[]{:S(2)}) copy-start(bf16[512,2048]{1,0:T(8,128)(2,1)} %all-gather.5.cloned.1.call-done) | copy-start | bytes 6291460
  118.8 105.5 %collective-permute-start.1 = (bf16[512,128]{0,1:T(8,128)(2,1)}, bf16[512,128]{0,1:T(8,128)(2,1)S(1)}, u32[]{:S(2)}, u32[]{:S(2)}) collective-permute-start(bf16[512,128]{0,1:T(8,128)(2,1)} %fusion.1), channel_id=1, source_target_pairs={{0,8},{8,0},{1,9},{9,1},{2,10},{10,2},{3,11},{11,3},{4,12},{12,4},... | collective-permute-start | bytes 393224 | tf_op jit(solution)/shard_map/ppermute | solution.py:69
  170.1 55.1 %collective-permute-start.2 = (bf16[512,128]{0,1:T(8,128)(2,1)}, bf16[512,128]{0,1:T(8,128)(2,1)}, u32[]{:S(2)}, u32[]{:S(2)}) collective-permute-start(bf16[512,128]{0,1:T(8,128)(2,1)} %fusion.2), channel_id=1, source_target_pairs={{0,8},{8,0},{1,9},{9,1},{2,10},{10,2},{3,11},{11,3},{4,12},{12,4},... | collective-permute-start | bytes 393224 | tf_op jit(solution)/shard_map/ppermute | solution.py:69
  220.5 3.8 %copy-start.1 = (bf16[512,2048]{1,0:T(8,128)(2,1)S(1)}, bf16[512,2048]{1,0:T(8,128)(2,1)}, u32[]{:S(2)}) copy-start(bf16[512,2048]{1,0:T(8,128)(2,1)} %all-gather.7.cloned.1.call-done) | copy-start | bytes 6291460
  220.5 3.8 %copy-start.5 = (bf16[2048,128]{0,1:T(8,128)(2,1)S(1)}, bf16[2048,128]{0,1:T(8,128)(2,1)}, u32[]{:S(2)}) copy-start(bf16[2048,128]{0,1:T(8,128)(2,1)} %copy-done.4) | copy-start | bytes 1572868
  220.5 8.5 %collective-permute-start.3 = (bf16[512,128]{0,1:T(8,128)(2,1)S(1)}, bf16[512,128]{0,1:T(8,128)(2,1)S(1)}, u32[]{:S(2)}, u32[]{:S(2)}) collective-permute-start(bf16[512,128]{0,1:T(8,128)(2,1)S(1)} %fusion.3), channel_id=1, source_target_pairs={{0,8},{8,0},{1,9},{9,1},{2,10},{10,2},{3,11},{11,3},{4,12},{12,4},... | collective-permute-start | bytes 393224 | tf_op jit(solution)/shard_map/ppermute | solution.py:69
  224.3 1.6 copy-start.2
  225.2 3.8 %copy-start.3 = (bf16[512,2048]{1,0:T(8,128)(2,1)S(1)}, bf16[512,2048]{1,0:T(8,128)(2,1)}, u32[]{:S(2)}) copy-start(bf16[512,2048]{1,0:T(8,128)(2,1)} %all-gather.11.cloned.1.call-done) | copy-start | bytes 6291460
Sparse Core Ops, SparseCore 0:
  9.4 55.1 all-gather.4
  66.6 49.1 all-gather.6
  117.8 49.2 all-gather.8
  168.9 49.1 all-gather.10

commit v2 on v1

v2 whole, which is shorter than its diff:
```python
import jax
import jax.numpy as jnp
from jax import lax
from jax.experimental import pallas as pl
from jax.experimental.pallas import tpu as pltpu
from jax.sharding import Mesh, PartitionSpec as P

PANEL_W = 4096
X_HI = 2
PAD = 8
TILE_M = 256

inv_root = 0.7071067811865476


def butterfly(top, bottom):
    top = top.astype(jnp.float32)
    bottom = bottom.astype(jnp.float32)
    return jnp.concatenate([(top + bottom) * inv_root, (top - bottom) * inv_root], axis=0)


def product_body(offsets, place_ref, upper_ref, stored_ref, *refs):
    blocks, (far_ref, rest_ref) = refs[:-2], refs[-2:]
    y_count = upper_ref.shape[0]
    total = jnp.zeros((blocks[0].shape[0], upper_ref.shape[2]), jnp.float32)
    for offset, block in zip(offsets, blocks):
        rows = upper_ref[(place_ref[1] + offset + y_count) % y_count]
        total += jnp.dot(block[...], rows, preferred_element_type=jnp.float32)
    width = far_ref.shape[1]
    left, right = total[:, :width], total[:, width:]
    at_left = place_ref[0] == 0
    far_ref[...] = jnp.where(at_left, right, left).astype(far_ref.dtype)
    rest_ref[...] = stored_ref[...].astype(jnp.float32) - jnp.where(at_left, left, right)


def products(place, upper, stored, blocks):
    offsets = tuple(offset for offset, _ in blocks)
    rows, depth = blocks[0][1].shape
    width = stored.shape[1]
    tile = lambda i, place: (i, 0)
    return pl.pallas_call(
        lambda *refs: product_body(offsets, *refs),
        grid_spec=pltpu.PrefetchScalarGridSpec(
            num_scalar_prefetch=1,
            grid=(rows // TILE_M,),
            in_specs=[
                pl.BlockSpec(upper.shape, lambda i, place: (0, 0, 0)),
                pl.BlockSpec((TILE_M, width), tile),
                *[pl.BlockSpec((TILE_M, depth), tile) for _ in blocks],
            ],
            out_specs=[pl.BlockSpec((TILE_M, width), tile), pl.BlockSpec((TILE_M, width), tile)],
        ),
        out_shape=[
            jax.ShapeDtypeStruct((rows, width), jnp.bfloat16),
            jax.ShapeDtypeStruct((rows, width), jnp.float32),
        ],
        name="products",
    )(place, upper, stored, *[block for _, block in blocks])


def per_device(slab_block, scale_first, scale_second, panel_lower):
    row_count, col_width = slab_block.shape
    groups = lax.axis_size("row")
    y_count = lax.axis_size("y")
    block_width = panel_lower.shape[1]
    share = row_count // groups
    half = row_count // 2
    quarter = row_count // 4

    up = [(i, (i + 1) % y_count) for i in range(y_count)]
    down = [(i, (i - 1) % y_count) for i in range(y_count)]
    halves = [panel_lower[:half], panel_lower[half:]]
    held = [[(0, halves[0])], [(0, halves[1])]]
    moving = {(0, -1): halves[0], (1, 1): halves[1], (1, -1): halves[1], (0, 1): halves[0]}
    steps = []
    for distance in range(1, y_count // 2 + 1):
        last = 2 * distance == y_count
        keys = ((0, -1), (1, 1)) if last else tuple(moving)
        for part, sign in keys:
            moving[part, sign] = lax.ppermute(moving[part, sign], "y", up if sign < 0 else down)
        steps.append({key: moving[key] for key in keys})

    first = (scale_first.astype(jnp.float32)[:, None] * slab_block.astype(jnp.float32)).astype(
        jnp.bfloat16
    )
    scale_rows = jnp.pad(
        jnp.transpose(scale_second.reshape(share, groups))[None], ((0, PAD - 1), (0, 0), (0, col_width - share))
    )
    packed = jnp.concatenate([first.reshape(share, groups, col_width), scale_rows], axis=0)
    packed = lax.all_to_all(packed, "row", split_axis=1, concat_axis=0, tiled=True)
    packed, steps[0] = lax.optimization_barrier((packed, steps[0]))
    packed = packed.reshape(groups, share + PAD, col_width)
    cyclic = packed[:, :share].reshape(row_count, col_width)
    scale_cyclic = packed[:, share, :share].reshape(row_count)

    level_one = butterfly(cyclic[:half], cyclic[half:])
    second = (scale_cyclic.astype(jnp.float32)[:, None] * level_one).astype(jnp.bfloat16)
    stored = jnp.concatenate(
        [
            butterfly(second[:quarter], second[quarter:half]),
            butterfly(second[half : half + quarter], second[half + quarter :]),
        ],
        axis=0,
    ).astype(jnp.bfloat16)

    top_count = PANEL_W // groups // X_HI
    top = stored[: top_count * X_HI].reshape(1, X_HI, top_count, col_width)
    send = jnp.broadcast_to(top, (groups, X_HI, top_count, col_width)).reshape(
        groups * X_HI, top_count, col_width
    )
    got = lax.all_to_all(send, ("row", "x_hi"), split_axis=0, concat_axis=0)
    got, steps[1], steps[2] = lax.optimization_barrier((got, steps[1], steps[2]))
    got = got.reshape(groups, X_HI, top_count, col_width)
    upper = jnp.transpose(got, (2, 0, 1, 3)).reshape(y_count, block_width, X_HI * col_width)

    for distance, step in enumerate(steps, 1):
        for (part, sign), block in step.items():
            held[part].append((sign * distance, block))

    place = jnp.stack([lax.axis_index("x_hi"), lax.axis_index("y")]).astype(jnp.int32)
    swap = [(i, X_HI - 1 - i) for i in range(X_HI)]
    out = []
    for part in range(2):
        far, rest = products(place, upper, stored[part * half : (part + 1) * half], held[part])
        came = lax.ppermute(far, "x_hi", swap)
        out.append((rest - came.astype(jnp.float32)).astype(jnp.bfloat16))
    return jnp.concatenate(out, axis=0)


def solution(mesh):
    rows, cols = mesh.devices.shape
    split = Mesh(mesh.devices.reshape(rows, X_HI, cols // X_HI), ("row", "x_hi", "y"))
    col = ("x_hi", "y")
    placed = (P("row", col), P("row"), P("row"), P("row", col))
    return jax.shard_map(
        per_device, mesh=split, in_specs=placed, out_specs=P("row", col), check_vma=False
    )
```

time: 238 us -> 153 us (0.64)
  the two profiles are of different devices: /device:TPU:16 before, /device:TPU:24 now
where the time goes in v2:
time: 153 us; the launch traced here: 152 us
  starting transfers between devices  72.1 us (47%)
  waiting for transfers between devices  54.4 us (36%)
  Pallas kernels  12.3 us (8%)
  local copies, waits for them, and re-layouts  7.5 us (5%)
  other arithmetic  5.82 us (4%)
    ppermute x14, waiting for transfers between devices, per_device(): lax.ppermute(moving[part, sign], 'y', up if sign < 0 else down)  45.9 us
    ppermute x14, starting transfers between devices, per_device(): lax.ppermute(moving[part, sign], 'y', up if sign < 0 else down)  42.8 us
    pallas_call x2, Pallas kernels, products(): pl.pallas_call(lambda *refs: product_body(offsets, *refs), grid_spec=pltp...  12.3 us
    all_to_all x1, starting transfers between devices, per_device(): lax.all_to_all(packed, 'row', split_axis=1, concat_axis=0, tiled=True)  11.6 us
    all_to_all x1, starting transfers between devices, per_device(): got = lax.all_to_all(send, ('row', 'x_hi'), split_axis=0, concat_axis=0)  10.2 us
    ppermute x2, waiting for transfers between devices, per_device(): came = lax.ppermute(far, 'x_hi', swap)  8.5 us
    ppermute x2, starting transfers between devices, per_device(): came = lax.ppermute(far, 'x_hi', swap)  7.46 us
  transfers between devices with their start and end apart: 18, of which 13 were waited for; matrix products, arithmetic and copies ran while one was open for 3% of the time, Pallas kernels for 8%

profile of v2, /device:TPU:24, one launch (start us, length us, event | category | flops | bytes accessed | tf_op | source)
XLA Modules:
  0.0 152.5 jit_solution(7074537836078666672)
XLA Ops:
  4.0 11.6 %all-to-all-start = ((bf16[72,32,128]{2,0,1:T(8,128)(2,1)}), bf16[72,32,128]{2,0,1:T(8,128)(2,1)S(1)}, u32[]{:S(2)}, u32[]{:S(2)}) async-start(bf16[72,32,128]{2,0,1:T(8,128)(2,1)} %copy.12), calls=%async_computation | async-start | bytes 1179648 | tf_op jit(solution)/shard_map/all_to_all | solution.py:90
  15.8 4.7 %collective-permute-start = (bf16[1024,256]{1,0:T(8,128)(2,1)S(1)}, bf16[1024,256]{1,0:T(8,128)(2,1)S(1)}, u32[]{:S(2)}, u32[]{:S(2)}) collective-permute-start(bf16[1024,256]{1,0:T(8,128)(2,1)S(1)} %get-tuple-element.42.refs_3_), channel_id=1, source_target_pairs={{0,1},{1,2},{2,3},{3,4},{4,5},{5,6},{6,7},{7,0},{8,9},{9,10},{10,1... | collective-permute-start | bytes 1572872 | tf_op jit(solution)/shard_map/ppermute | solution.py:80
  20.5 1.9 %collective-permute-start.1 = (bf16[1024,256]{1,0:T(8,128)(2,1)S(1)}, bf16[1024,256]{1,0:T(8,128)(2,1)S(1)}, u32[]{:S(2)}, u32[]{:S(2)}) collective-permute-start(bf16[1024,256]{1,0:T(8,128)(2,1)S(1)} %get-tuple-element.42.refs_3_), channel_id=1, source_target_pairs={{0,7},{1,0},{2,1},{3,2},{4,3},{5,4},{6,5},{7,6},{8,15},{9,8},{10,9... | collective-permute-start | bytes 1572872 | tf_op jit(solution)/shard_map/ppermute | solution.py:80
  22.4 5.1 %collective-permute-start.2 = (bf16[1024,256]{1,0:T(8,128)(2,1)S(1)}, bf16[1024,256]{1,0:T(8,128)(2,1)S(1)}, u32[]{:S(2)}, u32[]{:S(2)}) collective-permute-start(bf16[1024,256]{1,0:T(8,128)(2,1)S(1)} %get-tuple-element.41.refs_3_), channel_id=1, source_target_pairs={{0,1},{1,2},{2,3},{3,4},{4,5},{5,6},{6,7},{7,0},{8,9},{9,10},{10,1... | collective-permute-start | bytes 1572872 | tf_op jit(solution)/shard_map/ppermute | solution.py:80
  27.6 1.9 %collective-permute-start.3 = (bf16[1024,256]{1,0:T(8,128)(2,1)S(1)}, bf16[1024,256]{1,0:T(8,128)(2,1)S(1)}, u32[]{:S(2)}, u32[]{:S(2)}) collective-permute-start(bf16[1024,256]{1,0:T(8,128)(2,1)S(1)} %get-tuple-element.41.refs_3_), channel_id=1, source_target_pairs={{0,7},{1,0},{2,1},{3,2},{4,3},{5,4},{6,5},{7,6},{8,15},{9,8},{10,9... | collective-permute-start | bytes 1572872 | tf_op jit(solution)/shard_map/ppermute | solution.py:80
  29.5 3.2 %collective-permute-done.refs_4_ = bf16[1024,256]{1,0:T(8,128)(2,1)S(1)} collective-permute-done((bf16[1024,256]{1,0:T(8,128)(2,1)S(1)}, bf16[1024,256]{1,0:T(8,128)(2,1)S(1)}, u32[]{:S(2)}, u32[]{:S(2)}) %collective-permute-start) | collective-permute-done | bytes 524320 | tf_op jit(solution)/shard_map/ppermute | solution.py:80
  32.7 5.6 %collective-permute-done.1.refs_5_ = bf16[1024,256]{1,0:T(8,128)(2,1)S(1)} collective-permute-done((bf16[1024,256]{1,0:T(8,128)(2,1)S(1)}, bf16[1024,256]{1,0:T(8,128)(2,1)S(1)}, u32[]{:S(2)}, u32[]{:S(2)}) %collective-permute-start.1) | collective-permute-done | bytes 524320 | tf_op jit(solution)/shard_map/ppermute | solution.py:80
  38.4 4.9 %collective-permute-done.2.refs_4_ = bf16[1024,256]{1,0:T(8,128)(2,1)S(1)} collective-permute-done((bf16[1024,256]{1,0:T(8,128)(2,1)S(1)}, bf16[1024,256]{1,0:T(8,128)(2,1)S(1)}, u32[]{:S(2)}, u32[]{:S(2)}) %collective-permute-start.2) | collective-permute-done | bytes 524320 | tf_op jit(solution)/shard_map/ppermute | solution.py:80
  43.3 5.3 %collective-permute-done.3.refs_5_ = bf16[1024,256]{1,0:T(8,128)(2,1)S(1)} collective-permute-done((bf16[1024,256]{1,0:T(8,128)(2,1)S(1)}, bf16[1024,256]{1,0:T(8,128)(2,1)S(1)}, u32[]{:S(2)}, u32[]{:S(2)}) %collective-permute-start.3) | collective-permute-done | bytes 524320 | tf_op jit(solution)/shard_map/ppermute | solution.py:80
  51.5 10.2 %all-to-all-start.1 = ((bf16[64,64,128]{2,1,0:T(8,128)(2,1)}), bf16[64,64,128]{2,1,0:T(8,128)(2,1)S(1)}, u32[]{:S(2)}, u32[]{:S(2)}) async-start(bf16[64,64,128]{2,1,0:T(8,128)(2,1)} %bitcast.12), calls=%async_computation.1 | async-start | bytes 2097152 | tf_op jit(solution)/shard_map/all_to_all | solution.py:111
  61.7 1.9 %collective-permute-start.4 = (bf16[1024,256]{1,0:T(8,128)(2,1)S(1)}, bf16[1024,256]{1,0:T(8,128)(2,1)S(1)}, u32[]{:S(2)}, u32[]{:S(2)}) collective-permute-start(bf16[1024,256]{1,0:T(8,128)(2,1)S(1)} %copy-done.10), channel_id=1, source_target_pairs={{0,1},{1,2},{2,3},{3,4},{4,5},{5,6},{6,7},{7,0},{8,9},{9,10},{10,1... | collective-permute-start | bytes 1572872 | tf_op jit(solution)/shard_map/ppermute | solution.py:80
  63.6 3.9 %collective-permute-start.7 = (bf16[1024,256]{1,0:T(8,128)(2,1)S(1)}, bf16[1024,256]{1,0:T(8,128)(2,1)S(1)}, u32[]{:S(2)}, u32[]{:S(2)}) collective-permute-start(bf16[1024,256]{1,0:T(8,128)(2,1)S(1)} %copy-done.8), channel_id=1, source_target_pairs={{0,7},{1,0},{2,1},{3,2},{4,3},{5,4},{6,5},{7,6},{8,15},{9,8},{10,9... | collective-permute-start | bytes 1572872 | tf_op jit(solution)/shard_map/ppermute | solution.py:80
  67.6 3.1 %collective-permute-start.6 = (bf16[1024,256]{1,0:T(8,128)(2,1)S(1)}, bf16[1024,256]{1,0:T(8,128)(2,1)}, u32[]{:S(2)}, u32[]{:S(2)}) collective-permute-start(bf16[1024,256]{1,0:T(8,128)(2,1)S(1)} %copy-done.6), channel_id=1, source_target_pairs={{0,1},{1,2},{2,3},{3,4},{4,5},{5,6},{6,7},{7,0},{8,9},{9,10},{10,1... | collective-permute-start | bytes 1572872 | tf_op jit(solution)/shard_map/ppermute | solution.py:80
  70.7 2.7 %collective-permute-start.5 = (bf16[1024,256]{1,0:T(8,128)(2,1)}, bf16[1024,256]{1,0:T(8,128)(2,1)}, u32[]{:S(2)}, u32[]{:S(2)}) collective-permute-start(bf16[1024,256]{1,0:T(8,128)(2,1)} %copy-done.11), channel_id=1, source_target_pairs={{0,7},{1,0},{2,1},{3,2},{4,3},{5,4},{6,5},{7,6},{8,15},{9,8},{10,9... | collective-permute-start | bytes 1572872 | tf_op jit(solution)/shard_map/ppermute | solution.py:80
  73.4 4.9 %collective-permute-done.4.refs_6_ = bf16[1024,256]{1,0:T(8,128)(2,1)S(1)} collective-permute-done((bf16[1024,256]{1,0:T(8,128)(2,1)S(1)}, bf16[1024,256]{1,0:T(8,128)(2,1)S(1)}, u32[]{:S(2)}, u32[]{:S(2)}) %collective-permute-start.4) | collective-permute-done | bytes 524320 | tf_op jit(solution)/shard_map/ppermute | solution.py:80
  78.3 3.1 %collective-permute-start.8 = (bf16[1024,256]{1,0:T(8,128)(2,1)S(1)}, bf16[1024,256]{1,0:T(8,128)(2,1)}, u32[]{:S(2)}, u32[]{:S(2)}) collective-permute-start(bf16[1024,256]{1,0:T(8,128)(2,1)S(1)} %collective-permute-done.4.refs_6_), channel_id=1, source_target_pairs={{0,1},{1,2},{2,3},{3,4},{4,5},{5,6},{6,7},{7,0},{8,9},{9,10},{10,1... | collective-permute-start | bytes 1572872 | tf_op jit(solution)/shard_map/ppermute | solution.py:80
  81.5 2.7 %collective-permute-start.11 = (bf16[1024,256]{1,0:T(8,128)(2,1)S(1)}, bf16[1024,256]{1,0:T(8,128)(2,1)S(1)}, u32[]{:S(2)}, u32[]{:S(2)}) collective-permute-start(bf16[1024,256]{1,0:T(8,128)(2,1)S(1)} %collective-permute-done.7.refs_7_), channel_id=1, source_target_pairs={{0,7},{1,0},{2,1},{3,2},{4,3},{5,4},{6,5},{7,6},{8,15},{9,8},{10,9... | collective-permute-start | bytes 1572872 | tf_op jit(solution)/shard_map/ppermute | solution.py:80
  84.2 5.4 %collective-permute-done.6.refs_6_ = bf16[1024,256]{1,0:T(8,128)(2,1)} collective-permute-done((bf16[1024,256]{1,0:T(8,128)(2,1)S(1)}, bf16[1024,256]{1,0:T(8,128)(2,1)}, u32[]{:S(2)}, u32[]{:S(2)}) %collective-permute-start.6) | collective-permute-done | bytes 524320 | tf_op jit(solution)/shard_map/ppermute | solution.py:80
  89.7 3.1 %collective-permute-start.10 = (bf16[1024,256]{1,0:T(8,128)(2,1)}, bf16[1024,256]{1,0:T(8,128)(2,1)S(1)}, u32[]{:S(2)}, u32[]{:S(2)}) collective-permute-start(bf16[1024,256]{1,0:T(8,128)(2,1)} %collective-permute-done.6.refs_6_), channel_id=1, source_target_pairs={{0,1},{1,2},{2,3},{3,4},{4,5},{5,6},{6,7},{7,0},{8,9},{9,10},{10,1... | collective-permute-start | bytes 1572872 | tf_op jit(solution)/shard_map/ppermute | solution.py:80
  92.8 2.7 %collective-permute-start.9 = (bf16[1024,256]{1,0:T(8,128)(2,1)}, bf16[1024,256]{1,0:T(8,128)(2,1)S(1)}, u32[]{:S(2)}, u32[]{:S(2)}) collective-permute-start(bf16[1024,256]{1,0:T(8,128)(2,1)} %collective-permute-done.5.refs_7_), channel_id=1, source_target_pairs={{0,7},{1,0},{2,1},{3,2},{4,3},{5,4},{6,5},{7,6},{8,15},{9,8},{10,9... | collective-permute-start | bytes 1572872 | tf_op jit(solution)/shard_map/ppermute | solution.py:80
  95.6 5.3 %collective-permute-done.8.refs_8_ = bf16[1024,256]{1,0:T(8,128)(2,1)} collective-permute-done((bf16[1024,256]{1,0:T(8,128)(2,1)S(1)}, bf16[1024,256]{1,0:T(8,128)(2,1)}, u32[]{:S(2)}, u32[]{:S(2)}) %collective-permute-start.8) | collective-permute-done | bytes 524320 | tf_op jit(solution)/shard_map/ppermute | solution.py:80
  100.9 3.1 %collective-permute-start.12 = (bf16[1024,256]{1,0:T(8,128)(2,1)}, bf16[1024,256]{1,0:T(8,128)(2,1)}, u32[]{:S(2)}, u32[]{:S(2)}) collective-permute-start(bf16[1024,256]{1,0:T(8,128)(2,1)} %collective-permute-done.8.refs_8_), channel_id=1, source_target_pairs={{0,1},{1,2},{2,3},{3,4},{4,5},{5,6},{6,7},{7,0},{8,9},{9,10},{10,1... | collective-permute-start | bytes 1572872 | tf_op jit(solution)/shard_map/ppermute | solution.py:80
  104.0 2.8 %collective-permute-start.14 = (bf16[1024,256]{1,0:T(8,128)(2,1)S(1)}, bf16[1024,256]{1,0:T(8,128)(2,1)}, u32[]{:S(2)}, u32[]{:S(2)}) collective-permute-start(bf16[1024,256]{1,0:T(8,128)(2,1)S(1)} %collective-permute-done.11.refs_9_), channel_id=1, source_target_pairs={{0,7},{1,0},{2,1},{3,2},{4,3},{5,4},{6,5},{7,6},{8,15},{9,8},{10,9... | collective-permute-start | bytes 1572872 | tf_op jit(solution)/shard_map/ppermute | solution.py:80
  108.2 3.9 %collective-permute-done.10.refs_8_ = bf16[1024,256]{1,0:T(8,128)(2,1)S(1)} collective-permute-done((bf16[1024,256]{1,0:T(8,128)(2,1)}, bf16[1024,256]{1,0:T(8,128)(2,1)S(1)}, u32[]{:S(2)}, u32[]{:S(2)}) %collective-permute-start.10) | collective-permute-done | bytes 524320 | tf_op jit(solution)/shard_map/ppermute | solution.py:80
  112.1 3.1 %collective-permute-done.9.refs_9_ = bf16[1024,256]{1,0:T(8,128)(2,1)S(1)} collective-permute-done((bf16[1024,256]{1,0:T(8,128)(2,1)}, bf16[1024,256]{1,0:T(8,128)(2,1)S(1)}, u32[]{:S(2)}, u32[]{:S(2)}) %collective-permute-start.9) | collective-permute-done | bytes 524320 | tf_op jit(solution)/shard_map/ppermute | solution.py:80
  117.1 1.5 reshape.44.refs_1_
  118.6 3.9 %collective-permute-done.12.refs_10_ = bf16[1024,256]{1,0:T(8,128)(2,1)} collective-permute-done((bf16[1024,256]{1,0:T(8,128)(2,1)}, bf16[1024,256]{1,0:T(8,128)(2,1)}, u32[]{:S(2)}, u32[]{:S(2)}) %collective-permute-start.12) | collective-permute-done | bytes 524320 | tf_op jit(solution)/shard_map/ppermute | solution.py:80
  122.5 6.1 %products.2 = (bf16[1024,128]{1,0:T(8,128)(2,1)}, f32[1024,128]{1,0:T(8,128)}) custom-call(s32[2]{0:T(128)} %pad_add_fusion.refs_0_, bf16[8,256,256]{2,1,0:T(8,128)(2,1)} %reshape.44.refs_1_, bf16[1024,128]{1,0:T(8,128)(2,1)} %pad_maximum_fusion.1.refs_2_, bf16[1024,256]{1,0:T(8,128)(2,1)} %copy-done.1, bf16[1024,256]{1,0:T(8,128)(2,1)} %copy-done.9, ...), custom_call_target="tpu_custom_call" | custom-call | tf_op jit(solution)/shard_map/products/pallas_call | solution.py:41
  128.6 5.1 %collective-permute-start.13 = (bf16[1024,128]{1,0:T(8,128)(2,1)}, bf16[1024,128]{1,0:T(8,128)(2,1)S(1)}, u32[]{:S(2)}, u32[]{:S(2)}) collective-permute-start(bf16[1024,128]{1,0:T(8,128)(2,1)} %get-tuple-element.32), channel_id=1, source_target_pairs={{0,8},{8,0},{1,9},{9,1},{2,10},{10,2},{3,11},{11,3},{4,12},{12,4},... | collective-permute-start | bytes 786440 | tf_op jit(solution)/shard_map/ppermute | solution.py:125
  134.4 6.2 %products.3 = (bf16[1024,128]{1,0:T(8,128)(2,1)}, f32[1024,128]{1,0:T(8,128)}) custom-call(s32[2]{0:T(128)} %pad_add_fusion.refs_0_, bf16[8,256,256]{2,1,0:T(8,128)(2,1)} %reshape.44.refs_1_, bf16[1024,128]{1,0:T(8,128)(2,1)} %pad_maximum_fusion.2.refs_2_, bf16[1024,256]{1,0:T(8,128)(2,1)} %copy-done, bf16[1024,256]{1,0:T(8,128)(2,1)} %copy-done.5, ...), custom_call_target="tpu_custom_call" | custom-call | tf_op jit(solution)/shard_map/products/pallas_call | solution.py:41
  140.6 2.4 %collective-permute-start.15 = (bf16[1024,128]{1,0:T(8,128)(2,1)}, bf16[1024,128]{1,0:T(8,128)(2,1)S(1)}, u32[]{:S(2)}, u32[]{:S(2)}) collective-permute-start(bf16[1024,128]{1,0:T(8,128)(2,1)} %get-tuple-element.40), channel_id=1, source_target_pairs={{0,8},{8,0},{1,9},{9,1},{2,10},{10,2},{3,11},{11,3},{4,12},{12,4},... | collective-permute-start | bytes 786440 | tf_op jit(solution)/shard_map/ppermute | solution.py:125
  143.1 8.5 %collective-permute-done.15 = bf16[1024,128]{1,0:T(8,128)(2,1)S(1)} collective-permute-done((bf16[1024,128]{1,0:T(8,128)(2,1)}, bf16[1024,128]{1,0:T(8,128)(2,1)S(1)}, u32[]{:S(2)}, u32[]{:S(2)}) %collective-permute-start.15) | collective-permute-done | bytes 262176 | tf_op jit(solution)/shard_map/ppermute | solution.py:125
  (62 shorter events, 11.9 us)
Async XLA Ops:
  3.0 12.7 %copy-start.2 = (bf16[2048,256]{1,0:T(8,128)(2,1)S(1)}, bf16[2048,256]{1,0:T(8,128)(2,1)}, u32[]{:S(2)}) copy-start(bf16[2048,256]{1,0:T(8,128)(2,1)} %param.7) | copy-start | bytes 3145732
  4.0 44.6 %all-to-all-start = ((bf16[72,32,128]{2,0,1:T(8,128)(2,1)}), bf16[72,32,128]{2,0,1:T(8,128)(2,1)S(1)}, u32[]{:S(2)}, u32[]{:S(2)}) async-start(bf16[72,32,128]{2,0,1:T(8,128)(2,1)} %copy.12), calls=%async_computation | async-start | bytes 1179648 | tf_op jit(solution)/shard_map/all_to_all | solution.py:90
  15.8 34.3 %copy-start = (bf16[1024,256]{1,0:T(8,128)(2,1)}, bf16[1024,256]{1,0:T(8,128)(2,1)S(1)}, u32[]{:S(2)}) copy-start(bf16[1024,256]{1,0:T(8,128)(2,1)S(1)} %get-tuple-element.41.refs_3_) | copy-start | bytes 1572868
  15.8 34.3 %copy-start.1 = (bf16[1024,256]{1,0:T(8,128)(2,1)}, bf16[1024,256]{1,0:T(8,128)(2,1)S(1)}, u32[]{:S(2)}) copy-start(bf16[1024,256]{1,0:T(8,128)(2,1)S(1)} %get-tuple-element.42.refs_3_) | copy-start | bytes 1572868
  15.8 16.9 %collective-permute-start = (bf16[1024,256]{1,0:T(8,128)(2,1)S(1)}, bf16[1024,256]{1,0:T(8,128)(2,1)S(1)}, u32[]{:S(2)}, u32[]{:S(2)}) collective-permute-start(bf16[1024,256]{1,0:T(8,128)(2,1)S(1)} %get-tuple-element.42.refs_3_), channel_id=1, source_target_pairs={{0,1},{1,2},{2,3},{3,4},{4,5},{5,6},{6,7},{7,0},{8,9},{9,10},{10,1... | collective-permute-start | bytes 1572872 | tf_op jit(solution)/shard_map/ppermute | solution.py:80
  20.5 17.9 %collective-permute-start.1 = (bf16[1024,256]{1,0:T(8,128)(2,1)S(1)}, bf16[1024,256]{1,0:T(8,128)(2,1)S(1)}, u32[]{:S(2)}, u32[]{:S(2)}) collective-permute-start(bf16[1024,256]{1,0:T(8,128)(2,1)S(1)} %get-tuple-element.42.refs_3_), channel_id=1, source_target_pairs={{0,7},{1,0},{2,1},{3,2},{4,3},{5,4},{6,5},{7,6},{8,15},{9,8},{10,9... | collective-permute-start | bytes 1572872 | tf_op jit(solution)/shard_map/ppermute | solution.py:80
  22.4 20.9 %collective-permute-start.2 = (bf16[1024,256]{1,0:T(8,128)(2,1)S(1)}, bf16[1024,256]{1,0:T(8,128)(2,1)S(1)}, u32[]{:S(2)}, u32[]{:S(2)}) collective-permute-start(bf16[1024,256]{1,0:T(8,128)(2,1)S(1)} %get-tuple-element.41.refs_3_), channel_id=1, source_target_pairs={{0,1},{1,2},{2,3},{3,4},{4,5},{5,6},{6,7},{7,0},{8,9},{9,10},{10,1... | collective-permute-start | bytes 1572872 | tf_op jit(solution)/shard_map/ppermute | solution.py:80
  27.6 21.1 %collective-permute-start.3 = (bf16[1024,256]{1,0:T(8,128)(2,1)S(1)}, bf16[1024,256]{1,0:T(8,128)(2,1)S(1)}, u32[]{:S(2)}, u32[]{:S(2)}) collective-permute-start(bf16[1024,256]{1,0:T(8,128)(2,1)S(1)} %get-tuple-element.41.refs_3_), channel_id=1, source_target_pairs={{0,7},{1,0},{2,1},{3,2},{4,3},{5,4},{6,5},{7,6},{8,15},{9,8},{10,9... | collective-permute-start | bytes 1572872 | tf_op jit(solution)/shard_map/ppermute | solution.py:80
  32.7 10.6 %copy-start.9 = (bf16[1024,256]{1,0:T(8,128)(2,1)}, bf16[1024,256]{1,0:T(8,128)(2,1)S(1)}, u32[]{:S(2)}) copy-start(bf16[1024,256]{1,0:T(8,128)(2,1)S(1)} %collective-permute-done.refs_4_) | copy-start | bytes 1572868
  38.4 4.9 %copy-start.11 = (bf16[1024,256]{1,0:T(8,128)(2,1)}, bf16[1024,256]{1,0:T(8,128)(2,1)S(1)}, u32[]{:S(2)}) copy-start(bf16[1024,256]{1,0:T(8,128)(2,1)S(1)} %collective-permute-done.1.refs_5_) | copy-start | bytes 1572868
  43.3 5.3 %copy-start.5 = (bf16[1024,256]{1,0:T(8,128)(2,1)}, bf16[1024,256]{1,0:T(8,128)(2,1)S(1)}, u32[]{:S(2)}) copy-start(bf16[1024,256]{1,0:T(8,128)(2,1)S(1)} %collective-permute-done.2.refs_4_) | copy-start | bytes 1572868
  51.5 10.2 %copy-start.10 = (bf16[1024,256]{1,0:T(8,128)(2,1)S(1)}, bf16[1024,256]{1,0:T(8,128)(2,1)}, u32[]{:S(2)}) copy-start(bf16[1024,256]{1,0:T(8,128)(2,1)} %copy-done.9) | copy-start | bytes 1572868
  51.5 12.1 %copy-start.8 = (bf16[1024,256]{1,0:T(8,128)(2,1)S(1)}, bf16[1024,256]{1,0:T(8,128)(2,1)}, u32[]{:S(2)}) copy-start(bf16[1024,256]{1,0:T(8,128)(2,1)} %copy-done.7) | copy-start | bytes 1572868
  51.5 16.1 %copy-start.6 = (bf16[1024,256]{1,0:T(8,128)(2,1)S(1)}, bf16[1024,256]{1,0:T(8,128)(2,1)}, u32[]{:S(2)}) copy-start(bf16[1024,256]{1,0:T(8,128)(2,1)} %copy-done.5) | copy-start | bytes 1572868
  51.5 63.7 %all-to-all-start.1 = ((bf16[64,64,128]{2,1,0:T(8,128)(2,1)}), bf16[64,64,128]{2,1,0:T(8,128)(2,1)S(1)}, u32[]{:S(2)}, u32[]{:S(2)}) async-start(bf16[64,64,128]{2,1,0:T(8,128)(2,1)} %bitcast.12), calls=%async_computation.1 | async-start | bytes 2097152 | tf_op jit(solution)/shard_map/all_to_all | solution.py:111
  61.7 16.7 %collective-permute-start.4 = (bf16[1024,256]{1,0:T(8,128)(2,1)S(1)}, bf16[1024,256]{1,0:T(8,128)(2,1)S(1)}, u32[]{:S(2)}, u32[]{:S(2)}) collective-permute-start(bf16[1024,256]{1,0:T(8,128)(2,1)S(1)} %copy-done.10), channel_id=1, source_target_pairs={{0,1},{1,2},{2,3},{3,4},{4,5},{5,6},{6,7},{7,0},{8,9},{9,10},{10,1... | collective-permute-start | bytes 1572872 | tf_op jit(solution)/shard_map/ppermute | solution.py:80
  63.6 17.9 %collective-permute-start.7 = (bf16[1024,256]{1,0:T(8,128)(2,1)S(1)}, bf16[1024,256]{1,0:T(8,128)(2,1)S(1)}, u32[]{:S(2)}, u32[]{:S(2)}) collective-permute-start(bf16[1024,256]{1,0:T(8,128)(2,1)S(1)} %copy-done.8), channel_id=1, source_target_pairs={{0,7},{1,0},{2,1},{3,2},{4,3},{5,4},{6,5},{7,6},{8,15},{9,8},{10,9... | collective-permute-start | bytes 1572872 | tf_op jit(solution)/shard_map/ppermute | solution.py:80
  67.6 22.1 %collective-permute-start.6 = (bf16[1024,256]{1,0:T(8,128)(2,1)S(1)}, bf16[1024,256]{1,0:T(8,128)(2,1)}, u32[]{:S(2)}, u32[]{:S(2)}) collective-permute-start(bf16[1024,256]{1,0:T(8,128)(2,1)S(1)} %copy-done.6), channel_id=1, source_target_pairs={{0,1},{1,2},{2,3},{3,4},{4,5},{5,6},{6,7},{7,0},{8,9},{9,10},{10,1... | collective-permute-start | bytes 1572872 | tf_op jit(solution)/shard_map/ppermute | solution.py:80
  70.7 22.1 %collective-permute-start.5 = (bf16[1024,256]{1,0:T(8,128)(2,1)}, bf16[1024,256]{1,0:T(8,128)(2,1)}, u32[]{:S(2)}, u32[]{:S(2)}) collective-permute-start(bf16[1024,256]{1,0:T(8,128)(2,1)} %copy-done.11), channel_id=1, source_target_pairs={{0,7},{1,0},{2,1},{3,2},{4,3},{5,4},{6,5},{7,6},{8,15},{9,8},{10,9... | collective-permute-start | bytes 1572872 | tf_op jit(solution)/shard_map/ppermute | solution.py:80
  78.3 25.7 %copy-start.13 = (bf16[1024,256]{1,0:T(8,128)(2,1)}, bf16[1024,256]{1,0:T(8,128)(2,1)S(1)}, u32[]{:S(2)}) copy-start(bf16[1024,256]{1,0:T(8,128)(2,1)S(1)} %collective-permute-done.4.refs_6_) | copy-start | bytes 1572868
  78.3 22.6 %collective-permute-start.8 = (bf16[1024,256]{1,0:T(8,128)(2,1)S(1)}, bf16[1024,256]{1,0:T(8,128)(2,1)}, u32[]{:S(2)}, u32[]{:S(2)}) collective-permute-start(bf16[1024,256]{1,0:T(8,128)(2,1)S(1)} %collective-permute-done.4.refs_6_), channel_id=1, source_target_pairs={{0,1},{1,2},{2,3},{3,4},{4,5},{5,6},{6,7},{7,0},{8,9},{9,10},{10,1... | collective-permute-start | bytes 1572872 | tf_op jit(solution)/shard_map/ppermute | solution.py:80
  81.5 8.2 %copy-start.12 = (bf16[1024,256]{1,0:T(8,128)(2,1)}, bf16[1024,256]{1,0:T(8,128)(2,1)S(1)}, u32[]{:S(2)}) copy-start(bf16[1024,256]{1,0:T(8,128)(2,1)S(1)} %collective-permute-done.7.refs_7_) | copy-start | bytes 1572868
  81.5 22.5 %collective-permute-start.11 = (bf16[1024,256]{1,0:T(8,128)(2,1)S(1)}, bf16[1024,256]{1,0:T(8,128)(2,1)S(1)}, u32[]{:S(2)}, u32[]{:S(2)}) collective-permute-start(bf16[1024,256]{1,0:T(8,128)(2,1)S(1)} %collective-permute-done.7.refs_7_), channel_id=1, source_target_pairs={{0,7},{1,0},{2,1},{3,2},{4,3},{5,4},{6,5},{7,6},{8,15},{9,8},{10,9... | collective-permute-start | bytes 1572872 | tf_op jit(solution)/shard_map/ppermute | solution.py:80
  89.7 22.4 %collective-permute-start.10 = (bf16[1024,256]{1,0:T(8,128)(2,1)}, bf16[1024,256]{1,0:T(8,128)(2,1)S(1)}, u32[]{:S(2)}, u32[]{:S(2)}) collective-permute-start(bf16[1024,256]{1,0:T(8,128)(2,1)} %collective-permute-done.6.refs_6_), channel_id=1, source_target_pairs={{0,1},{1,2},{2,3},{3,4},{4,5},{5,6},{6,7},{7,0},{8,9},{9,10},{10,1... | collective-permute-start | bytes 1572872 | tf_op jit(solution)/shard_map/ppermute | solution.py:80
  92.8 22.4 %collective-permute-start.9 = (bf16[1024,256]{1,0:T(8,128)(2,1)}, bf16[1024,256]{1,0:T(8,128)(2,1)S(1)}, u32[]{:S(2)}, u32[]{:S(2)}) collective-permute-start(bf16[1024,256]{1,0:T(8,128)(2,1)} %collective-permute-done.5.refs_7_), channel_id=1, source_target_pairs={{0,7},{1,0},{2,1},{3,2},{4,3},{5,4},{6,5},{7,6},{8,15},{9,8},{10,9... | collective-permute-start | bytes 1572872 | tf_op jit(solution)/shard_map/ppermute | solution.py:80
  100.9 21.6 %collective-permute-start.12 = (bf16[1024,256]{1,0:T(8,128)(2,1)}, bf16[1024,256]{1,0:T(8,128)(2,1)}, u32[]{:S(2)}, u32[]{:S(2)}) collective-permute-start(bf16[1024,256]{1,0:T(8,128)(2,1)} %collective-permute-done.8.refs_8_), channel_id=1, source_target_pairs={{0,1},{1,2},{2,3},{3,4},{4,5},{5,6},{6,7},{7,0},{8,9},{9,10},{10,1... | collective-permute-start | bytes 1572872 | tf_op jit(solution)/shard_map/ppermute | solution.py:80
  104.0 13.0 %copy-start.14 = (bf16[1024,256]{1,0:T(8,128)(2,1)}, bf16[1024,256]{1,0:T(8,128)(2,1)S(1)}, u32[]{:S(2)}) copy-start(bf16[1024,256]{1,0:T(8,128)(2,1)S(1)} %collective-permute-done.11.refs_9_) | copy-start | bytes 1572868
  104.0 30.3 %collective-permute-start.14 = (bf16[1024,256]{1,0:T(8,128)(2,1)S(1)}, bf16[1024,256]{1,0:T(8,128)(2,1)}, u32[]{:S(2)}, u32[]{:S(2)}) collective-permute-start(bf16[1024,256]{1,0:T(8,128)(2,1)S(1)} %collective-permute-done.11.refs_9_), channel_id=1, source_target_pairs={{0,7},{1,0},{2,1},{3,2},{4,3},{5,4},{6,5},{7,6},{8,15},{9,8},{10,9... | collective-permute-start | bytes 1572872 | tf_op jit(solution)/shard_map/ppermute | solution.py:80
  128.6 14.4 %collective-permute-start.13 = (bf16[1024,128]{1,0:T(8,128)(2,1)}, bf16[1024,128]{1,0:T(8,128)(2,1)S(1)}, u32[]{:S(2)}, u32[]{:S(2)}) collective-permute-start(bf16[1024,128]{1,0:T(8,128)(2,1)} %get-tuple-element.32), channel_id=1, source_target_pairs={{0,8},{8,0},{1,9},{9,1},{2,10},{10,2},{3,11},{11,3},{4,12},{12,4},... | collective-permute-start | bytes 786440 | tf_op jit(solution)/shard_map/ppermute | solution.py:125
  134.4 8.6 %copy-start.3 = (f32[1024,128]{1,0:T(8,128)S(1)}, f32[1024,128]{1,0:T(8,128)}, u32[]{:S(2)}) copy-start(f32[1024,128]{1,0:T(8,128)} %get-tuple-element.31) | copy-start | bytes 1572868
  140.6 11.0 %copy-start.4 = (f32[1024,128]{1,0:T(8,128)S(1)}, f32[1024,128]{1,0:T(8,128)}, u32[]{:S(2)}) copy-start(f32[1024,128]{1,0:T(8,128)} %get-tuple-element.39) | copy-start | bytes 1572868
  140.6 11.0 %collective-permute-start.15 = (bf16[1024,128]{1,0:T(8,128)(2,1)}, bf16[1024,128]{1,0:T(8,128)(2,1)S(1)}, u32[]{:S(2)}, u32[]{:S(2)}) collective-permute-start(bf16[1024,128]{1,0:T(8,128)(2,1)} %get-tuple-element.40), channel_id=1, source_target_pairs={{0,8},{8,0},{1,9},{9,1},{2,10},{10,2},{3,11},{11,3},{4,12},{12,4},... | collective-permute-start | bytes 786440 | tf_op jit(solution)/shard_map/ppermute | solution.py:125
  (3 other events, 4.7 us)

commit v3 on v1

v3 whole, which is shorter than its diff:
```python
import jax
import jax.numpy as jnp
from jax import lax
from jax.experimental import pallas as pl
from jax.experimental.pallas import tpu as pltpu
from jax.sharding import Mesh, PartitionSpec as P

PANEL_W = 4096
X_HI = 2
CORES = 2
PAD = 8
TILE_M = 256
ROW = ("chip", "core")

inv_root = 0.7071067811865476


def butterfly(top, bottom):
    top = top.astype(jnp.float32)
    bottom = bottom.astype(jnp.float32)
    return jnp.concatenate([(top + bottom) * inv_root, (top - bottom) * inv_root], axis=0)


def after(value, *others):
    return lax.optimization_barrier((value, *others))[0]


def load_tiles(refs, split, tiles):
    in_first = pl.program_id(0) < tiles // 2
    out, refs = [], list(refs)
    for halves in split:
        if halves:
            first, second = refs.pop(0), refs.pop(0)
            out.append(jnp.where(in_first, first[...], second[...]))
        else:
            out.append(refs.pop(0)[...])
    return out


def block_specs(blocks, tiles):
    specs, flat, split = [], [], []
    for block in blocks:
        if isinstance(block, tuple):
            shape = (TILE_M, block[0].shape[1])
            specs.append(pl.BlockSpec(shape, lambda i, place: (jnp.minimum(i, tiles // 2 - 1), 0)))
            specs.append(pl.BlockSpec(shape, lambda i, place: (jnp.maximum(i - tiles // 2, 0), 0)))
            flat += block
        else:
            specs.append(pl.BlockSpec((TILE_M, block.shape[1]), lambda i, place: (i, 0)))
            flat.append(block)
        split.append(isinstance(block, tuple))
    return specs, flat, split


def early_products(place, upper, stored, offsets, blocks):
    rows, width = stored.shape
    y_count, depth, both = upper.shape
    tiles = rows // TILE_M
    specs, flat, split = block_specs(blocks, tiles)
    tile = pl.BlockSpec((TILE_M, width), lambda i, place: (i, 0))

    def body(place_ref, upper_ref, stored_ref, *refs):
        *block_refs, far_ref, rest_ref, turned = refs

        @pl.when(pl.program_id(0) == 0)
        def _():
            for n, offset in enumerate(offsets):
                turned[n * depth : (n + 1) * depth] = upper_ref[(place_ref[1] + offset + y_count) % y_count]

        lhs = jnp.concatenate(load_tiles(block_refs, split, tiles), axis=1)
        total = jnp.dot(lhs, turned[...], preferred_element_type=jnp.float32)
        left, right = total[:, :width], total[:, width:]
        at_left = place_ref[0] == 0
        far_ref[...] = jnp.where(at_left, right, left)
        rest_ref[...] = stored_ref[...].astype(jnp.float32) - jnp.where(at_left, left, right)

    return pl.pallas_call(
        body,
        grid_spec=pltpu.PrefetchScalarGridSpec(
            num_scalar_prefetch=1,
            grid=(tiles,),
            in_specs=[pl.BlockSpec(upper.shape, lambda i, place: (0, 0, 0)), tile, *specs],
            out_specs=[tile, tile],
            scratch_shapes=[pltpu.VMEM((len(offsets) * depth, both), upper.dtype)],
        ),
        out_shape=[jax.ShapeDtypeStruct((rows, width), jnp.float32)] * 2,
        name="early_products",
    )(place, upper, stored, *flat)


def last_product(place, upper, base, block, partner, out_dtype, sign):
    rows, width = base.shape
    y_count, depth, both = upper.shape
    tiles = rows // TILE_M
    specs, flat, split = block_specs([block], tiles)
    tile = pl.BlockSpec((TILE_M, width), lambda i, place: (i, 0))

    def body(place_ref, upper_ref, base_ref, *refs):
        *block_refs, out_ref = refs
        (lhs,) = load_tiles(block_refs, split, tiles)
        term = jnp.dot(lhs, upper_ref[0], preferred_element_type=jnp.float32)
        out_ref[...] = (base_ref[...] + sign * term).astype(out_ref.dtype)

    def upper_map(i, place):
        side = 1 - place[0] if partner else place[0]
        return ((place[1] + y_count // 2) % y_count, 0, side)

    return pl.pallas_call(
        body,
        grid_spec=pltpu.PrefetchScalarGridSpec(
            num_scalar_prefetch=1,
            grid=(tiles,),
            in_specs=[pl.BlockSpec((1, depth, width), upper_map), tile, *specs],
            out_specs=tile,
        ),
        out_shape=jax.ShapeDtypeStruct((rows, width), out_dtype),
        name="last_far" if partner else "last_own",
    )(place, upper, base, *flat)


def per_device(slab_block, scale_first, scale_second, panel_lower):
    row_count, col_width = slab_block.shape
    chips = lax.axis_size("chip")
    groups = chips * CORES
    y_count = lax.axis_size("y")
    block_width = panel_lower.shape[1]
    share = row_count // groups
    half = row_count // 2
    quarter = row_count // 4

    up = [(i, (i + 1) % y_count) for i in range(y_count)]
    down = [(i, (i - 1) % y_count) for i in range(y_count)]
    route = {-1: up, 1: down}
    near = tuple(lax.ppermute(panel_lower, "y", route[sign]) for sign in route)

    first = (scale_first.astype(jnp.float32)[:, None] * slab_block.astype(jnp.float32)).astype(
        jnp.bfloat16
    )
    scale_rows = jnp.pad(
        jnp.transpose(scale_second.reshape(share, groups))[None], ((0, PAD - 1), (0, 0), (0, col_width - share))
    )
    packed = jnp.concatenate([first.reshape(share, groups, col_width), scale_rows], axis=0)
    packed = lax.all_to_all(packed, ROW, split_axis=1, concat_axis=0, tiled=True)
    moving = {}
    for part, sign in ((0, -1), (1, 1), (1, -1), (0, 1)):
        source = near[0] if sign < 0 else near[1]
        moving[part, sign] = source[part * half : (part + 1) * half]
    packed = after(packed, *moving.values())
    packed = packed.reshape(groups, share + PAD, col_width)
    cyclic = packed[:, :share].reshape(row_count, col_width)
    scale_cyclic = packed[:, share, :share].reshape(row_count)

    steps = []
    for distance in range(2, y_count // 2 + 1):
        for part, sign in ((0, -1), (1, 1)) if 2 * distance == y_count else ((0, -1), (1, 1), (1, -1), (0, 1)):
            moving[part, sign] = lax.ppermute(moving[part, sign], "y", route[sign])
        steps.append(dict(moving))

    level_one = butterfly(cyclic[:half], cyclic[half:])
    second = (scale_cyclic.astype(jnp.float32)[:, None] * level_one).astype(jnp.bfloat16)
    stored = jnp.concatenate(
        [
            butterfly(second[:quarter], second[quarter:half]),
            butterfly(second[half : half + quarter], second[half + quarter :]),
        ],
        axis=0,
    ).astype(jnp.bfloat16)

    top_count = PANEL_W // groups // X_HI
    top = stored[: top_count * X_HI].reshape(1, X_HI, top_count, col_width)
    send = jnp.broadcast_to(top, (chips, X_HI, top_count, col_width)).reshape(
        chips * X_HI, top_count, col_width
    )
    send = after(send, steps[0][0, -1], steps[0][1, 1])
    got = lax.all_to_all(send, ("chip", "x_hi"), split_axis=0, concat_axis=0)
    twin = lax.ppermute(got, "core", [(0, 1), (1, 0)])
    core_zero = lax.axis_index("core") == 0
    upper = jnp.stack([jnp.where(core_zero, got, twin), jnp.where(core_zero, twin, got)])
    upper = upper.reshape(CORES, chips, X_HI, top_count, col_width)
    upper = jnp.transpose(upper, (3, 1, 0, 2, 4)).reshape(y_count, block_width, X_HI * col_width)
    upper = after(upper, *steps[0].values(), *steps[1].values())

    place = jnp.stack([lax.axis_index("x_hi"), lax.axis_index("y")]).astype(jnp.int32)
    offsets, blocks = [0, -1, 1], [panel_lower, *near]
    for distance, step in enumerate(steps[:-1], 2):
        for sign in route:
            offsets.append(sign * distance)
            blocks.append((step[0, sign], step[1, sign]))
    last = (steps[-1][0, -1], steps[-1][1, 1])
    far, rest = early_products(place, upper, stored, offsets, blocks)
    far = last_product(place, upper, far, last, True, jnp.bfloat16, 1)
    came = lax.ppermute(far, "x_hi", [(i, X_HI - 1 - i) for i in range(X_HI)])
    rest = last_product(place, upper, rest, last, False, jnp.float32, -1)
    return (rest - came.astype(jnp.float32)).astype(jnp.bfloat16)


def solution(mesh):
    rows, cols = mesh.devices.shape
    split = Mesh(
        mesh.devices.reshape(rows // CORES, CORES, X_HI, cols // X_HI), ("chip", "core", "x_hi", "y")
    )
    col = ("x_hi", "y")
    placed = (P(ROW, col), P(ROW), P(ROW), P(ROW, col))
    return jax.shard_map(
        per_device, mesh=split, in_specs=placed, out_specs=P(ROW, col), check_vma=False
    )
```

time: 238 us -> 147 us (0.62)
  the two profiles are of different devices: /device:TPU:16 before, /device:TPU:2 now
where the time goes in v3:
time: 147 us; the launch traced here: 146 us
  starting transfers between devices  74.5 us (51%)
  waiting for transfers between devices  29 us (20%)
  Pallas kernels  23.4 us (16%)
  other arithmetic  10.5 us (7%)
  local copies, waits for them, and re-layouts  8.42 us (6%)
    ppermute x10, starting transfers between devices, per_device(): moving[part, sign] = lax.ppermute(moving[part, sign], 'y', route[sign])  35.8 us
    ppermute x10, waiting for transfers between devices, per_device(): moving[part, sign] = lax.ppermute(moving[part, sign], 'y', route[sign])  16.2 us
    pallas_call x2, Pallas kernels, last_product(): pl.pallas_call(body, grid_spec=pltpu.PrefetchScalarGridSpec(num_scalar_pr...  13.7 us
    all_to_all x1, starting transfers between devices, per_device(): got = lax.all_to_all(send, ('chip', 'x_hi'), split_axis=0, concat_axis=0)  13.5 us
    all_to_all x1, starting transfers between devices, per_device(): lax.all_to_all(packed, ROW, split_axis=1, concat_axis=0, tiled=True)  11.9 us
    ppermute x2, waiting for transfers between devices, per_device(): lax.ppermute(panel_lower, 'y', route[sign])  10.7 us
    pallas_call x1, Pallas kernels, early_products(): pl.pallas_call(body, grid_spec=pltpu.PrefetchScalarGridSpec(num_scalar_pr...  9.67 us
    ppermute x2, starting transfers between devices, per_device(): lax.ppermute(panel_lower, 'y', route[sign])  7.42 us
  transfers between devices with their start and end apart: 16, of which 6 were waited for; matrix products, arithmetic and copies ran while one was open for 10% of the time, Pallas kernels for 11%

profile of v3, /device:TPU:2, one launch (start us, length us, event | category | flops | bytes accessed | tf_op | source)
XLA Modules:
  0.0 146.2 jit_solution(7258779126406173003)
XLA Ops:
  0.0 5.5 %collective-permute-start.1 = (bf16[2048,256]{1,0:T(8,128)(2,1)}, bf16[2048,256]{1,0:T(8,128)(2,1)S(1)}, u32[]{:S(2)}, u32[]{:S(2)}) collective-permute-start(bf16[2048,256]{1,0:T(8,128)(2,1)} %refs_0_.1), channel_id=1, source_target_pairs={{0,7},{1,0},{2,1},{3,2},{4,3},{5,4},{6,5},{7,6},{8,15},{9,8},{10,9... | collective-permute-start | bytes 3145736 | tf_op jit(solution)/shard_map/ppermute | solution.py:134
  5.5 1.9 %collective-permute-start = (bf16[2048,256]{1,0:T(8,128)(2,1)}, bf16[2048,256]{1,0:T(8,128)(2,1)S(1)}, u32[]{:S(2)}, u32[]{:S(2)}) collective-permute-start(bf16[2048,256]{1,0:T(8,128)(2,1)} %refs_0_.1), channel_id=1, source_target_pairs={{0,1},{1,2},{2,3},{3,4},{4,5},{5,6},{6,7},{7,0},{8,9},{9,10},{10,1... | collective-permute-start | bytes 3145736 | tf_op jit(solution)/shard_map/ppermute | solution.py:134
  8.1 1.4 multiply_convert_fusion
  10.8 11.9 %all-to-all-start = ((bf16[72,32,128]{2,0,1:T(8,128)(2,1)}), bf16[72,32,128]{2,0,1:T(8,128)(2,1)S(1)}, u32[]{:S(2)}, u32[]{:S(2)}) async-start(bf16[72,32,128]{2,0,1:T(8,128)(2,1)} %copy.12), calls=%async_computation | async-start | bytes 1179648 | tf_op jit(solution)/shard_map/all_to_all | solution.py:143
  22.7 10.7 %collective-permute-done.refs_1_ = bf16[2048,256]{1,0:T(8,128)(2,1)S(1)} collective-permute-done((bf16[2048,256]{1,0:T(8,128)(2,1)}, bf16[2048,256]{1,0:T(8,128)(2,1)S(1)}, u32[]{:S(2)}, u32[]{:S(2)}) %collective-permute-start) | collective-permute-done | bytes 1048608 | tf_op jit(solution)/shard_map/ppermute | solution.py:134
  33.4 1.1 fusion.15
  34.8 1.9 %collective-permute-start.2 = (bf16[1024,256]{1,0:T(8,128)(2,1)}, bf16[1024,256]{1,0:T(8,128)(2,1)S(1)}, u32[]{:S(2)}, u32[]{:S(2)}) collective-permute-start(bf16[1024,256]{1,0:T(8,128)(2,1)} %get-tuple-element.20), channel_id=1, source_target_pairs={{0,1},{1,2},{2,3},{3,4},{4,5},{5,6},{6,7},{7,0},{8,9},{9,10},{10,1... | collective-permute-start | bytes 1572872 | tf_op jit(solution)/shard_map/ppermute | solution.py:156
  36.7 1.1 fusion.14
  38.0 5.1 %collective-permute-start.3 = (bf16[1024,256]{1,0:T(8,128)(2,1)}, bf16[1024,256]{1,0:T(8,128)(2,1)S(1)}, u32[]{:S(2)}, u32[]{:S(2)}) collective-permute-start(bf16[1024,256]{1,0:T(8,128)(2,1)} %get-tuple-element.18), channel_id=1, source_target_pairs={{0,7},{1,0},{2,1},{3,2},{4,3},{5,4},{6,5},{7,6},{8,15},{9,8},{10,9... | collective-permute-start | bytes 1572872 | tf_op jit(solution)/shard_map/ppermute | solution.py:156
  44.5 6.0 %collective-permute-done.2.refs_3_ = bf16[1024,256]{1,0:T(8,128)(2,1)S(1)} collective-permute-done((bf16[1024,256]{1,0:T(8,128)(2,1)}, bf16[1024,256]{1,0:T(8,128)(2,1)S(1)}, u32[]{:S(2)}, u32[]{:S(2)}) %collective-permute-start.2) | collective-permute-done | bytes 524320 | tf_op jit(solution)/shard_map/ppermute | solution.py:156
  50.5 2.6 %collective-permute-done.3.refs_6_ = bf16[1024,256]{1,0:T(8,128)(2,1)S(1)} collective-permute-done((bf16[1024,256]{1,0:T(8,128)(2,1)}, bf16[1024,256]{1,0:T(8,128)(2,1)S(1)}, u32[]{:S(2)}, u32[]{:S(2)}) %collective-permute-start.3) | collective-permute-done | bytes 524320 | tf_op jit(solution)/shard_map/ppermute | solution.py:156
  54.1 13.5 %all-to-all-start.1 = ((bf16[32,64,128]{2,1,0:T(8,128)(2,1)}), bf16[32,64,128]{2,1,0:T(8,128)(2,1)S(1)}, u32[]{:S(2)}, u32[]{:S(2)}) async-start(bf16[32,64,128]{2,1,0:T(8,128)(2,1)} %bitcast.12), calls=%async_computation.1 | async-start | bytes 1048576 | tf_op jit(solution)/shard_map/all_to_all | solution.py:175
  67.6 5.5 %collective-permute-start.6 = (bf16[1024,256]{1,0:T(8,128)(2,1)}, bf16[1024,256]{1,0:T(8,128)(2,1)S(1)}, u32[]{:S(2)}, u32[]{:S(2)}) collective-permute-start(bf16[1024,256]{1,0:T(8,128)(2,1)} %get-tuple-element.17), channel_id=1, source_target_pairs={{0,7},{1,0},{2,1},{3,2},{4,3},{5,4},{6,5},{7,6},{8,15},{9,8},{10,9... | collective-permute-start | bytes 1572872 | tf_op jit(solution)/shard_map/ppermute | solution.py:156
  73.1 1.9 %collective-permute-start.5 = (bf16[1024,256]{1,0:T(8,128)(2,1)S(1)}, bf16[1024,256]{1,0:T(8,128)(2,1)}, u32[]{:S(2)}, u32[]{:S(2)}) collective-permute-start(bf16[1024,256]{1,0:T(8,128)(2,1)S(1)} %copy-done.7), channel_id=1, source_target_pairs={{0,1},{1,2},{2,3},{3,4},{4,5},{5,6},{6,7},{7,0},{8,9},{9,10},{10,1... | collective-permute-start | bytes 1572872 | tf_op jit(solution)/shard_map/ppermute | solution.py:156
  75.0 1.9 %collective-permute-start.7 = (bf16[1024,256]{1,0:T(8,128)(2,1)S(1)}, bf16[1024,256]{1,0:T(8,128)(2,1)}, u32[]{:S(2)}, u32[]{:S(2)}) collective-permute-start(bf16[1024,256]{1,0:T(8,128)(2,1)S(1)} %collective-permute-done.2.refs_3_), channel_id=1, source_target_pairs={{0,1},{1,2},{2,3},{3,4},{4,5},{5,6},{6,7},{7,0},{8,9},{9,10},{10,1... | collective-permute-start | bytes 1572872 | tf_op jit(solution)/shard_map/ppermute | solution.py:156
  76.9 5.1 %collective-permute-start.8 = (bf16[1024,256]{1,0:T(8,128)(2,1)S(1)}, bf16[1024,256]{1,0:T(8,128)(2,1)}, u32[]{:S(2)}, u32[]{:S(2)}) collective-permute-start(bf16[1024,256]{1,0:T(8,128)(2,1)S(1)} %collective-permute-done.3.refs_6_), channel_id=1, source_target_pairs={{0,7},{1,0},{2,1},{3,2},{4,3},{5,4},{6,5},{7,6},{8,15},{9,8},{10,9... | collective-permute-start | bytes 1572872 | tf_op jit(solution)/shard_map/ppermute | solution.py:156
  82.1 1.9 %collective-permute-start.4 = (bf16[32,64,128]{2,1,0:T(8,128)(2,1)S(1)}, bf16[32,64,128]{2,1,0:T(8,128)(2,1)}, u32[]{:S(2)}, u32[]{:S(2)}) collective-permute-start(bf16[32,64,128]{2,1,0:T(8,128)(2,1)S(1)} %all-to-all-done.1), channel_id=1, source_target_pairs={{0,16},{16,0},{1,17},{17,1},{2,18},{18,2},{3,19},{19,3},{4,20},{20... | collective-permute-start | bytes 1572872 | tf_op jit(solution)/shard_map/ppermute | solution.py:176
  84.7 5.4 %collective-permute-start.10 = (bf16[1024,256]{1,0:T(8,128)(2,1)S(1)}, bf16[1024,256]{1,0:T(8,128)(2,1)}, u32[]{:S(2)}, u32[]{:S(2)}) collective-permute-start(bf16[1024,256]{1,0:T(8,128)(2,1)S(1)} %collective-permute-done.6.refs_5_), channel_id=1, source_target_pairs={{0,7},{1,0},{2,1},{3,2},{4,3},{5,4},{6,5},{7,6},{8,15},{9,8},{10,9... | collective-permute-start | bytes 1572872 | tf_op jit(solution)/shard_map/ppermute | solution.py:156
  91.2 1.9 %collective-permute-start.9 = (bf16[1024,256]{1,0:T(8,128)(2,1)}, bf16[1024,256]{1,0:T(8,128)(2,1)}, u32[]{:S(2)}, u32[]{:S(2)}) collective-permute-start(bf16[1024,256]{1,0:T(8,128)(2,1)} %collective-permute-done.5.refs_4_), channel_id=1, source_target_pairs={{0,1},{1,2},{2,3},{3,4},{4,5},{5,6},{6,7},{7,0},{8,9},{9,10},{10,1... | collective-permute-start | bytes 1572872 | tf_op jit(solution)/shard_map/ppermute | solution.py:156
  93.1 6.5 %collective-permute-done.7.refs_7_ = bf16[1024,256]{1,0:T(8,128)(2,1)} collective-permute-done((bf16[1024,256]{1,0:T(8,128)(2,1)S(1)}, bf16[1024,256]{1,0:T(8,128)(2,1)}, u32[]{:S(2)}, u32[]{:S(2)}) %collective-permute-start.7) | collective-permute-done | bytes 524320 | tf_op jit(solution)/shard_map/ppermute | solution.py:156
  99.6 1.9 %collective-permute-start.11 = (bf16[1024,256]{1,0:T(8,128)(2,1)}, bf16[1024,256]{1,0:T(8,128)(2,1)S(1)}, u32[]{:S(2)}, u32[]{:S(2)}) collective-permute-start(bf16[1024,256]{1,0:T(8,128)(2,1)} %collective-permute-done.7.refs_7_), channel_id=1, source_target_pairs={{0,1},{1,2},{2,3},{3,4},{4,5},{5,6},{6,7},{7,0},{8,9},{9,10},{10,1... | collective-permute-start | bytes 1572872 | tf_op jit(solution)/shard_map/ppermute | solution.py:156
  101.5 5.1 %collective-permute-start.12 = (bf16[1024,256]{1,0:T(8,128)(2,1)}, bf16[1024,256]{1,0:T(8,128)(2,1)S(1)}, u32[]{:S(2)}, u32[]{:S(2)}) collective-permute-start(bf16[1024,256]{1,0:T(8,128)(2,1)} %collective-permute-done.8.refs_10_), channel_id=1, source_target_pairs={{0,7},{1,0},{2,1},{3,2},{4,3},{5,4},{6,5},{7,6},{8,15},{9,8},{10,9... | collective-permute-start | bytes 1572872 | tf_op jit(solution)/shard_map/ppermute | solution.py:156
  106.6 1.7 %pad_maximum_fusion.stored_ref = bf16[2048,128]{1,0:T(8,128)(2,1)} fusion(bf16[512,128]{1,0:T(8,128)(2,1)} %get-tuple-element.25, bf16[512,128]{1,0:T(8,128)(2,1)S(1)} %get-tuple-element.24, bf16[512,128]{1,0:T(8,128)(2,1)S(1)} %get-tuple-element.23, bf16[512,128]{1,0:T(8,128)(2,1)S(1)} %get-tuple-element.26), kind=kLoop, calls=%fused_computation.12 | loop fusion | flops 2097152 | bytes 1048576 | tf_op jit(solution)/shard_map/concatenate | solution.py:161
  108.4 1.1 broadcast_select_fusion.1
  110.6 1.5 %maximum_bitcast_fusion = bf16[64,16,2,2,128]{4,3,2,1,0:T(2,128)(2,1)S(1)} fusion(bf16[1,16,2,64,128]{4,2,0,1,3:T(2,128)(2,1)S(1)} %copy.14, bf16[1,16,2,64,128]{4,2,0,1,3:T(2,128)(2,1)S(1)} %copy.13), kind=kLoop, calls=%fused_computation.4 | loop fusion | flops 524288 | bytes 2097152 | tf_op jit(solution)/shard_map/transpose | solution.py:180
  112.1 1.5 %reshape.45.upper_ref = bf16[8,256,256]{2,1,0:T(8,128)(2,1)} reshape(bf16[64,16,2,2,128]{4,3,2,1,0:T(2,128)(2,1)S(1)} %maximum_bitcast_fusion) | data formatting | bytes 2097152 | tf_op jit(solution)/shard_map/reshape | solution.py:180
  113.6 9.7 %early_products.1 = (f32[2048,128]{1,0:T(8,128)}, f32[2048,128]{1,0:T(8,128)}) custom-call(s32[2]{0:T(128)} %pad_add_fusion.place_ref, bf16[8,256,256]{2,1,0:T(8,128)(2,1)} %reshape.45.upper_ref, bf16[2048,128]{1,0:T(8,128)(2,1)} %pad_maximum_fusion.stored_ref, bf16[2048,256]{1,0:T(8,128)(2,1)} %refs_0_.1, bf16[2048,256]{1,0:T(8,128)(2,1)} %copy-done.1, ...), custom_call_target="tpu_custom_call" | custom-call | tf_op jit(solution)/shard_map/early_products/pallas_call | solution.py:77
  124.3 6.8 %last_far.1 = bf16[2048,128]{1,0:T(8,128)(2,1)} custom-call(s32[2]{0:T(128)} %pad_add_fusion.place_ref, bf16[8,256,256]{2,1,0:T(8,128)(2,1)} %reshape.45.upper_ref, f32[2048,128]{1,0:T(8,128)} %get-tuple-element.14.base_ref, bf16[1024,256]{1,0:T(8,128)(2,1)} %copy-done.2, bf16[1024,256]{1,0:T(8,128)(2,1)} %copy-done.3), custom_call_target="tpu_custom_call" | custom-call | tf_op jit(solution)/shard_map/last_far/pallas_call | solution.py:108
  131.1 4.0 %collective-permute-start.13 = (bf16[2048,128]{1,0:T(8,128)(2,1)}, bf16[2048,128]{1,0:T(8,128)(2,1)S(1)}, u32[]{:S(2)}, u32[]{:S(2)}) collective-permute-start(bf16[2048,128]{1,0:T(8,128)(2,1)} %last_far.1), channel_id=1, source_target_pairs={{0,8},{8,0},{1,9},{9,1},{2,10},{10,2},{3,11},{11,3},{4,12},{12,4},... | collective-permute-start | bytes 1572872 | tf_op jit(solution)/shard_map/ppermute | solution.py:192
  135.0 6.9 %last_own.1 = f32[2048,128]{1,0:T(8,128)} custom-call(s32[2]{0:T(128)} %pad_add_fusion.place_ref, bf16[8,256,256]{2,1,0:T(8,128)(2,1)} %reshape.45.upper_ref, f32[2048,128]{1,0:T(8,128)} %get-tuple-element.13.base_ref, bf16[1024,256]{1,0:T(8,128)(2,1)} %copy-done.2, bf16[1024,256]{1,0:T(8,128)(2,1)} %copy-done.3), custom_call_target="tpu_custom_call" | custom-call | tf_op jit(solution)/shard_map/last_own/pallas_call | solution.py:108
  141.9 2.1 %collective-permute-done.13 = bf16[2048,128]{1,0:T(8,128)(2,1)S(1)} collective-permute-done((bf16[2048,128]{1,0:T(8,128)(2,1)}, bf16[2048,128]{1,0:T(8,128)(2,1)S(1)}, u32[]{:S(2)}, u32[]{:S(2)}) %collective-permute-start.13) | collective-permute-done | bytes 524320 | tf_op jit(solution)/shard_map/ppermute | solution.py:192
  144.1 2.1 %subtract_convert_fusion = bf16[2048,128]{1,0:T(8,128)(2,1)} fusion(f32[2048,128]{1,0:T(8,128)} %last_own.1, bf16[2048,128]{1,0:T(8,128)(2,1)S(1)} %collective-permute-done.13), kind=kLoop, calls=%fused_computation.5 | loop fusion | flops 786432 | bytes 2097152 | tf_op jit(solution)/shard_map/convert_element_type | solution.py:194
  (44 shorter events, 8.5 us)
Async XLA Ops:
  0.0 9.5 %copy-start.8 = (bf16[2048]{0:T(1024)(128)(2,1)S(1)}, bf16[2048]{0:T(1024)(128)(2,1)}, u32[]{:S(2)}) copy-start(bf16[2048]{0:T(1024)(128)(2,1)} %param.6) | copy-start | bytes 12292
  0.0 36.7 %collective-permute-start.1 = (bf16[2048,256]{1,0:T(8,128)(2,1)}, bf16[2048,256]{1,0:T(8,128)(2,1)S(1)}, u32[]{:S(2)}, u32[]{:S(2)}) collective-permute-start(bf16[2048,256]{1,0:T(8,128)(2,1)} %refs_0_.1), channel_id=1, source_target_pairs={{0,7},{1,0},{2,1},{3,2},{4,3},{5,4},{6,5},{7,6},{8,15},{9,8},{10,9... | collective-permute-start | bytes 3145736 | tf_op jit(solution)/shard_map/ppermute | solution.py:134
  5.5 27.9 %collective-permute-start = (bf16[2048,256]{1,0:T(8,128)(2,1)}, bf16[2048,256]{1,0:T(8,128)(2,1)S(1)}, u32[]{:S(2)}, u32[]{:S(2)}) collective-permute-start(bf16[2048,256]{1,0:T(8,128)(2,1)} %refs_0_.1), channel_id=1, source_target_pairs={{0,1},{1,2},{2,3},{3,4},{4,5},{5,6},{6,7},{7,0},{8,9},{9,10},{10,1... | collective-permute-start | bytes 3145736 | tf_op jit(solution)/shard_map/ppermute | solution.py:134
  10.8 32.3 %all-to-all-start = ((bf16[72,32,128]{2,0,1:T(8,128)(2,1)}), bf16[72,32,128]{2,0,1:T(8,128)(2,1)S(1)}, u32[]{:S(2)}, u32[]{:S(2)}) async-start(bf16[72,32,128]{2,0,1:T(8,128)(2,1)} %copy.12), calls=%async_computation | async-start | bytes 1179648 | tf_op jit(solution)/shard_map/all_to_all | solution.py:143
  33.4 1.3 copy-start.1
  34.8 15.8 %collective-permute-start.2 = (bf16[1024,256]{1,0:T(8,128)(2,1)}, bf16[1024,256]{1,0:T(8,128)(2,1)S(1)}, u32[]{:S(2)}, u32[]{:S(2)}) collective-permute-start(bf16[1024,256]{1,0:T(8,128)(2,1)} %get-tuple-element.20), channel_id=1, source_target_pairs={{0,1},{1,2},{2,3},{3,4},{4,5},{5,6},{6,7},{7,0},{8,9},{9,10},{10,1... | collective-permute-start | bytes 1572872 | tf_op jit(solution)/shard_map/ppermute | solution.py:156
  36.7 1.3 copy-start
  38.0 15.1 %collective-permute-start.3 = (bf16[1024,256]{1,0:T(8,128)(2,1)}, bf16[1024,256]{1,0:T(8,128)(2,1)S(1)}, u32[]{:S(2)}, u32[]{:S(2)}) collective-permute-start(bf16[1024,256]{1,0:T(8,128)(2,1)} %get-tuple-element.18), channel_id=1, source_target_pairs={{0,7},{1,0},{2,1},{3,2},{4,3},{5,4},{6,5},{7,6},{8,15},{9,8},{10,9... | collective-permute-start | bytes 1572872 | tf_op jit(solution)/shard_map/ppermute | solution.py:156
  44.5 28.5 %copy-start.7 = (bf16[1024,256]{1,0:T(8,128)(2,1)S(1)}, bf16[1024,256]{1,0:T(8,128)(2,1)}, u32[]{:S(2)}) copy-start(bf16[1024,256]{1,0:T(8,128)(2,1)} %get-tuple-element.19) | copy-start | bytes 1572868
  50.5 57.8 %copy-start.4 = (bf16[1024,256]{1,0:T(8,128)(2,1)}, bf16[1024,256]{1,0:T(8,128)(2,1)S(1)}, u32[]{:S(2)}) copy-start(bf16[1024,256]{1,0:T(8,128)(2,1)S(1)} %collective-permute-done.2.refs_3_) | copy-start | bytes 1572868
  53.1 48.3 %copy-start.5 = (bf16[1024,256]{1,0:T(8,128)(2,1)}, bf16[1024,256]{1,0:T(8,128)(2,1)S(1)}, u32[]{:S(2)}) copy-start(bf16[1024,256]{1,0:T(8,128)(2,1)S(1)} %collective-permute-done.3.refs_6_) | copy-start | bytes 1572868
  54.1 28.0 %all-to-all-start.1 = ((bf16[32,64,128]{2,1,0:T(8,128)(2,1)}), bf16[32,64,128]{2,1,0:T(8,128)(2,1)S(1)}, u32[]{:S(2)}, u32[]{:S(2)}) async-start(bf16[32,64,128]{2,1,0:T(8,128)(2,1)} %bitcast.12), calls=%async_computation.1 | async-start | bytes 1048576 | tf_op jit(solution)/shard_map/all_to_all | solution.py:175
  67.6 17.1 %collective-permute-start.6 = (bf16[1024,256]{1,0:T(8,128)(2,1)}, bf16[1024,256]{1,0:T(8,128)(2,1)S(1)}, u32[]{:S(2)}, u32[]{:S(2)}) collective-permute-start(bf16[1024,256]{1,0:T(8,128)(2,1)} %get-tuple-element.17), channel_id=1, source_target_pairs={{0,7},{1,0},{2,1},{3,2},{4,3},{5,4},{6,5},{7,6},{8,15},{9,8},{10,9... | collective-permute-start | bytes 1572872 | tf_op jit(solution)/shard_map/ppermute | solution.py:156
  73.1 18.1 %collective-permute-start.5 = (bf16[1024,256]{1,0:T(8,128)(2,1)S(1)}, bf16[1024,256]{1,0:T(8,128)(2,1)}, u32[]{:S(2)}, u32[]{:S(2)}) collective-permute-start(bf16[1024,256]{1,0:T(8,128)(2,1)S(1)} %copy-done.7), channel_id=1, source_target_pairs={{0,1},{1,2},{2,3},{3,4},{4,5},{5,6},{6,7},{7,0},{8,9},{9,10},{10,1... | collective-permute-start | bytes 1572872 | tf_op jit(solution)/shard_map/ppermute | solution.py:156
  75.0 24.5 %collective-permute-start.7 = (bf16[1024,256]{1,0:T(8,128)(2,1)S(1)}, bf16[1024,256]{1,0:T(8,128)(2,1)}, u32[]{:S(2)}, u32[]{:S(2)}) collective-permute-start(bf16[1024,256]{1,0:T(8,128)(2,1)S(1)} %collective-permute-done.2.refs_3_), channel_id=1, source_target_pairs={{0,1},{1,2},{2,3},{3,4},{4,5},{5,6},{6,7},{7,0},{8,9},{9,10},{10,1... | collective-permute-start | bytes 1572872 | tf_op jit(solution)/shard_map/ppermute | solution.py:156
  76.9 24.5 %collective-permute-start.8 = (bf16[1024,256]{1,0:T(8,128)(2,1)S(1)}, bf16[1024,256]{1,0:T(8,128)(2,1)}, u32[]{:S(2)}, u32[]{:S(2)}) collective-permute-start(bf16[1024,256]{1,0:T(8,128)(2,1)S(1)} %collective-permute-done.3.refs_6_), channel_id=1, source_target_pairs={{0,7},{1,0},{2,1},{3,2},{4,3},{5,4},{6,5},{7,6},{8,15},{9,8},{10,9... | collective-permute-start | bytes 1572872 | tf_op jit(solution)/shard_map/ppermute | solution.py:156
  82.1 26.3 %collective-permute-start.4 = (bf16[32,64,128]{2,1,0:T(8,128)(2,1)S(1)}, bf16[32,64,128]{2,1,0:T(8,128)(2,1)}, u32[]{:S(2)}, u32[]{:S(2)}) collective-permute-start(bf16[32,64,128]{2,1,0:T(8,128)(2,1)S(1)} %all-to-all-done.1), channel_id=1, source_target_pairs={{0,16},{16,0},{1,17},{17,1},{2,18},{18,2},{3,19},{19,3},{4,20},{20... | collective-permute-start | bytes 1572872 | tf_op jit(solution)/shard_map/ppermute | solution.py:176
  84.7 24.8 %copy-start.6 = (bf16[1024,256]{1,0:T(8,128)(2,1)}, bf16[1024,256]{1,0:T(8,128)(2,1)S(1)}, u32[]{:S(2)}) copy-start(bf16[1024,256]{1,0:T(8,128)(2,1)S(1)} %collective-permute-done.6.refs_5_) | copy-start | bytes 1572868
  84.7 28.9 %collective-permute-start.10 = (bf16[1024,256]{1,0:T(8,128)(2,1)S(1)}, bf16[1024,256]{1,0:T(8,128)(2,1)}, u32[]{:S(2)}, u32[]{:S(2)}) collective-permute-start(bf16[1024,256]{1,0:T(8,128)(2,1)S(1)} %collective-permute-done.6.refs_5_), channel_id=1, source_target_pairs={{0,7},{1,0},{2,1},{3,2},{4,3},{5,4},{6,5},{7,6},{8,15},{9,8},{10,9... | collective-permute-start | bytes 1572872 | tf_op jit(solution)/shard_map/ppermute | solution.py:156
  91.2 22.4 %collective-permute-start.9 = (bf16[1024,256]{1,0:T(8,128)(2,1)}, bf16[1024,256]{1,0:T(8,128)(2,1)}, u32[]{:S(2)}, u32[]{:S(2)}) collective-permute-start(bf16[1024,256]{1,0:T(8,128)(2,1)} %collective-permute-done.5.refs_4_), channel_id=1, source_target_pairs={{0,1},{1,2},{2,3},{3,4},{4,5},{5,6},{6,7},{7,0},{8,9},{9,10},{10,1... | collective-permute-start | bytes 1572872 | tf_op jit(solution)/shard_map/ppermute | solution.py:156
  99.6 23.7 %collective-permute-start.11 = (bf16[1024,256]{1,0:T(8,128)(2,1)}, bf16[1024,256]{1,0:T(8,128)(2,1)S(1)}, u32[]{:S(2)}, u32[]{:S(2)}) collective-permute-start(bf16[1024,256]{1,0:T(8,128)(2,1)} %collective-permute-done.7.refs_7_), channel_id=1, source_target_pairs={{0,1},{1,2},{2,3},{3,4},{4,5},{5,6},{6,7},{7,0},{8,9},{9,10},{10,1... | collective-permute-start | bytes 1572872 | tf_op jit(solution)/shard_map/ppermute | solution.py:156
  101.5 21.8 %collective-permute-start.12 = (bf16[1024,256]{1,0:T(8,128)(2,1)}, bf16[1024,256]{1,0:T(8,128)(2,1)S(1)}, u32[]{:S(2)}, u32[]{:S(2)}) collective-permute-start(bf16[1024,256]{1,0:T(8,128)(2,1)} %collective-permute-done.8.refs_10_), channel_id=1, source_target_pairs={{0,7},{1,0},{2,1},{3,2},{4,3},{5,4},{6,5},{7,6},{8,15},{9,8},{10,9... | collective-permute-start | bytes 1572872 | tf_op jit(solution)/shard_map/ppermute | solution.py:156
  123.3 0.8 copy-start.2
  123.3 1.0 copy-start.3
  131.1 13.0 %collective-permute-start.13 = (bf16[2048,128]{1,0:T(8,128)(2,1)}, bf16[2048,128]{1,0:T(8,128)(2,1)S(1)}, u32[]{:S(2)}, u32[]{:S(2)}) collective-permute-start(bf16[2048,128]{1,0:T(8,128)(2,1)} %last_far.1), channel_id=1, source_target_pairs={{0,8},{8,0},{1,9},{9,1},{2,10},{10,2},{3,11},{11,3},{4,12},{12,4},... | collective-permute-start | bytes 1572872 | tf_op jit(solution)/shard_map/ppermute | solution.py:192

commit v4 on v3

v4 whole, which is shorter than its diff:
```python
import jax
import jax.numpy as jnp
from jax import lax
from jax.experimental import pallas as pl
from jax.experimental.pallas import tpu as pltpu
from jax.sharding import Mesh, PartitionSpec as P

PANEL_W = 4096
X_HI = 2
CORES = 2
PAD = 8
TILE_M = 256
ROW = ("chip", "core")

inv_root = 0.7071067811865476


def butterfly(top, bottom):
    top = top.astype(jnp.float32)
    bottom = bottom.astype(jnp.float32)
    return jnp.concatenate([(top + bottom) * inv_root, (top - bottom) * inv_root], axis=0)


def after(value, *others):
    return lax.optimization_barrier((value, *others))[0]


VM = pltpu.VMEM


def grant(mib):
    return pltpu.CompilerParams(vmem_limit_bytes=mib << 20)


def whole():
    return pl.BlockSpec(memory_space=VM)


def order_upper(core, got, twin, y_count):
    pairs, top, width = got.shape
    chips = pairs // X_HI
    low = top // y_count
    depth = CORES * chips * low

    def body(core_ref, got_ref, twin_ref, out_ref):
        want = lax.broadcasted_iota(jnp.int32, (depth, depth), 0)
        have = lax.broadcasted_iota(jnp.int32, (depth, depth), 1)
        side = (want % CORES + core_ref[0]) % CORES
        source = side * (chips * low) + want // CORES % chips * low + want // (CORES * chips)
        move = jnp.where(source == have, 1.0, 0.0).astype(got.dtype)
        for y in range(y_count):
            for x in range(X_HI):
                pick = [
                    ref[chip * X_HI + x, y * low : (y + 1) * low] for ref in (got_ref, twin_ref) for chip in range(chips)
                ]
                rows = jnp.dot(move, jnp.concatenate(pick, axis=0), preferred_element_type=jnp.float32)
                out_ref[y, :, x * width : (x + 1) * width] = rows.astype(got.dtype)

    return pl.pallas_call(
        body,
        in_specs=[pl.BlockSpec(memory_space=pltpu.SMEM), whole(), whole()],
        out_specs=whole(),
        out_shape=jax.ShapeDtypeStruct((y_count, depth, X_HI * width), got.dtype),
        compiler_params=grant(8),
        name="order_upper",
    )(core, got, twin)


def early_products(place, upper, stored, offsets, blocks):
    rows, width = stored.shape
    y_count, depth, both = upper.shape

    def body(place_ref, upper_ref, stored_ref, *refs):
        *block_refs, far_ref, rest_ref, turned = refs
        for n, offset in enumerate(offsets):
            turned[n * depth : (n + 1) * depth] = upper_ref[(place_ref[1] + offset + y_count) % y_count]
        at_left = place_ref[0] == 0

        def one(i, carry):
            part = pl.ds(pl.multiple_of(i * TILE_M, TILE_M), TILE_M)
            lhs = jnp.concatenate([ref[part] for ref in block_refs], axis=1)
            total = jnp.dot(lhs, turned[...], preferred_element_type=jnp.float32)
            left, right = total[:, :width], total[:, width:]
            far_ref[part] = jnp.where(at_left, right, left)
            rest_ref[part] = stored_ref[part].astype(jnp.float32) - jnp.where(at_left, left, right)
            return carry

        lax.fori_loop(0, rows // TILE_M, one, 0)

    return pl.pallas_call(
        body,
        in_specs=[pl.BlockSpec(memory_space=pltpu.SMEM)] + [whole()] * (2 + len(blocks)),
        out_specs=[whole(), whole()],
        out_shape=[jax.ShapeDtypeStruct((rows, width), jnp.float32)] * 2,
        scratch_shapes=[VM((len(offsets) * depth, both), upper.dtype)],
        compiler_params=grant(16),
        name="early_products",
    )(place, upper, stored, *blocks)


def last_product(place, upper, base, halves, partner, out_dtype, sign):
    rows, width = base.shape
    y_count, depth, both = upper.shape
    half = rows // len(halves)

    def body(place_ref, upper_ref, base_ref, *refs):
        *half_refs, out_ref = refs
        side = (place_ref[0] + 1) % X_HI if partner else place_ref[0]
        columns = upper_ref[(place_ref[1] + y_count // 2) % y_count]
        columns = jnp.where(side == 0, columns[:, :width], columns[:, width:])
        for n, ref in enumerate(half_refs):
            for start in range(0, half, TILE_M):
                part = slice(n * half + start, n * half + start + TILE_M)
                term = jnp.dot(ref[start : start + TILE_M], columns, preferred_element_type=jnp.float32)
                out_ref[part] = (base_ref[part] + sign * term).astype(out_ref.dtype)

    return pl.pallas_call(
        body,
        in_specs=[pl.BlockSpec(memory_space=pltpu.SMEM)] + [whole()] * (2 + len(halves)),
        out_specs=whole(),
        out_shape=jax.ShapeDtypeStruct((rows, width), out_dtype),
        compiler_params=grant(8),
        name="last_far" if partner else "last_own",
    )(place, upper, base, *halves)


def per_device(slab_block, scale_first, scale_second, panel_lower):
    row_count, col_width = slab_block.shape
    chips = lax.axis_size("chip")
    groups = chips * CORES
    y_count = lax.axis_size("y")
    block_width = panel_lower.shape[1]
    share = row_count // groups
    half = row_count // 2
    quarter = row_count // 4

    up = [(i, (i + 1) % y_count) for i in range(y_count)]
    down = [(i, (i - 1) % y_count) for i in range(y_count)]
    route = {-1: up, 1: down}
    near = tuple(lax.ppermute(panel_lower, "y", route[sign]) for sign in route)

    first = (scale_first.astype(jnp.float32)[:, None] * slab_block.astype(jnp.float32)).astype(
        jnp.bfloat16
    )
    scale_rows = jnp.pad(
        jnp.transpose(scale_second.reshape(share, groups))[None], ((0, PAD - 1), (0, 0), (0, col_width - share))
    )
    packed = jnp.concatenate([first.reshape(share, groups, col_width), scale_rows], axis=0)
    packed = lax.all_to_all(packed, ROW, split_axis=1, concat_axis=0, tiled=True)
    packed = after(packed, *near)
    packed = packed.reshape(groups, share + PAD, col_width)
    cyclic = packed[:, :share].reshape(row_count, col_width)
    scale_cyclic = packed[:, share, :share].reshape(row_count)

    steps, moving = [near], near
    for distance in range(2, y_count // 2):
        moving = tuple(lax.ppermute(block, "y", route[sign]) for block, sign in zip(moving, route))
        steps.append(moving)
    last = (lax.ppermute(moving[0][:half], "y", up), lax.ppermute(moving[1][half:], "y", down))

    level_one = butterfly(cyclic[:half], cyclic[half:])
    second = (scale_cyclic.astype(jnp.float32)[:, None] * level_one).astype(jnp.bfloat16)
    stored = jnp.concatenate(
        [
            butterfly(second[:quarter], second[quarter:half]),
            butterfly(second[half : half + quarter], second[half + quarter :]),
        ],
        axis=0,
    ).astype(jnp.bfloat16)

    top_count = PANEL_W // groups // X_HI
    top = stored[: top_count * X_HI].reshape(1, X_HI, top_count, col_width)
    send = jnp.broadcast_to(top, (chips, X_HI, top_count, col_width)).reshape(
        chips * X_HI, top_count, col_width
    )
    send = after(send, *steps[1])
    got = lax.all_to_all(send, ("chip", "x_hi"), split_axis=0, concat_axis=0)
    twin = lax.ppermute(got, "core", [(0, 1), (1, 0)])
    core = lax.axis_index("core").astype(jnp.int32).reshape(1)
    upper = order_upper(core, got, twin, y_count)
    upper = after(upper, *steps[2])

    place = jnp.stack([lax.axis_index("x_hi"), lax.axis_index("y")]).astype(jnp.int32)
    offsets, blocks = [0], [panel_lower]
    for distance, step in enumerate(steps, 1):
        offsets += [-distance, distance]
        blocks += step
    far, rest = early_products(place, upper, stored, offsets, blocks)
    far = last_product(place, upper, far, last, True, jnp.bfloat16, 1)
    came = lax.ppermute(far, "x_hi", [(i, X_HI - 1 - i) for i in range(X_HI)])
    rest = last_product(place, upper, rest, last, False, jnp.float32, -1)
    return (rest - came.astype(jnp.float32)).astype(jnp.bfloat16)


def solution(mesh):
    rows, cols = mesh.devices.shape
    split = Mesh(
        mesh.devices.reshape(rows // CORES, CORES, X_HI, cols // X_HI), ("chip", "core", "x_hi", "y")
    )
    col = ("x_hi", "y")
    placed = (P(ROW, col), P(ROW), P(ROW), P(ROW, col))
    return jax.shard_map(
        per_device, mesh=split, in_specs=placed, out_specs=P(ROW, col), check_vma=False
    )
```

time: 147 us -> 138 us (0.939)
  the two profiles are of different devices: /device:TPU:2 before, /device:TPU:24 now
where the time goes in v4:
time: 138 us; the launch traced here: 137 us
  starting transfers between devices  45.9 us (33%)
  waiting for transfers between devices  42.7 us (31%)
  blocking collectives  28.9 us (21%)
  Pallas kernels  9.84 us (7%)
  other arithmetic  5.48 us (4%)
  local copies, waits for them, and re-layouts  3.76 us (3%)
    all_to_all x1, blocking collectives, per_device(): got = lax.all_to_all(send, ('chip', 'x_hi'), split_axis=0, concat_axis=0)  28.9 us
    ppermute x4, starting transfers between devices, per_device(): lax.ppermute(block, 'y', route[sign])  15 us
    ppermute x4, waiting for transfers between devices, per_device(): lax.ppermute(block, 'y', route[sign])  12 us
    all_to_all x1, starting transfers between devices, per_device(): lax.all_to_all(packed, ROW, split_axis=1, concat_axis=0, tiled=True)  11.6 us
    ppermute x1, waiting for transfers between devices, per_device(): came = lax.ppermute(far, 'x_hi', [(i, X_HI - 1 - i) for i in range(X_HI)])  11.1 us
    all_to_all x1, waiting for transfers between devices, per_device(): lax.all_to_all(packed, ROW, split_axis=1, concat_axis=0, tiled=True)  6.91 us
    ppermute x2, starting transfers between devices, per_device(): lax.ppermute(panel_lower, 'y', route[sign])  6.61 us
    ppermute x1, waiting for transfers between devices, per_device(): lax.ppermute(moving[1][half:], 'y', down)  6.16 us
  transfers between devices with their start and end apart: 11, of which 6 were waited for; matrix products, arithmetic and copies ran while one was open for 6% of the time, Pallas kernels for 6%

profile of v4, /device:TPU:24, one launch (start us, length us, event | category | flops | bytes accessed | tf_op | source)
XLA Modules:
  0.0 136.9 jit_solution(9190199342043332585)
XLA Ops:
  0.0 4.7 %collective-permute-start = (bf16[2048,256]{1,0:T(8,128)(2,1)}, bf16[2048,256]{1,0:T(8,128)(2,1)S(1)}, u32[]{:S(2)}, u32[]{:S(2)}) collective-permute-start(bf16[2048,256]{1,0:T(8,128)(2,1)} %refs_0_.1), channel_id=1, source_target_pairs={{0,1},{1,2},{2,3},{3,4},{4,5},{5,6},{6,7},{7,0},{8,9},{9,10},{10,1... | collective-permute-start | bytes 3145736 | tf_op jit(solution)/shard_map/ppermute | solution.py:140
  4.7 1.9 %collective-permute-start.1 = (bf16[2048,256]{1,0:T(8,128)(2,1)}, bf16[2048,256]{1,0:T(8,128)(2,1)S(1)}, u32[]{:S(2)}, u32[]{:S(2)}) collective-permute-start(bf16[2048,256]{1,0:T(8,128)(2,1)} %refs_0_.1), channel_id=1, source_target_pairs={{0,7},{1,0},{2,1},{3,2},{4,3},{5,4},{6,5},{7,6},{8,15},{9,8},{10,9... | collective-permute-start | bytes 3145736 | tf_op jit(solution)/shard_map/ppermute | solution.py:140
  6.6 0.7 convert_element_type.51
  7.3 0.8 reshape.38
  8.2 1.4 %multiply_convert_fusion = bf16[2048,128]{1,0:T(8,128)(2,1)S(1)} fusion(bf16[2048,128]{1,0:T(8,128)(2,1)} %param.4, f32[2048]{0:T(1024)S(1)} %convert_element_type.51), kind=kLoop, calls=%fused_computation.5 | loop fusion | flops 786432 | bytes 1056768 | tf_op jit(solution)/shard_map/convert_element_type | solution.py:142
  9.6 1.1 copy.9
  10.7 11.6 %all-to-all-start = ((bf16[72,32,128]{2,0,1:T(8,128)(2,1)}), bf16[72,32,128]{2,0,1:T(8,128)(2,1)S(1)}, u32[]{:S(2)}, u32[]{:S(2)}) async-start(bf16[72,32,128]{2,0,1:T(8,128)(2,1)} %copy.9), calls=%async_computation | async-start | bytes 1179648 | tf_op jit(solution)/shard_map/all_to_all | solution.py:149
  22.3 5.1 %collective-permute-done.refs_1_ = bf16[2048,256]{1,0:T(8,128)(2,1)S(1)} collective-permute-done((bf16[2048,256]{1,0:T(8,128)(2,1)}, bf16[2048,256]{1,0:T(8,128)(2,1)S(1)}, u32[]{:S(2)}, u32[]{:S(2)}) %collective-permute-start) | collective-permute-done | bytes 1048608 | tf_op jit(solution)/shard_map/ppermute | solution.py:140
  27.4 5.5 %collective-permute-start.2 = (bf16[2048,256]{1,0:T(8,128)(2,1)S(1)}, bf16[2048,256]{1,0:T(8,128)(2,1)}, u32[]{:S(2)}, u32[]{:S(2)}) collective-permute-start(bf16[2048,256]{1,0:T(8,128)(2,1)S(1)} %collective-permute-done.refs_1_), channel_id=1, source_target_pairs={{0,1},{1,2},{2,3},{3,4},{4,5},{5,6},{6,7},{7,0},{8,9},{9,10},{10,1... | collective-permute-start | bytes 3145736 | tf_op jit(solution)/shard_map/ppermute | solution.py:157
  32.9 1.9 %collective-permute-start.3 = (bf16[2048,256]{1,0:T(8,128)(2,1)S(1)}, bf16[2048,256]{1,0:T(8,128)(2,1)}, u32[]{:S(2)}, u32[]{:S(2)}) collective-permute-start(bf16[2048,256]{1,0:T(8,128)(2,1)S(1)} %collective-permute-done.1.refs_2_), channel_id=1, source_target_pairs={{0,7},{1,0},{2,1},{3,2},{4,3},{5,4},{6,5},{7,6},{8,15},{9,8},{10,9... | collective-permute-start | bytes 3145736 | tf_op jit(solution)/shard_map/ppermute | solution.py:157
  34.8 6.9 %all-to-all-done = bf16[72,32,128]{2,0,1:T(8,128)(2,1)S(1)} async-done(((bf16[72,32,128]{2,0,1:T(8,128)(2,1)}), bf16[72,32,128]{2,0,1:T(8,128)(2,1)S(1)}, u32[]{:S(2)}, u32[]{:S(2)}) %all-to-all-start) | async-done | bytes 589856 | tf_op jit(solution)/shard_map/all_to_all | solution.py:149
  42.0 0.3 fusion.1
  42.4 12.0 %collective-permute-done.2.refs_3_ = bf16[2048,256]{1,0:T(8,128)(2,1)} collective-permute-done((bf16[2048,256]{1,0:T(8,128)(2,1)S(1)}, bf16[2048,256]{1,0:T(8,128)(2,1)}, u32[]{:S(2)}, u32[]{:S(2)}) %collective-permute-start.2) | collective-permute-done | bytes 1048608 | tf_op jit(solution)/shard_map/ppermute | solution.py:157
  54.4 5.7 %collective-permute-start.5 = (bf16[2048,256]{1,0:T(8,128)(2,1)}, bf16[2048,256]{1,0:T(8,128)(2,1)S(1)}, u32[]{:S(2)}, u32[]{:S(2)}) collective-permute-start(bf16[2048,256]{1,0:T(8,128)(2,1)} %collective-permute-done.2.refs_3_), channel_id=1, source_target_pairs={{0,1},{1,2},{2,3},{3,4},{4,5},{5,6},{6,7},{7,0},{8,9},{9,10},{10,1... | collective-permute-start | bytes 3145736 | tf_op jit(solution)/shard_map/ppermute | solution.py:157
  60.1 1.9 %collective-permute-start.6 = (bf16[2048,256]{1,0:T(8,128)(2,1)}, bf16[2048,256]{1,0:T(8,128)(2,1)S(1)}, u32[]{:S(2)}, u32[]{:S(2)}) collective-permute-start(bf16[2048,256]{1,0:T(8,128)(2,1)} %collective-permute-done.3.refs_4_), channel_id=1, source_target_pairs={{0,7},{1,0},{2,1},{3,2},{4,3},{5,4},{6,5},{7,6},{8,15},{9,8},{10,9... | collective-permute-start | bytes 3145736 | tf_op jit(solution)/shard_map/ppermute | solution.py:157
  62.1 0.8 fusion.8
  63.0 28.9 %all_to_all.23.got_ref = bf16[32,64,128]{2,1,0:T(8,128)(2,1)S(1)} all-to-all(bf16[32,64,128]{2,1,0:T(8,128)(2,1)S(1)} %bitcast.22), channel_id=1, replica_groups=mesh['chip'=16,'core'=2,'x_hi'=2,'y'=8] {'chip','x_hi'}, dimensions={0} | all-to-all | bytes 1048576 | tf_op jit(solution)/shard_map/all_to_all | solution.py:177
  91.9 1.9 %collective-permute-start.4 = (bf16[32,64,128]{2,1,0:T(8,128)(2,1)S(1)}, bf16[32,64,128]{2,1,0:T(8,128)(2,1)}, u32[]{:S(2)}, u32[]{:S(2)}) collective-permute-start(bf16[32,64,128]{2,1,0:T(8,128)(2,1)S(1)} %all_to_all.23.got_ref), channel_id=1, source_target_pairs={{0,16},{16,0},{1,17},{17,1},{2,18},{18,2},{3,19},{19,3},{4,20},{20... | collective-permute-start | bytes 1572872 | tf_op jit(solution)/shard_map/ppermute | solution.py:178
  93.8 0.8 slice.54
  94.7 4.8 %collective-permute-start.7 = (bf16[1024,256]{1,0:T(8,128)(2,1)}, bf16[1024,256]{1,0:T(8,128)(2,1)S(1)}, u32[]{:S(2)}, u32[]{:S(2)}) collective-permute-start(bf16[1024,256]{1,0:T(8,128)(2,1)} %slice.54), channel_id=1, source_target_pairs={{0,1},{1,2},{2,3},{3,4},{4,5},{5,6},{6,7},{7,0},{8,9},{9,10},{10,1... | collective-permute-start | bytes 1572872 | tf_op jit(solution)/shard_map/ppermute | solution.py:159
  99.5 0.8 slice.55
  100.4 1.9 %collective-permute-start.8 = (bf16[1024,256]{1,0:T(8,128)(2,1)}, bf16[1024,256]{1,0:T(8,128)(2,1)}, u32[]{:S(2)}, u32[]{:S(2)}) collective-permute-start(bf16[1024,256]{1,0:T(8,128)(2,1)} %slice.55), channel_id=1, source_target_pairs={{0,7},{1,0},{2,1},{3,2},{4,3},{5,4},{6,5},{7,6},{8,15},{9,8},{10,9... | collective-permute-start | bytes 1572872 | tf_op jit(solution)/shard_map/ppermute | solution.py:159
  102.4 1.0 pad_maximum_fusion.stored_ref
  103.4 2.0 %order_upper.1.upper_ref = bf16[8,256,256]{2,1,0:T(8,128)(2,1)S(1)} custom-call(s32[1]{0:T(128)} %bitcast.2.core_ref, bf16[32,64,128]{2,1,0:T(8,128)(2,1)S(1)} %all_to_all.23.got_ref, bf16[32,64,128]{2,1,0:T(8,128)(2,1)} %collective-permute-done.4.twin_ref), custom_call_target="tpu_custom_call" | custom-call | tf_op jit(solution)/shard_map/order_upper/pallas_call | solution.py:59
  105.4 4.9 %early_products.1 = (f32[2048,128]{1,0:T(8,128)S(1)}, f32[2048,128]{1,0:T(8,128)S(1)}) custom-call(s32[2]{0:T(128)S(1)} %pad_add_fusion.place_ref, bf16[8,256,256]{2,1,0:T(8,128)(2,1)S(1)} %order_upper.1.upper_ref, bf16[2048,128]{1,0:T(8,128)(2,1)S(1)} %pad_maximum_fusion.stored_ref, bf16[2048,256]{1,0:T(8,128)(2,1)S(1)} %copy-done, ...), custom_call_target="tpu_custom_call" | custom-call | tf_op jit(solution)/shard_map/early_products/pallas_call | solution.py:90
  110.3 1.3 collective-permute-done.7.refs_0_
  111.7 6.2 %collective-permute-done.8.refs_1_ = bf16[1024,256]{1,0:T(8,128)(2,1)} collective-permute-done((bf16[1024,256]{1,0:T(8,128)(2,1)}, bf16[1024,256]{1,0:T(8,128)(2,1)}, u32[]{:S(2)}, u32[]{:S(2)}) %collective-permute-start.8) | collective-permute-done | bytes 524320 | tf_op jit(solution)/shard_map/ppermute | solution.py:159
  117.8 1.5 %last_far.1 = bf16[2048,128]{1,0:T(8,128)(2,1)S(1)} custom-call(s32[2]{0:T(128)S(1)} %pad_add_fusion.place_ref, bf16[8,256,256]{2,1,0:T(8,128)(2,1)S(1)} %order_upper.1.upper_ref, f32[2048,128]{1,0:T(8,128)S(1)} %get-tuple-element.14.base_ref, bf16[1024,256]{1,0:T(8,128)(2,1)S(1)} %collective-permute-done.7.refs_0_, ...), custom_call_target="tpu_custom_call" | custom-call | tf_op jit(solution)/shard_map/last_far/pallas_call | solution.py:117
  119.3 4.0 %collective-permute-start.9 = (bf16[2048,128]{1,0:T(8,128)(2,1)S(1)}, bf16[2048,128]{1,0:T(8,128)(2,1)S(1)}, u32[]{:S(2)}, u32[]{:S(2)}) collective-permute-start(bf16[2048,128]{1,0:T(8,128)(2,1)S(1)} %last_far.1), channel_id=1, source_target_pairs={{0,8},{8,0},{1,9},{9,1},{2,10},{10,2},{3,11},{11,3},{4,12},{12,4},... | collective-permute-start | bytes 1572872 | tf_op jit(solution)/shard_map/ppermute | solution.py:190
  123.3 1.5 %last_own.1 = f32[2048,128]{1,0:T(8,128)S(1)} custom-call(s32[2]{0:T(128)S(1)} %pad_add_fusion.place_ref, bf16[8,256,256]{2,1,0:T(8,128)(2,1)S(1)} %order_upper.1.upper_ref, f32[2048,128]{1,0:T(8,128)S(1)} %get-tuple-element.13.base_ref, bf16[1024,256]{1,0:T(8,128)(2,1)S(1)} %collective-permute-done.7.refs_0_, bf16[1024,256]{1,0:T(8,128)(2,1)} %collective-permute-done.8.refs_1_), custom_call_target="tpu_custom_call" | custom-call | tf_op jit(solution)/shard_map/last_own/pallas_call | solution.py:117
  124.8 11.1 %collective-permute-done.9 = bf16[2048,128]{1,0:T(8,128)(2,1)S(1)} collective-permute-done((bf16[2048,128]{1,0:T(8,128)(2,1)S(1)}, bf16[2048,128]{1,0:T(8,128)(2,1)S(1)}, u32[]{:S(2)}, u32[]{:S(2)}) %collective-permute-start.9) | collective-permute-done | bytes 524320 | tf_op jit(solution)/shard_map/ppermute | solution.py:190
  136.0 0.9 subtract_convert_fusion
  (23 shorter events, 0.6 us)
Async XLA Ops:
  0.0 27.4 %collective-permute-start = (bf16[2048,256]{1,0:T(8,128)(2,1)}, bf16[2048,256]{1,0:T(8,128)(2,1)S(1)}, u32[]{:S(2)}, u32[]{:S(2)}) collective-permute-start(bf16[2048,256]{1,0:T(8,128)(2,1)} %refs_0_.1), channel_id=1, source_target_pairs={{0,1},{1,2},{2,3},{3,4},{4,5},{5,6},{6,7},{7,0},{8,9},{9,10},{10,1... | collective-permute-start | bytes 3145736 | tf_op jit(solution)/shard_map/ppermute | solution.py:140
  4.7 28.2 %collective-permute-start.1 = (bf16[2048,256]{1,0:T(8,128)(2,1)}, bf16[2048,256]{1,0:T(8,128)(2,1)S(1)}, u32[]{:S(2)}, u32[]{:S(2)}) collective-permute-start(bf16[2048,256]{1,0:T(8,128)(2,1)} %refs_0_.1), channel_id=1, source_target_pairs={{0,7},{1,0},{2,1},{3,2},{4,3},{5,4},{6,5},{7,6},{8,15},{9,8},{10,9... | collective-permute-start | bytes 3145736 | tf_op jit(solution)/shard_map/ppermute | solution.py:140
  10.7 31.1 %all-to-all-start = ((bf16[72,32,128]{2,0,1:T(8,128)(2,1)}), bf16[72,32,128]{2,0,1:T(8,128)(2,1)S(1)}, u32[]{:S(2)}, u32[]{:S(2)}) async-start(bf16[72,32,128]{2,0,1:T(8,128)(2,1)} %copy.9), calls=%async_computation | async-start | bytes 1179648 | tf_op jit(solution)/shard_map/all_to_all | solution.py:149
  27.4 15.0 %copy-start.1 = (bf16[2048,256]{1,0:T(8,128)(2,1)}, bf16[2048,256]{1,0:T(8,128)(2,1)S(1)}, u32[]{:S(2)}) copy-start(bf16[2048,256]{1,0:T(8,128)(2,1)S(1)} %collective-permute-done.refs_1_) | copy-start | bytes 3145732
  27.4 27.0 %collective-permute-start.2 = (bf16[2048,256]{1,0:T(8,128)(2,1)S(1)}, bf16[2048,256]{1,0:T(8,128)(2,1)}, u32[]{:S(2)}, u32[]{:S(2)}) collective-permute-start(bf16[2048,256]{1,0:T(8,128)(2,1)S(1)} %collective-permute-done.refs_1_), channel_id=1, source_target_pairs={{0,1},{1,2},{2,3},{3,4},{4,5},{5,6},{6,7},{7,0},{8,9},{9,10},{10,1... | collective-permute-start | bytes 3145736 | tf_op jit(solution)/shard_map/ppermute | solution.py:157
  32.9 9.5 %copy-start.3 = (bf16[2048,256]{1,0:T(8,128)(2,1)}, bf16[2048,256]{1,0:T(8,128)(2,1)S(1)}, u32[]{:S(2)}) copy-start(bf16[2048,256]{1,0:T(8,128)(2,1)S(1)} %collective-permute-done.1.refs_2_) | copy-start | bytes 3145732
  32.9 27.2 %collective-permute-start.3 = (bf16[2048,256]{1,0:T(8,128)(2,1)S(1)}, bf16[2048,256]{1,0:T(8,128)(2,1)}, u32[]{:S(2)}, u32[]{:S(2)}) collective-permute-start(bf16[2048,256]{1,0:T(8,128)(2,1)S(1)} %collective-permute-done.1.refs_2_), channel_id=1, source_target_pairs={{0,7},{1,0},{2,1},{3,2},{4,3},{5,4},{6,5},{7,6},{8,15},{9,8},{10,9... | collective-permute-start | bytes 3145736 | tf_op jit(solution)/shard_map/ppermute | solution.py:157
  54.4 39.4 %collective-permute-start.5 = (bf16[2048,256]{1,0:T(8,128)(2,1)}, bf16[2048,256]{1,0:T(8,128)(2,1)S(1)}, u32[]{:S(2)}, u32[]{:S(2)}) collective-permute-start(bf16[2048,256]{1,0:T(8,128)(2,1)} %collective-permute-done.2.refs_3_), channel_id=1, source_target_pairs={{0,1},{1,2},{2,3},{3,4},{4,5},{5,6},{6,7},{7,0},{8,9},{9,10},{10,1... | collective-permute-start | bytes 3145736 | tf_op jit(solution)/shard_map/ppermute | solution.py:157
  60.1 39.4 %collective-permute-start.6 = (bf16[2048,256]{1,0:T(8,128)(2,1)}, bf16[2048,256]{1,0:T(8,128)(2,1)S(1)}, u32[]{:S(2)}, u32[]{:S(2)}) collective-permute-start(bf16[2048,256]{1,0:T(8,128)(2,1)} %collective-permute-done.3.refs_4_), channel_id=1, source_target_pairs={{0,7},{1,0},{2,1},{3,2},{4,3},{5,4},{6,5},{7,6},{8,15},{9,8},{10,9... | collective-permute-start | bytes 3145736 | tf_op jit(solution)/shard_map/ppermute | solution.py:157
  91.9 11.5 %collective-permute-start.4 = (bf16[32,64,128]{2,1,0:T(8,128)(2,1)S(1)}, bf16[32,64,128]{2,1,0:T(8,128)(2,1)}, u32[]{:S(2)}, u32[]{:S(2)}) collective-permute-start(bf16[32,64,128]{2,1,0:T(8,128)(2,1)S(1)} %all_to_all.23.got_ref), channel_id=1, source_target_pairs={{0,16},{16,0},{1,17},{17,1},{2,18},{18,2},{3,19},{19,3},{4,20},{20... | collective-permute-start | bytes 1572872 | tf_op jit(solution)/shard_map/ppermute | solution.py:178
  94.7 17.0 %collective-permute-start.7 = (bf16[1024,256]{1,0:T(8,128)(2,1)}, bf16[1024,256]{1,0:T(8,128)(2,1)S(1)}, u32[]{:S(2)}, u32[]{:S(2)}) collective-permute-start(bf16[1024,256]{1,0:T(8,128)(2,1)} %slice.54), channel_id=1, source_target_pairs={{0,1},{1,2},{2,3},{3,4},{4,5},{5,6},{6,7},{7,0},{8,9},{9,10},{10,1... | collective-permute-start | bytes 1572872 | tf_op jit(solution)/shard_map/ppermute | solution.py:159
  100.4 17.5 %collective-permute-start.8 = (bf16[1024,256]{1,0:T(8,128)(2,1)}, bf16[1024,256]{1,0:T(8,128)(2,1)}, u32[]{:S(2)}, u32[]{:S(2)}) collective-permute-start(bf16[1024,256]{1,0:T(8,128)(2,1)} %slice.55), channel_id=1, source_target_pairs={{0,7},{1,0},{2,1},{3,2},{4,3},{5,4},{6,5},{7,6},{8,15},{9,8},{10,9... | collective-permute-start | bytes 1572872 | tf_op jit(solution)/shard_map/ppermute | solution.py:159
  102.4 3.0 %copy-start.4 = (bf16[2048,256]{1,0:T(8,128)(2,1)S(1)}, bf16[2048,256]{1,0:T(8,128)(2,1)}, u32[]{:S(2)}) copy-start(bf16[2048,256]{1,0:T(8,128)(2,1)} %copy-done.3) | copy-start | bytes 3145732
  103.4 2.0 %copy-start = (bf16[2048,256]{1,0:T(8,128)(2,1)S(1)}, bf16[2048,256]{1,0:T(8,128)(2,1)}, u32[]{:S(2)}) copy-start(bf16[2048,256]{1,0:T(8,128)(2,1)} %refs_0_.1) | copy-start | bytes 3145732
  103.4 2.0 %copy-start.2 = (bf16[2048,256]{1,0:T(8,128)(2,1)S(1)}, bf16[2048,256]{1,0:T(8,128)(2,1)}, u32[]{:S(2)}) copy-start(bf16[2048,256]{1,0:T(8,128)(2,1)} %copy-done.1) | copy-start | bytes 3145732
  119.3 16.6 %collective-permute-start.9 = (bf16[2048,128]{1,0:T(8,128)(2,1)S(1)}, bf16[2048,128]{1,0:T(8,128)(2,1)S(1)}, u32[]{:S(2)}, u32[]{:S(2)}) collective-permute-start(bf16[2048,128]{1,0:T(8,128)(2,1)S(1)} %last_far.1), channel_id=1, source_target_pairs={{0,8},{8,0},{1,9},{9,1},{2,10},{10,2},{3,11},{11,3},{4,12},{12,4},... | collective-permute-start | bytes 1572872 | tf_op jit(solution)/shard_map/ppermute | solution.py:190

commit v5 on v4

--- a/solution.py
+++ b/solution.py
@@ -10,6 +10,7 @@
 CORES = 2
 PAD = 8
 TILE_M = 256
+SPLIT = 1024
 ROW = ("chip", "core")
 
 inv_root = 0.7071067811865476
@@ -66,62 +67,71 @@
     )(core, got, twin)
 
 
-def early_products(place, upper, stored, offsets, blocks):
-    rows, width = stored.shape
+def early_products(place, upper, stored, offsets, blocks, bounds):
+    width = stored.shape[1]
     y_count, depth, both = upper.shape
+    flat, where = [], []
+    for block in blocks:
+        where.append(len(flat))
+        flat += block
 
     def body(place_ref, upper_ref, stored_ref, *refs):
-        *block_refs, far_ref, rest_ref, turned = refs
+        block_refs, out_refs, turned = refs[: len(flat)], refs[len(flat) : -1], refs[-1]
         for n, offset in enumerate(offsets):
             turned[n * depth : (n + 1) * depth] = upper_ref[(place_ref[1] + offset + y_count) % y_count]
         at_left = place_ref[0] == 0
 
-        def one(i, carry):
-            part = pl.ds(pl.multiple_of(i * TILE_M, TILE_M), TILE_M)
-            lhs = jnp.concatenate([ref[part] for ref in block_refs], axis=1)
-            total = jnp.dot(lhs, turned[...], preferred_element_type=jnp.float32)
-            left, right = total[:, :width], total[:, width:]
-            far_ref[part] = jnp.where(at_left, right, left)
-            rest_ref[part] = stored_ref[part].astype(jnp.float32) - jnp.where(at_left, left, right)
-            return carry
-
-        lax.fori_loop(0, rows // TILE_M, one, 0)
-
+        for p, (start, stop) in enumerate(bounds):
+            far_ref, rest_ref = out_refs[2 * p : 2 * p + 2]
+
+            def one(i, carry):
+                local = pl.ds(pl.multiple_of(i * TILE_M, TILE_M), TILE_M)
+                full = pl.ds(pl.multiple_of(start + i * TILE_M, TILE_M), TILE_M)
+                tiles = [
+                    block_refs[n][full] if len(block) == 1 else block_refs[n + p][local]
+                    for n, block in zip(where, blocks)
+                ]
+                total = jnp.dot(jnp.concatenate(tiles, axis=1), turned[...], preferred_element_type=jnp.float32)
+                left, right = total[:, :width], total[:, width:]
+                far_ref[local] = jnp.where(at_left, right, left)
+                rest_ref[local] = stored_ref[full].astype(jnp.float32) - jnp.where(at_left, left, right)
+                return carry
+
+            lax.fori_loop(0, (stop - start) // TILE_M, one, 0)
+
+    shapes = [jax.ShapeDtypeStruct((stop - start, width), jnp.float32) for start, stop in bounds for _ in range(2)]
     return pl.pallas_call(
         body,
-        in_specs=[pl.BlockSpec(memory_space=pltpu.SMEM)] + [whole()] * (2 + len(blocks)),
-        out_specs=[whole(), whole()],
-        out_shape=[jax.ShapeDtypeStruct((rows, width), jnp.float32)] * 2,
+        in_specs=[pl.BlockSpec(memory_space=pltpu.SMEM)] + [whole()] * (2 + len(flat)),
+        out_specs=[whole()] * len(shapes),
+        out_shape=shapes,
         scratch_shapes=[VM((len(offsets) * depth, both), upper.dtype)],
         compiler_params=grant(16),
         name="early_products",
-    )(place, upper, stored, *blocks)
-
-
-def last_product(place, upper, base, halves, partner, out_dtype, sign):
+    )(place, upper, stored, *flat)
+
+
+def last_product(place, upper, base, block, partner, out_dtype, sign):
     rows, width = base.shape
-    y_count, depth, both = upper.shape
-    half = rows // len(halves)
-
-    def body(place_ref, upper_ref, base_ref, *refs):
-        *half_refs, out_ref = refs
+    y_count = upper.shape[0]
+
+    def body(place_ref, upper_ref, base_ref, block_ref, out_ref):
         side = (place_ref[0] + 1) % X_HI if partner else place_ref[0]
         columns = upper_ref[(place_ref[1] + y_count // 2) % y_count]
         columns = jnp.where(side == 0, columns[:, :width], columns[:, width:])
-        for n, ref in enumerate(half_refs):
-            for start in range(0, half, TILE_M):
-                part = slice(n * half + start, n * half + start + TILE_M)
-                term = jnp.dot(ref[start : start + TILE_M], columns, preferred_element_type=jnp.float32)
-                out_ref[part] = (base_ref[part] + sign * term).astype(out_ref.dtype)
+        for start in range(0, rows, TILE_M):
+            part = slice(start, start + TILE_M)
+            term = jnp.dot(block_ref[part], columns, preferred_element_type=jnp.float32)
+            out_ref[part] = (base_ref[part] + sign * term).astype(out_ref.dtype)
 
     return pl.pallas_call(
         body,
-        in_specs=[pl.BlockSpec(memory_space=pltpu.SMEM)] + [whole()] * (2 + len(halves)),
+        in_specs=[pl.BlockSpec(memory_space=pltpu.SMEM)] + [whole()] * 3,
         out_specs=whole(),
         out_shape=jax.ShapeDtypeStruct((rows, width), out_dtype),
         compiler_params=grant(8),
         name="last_far" if partner else "last_own",
-    )(place, upper, base, *halves)
+    )(place, upper, base, block)
 
 
 def per_device(slab_block, scale_first, scale_second, panel_lower):
@@ -147,16 +157,22 @@
     )
     packed = jnp.concatenate([first.reshape(share, groups, col_width), scale_rows], axis=0)
     packed = lax.all_to_all(packed, ROW, split_axis=1, concat_axis=0, tiled=True)
-    packed = after(packed, *near)
+    bounds = ((0, SPLIT), (SPLIT, row_count))
+    first_keys, second_keys = ((0, -1), (1, 1)), ((1, -1), (0, 1))
+    moving = {}
+    for part, sign in first_keys + second_keys:
+        start, stop = bounds[part]
+        moving[part, sign] = near[0 if sign < 0 else 1][start:stop]
+    steps = []
+    for distance in range(2, y_count // 2 + 1):
+        keys = first_keys if 2 * distance == y_count else first_keys + second_keys
+        for part, sign in keys:
+            moving[part, sign] = lax.ppermute(moving[part, sign], "y", route[sign])
+        steps.append({key: moving[key] for key in keys})
+    packed = after(packed, *(steps[0][key] for key in first_keys))
     packed = packed.reshape(groups, share + PAD, col_width)
     cyclic = packed[:, :share].reshape(row_count, col_width)
     scale_cyclic = packed[:, share, :share].reshape(row_count)
-
-    steps, moving = [near], near
-    for distance in range(2, y_count // 2):
-        moving = tuple(lax.ppermute(block, "y", route[sign]) for block, sign in zip(moving, route))
-        steps.append(moving)
-    last = (lax.ppermute(moving[0][:half], "y", up), lax.ppermute(moving[1][half:], "y", down))
 
     level_one = butterfly(cyclic[:half], cyclic[half:])
     second = (scale_cyclic.astype(jnp.float32)[:, None] * level_one).astype(jnp.bfloat16)
@@ -173,23 +189,26 @@
     send = jnp.broadcast_to(top, (chips, X_HI, top_count, col_width)).reshape(
         chips * X_HI, top_count, col_width
     )
-    send = after(send, *steps[1])
     got = lax.all_to_all(send, ("chip", "x_hi"), split_axis=0, concat_axis=0)
+    got = after(got, *steps[1].values())
     twin = lax.ppermute(got, "core", [(0, 1), (1, 0)])
     core = lax.axis_index("core").astype(jnp.int32).reshape(1)
     upper = order_upper(core, got, twin, y_count)
-    upper = after(upper, *steps[2])
-
     place = jnp.stack([lax.axis_index("x_hi"), lax.axis_index("y")]).astype(jnp.int32)
-    offsets, blocks = [0], [panel_lower]
-    for distance, step in enumerate(steps, 1):
-        offsets += [-distance, distance]
-        blocks += step
-    far, rest = early_products(place, upper, stored, offsets, blocks)
-    far = last_product(place, upper, far, last, True, jnp.bfloat16, 1)
-    came = lax.ppermute(far, "x_hi", [(i, X_HI - 1 - i) for i in range(X_HI)])
-    rest = last_product(place, upper, rest, last, False, jnp.float32, -1)
-    return (rest - came.astype(jnp.float32)).astype(jnp.bfloat16)
+    offsets, blocks = [0, -1, 1], [(panel_lower,), near[:1], near[1:]]
+    for distance, step in enumerate(steps[:-1], 2):
+        for sign in route:
+            offsets.append(sign * distance)
+            blocks.append((step[0, sign], step[1, sign]))
+    sums = early_products(place, upper, stored, offsets, blocks, bounds)
+    swap = [(i, X_HI - 1 - i) for i in range(X_HI)]
+    out = []
+    for key, far, rest in zip(first_keys, sums[::2], sums[1::2]):
+        far = last_product(place, upper, far, steps[-1][key], True, jnp.bfloat16, 1)
+        came = lax.ppermute(far, "x_hi", swap)
+        rest = last_product(place, upper, rest, steps[-1][key], False, jnp.float32, -1)
+        out.append((rest - came.astype(jnp.float32)).astype(jnp.bfloat16))
+    return jnp.concatenate(out, axis=0)
 
 
 def solution(mesh):

time: 138 us -> 138 us (level)
  blocking collectives: 28.9 us -> 0 us
  starting transfers between devices: 45.9 us -> 73 us
  waiting for transfers between devices: 42.7 us -> 34.5 us
  local copies, waits for them, and re-layouts: 3.76 us -> 8.68 us
  other arithmetic: 5.48 us -> 9.73 us
    all_to_all x1 -> x0, blocking collectives: 28.9 us -> none  [per_device(): got = lax.all_to_all(send, ('chip', 'x_hi'), split_axis=0, concat_axis=0)]
    ppermute x7 -> x12, starting transfers between devices: 25.8 us -> 39.6 us  [the longest x10 32 us: per_device(): moving[part, sign] = lax.ppermute(moving[part, sign], 'y', route[sign])]
    all_to_all x0 -> x1, starting transfers between devices: none -> 13.2 us  [per_device(): got = lax.all_to_all(send, ('chip', 'x_hi'), split_axis=0, concat_axis=0)]
    all_to_all x1, waiting for transfers between devices: 6.91 us -> 0.01 us  [per_device(): lax.all_to_all(packed, ROW, split_axis=1, concat_axis=0, tiled=True)]
    unnamed x10 -> x26, local copies, waits for them, and re-layouts: 0.02 us -> 3.71 us
    mul x1, other arithmetic: 0.13 us -> 2.34 us  [butterfly(): (top + bottom) * inv_root]
    pallas_call x2 -> x4, Pallas kernels: 2.98 us -> 4.36 us  [last_product(): pl.pallas_call(body, in_specs=[pl.BlockSpec(memory_space=pltpu.SMEM)] + [...]
    ppermute x7 -> x12, waiting for transfers between devices: 30.7 us -> 29.5 us  [the longest x10 23 us: per_device(): moving[part, sign] = lax.ppermute(moving[part, sign], 'y', route[sign])]
  transfers between devices with their start and end apart: 11 -> 17, of which waited for: 6 -> 10; matrix products, arithmetic and copies ran while one was open for 6% -> 10% of each run, Pallas kernels for 6% -> 8%
where the time goes in v5:
time: 138 us; the launch traced here: 137 us
  starting transfers between devices  73 us (53%)
  waiting for transfers between devices  34.5 us (25%)
  Pallas kernels  10.9 us (8%)
  other arithmetic  9.73 us (7%)
  local copies, waits for them, and re-layouts  8.68 us (6%)
    ppermute x10, starting transfers between devices, per_device(): moving[part, sign] = lax.ppermute(moving[part, sign], 'y', route[sign])  32 us
    ppermute x10, waiting for transfers between devices, per_device(): moving[part, sign] = lax.ppermute(moving[part, sign], 'y', route[sign])  23 us
    all_to_all x1, starting transfers between devices, per_device(): got = lax.all_to_all(send, ('chip', 'x_hi'), split_axis=0, concat_axis=0)  13.2 us
    all_to_all x1, starting transfers between devices, per_device(): lax.all_to_all(packed, ROW, split_axis=1, concat_axis=0, tiled=True)  11.8 us
    ppermute x2, starting transfers between devices, per_device(): came = lax.ppermute(far, 'x_hi', swap)  7.59 us
    ppermute x2, starting transfers between devices, per_device(): lax.ppermute(panel_lower, 'y', route[sign])  6.61 us
    ppermute x2, waiting for transfers between devices, per_device(): came = lax.ppermute(far, 'x_hi', swap)  6.49 us
    ppermute x2, waiting for transfers between devices, per_device(): lax.ppermute(panel_lower, 'y', route[sign])  4.96 us
  transfers between devices with their start and end apart: 17, of which 10 were waited for; matrix products, arithmetic and copies ran while one was open for 10% of the time, Pallas kernels for 8%

profile of v5, /device:TPU:24, one launch (start us, length us, event | category | flops | bytes accessed | tf_op | source)
XLA Modules:
  0.0 137.2 jit_solution(13106681409562698086)
XLA Ops:
  0.0 4.7 %collective-permute-start = (bf16[2048,256]{1,0:T(8,128)(2,1)}, bf16[2048,256]{1,0:T(8,128)(2,1)S(1)}, u32[]{:S(2)}, u32[]{:S(2)}) collective-permute-start(bf16[2048,256]{1,0:T(8,128)(2,1)} %refs_0_.1), channel_id=1, source_target_pairs={{0,1},{1,2},{2,3},{3,4},{4,5},{5,6},{6,7},{7,0},{8,9},{9,10},{10,1... | collective-permute-start | bytes 3145736 | tf_op jit(solution)/shard_map/ppermute | solution.py:150
  4.7 1.9 %collective-permute-start.2 = (bf16[2048,256]{1,0:T(8,128)(2,1)}, bf16[2048,256]{1,0:T(8,128)(2,1)S(1)}, u32[]{:S(2)}, u32[]{:S(2)}) collective-permute-start(bf16[2048,256]{1,0:T(8,128)(2,1)} %refs_0_.1), channel_id=1, source_target_pairs={{0,7},{1,0},{2,1},{3,2},{4,3},{5,4},{6,5},{7,6},{8,15},{9,8},{10,9... | collective-permute-start | bytes 3145736 | tf_op jit(solution)/shard_map/ppermute | solution.py:150
  8.2 1.4 %multiply_convert_fusion = bf16[2048,128]{1,0:T(8,128)(2,1)S(1)} fusion(bf16[2048,128]{1,0:T(8,128)(2,1)} %param.4, f32[2048]{0:T(1024)S(1)} %convert_element_type.57), kind=kLoop, calls=%fused_computation.4 | loop fusion | flops 786432 | bytes 1056768 | tf_op jit(solution)/shard_map/convert_element_type | solution.py:152
  10.7 11.8 %all-to-all-start = ((bf16[72,32,128]{2,0,1:T(8,128)(2,1)}), bf16[72,32,128]{2,0,1:T(8,128)(2,1)}, u32[]{:S(2)}, u32[]{:S(2)}) async-start(bf16[72,32,128]{2,0,1:T(8,128)(2,1)} %copy.9), calls=%async_computation | async-start | bytes 1179648 | tf_op jit(solution)/shard_map/all_to_all | solution.py:159
  22.4 5.0 %collective-permute-done.refs_1_ = bf16[2048,256]{1,0:T(8,128)(2,1)S(1)} collective-permute-done((bf16[2048,256]{1,0:T(8,128)(2,1)}, bf16[2048,256]{1,0:T(8,128)(2,1)S(1)}, u32[]{:S(2)}, u32[]{:S(2)}) %collective-permute-start) | collective-permute-done | bytes 1048608 | tf_op jit(solution)/shard_map/ppermute | solution.py:150
  28.4 5.5 %collective-permute-start.1 = (bf16[1024,256]{1,0:T(8,128)(2,1)}, bf16[1024,256]{1,0:T(8,128)(2,1)S(1)}, u32[]{:S(2)}, u32[]{:S(2)}) collective-permute-start(bf16[1024,256]{1,0:T(8,128)(2,1)} %get-tuple-element.20), channel_id=1, source_target_pairs={{0,1},{1,2},{2,3},{3,4},{4,5},{5,6},{6,7},{7,0},{8,9},{9,10},{10,1... | collective-permute-start | bytes 1572872 | tf_op jit(solution)/shard_map/ppermute | solution.py:170
  35.0 1.9 %collective-permute-start.3 = (bf16[1024,256]{1,0:T(8,128)(2,1)}, bf16[1024,256]{1,0:T(8,128)(2,1)S(1)}, u32[]{:S(2)}, u32[]{:S(2)}) collective-permute-start(bf16[1024,256]{1,0:T(8,128)(2,1)} %get-tuple-element.18), channel_id=1, source_target_pairs={{0,7},{1,0},{2,1},{3,2},{4,3},{5,4},{6,5},{7,6},{8,15},{9,8},{10,9... | collective-permute-start | bytes 1572872 | tf_op jit(solution)/shard_map/ppermute | solution.py:170
  36.9 5.1 %collective-permute-start.6 = (bf16[1024,256]{1,0:T(8,128)(2,1)}, bf16[1024,256]{1,0:T(8,128)(2,1)}, u32[]{:S(2)}, u32[]{:S(2)}) collective-permute-start(bf16[1024,256]{1,0:T(8,128)(2,1)} %get-tuple-element.19), channel_id=1, source_target_pairs={{0,1},{1,2},{2,3},{3,4},{4,5},{5,6},{6,7},{7,0},{8,9},{9,10},{10,1... | collective-permute-start | bytes 1572872 | tf_op jit(solution)/shard_map/ppermute | solution.py:170
  42.0 1.9 %collective-permute-start.8 = (bf16[1024,256]{1,0:T(8,128)(2,1)}, bf16[1024,256]{1,0:T(8,128)(2,1)}, u32[]{:S(2)}, u32[]{:S(2)}) collective-permute-start(bf16[1024,256]{1,0:T(8,128)(2,1)} %get-tuple-element.17), channel_id=1, source_target_pairs={{0,7},{1,0},{2,1},{3,2},{4,3},{5,4},{6,5},{7,6},{8,15},{9,8},{10,9... | collective-permute-start | bytes 1572872 | tf_op jit(solution)/shard_map/ppermute | solution.py:170
  44.0 2.6 %collective-permute-done.1.refs_3_ = bf16[1024,256]{1,0:T(8,128)(2,1)S(1)} collective-permute-done((bf16[1024,256]{1,0:T(8,128)(2,1)}, bf16[1024,256]{1,0:T(8,128)(2,1)S(1)}, u32[]{:S(2)}, u32[]{:S(2)}) %collective-permute-start.1) | collective-permute-done | bytes 524320 | tf_op jit(solution)/shard_map/ppermute | solution.py:170
  46.6 6.5 %collective-permute-done.3.refs_6_ = bf16[1024,256]{1,0:T(8,128)(2,1)S(1)} collective-permute-done((bf16[1024,256]{1,0:T(8,128)(2,1)}, bf16[1024,256]{1,0:T(8,128)(2,1)S(1)}, u32[]{:S(2)}, u32[]{:S(2)}) %collective-permute-start.3) | collective-permute-done | bytes 524320 | tf_op jit(solution)/shard_map/ppermute | solution.py:170
  53.1 2.3 %fusion.3 = (f32[16,64,128]{2,1,0:T(8,128)}, f32[16,64,128]{2,1,0:T(8,128)}) fusion(bf16[32,72,128]{2,1,0:T(8,128)(2,1)} %bitcast.9), kind=kLoop, calls=%fused_computation.8 | loop fusion | flops 786432 | bytes 1572864 | tf_op jit(solution)/shard_map/mul | solution.py:22
  56.4 1.5 %fusion.1 = bf16[2048,128]{1,0:T(8,128)(2,1)S(1)} fusion(f32[1024,128]{1,0:T(8,128)} %bitcast.18, f32[1024,128]{1,0:T(8,128)} %bitcast.17, f32[2048]{0:T(1024)S(1)} %reshape.41), kind=kLoop, calls=%fused_computation.3 | loop fusion | flops 786432 | bytes 1581056 | tf_op jit(solution)/shard_map/convert_element_type | solution.py:178
  59.7 13.2 %all-to-all-start.1 = ((bf16[32,64,128]{2,1,0:T(8,128)(2,1)}), bf16[32,64,128]{2,1,0:T(8,128)(2,1)S(1)}, u32[]{:S(2)}, u32[]{:S(2)}) async-start(bf16[32,64,128]{2,1,0:T(8,128)(2,1)} %bitcast.19), calls=%async_computation.1 | async-start | bytes 1048576 | tf_op jit(solution)/shard_map/all_to_all | solution.py:192
  72.9 1.9 %collective-permute-start.4 = (bf16[1024,256]{1,0:T(8,128)(2,1)S(1)}, bf16[1024,256]{1,0:T(8,128)(2,1)S(1)}, u32[]{:S(2)}, u32[]{:S(2)}) collective-permute-start(bf16[1024,256]{1,0:T(8,128)(2,1)S(1)} %collective-permute-done.1.refs_3_), channel_id=1, source_target_pairs={{0,1},{1,2},{2,3},{3,4},{4,5},{5,6},{6,7},{7,0},{8,9},{9,10},{10,1... | collective-permute-start | bytes 1572872 | tf_op jit(solution)/shard_map/ppermute | solution.py:170
  74.8 3.9 %collective-permute-start.5 = (bf16[1024,256]{1,0:T(8,128)(2,1)}, bf16[1024,256]{1,0:T(8,128)(2,1)S(1)}, u32[]{:S(2)}, u32[]{:S(2)}) collective-permute-start(bf16[1024,256]{1,0:T(8,128)(2,1)} %copy-done.3), channel_id=1, source_target_pairs={{0,7},{1,0},{2,1},{3,2},{4,3},{5,4},{6,5},{7,6},{8,15},{9,8},{10,9... | collective-permute-start | bytes 1572872 | tf_op jit(solution)/shard_map/ppermute | solution.py:170
  78.8 3.1 %collective-permute-start.7 = (bf16[1024,256]{1,0:T(8,128)(2,1)}, bf16[1024,256]{1,0:T(8,128)(2,1)S(1)}, u32[]{:S(2)}, u32[]{:S(2)}) collective-permute-start(bf16[1024,256]{1,0:T(8,128)(2,1)} %collective-permute-done.6.refs_4_), channel_id=1, source_target_pairs={{0,1},{1,2},{2,3},{3,4},{4,5},{5,6},{6,7},{7,0},{8,9},{9,10},{10,1... | collective-permute-start | bytes 1572872 | tf_op jit(solution)/shard_map/ppermute | solution.py:170
  81.9 2.7 %collective-permute-start.9 = (bf16[1024,256]{1,0:T(8,128)(2,1)}, bf16[1024,256]{1,0:T(8,128)(2,1)S(1)}, u32[]{:S(2)}, u32[]{:S(2)}) collective-permute-start(bf16[1024,256]{1,0:T(8,128)(2,1)} %collective-permute-done.8.refs_5_), channel_id=1, source_target_pairs={{0,7},{1,0},{2,1},{3,2},{4,3},{5,4},{6,5},{7,6},{8,15},{9,8},{10,9... | collective-permute-start | bytes 1572872 | tf_op jit(solution)/shard_map/ppermute | solution.py:170
  84.6 4.9 %collective-permute-done.4.refs_7_ = bf16[1024,256]{1,0:T(8,128)(2,1)S(1)} collective-permute-done((bf16[1024,256]{1,0:T(8,128)(2,1)S(1)}, bf16[1024,256]{1,0:T(8,128)(2,1)S(1)}, u32[]{:S(2)}, u32[]{:S(2)}) %collective-permute-start.4) | collective-permute-done | bytes 524320 | tf_op jit(solution)/shard_map/ppermute | solution.py:170
  89.6 2.5 %collective-permute-done.5.refs_10_ = bf16[1024,256]{1,0:T(8,128)(2,1)S(1)} collective-permute-done((bf16[1024,256]{1,0:T(8,128)(2,1)}, bf16[1024,256]{1,0:T(8,128)(2,1)S(1)}, u32[]{:S(2)}, u32[]{:S(2)}) %collective-permute-start.5) | collective-permute-done | bytes 524320 | tf_op jit(solution)/shard_map/ppermute | solution.py:170
  92.1 3.1 %collective-permute-done.7.refs_8_ = bf16[1024,256]{1,0:T(8,128)(2,1)S(1)} collective-permute-done((bf16[1024,256]{1,0:T(8,128)(2,1)}, bf16[1024,256]{1,0:T(8,128)(2,1)S(1)}, u32[]{:S(2)}, u32[]{:S(2)}) %collective-permute-start.7) | collective-permute-done | bytes 524320 | tf_op jit(solution)/shard_map/ppermute | solution.py:170
  96.0 2.6 %collective-permute-done.9.refs_9_ = bf16[1024,256]{1,0:T(8,128)(2,1)S(1)} collective-permute-done((bf16[1024,256]{1,0:T(8,128)(2,1)}, bf16[1024,256]{1,0:T(8,128)(2,1)S(1)}, u32[]{:S(2)}, u32[]{:S(2)}) %collective-permute-start.9) | collective-permute-done | bytes 524320 | tf_op jit(solution)/shard_map/ppermute | solution.py:170
  99.4 1.9 %collective-permute-start.10 = (bf16[32,64,128]{2,1,0:T(8,128)(2,1)S(1)}, bf16[32,64,128]{2,1,0:T(8,128)(2,1)}, u32[]{:S(2)}, u32[]{:S(2)}) collective-permute-start(bf16[32,64,128]{2,1,0:T(8,128)(2,1)S(1)} %all-to-all-done.1.got_ref), channel_id=1, source_target_pairs={{0,16},{16,0},{1,17},{17,1},{2,18},{18,2},{3,19},{19,3},{4,20},{20... | collective-permute-start | bytes 1572872 | tf_op jit(solution)/shard_map/ppermute | solution.py:194
  101.3 1.9 %collective-permute-start.11 = (bf16[1024,256]{1,0:T(8,128)(2,1)}, bf16[1024,256]{1,0:T(8,128)(2,1)S(1)}, u32[]{:S(2)}, u32[]{:S(2)}) collective-permute-start(bf16[1024,256]{1,0:T(8,128)(2,1)} %copy-done.7), channel_id=1, source_target_pairs={{0,1},{1,2},{2,3},{3,4},{4,5},{5,6},{6,7},{7,0},{8,9},{9,10},{10,1... | collective-permute-start | bytes 1572872 | tf_op jit(solution)/shard_map/ppermute | solution.py:170
  103.2 3.9 %collective-permute-start.13 = (bf16[1024,256]{1,0:T(8,128)(2,1)}, bf16[1024,256]{1,0:T(8,128)(2,1)}, u32[]{:S(2)}, u32[]{:S(2)}) collective-permute-start(bf16[1024,256]{1,0:T(8,128)(2,1)} %copy-done.5), channel_id=1, source_target_pairs={{0,7},{1,0},{2,1},{3,2},{4,3},{5,4},{6,5},{7,6},{8,15},{9,8},{10,9... | collective-permute-start | bytes 1572872 | tf_op jit(solution)/shard_map/ppermute | solution.py:170
  108.3 1.9 %order_upper.1.upper_ref = bf16[8,256,256]{2,1,0:T(8,128)(2,1)S(1)} custom-call(s32[1]{0:T(128)} %bitcast.2.core_ref, bf16[32,64,128]{2,1,0:T(8,128)(2,1)S(1)} %all-to-all-done.1.got_ref, bf16[32,64,128]{2,1,0:T(8,128)(2,1)} %collective-permute-done.10.twin_ref), custom_call_target="tpu_custom_call" | custom-call | tf_op jit(solution)/shard_map/order_upper/pallas_call | solution.py:60
  112.4 4.6 %early_products.1 = (f32[1024,128]{1,0:T(8,128)S(1)}, f32[1024,128]{1,0:T(8,128)S(1)}, f32[1024,128]{1,0:T(8,128)S(1)}, f32[1024,128]{1,0:T(8,128)S(1)}) custom-call(s32[2]{0:T(128)S(1)} %pad_add_fusion.place_ref, bf16[8,256,256]{2,1,0:T(8,128)(2,1)S(1)} %order_upper.1.upper_ref, bf16[2048,128]{1,0:T(8,128)(2,1)S(1)} %pad_maximum_fusion.stored_ref, ...), custom_call_target="tpu_custom_call" | custom-call | tf_op jit(solution)/shard_map/early_products/pallas_call | solution.py:103
  118.5 5.2 %collective-permute-start.12 = (bf16[1024,128]{1,0:T(8,128)(2,1)S(1)}, bf16[1024,128]{1,0:T(8,128)(2,1)S(1)}, u32[]{:S(2)}, u32[]{:S(2)}) collective-permute-start(bf16[1024,128]{1,0:T(8,128)(2,1)S(1)} %last_far.2), channel_id=1, source_target_pairs={{0,8},{8,0},{1,9},{9,1},{2,10},{10,2},{3,11},{11,3},{4,12},{12,4},... | collective-permute-start | bytes 786440 | tf_op jit(solution)/shard_map/ppermute | solution.py:208
  123.8 1.3 last_far.3
  125.1 2.4 %collective-permute-start.14 = (bf16[1024,128]{1,0:T(8,128)(2,1)S(1)}, bf16[1024,128]{1,0:T(8,128)(2,1)S(1)}, u32[]{:S(2)}, u32[]{:S(2)}) collective-permute-start(bf16[1024,128]{1,0:T(8,128)(2,1)S(1)} %last_far.3), channel_id=1, source_target_pairs={{0,8},{8,0},{1,9},{9,1},{2,10},{10,2},{3,11},{11,3},{4,12},{12,4},... | collective-permute-start | bytes 786440 | tf_op jit(solution)/shard_map/ppermute | solution.py:208
  128.4 1.3 last_own.3
  130.5 5.8 %collective-permute-done.14 = bf16[1024,128]{1,0:T(8,128)(2,1)S(1)} collective-permute-done((bf16[1024,128]{1,0:T(8,128)(2,1)S(1)}, bf16[1024,128]{1,0:T(8,128)(2,1)S(1)}, u32[]{:S(2)}, u32[]{:S(2)}) %collective-permute-start.14) | collective-permute-done | bytes 262176 | tf_op jit(solution)/shard_map/ppermute | solution.py:208
  (54 shorter events, 16.3 us)
Async XLA Ops:
  0.0 27.4 %collective-permute-start = (bf16[2048,256]{1,0:T(8,128)(2,1)}, bf16[2048,256]{1,0:T(8,128)(2,1)S(1)}, u32[]{:S(2)}, u32[]{:S(2)}) collective-permute-start(bf16[2048,256]{1,0:T(8,128)(2,1)} %refs_0_.1), channel_id=1, source_target_pairs={{0,1},{1,2},{2,3},{3,4},{4,5},{5,6},{6,7},{7,0},{8,9},{9,10},{10,1... | collective-permute-start | bytes 3145736 | tf_op jit(solution)/shard_map/ppermute | solution.py:150
  4.7 29.2 %collective-permute-start.2 = (bf16[2048,256]{1,0:T(8,128)(2,1)}, bf16[2048,256]{1,0:T(8,128)(2,1)S(1)}, u32[]{:S(2)}, u32[]{:S(2)}) collective-permute-start(bf16[2048,256]{1,0:T(8,128)(2,1)} %refs_0_.1), channel_id=1, source_target_pairs={{0,7},{1,0},{2,1},{3,2},{4,3},{5,4},{6,5},{7,6},{8,15},{9,8},{10,9... | collective-permute-start | bytes 3145736 | tf_op jit(solution)/shard_map/ppermute | solution.py:150
  10.7 33.3 %all-to-all-start = ((bf16[72,32,128]{2,0,1:T(8,128)(2,1)}), bf16[72,32,128]{2,0,1:T(8,128)(2,1)}, u32[]{:S(2)}, u32[]{:S(2)}) async-start(bf16[72,32,128]{2,0,1:T(8,128)(2,1)} %copy.9), calls=%async_computation | async-start | bytes 1179648 | tf_op jit(solution)/shard_map/all_to_all | solution.py:159
  28.4 18.2 %collective-permute-start.1 = (bf16[1024,256]{1,0:T(8,128)(2,1)}, bf16[1024,256]{1,0:T(8,128)(2,1)S(1)}, u32[]{:S(2)}, u32[]{:S(2)}) collective-permute-start(bf16[1024,256]{1,0:T(8,128)(2,1)} %get-tuple-element.20), channel_id=1, source_target_pairs={{0,1},{1,2},{2,3},{3,4},{4,5},{5,6},{6,7},{7,0},{8,9},{9,10},{10,1... | collective-permute-start | bytes 1572872 | tf_op jit(solution)/shard_map/ppermute | solution.py:170
  35.0 18.2 %collective-permute-start.3 = (bf16[1024,256]{1,0:T(8,128)(2,1)}, bf16[1024,256]{1,0:T(8,128)(2,1)S(1)}, u32[]{:S(2)}, u32[]{:S(2)}) collective-permute-start(bf16[1024,256]{1,0:T(8,128)(2,1)} %get-tuple-element.18), channel_id=1, source_target_pairs={{0,7},{1,0},{2,1},{3,2},{4,3},{5,4},{6,5},{7,6},{8,15},{9,8},{10,9... | collective-permute-start | bytes 1572872 | tf_op jit(solution)/shard_map/ppermute | solution.py:170
  36.9 41.9 %collective-permute-start.6 = (bf16[1024,256]{1,0:T(8,128)(2,1)}, bf16[1024,256]{1,0:T(8,128)(2,1)}, u32[]{:S(2)}, u32[]{:S(2)}) collective-permute-start(bf16[1024,256]{1,0:T(8,128)(2,1)} %get-tuple-element.19), channel_id=1, source_target_pairs={{0,1},{1,2},{2,3},{3,4},{4,5},{5,6},{6,7},{7,0},{8,9},{9,10},{10,1... | collective-permute-start | bytes 1572872 | tf_op jit(solution)/shard_map/ppermute | solution.py:170
  42.0 39.9 %collective-permute-start.8 = (bf16[1024,256]{1,0:T(8,128)(2,1)}, bf16[1024,256]{1,0:T(8,128)(2,1)}, u32[]{:S(2)}, u32[]{:S(2)}) collective-permute-start(bf16[1024,256]{1,0:T(8,128)(2,1)} %get-tuple-element.17), channel_id=1, source_target_pairs={{0,7},{1,0},{2,1},{3,2},{4,3},{5,4},{6,5},{7,6},{8,15},{9,8},{10,9... | collective-permute-start | bytes 1572872 | tf_op jit(solution)/shard_map/ppermute | solution.py:170
  46.6 26.3 %copy-start.1 = (bf16[1024,256]{1,0:T(8,128)(2,1)}, bf16[1024,256]{1,0:T(8,128)(2,1)S(1)}, u32[]{:S(2)}) copy-start(bf16[1024,256]{1,0:T(8,128)(2,1)S(1)} %collective-permute-done.1.refs_3_) | copy-start | bytes 1572868
  53.1 4.8 %copy-start.3 = (bf16[1024,256]{1,0:T(8,128)(2,1)}, bf16[1024,256]{1,0:T(8,128)(2,1)S(1)}, u32[]{:S(2)}) copy-start(bf16[1024,256]{1,0:T(8,128)(2,1)S(1)} %collective-permute-done.3.refs_6_) | copy-start | bytes 1572868
  59.7 39.7 %all-to-all-start.1 = ((bf16[32,64,128]{2,1,0:T(8,128)(2,1)}), bf16[32,64,128]{2,1,0:T(8,128)(2,1)S(1)}, u32[]{:S(2)}, u32[]{:S(2)}) async-start(bf16[32,64,128]{2,1,0:T(8,128)(2,1)} %bitcast.19), calls=%async_computation.1 | async-start | bytes 1048576 | tf_op jit(solution)/shard_map/all_to_all | solution.py:192
  72.9 16.7 %collective-permute-start.4 = (bf16[1024,256]{1,0:T(8,128)(2,1)S(1)}, bf16[1024,256]{1,0:T(8,128)(2,1)S(1)}, u32[]{:S(2)}, u32[]{:S(2)}) collective-permute-start(bf16[1024,256]{1,0:T(8,128)(2,1)S(1)} %collective-permute-done.1.refs_3_), channel_id=1, source_target_pairs={{0,1},{1,2},{2,3},{3,4},{4,5},{5,6},{6,7},{7,0},{8,9},{9,10},{10,1... | collective-permute-start | bytes 1572872 | tf_op jit(solution)/shard_map/ppermute | solution.py:170
  74.8 17.2 %collective-permute-start.5 = (bf16[1024,256]{1,0:T(8,128)(2,1)}, bf16[1024,256]{1,0:T(8,128)(2,1)S(1)}, u32[]{:S(2)}, u32[]{:S(2)}) collective-permute-start(bf16[1024,256]{1,0:T(8,128)(2,1)} %copy-done.3), channel_id=1, source_target_pairs={{0,7},{1,0},{2,1},{3,2},{4,3},{5,4},{6,5},{7,6},{8,15},{9,8},{10,9... | collective-permute-start | bytes 1572872 | tf_op jit(solution)/shard_map/ppermute | solution.py:170
  78.8 16.4 %collective-permute-start.7 = (bf16[1024,256]{1,0:T(8,128)(2,1)}, bf16[1024,256]{1,0:T(8,128)(2,1)S(1)}, u32[]{:S(2)}, u32[]{:S(2)}) collective-permute-start(bf16[1024,256]{1,0:T(8,128)(2,1)} %collective-permute-done.6.refs_4_), channel_id=1, source_target_pairs={{0,1},{1,2},{2,3},{3,4},{4,5},{5,6},{6,7},{7,0},{8,9},{9,10},{10,1... | collective-permute-start | bytes 1572872 | tf_op jit(solution)/shard_map/ppermute | solution.py:170
  81.9 16.6 %collective-permute-start.9 = (bf16[1024,256]{1,0:T(8,128)(2,1)}, bf16[1024,256]{1,0:T(8,128)(2,1)S(1)}, u32[]{:S(2)}, u32[]{:S(2)}) collective-permute-start(bf16[1024,256]{1,0:T(8,128)(2,1)} %collective-permute-done.8.refs_5_), channel_id=1, source_target_pairs={{0,7},{1,0},{2,1},{3,2},{4,3},{5,4},{6,5},{7,6},{8,15},{9,8},{10,9... | collective-permute-start | bytes 1572872 | tf_op jit(solution)/shard_map/ppermute | solution.py:170
  89.6 5.6 %copy-start.7 = (bf16[1024,256]{1,0:T(8,128)(2,1)}, bf16[1024,256]{1,0:T(8,128)(2,1)S(1)}, u32[]{:S(2)}) copy-start(bf16[1024,256]{1,0:T(8,128)(2,1)S(1)} %collective-permute-done.4.refs_7_) | copy-start | bytes 1572868
  92.1 3.1 %copy-start.5 = (bf16[1024,256]{1,0:T(8,128)(2,1)}, bf16[1024,256]{1,0:T(8,128)(2,1)S(1)}, u32[]{:S(2)}) copy-start(bf16[1024,256]{1,0:T(8,128)(2,1)S(1)} %collective-permute-done.5.refs_10_) | copy-start | bytes 1572868
  95.2 0.8 copy-start.9
  98.6 0.8 copy-start.11
  99.4 8.9 %collective-permute-start.10 = (bf16[32,64,128]{2,1,0:T(8,128)(2,1)S(1)}, bf16[32,64,128]{2,1,0:T(8,128)(2,1)}, u32[]{:S(2)}, u32[]{:S(2)}) collective-permute-start(bf16[32,64,128]{2,1,0:T(8,128)(2,1)S(1)} %all-to-all-done.1.got_ref), channel_id=1, source_target_pairs={{0,16},{16,0},{1,17},{17,1},{2,18},{18,2},{3,19},{19,3},{4,20},{20... | collective-permute-start | bytes 1572872 | tf_op jit(solution)/shard_map/ppermute | solution.py:194
  101.3 16.4 %collective-permute-start.11 = (bf16[1024,256]{1,0:T(8,128)(2,1)}, bf16[1024,256]{1,0:T(8,128)(2,1)S(1)}, u32[]{:S(2)}, u32[]{:S(2)}) collective-permute-start(bf16[1024,256]{1,0:T(8,128)(2,1)} %copy-done.7), channel_id=1, source_target_pairs={{0,1},{1,2},{2,3},{3,4},{4,5},{5,6},{6,7},{7,0},{8,9},{9,10},{10,1... | collective-permute-start | bytes 1572872 | tf_op jit(solution)/shard_map/ppermute | solution.py:170
  103.2 20.5 %collective-permute-start.13 = (bf16[1024,256]{1,0:T(8,128)(2,1)}, bf16[1024,256]{1,0:T(8,128)(2,1)}, u32[]{:S(2)}, u32[]{:S(2)}) collective-permute-start(bf16[1024,256]{1,0:T(8,128)(2,1)} %copy-done.5), channel_id=1, source_target_pairs={{0,7},{1,0},{2,1},{3,2},{4,3},{5,4},{6,5},{7,6},{8,15},{9,8},{10,9... | collective-permute-start | bytes 1572872 | tf_op jit(solution)/shard_map/ppermute | solution.py:170
  107.2 3.0 %copy-start.6 = (bf16[1024,256]{1,0:T(8,128)(2,1)S(1)}, bf16[1024,256]{1,0:T(8,128)(2,1)}, u32[]{:S(2)}) copy-start(bf16[1024,256]{1,0:T(8,128)(2,1)} %copy-done.5) | copy-start | bytes 1572868
  107.2 3.0 %copy-start.8 = (bf16[1024,256]{1,0:T(8,128)(2,1)S(1)}, bf16[1024,256]{1,0:T(8,128)(2,1)}, u32[]{:S(2)}) copy-start(bf16[1024,256]{1,0:T(8,128)(2,1)} %copy-done.7) | copy-start | bytes 1572868
  108.3 2.0 %copy-start = (bf16[2048,256]{1,0:T(8,128)(2,1)S(1)}, bf16[2048,256]{1,0:T(8,128)(2,1)}, u32[]{:S(2)}) copy-start(bf16[2048,256]{1,0:T(8,128)(2,1)} %refs_0_.1) | copy-start | bytes 3145732
  108.3 2.0 %copy-start.2 = (bf16[1024,256]{1,0:T(8,128)(2,1)S(1)}, bf16[1024,256]{1,0:T(8,128)(2,1)}, u32[]{:S(2)}) copy-start(bf16[1024,256]{1,0:T(8,128)(2,1)} %copy-done.1) | copy-start | bytes 1572868
  108.3 2.0 %copy-start.4 = (bf16[1024,256]{1,0:T(8,128)(2,1)S(1)}, bf16[1024,256]{1,0:T(8,128)(2,1)}, u32[]{:S(2)}) copy-start(bf16[1024,256]{1,0:T(8,128)(2,1)} %copy-done.3) | copy-start | bytes 1572868
  110.3 1.0 copy-start.10
  111.3 1.0 copy-start.12
  118.5 11.9 %collective-permute-start.12 = (bf16[1024,128]{1,0:T(8,128)(2,1)S(1)}, bf16[1024,128]{1,0:T(8,128)(2,1)S(1)}, u32[]{:S(2)}, u32[]{:S(2)}) collective-permute-start(bf16[1024,128]{1,0:T(8,128)(2,1)S(1)} %last_far.2), channel_id=1, source_target_pairs={{0,8},{8,0},{1,9},{9,1},{2,10},{10,2},{3,11},{11,3},{4,12},{12,4},... | collective-permute-start | bytes 786440 | tf_op jit(solution)/shard_map/ppermute | solution.py:208
  125.1 11.1 %collective-permute-start.14 = (bf16[1024,128]{1,0:T(8,128)(2,1)S(1)}, bf16[1024,128]{1,0:T(8,128)(2,1)S(1)}, u32[]{:S(2)}, u32[]{:S(2)}) collective-permute-start(bf16[1024,128]{1,0:T(8,128)(2,1)S(1)} %last_far.3), channel_id=1, source_target_pairs={{0,8},{8,0},{1,9},{9,1},{2,10},{10,2},{3,11},{11,3},{4,12},{12,4},... | collective-permute-start | bytes 786440 | tf_op jit(solution)/shard_map/ppermute | solution.py:208

commit v6 on v5

--- a/solution.py
+++ b/solution.py
@@ -10,7 +10,7 @@
 CORES = 2
 PAD = 8
 TILE_M = 256
-SPLIT = 1024
+GATHERED = 1536
 ROW = ("chip", "core")
 
 inv_root = 0.7071067811865476
@@ -111,6 +111,36 @@
     )(place, upper, stored, *flat)
 
 
+def gathered_products(place, upper, stored, lhs):
+    rows, depth = lhs.shape
+    width = stored.shape[1]
+    tile = pl.BlockSpec((TILE_M, width), lambda i, place: (i, 0))
+    upper = upper.reshape(depth, upper.shape[2])
+
+    def body(place_ref, upper_ref, stored_ref, lhs_ref, far_ref, rest_ref):
+        total = jnp.dot(lhs_ref[...], upper_ref[...], preferred_element_type=jnp.float32)
+        left, right = total[:, :width], total[:, width:]
+        at_left = place_ref[0] == 0
+        far_ref[...] = jnp.where(at_left, right, left).astype(far_ref.dtype)
+        rest_ref[...] = stored_ref[...].astype(jnp.float32) - jnp.where(at_left, left, right)
+
+    return pl.pallas_call(
+        body,
+        grid_spec=pltpu.PrefetchScalarGridSpec(
+            num_scalar_prefetch=1,
+            grid=(rows // TILE_M,),
+            in_specs=[whole(), tile, pl.BlockSpec((TILE_M, depth), lambda i, place: (i, 0))],
+            out_specs=[tile, tile],
+        ),
+        out_shape=[
+            jax.ShapeDtypeStruct((rows, width), jnp.bfloat16),
+            jax.ShapeDtypeStruct((rows, width), jnp.float32),
+        ],
+        compiler_params=grant(56),
+        name="gathered_products",
+    )(place, upper, stored, lhs)
+
+
 def last_product(place, upper, base, block, partner, out_dtype, sign):
     rows, width = base.shape
     y_count = upper.shape[0]
@@ -147,7 +177,14 @@
     up = [(i, (i + 1) % y_count) for i in range(y_count)]
     down = [(i, (i - 1) % y_count) for i in range(y_count)]
     route = {-1: up, 1: down}
-    near = tuple(lax.ppermute(panel_lower, "y", route[sign]) for sign in route)
+    gathered = lax.all_gather(panel_lower[:GATHERED], "y", axis=1, tiled=True)
+    passed = panel_lower[GATHERED:]
+    steps, moving = [], (passed, passed)
+    for distance in range(1, y_count // 2):
+        moving = tuple(lax.ppermute(block, "y", route[sign]) for block, sign in zip(moving, route))
+        steps.append(moving)
+    middle = passed.shape[0] // 2
+    last = (lax.ppermute(moving[0][:middle], "y", up), lax.ppermute(moving[1][middle:], "y", down))
 
     first = (scale_first.astype(jnp.float32)[:, None] * slab_block.astype(jnp.float32)).astype(
         jnp.bfloat16
@@ -157,19 +194,7 @@
     )
     packed = jnp.concatenate([first.reshape(share, groups, col_width), scale_rows], axis=0)
     packed = lax.all_to_all(packed, ROW, split_axis=1, concat_axis=0, tiled=True)
-    bounds = ((0, SPLIT), (SPLIT, row_count))
-    first_keys, second_keys = ((0, -1), (1, 1)), ((1, -1), (0, 1))
-    moving = {}
-    for part, sign in first_keys + second_keys:
-        start, stop = bounds[part]
-        moving[part, sign] = near[0 if sign < 0 else 1][start:stop]
-    steps = []
-    for distance in range(2, y_count // 2 + 1):
-        keys = first_keys if 2 * distance == y_count else first_keys + second_keys
-        for part, sign in keys:
-            moving[part, sign] = lax.ppermute(moving[part, sign], "y", route[sign])
-        steps.append({key: moving[key] for key in keys})
-    packed = after(packed, *(steps[0][key] for key in first_keys))
+    packed = after(packed, *steps[1])
     packed = packed.reshape(groups, share + PAD, col_width)
     cyclic = packed[:, :share].reshape(row_count, col_width)
     scale_cyclic = packed[:, share, :share].reshape(row_count)
@@ -190,25 +215,31 @@
         chips * X_HI, top_count, col_width
     )
     got = lax.all_to_all(send, ("chip", "x_hi"), split_axis=0, concat_axis=0)
-    got = after(got, *steps[1].values())
+    got = after(got, *steps[2])
     twin = lax.ppermute(got, "core", [(0, 1), (1, 0)])
     core = lax.axis_index("core").astype(jnp.int32).reshape(1)
     upper = order_upper(core, got, twin, y_count)
     place = jnp.stack([lax.axis_index("x_hi"), lax.axis_index("y")]).astype(jnp.int32)
-    offsets, blocks = [0, -1, 1], [(panel_lower,), near[:1], near[1:]]
-    for distance, step in enumerate(steps[:-1], 2):
-        for sign in route:
-            offsets.append(sign * distance)
-            blocks.append((step[0, sign], step[1, sign]))
-    sums = early_products(place, upper, stored, offsets, blocks, bounds)
+    offsets, blocks = [0], [(passed,)]
+    for distance, step in enumerate(steps, 1):
+        offsets += [-distance, distance]
+        blocks += [(block,) for block in step]
+    bounds = ((0, middle), (middle, 2 * middle))
     swap = [(i, X_HI - 1 - i) for i in range(X_HI)]
-    out = []
-    for key, far, rest in zip(first_keys, sums[::2], sums[1::2]):
-        far = last_product(place, upper, far, steps[-1][key], True, jnp.bfloat16, 1)
-        came = lax.ppermute(far, "x_hi", swap)
-        rest = last_product(place, upper, rest, steps[-1][key], False, jnp.float32, -1)
-        out.append((rest - came.astype(jnp.float32)).astype(jnp.bfloat16))
-    return jnp.concatenate(out, axis=0)
+    sums = early_products(place, upper, stored[GATHERED:], offsets, blocks, bounds)
+    fars = [
+        last_product(place, upper, far, block, True, jnp.bfloat16, 1) for far, block in zip(sums[::2], last)
+    ]
+    came_passed = lax.ppermute(jnp.concatenate(fars, axis=0), "x_hi", swap)
+    rests = [
+        last_product(place, upper, rest, block, False, jnp.float32, -1) for rest, block in zip(sums[1::2], last)
+    ]
+    upper, _ = lax.optimization_barrier((upper, came_passed))
+    far, rest = gathered_products(place, upper, stored[:GATHERED], gathered)
+    came = lax.ppermute(far, "x_hi", swap)
+    rest = jnp.concatenate([rest, *rests], axis=0)
+    came = jnp.concatenate([came, came_passed], axis=0)
+    return (rest - came.astype(jnp.float32)).astype(jnp.bfloat16)
 
 
 def solution(mesh):

time: 138 us -> 149 us (1.080)
  the two profiles are of different devices: /device:TPU:24 before, /device:TPU:4 now
where the time goes in v6:
time: 149 us; the launch traced here: 148 us
  starting transfers between devices  55.5 us (37%)
  waiting for transfers between devices  52.6 us (35%)
  between operations  13.8 us (9%)
  Pallas kernels  12.8 us (9%)
  local copies, waits for them, and re-layouts  9.79 us (7%)
  other arithmetic  3.52 us (2%)
    ppermute x6, waiting for transfers between devices, per_device(): lax.ppermute(block, 'y', route[sign])  36.6 us
    ppermute x6, starting transfers between devices, per_device(): lax.ppermute(block, 'y', route[sign])  20.6 us
    all_to_all x1, starting transfers between devices, per_device(): lax.all_to_all(packed, ROW, split_axis=1, concat_axis=0, tiled=True)  11.3 us
    all_to_all x1, starting transfers between devices, per_device(): got = lax.all_to_all(send, ('chip', 'x_hi'), split_axis=0, concat_axis=0)  10.5 us
    ppermute x1, waiting for transfers between devices, per_device(): came = lax.ppermute(far, 'x_hi', swap)  10 us
    pallas_call x1, Pallas kernels, gathered_products(): pl.pallas_call(body, grid_spec=pltpu.PrefetchScalarGridSpec(num_scalar_pr...  7.95 us
    ppermute x1, waiting for transfers between devices, per_device(): came_passed = lax.ppermute(jnp.concatenate(fars, axis=0), 'x_hi', swap)  6 us
    ppermute x1, starting transfers between devices, per_device(): lax.ppermute(moving[1][middle:], 'y', down)  5.12 us
  transfers between devices with their start and end apart: 14, of which 7 were waited for; matrix products, arithmetic and copies ran while one was open for 5% of the time, Pallas kernels for 3%

profile of v6, /device:TPU:4, one launch (start us, length us, event | category | flops | bytes accessed | tf_op | source)
XLA Modules:
  0.0 148.1 jit_solution(2096982354029254407)
XLA Ops:
  6.5 2.2 %slice.59 = bf16[1536,256]{1,0:T(8,128)(2,1)} slice(bf16[2048,256]{1,0:T(8,128)(2,1)} %param.7), slice={[0:1536], [0:256]} | slice | bytes 1572864 | tf_op jit(solution)/shard_map/slice | solution.py:180
  9.4 1.0 copy.9
  10.4 11.3 %all-to-all-start = ((bf16[72,32,128]{2,0,1:T(8,128)(2,1)}), bf16[72,32,128]{2,0,1:T(8,128)(2,1)S(1)}, u32[]{:S(2)}, u32[]{:S(2)}) async-start(bf16[72,32,128]{2,0,1:T(8,128)(2,1)} %copy.9), calls=%async_computation | async-start | bytes 1179648 | tf_op jit(solution)/shard_map/all_to_all | solution.py:196
  21.8 1.0 slice.47.refs_0_
  22.8 5.4 %collective-permute-start.2 = (bf16[512,256]{1,0:T(8,128)(2,1)S(1)}, bf16[512,256]{1,0:T(8,128)(2,1)S(1)}, u32[]{:S(2)}, u32[]{:S(2)}) collective-permute-start(bf16[512,256]{1,0:T(8,128)(2,1)S(1)} %slice.47.refs_0_), channel_id=1, source_target_pairs={{0,7},{1,0},{2,1},{3,2},{4,3},{5,4},{6,5},{7,6},{8,15},{9,8},{10,9... | collective-permute-start | bytes 786440 | tf_op jit(solution)/shard_map/ppermute | solution.py:184
  28.1 1.9 %collective-permute-start = (bf16[512,256]{1,0:T(8,128)(2,1)S(1)}, bf16[512,256]{1,0:T(8,128)(2,1)S(1)}, u32[]{:S(2)}, u32[]{:S(2)}) collective-permute-start(bf16[512,256]{1,0:T(8,128)(2,1)S(1)} %slice.47.refs_0_), channel_id=1, source_target_pairs={{0,1},{1,2},{2,3},{3,4},{4,5},{5,6},{6,7},{7,0},{8,9},{9,10},{10,1... | collective-permute-start | bytes 786440 | tf_op jit(solution)/shard_map/ppermute | solution.py:184
  30.1 9.8 %collective-permute-done.2.refs_2_ = bf16[512,256]{1,0:T(8,128)(2,1)S(1)} collective-permute-done((bf16[512,256]{1,0:T(8,128)(2,1)S(1)}, bf16[512,256]{1,0:T(8,128)(2,1)S(1)}, u32[]{:S(2)}, u32[]{:S(2)}) %collective-permute-start.2) | collective-permute-done | bytes 262176 | tf_op jit(solution)/shard_map/ppermute | solution.py:184
  39.8 5.6 %collective-permute-start.3 = (bf16[512,256]{1,0:T(8,128)(2,1)S(1)}, bf16[512,256]{1,0:T(8,128)(2,1)S(1)}, u32[]{:S(2)}, u32[]{:S(2)}) collective-permute-start(bf16[512,256]{1,0:T(8,128)(2,1)S(1)} %collective-permute-done.2.refs_2_), channel_id=1, source_target_pairs={{0,7},{1,0},{2,1},{3,2},{4,3},{5,4},{6,5},{7,6},{8,15},{9,8},{10,9... | collective-permute-start | bytes 786440 | tf_op jit(solution)/shard_map/ppermute | solution.py:184
  45.5 1.9 %collective-permute-start.1 = (bf16[512,256]{1,0:T(8,128)(2,1)S(1)}, bf16[512,256]{1,0:T(8,128)(2,1)S(1)}, u32[]{:S(2)}, u32[]{:S(2)}) collective-permute-start(bf16[512,256]{1,0:T(8,128)(2,1)S(1)} %collective-permute-done.refs_1_), channel_id=1, source_target_pairs={{0,1},{1,2},{2,3},{3,4},{4,5},{5,6},{6,7},{7,0},{8,9},{9,10},{10,1... | collective-permute-start | bytes 786440 | tf_op jit(solution)/shard_map/ppermute | solution.py:184
  47.4 9.3 %collective-permute-done.3.refs_4_ = bf16[512,256]{1,0:T(8,128)(2,1)S(1)} collective-permute-done((bf16[512,256]{1,0:T(8,128)(2,1)S(1)}, bf16[512,256]{1,0:T(8,128)(2,1)S(1)}, u32[]{:S(2)}, u32[]{:S(2)}) %collective-permute-start.3) | collective-permute-done | bytes 262176 | tf_op jit(solution)/shard_map/ppermute | solution.py:184
  56.7 5.1 %collective-permute-done.1.refs_3_ = bf16[512,256]{1,0:T(8,128)(2,1)S(1)} collective-permute-done((bf16[512,256]{1,0:T(8,128)(2,1)S(1)}, bf16[512,256]{1,0:T(8,128)(2,1)S(1)}, u32[]{:S(2)}, u32[]{:S(2)}) %collective-permute-start.1) | collective-permute-done | bytes 262176 | tf_op jit(solution)/shard_map/ppermute | solution.py:184
  62.4 0.8 fusion.9
  63.3 0.9 broadcast_in_dim.14
  64.2 10.5 %all-to-all-start.1 = ((bf16[32,64,128]{2,1,0:T(8,128)(2,1)}), bf16[32,64,128]{2,1,0:T(8,128)(2,1)S(1)}, u32[]{:S(2)}, u32[]{:S(2)}) async-start(bf16[32,64,128]{2,1,0:T(8,128)(2,1)} %bitcast.13), calls=%async_computation.1 | async-start | bytes 1048576 | tf_op jit(solution)/shard_map/all_to_all | solution.py:217
  74.7 1.9 %collective-permute-start.5 = (bf16[512,256]{1,0:T(8,128)(2,1)S(1)}, bf16[512,256]{1,0:T(8,128)(2,1)S(1)}, u32[]{:S(2)}, u32[]{:S(2)}) collective-permute-start(bf16[512,256]{1,0:T(8,128)(2,1)S(1)} %collective-permute-done.3.refs_4_), channel_id=1, source_target_pairs={{0,7},{1,0},{2,1},{3,2},{4,3},{5,4},{6,5},{7,6},{8,15},{9,8},{10,9... | collective-permute-start | bytes 786440 | tf_op jit(solution)/shard_map/ppermute | solution.py:184
  76.6 3.9 %collective-permute-start.4 = (bf16[512,256]{1,0:T(8,128)(2,1)S(1)}, bf16[512,256]{1,0:T(8,128)(2,1)S(1)}, u32[]{:S(2)}, u32[]{:S(2)}) collective-permute-start(bf16[512,256]{1,0:T(8,128)(2,1)S(1)} %collective-permute-done.1.refs_3_), channel_id=1, source_target_pairs={{0,1},{1,2},{2,3},{3,4},{4,5},{5,6},{6,7},{7,0},{8,9},{9,10},{10,1... | collective-permute-start | bytes 786440 | tf_op jit(solution)/shard_map/ppermute | solution.py:184
  80.6 7.6 %collective-permute-done.5.refs_6_ = bf16[512,256]{1,0:T(8,128)(2,1)S(1)} collective-permute-done((bf16[512,256]{1,0:T(8,128)(2,1)S(1)}, bf16[512,256]{1,0:T(8,128)(2,1)S(1)}, u32[]{:S(2)}, u32[]{:S(2)}) %collective-permute-start.5) | collective-permute-done | bytes 262176 | tf_op jit(solution)/shard_map/ppermute | solution.py:184
  88.1 4.8 %collective-permute-done.4.refs_5_ = bf16[512,256]{1,0:T(8,128)(2,1)S(1)} collective-permute-done((bf16[512,256]{1,0:T(8,128)(2,1)S(1)}, bf16[512,256]{1,0:T(8,128)(2,1)S(1)}, u32[]{:S(2)}, u32[]{:S(2)}) %collective-permute-start.4) | collective-permute-done | bytes 262176 | tf_op jit(solution)/shard_map/ppermute | solution.py:184
  93.0 1.9 %collective-permute-start.6 = (bf16[32,64,128]{2,1,0:T(8,128)(2,1)S(1)}, bf16[32,64,128]{2,1,0:T(8,128)(2,1)S(1)}, u32[]{:S(2)}, u32[]{:S(2)}) collective-permute-start(bf16[32,64,128]{2,1,0:T(8,128)(2,1)S(1)} %all-to-all-done.1.got_ref), channel_id=1, source_target_pairs={{0,16},{16,0},{1,17},{17,1},{2,18},{18,2},{3,19},{19,3},{4,20},{20... | collective-permute-start | bytes 1572872 | tf_op jit(solution)/shard_map/ppermute | solution.py:219
  95.6 1.9 %collective-permute-start.7 = (bf16[256,256]{1,0:T(8,128)(2,1)}, bf16[256,256]{1,0:T(8,128)(2,1)S(1)}, u32[]{:S(2)}, u32[]{:S(2)}) collective-permute-start(bf16[256,256]{1,0:T(8,128)(2,1)} %slice.68), channel_id=1, source_target_pairs={{0,1},{1,2},{2,3},{3,4},{4,5},{5,6},{6,7},{7,0},{8,9},{9,10},{10,1... | collective-permute-start | bytes 393224 | tf_op jit(solution)/shard_map/ppermute | solution.py:187
  98.1 5.1 %collective-permute-start.8 = (bf16[256,256]{1,0:T(8,128)(2,1)}, bf16[256,256]{1,0:T(8,128)(2,1)S(1)}, u32[]{:S(2)}, u32[]{:S(2)}) collective-permute-start(bf16[256,256]{1,0:T(8,128)(2,1)} %slice.69), channel_id=1, source_target_pairs={{0,7},{1,0},{2,1},{3,2},{4,3},{5,4},{6,5},{7,6},{8,15},{9,8},{10,9... | collective-permute-start | bytes 393224 | tf_op jit(solution)/shard_map/ppermute | solution.py:187
  103.4 0.8 order_upper.1.upper_ref
  104.2 1.1 copy-done.3
  105.3 0.9 copy-done.5
  106.2 0.9 copy-done.7
  107.2 1.2 early_products.1
  109.9 1.9 %collective-permute-start.9 = (bf16[512,128]{1,0:T(8,128)(2,1)S(1)}, bf16[512,128]{1,0:T(8,128)(2,1)S(1)}, u32[]{:S(2)}, u32[]{:S(2)}) collective-permute-start(bf16[512,128]{1,0:T(8,128)(2,1)S(1)} %pad_maximum_fusion.1), channel_id=1, source_target_pairs={{0,8},{8,0},{1,9},{9,1},{2,10},{10,2},{3,11},{11,3},{4,12},{12,4},... | collective-permute-start | bytes 393224 | tf_op jit(solution)/shard_map/ppermute | solution.py:233
  112.7 6.0 %collective-permute-done.9 = bf16[512,128]{1,0:T(8,128)(2,1)S(1)} collective-permute-done((bf16[512,128]{1,0:T(8,128)(2,1)S(1)}, bf16[512,128]{1,0:T(8,128)(2,1)S(1)}, u32[]{:S(2)}, u32[]{:S(2)}) %collective-permute-start.9) | collective-permute-done | bytes 131104 | tf_op jit(solution)/shard_map/ppermute | solution.py:233
  118.7 8.0 %gathered_products.1 = (bf16[1536,128]{1,0:T(8,128)(2,1)}, f32[1536,128]{1,0:T(8,128)}) custom-call(s32[2]{0:T(128)} %copy-done.8, bf16[2048,256]{1,0:T(8,128)(2,1)} %bitcast.18, bf16[1536,128]{1,0:T(8,128)(2,1)} %pad_maximum_fusion.stored_ref, bf16[1536,2048]{1,0:T(8,128)(2,1)} %all-gather.2.cloned.1.call-done.lhs_ref), custom_call_target="tpu_custom_call" | custom-call | tf_op jit(solution)/shard_map/gathered_products/pallas_call | solution.py:127
  126.6 2.2 %collective-permute-start.10 = (bf16[1536,128]{1,0:T(8,128)(2,1)}, bf16[1536,128]{1,0:T(8,128)(2,1)S(1)}, u32[]{:S(2)}, u32[]{:S(2)}) collective-permute-start(bf16[1536,128]{1,0:T(8,128)(2,1)} %get-tuple-element.22), channel_id=1, source_target_pairs={{0,8},{8,0},{1,9},{9,1},{2,10},{10,2},{3,11},{11,3},{4,12},{12,4},... | collective-permute-start | bytes 1179656 | tf_op jit(solution)/shard_map/ppermute | solution.py:239
  130.3 10.0 %collective-permute-done.10 = bf16[1536,128]{1,0:T(8,128)(2,1)S(1)} collective-permute-done((bf16[1536,128]{1,0:T(8,128)(2,1)}, bf16[1536,128]{1,0:T(8,128)(2,1)S(1)}, u32[]{:S(2)}, u32[]{:S(2)}) %collective-permute-start.10) | collective-permute-done | bytes 393248 | tf_op jit(solution)/shard_map/ppermute | solution.py:239
  140.3 0.9 fusion.2
  (61 shorter events, 6.3 us)
Async XLA Ops:
  6.5 2.2 %copy-start.16 = (bf16[2048]{0:T(1024)(128)(2,1)S(1)}, bf16[2048]{0:T(1024)(128)(2,1)}, u32[]{:S(2)}) copy-start(bf16[2048]{0:T(1024)(128)(2,1)} %param.5) | copy-start | bytes 12292
  6.5 2.3 %copy-start.17 = (bf16[2048]{0:T(1024)(128)(2,1)S(1)}, bf16[2048]{0:T(1024)(128)(2,1)}, u32[]{:S(2)}) copy-start(bf16[2048]{0:T(1024)(128)(2,1)} %param.6) | copy-start | bytes 12292
  6.5 2.4 %copy-start.13 = (bf16[2048,128]{1,0:T(8,128)(2,1)S(1)}, bf16[2048,128]{1,0:T(8,128)(2,1)}, u32[]{:S(2)}) copy-start(bf16[2048,128]{1,0:T(8,128)(2,1)} %param.4) | copy-start | bytes 1572868
  6.5 112.1 %all-gather.2.cloned.1.call-start = ((), (), s32[]{:S(2)}) async-start(), calls=%async_computation.2 | async-start | bytes 7077888 | tf_op jit(solution)/shard_map/all_gather | solution.py:180
  10.4 51.4 %all-to-all-start = ((bf16[72,32,128]{2,0,1:T(8,128)(2,1)}), bf16[72,32,128]{2,0,1:T(8,128)(2,1)S(1)}, u32[]{:S(2)}, u32[]{:S(2)}) async-start(bf16[72,32,128]{2,0,1:T(8,128)(2,1)} %copy.9), calls=%async_computation | async-start | bytes 1179648 | tf_op jit(solution)/shard_map/all_to_all | solution.py:196
  22.8 17.1 %collective-permute-start.2 = (bf16[512,256]{1,0:T(8,128)(2,1)S(1)}, bf16[512,256]{1,0:T(8,128)(2,1)S(1)}, u32[]{:S(2)}, u32[]{:S(2)}) collective-permute-start(bf16[512,256]{1,0:T(8,128)(2,1)S(1)} %slice.47.refs_0_), channel_id=1, source_target_pairs={{0,7},{1,0},{2,1},{3,2},{4,3},{5,4},{6,5},{7,6},{8,15},{9,8},{10,9... | collective-permute-start | bytes 786440 | tf_op jit(solution)/shard_map/ppermute | solution.py:184
  28.1 17.3 %collective-permute-start = (bf16[512,256]{1,0:T(8,128)(2,1)S(1)}, bf16[512,256]{1,0:T(8,128)(2,1)S(1)}, u32[]{:S(2)}, u32[]{:S(2)}) collective-permute-start(bf16[512,256]{1,0:T(8,128)(2,1)S(1)} %slice.47.refs_0_), channel_id=1, source_target_pairs={{0,1},{1,2},{2,3},{3,4},{4,5},{5,6},{6,7},{7,0},{8,9},{9,10},{10,1... | collective-permute-start | bytes 786440 | tf_op jit(solution)/shard_map/ppermute | solution.py:184
  39.8 16.8 %collective-permute-start.3 = (bf16[512,256]{1,0:T(8,128)(2,1)S(1)}, bf16[512,256]{1,0:T(8,128)(2,1)S(1)}, u32[]{:S(2)}, u32[]{:S(2)}) collective-permute-start(bf16[512,256]{1,0:T(8,128)(2,1)S(1)} %collective-permute-done.2.refs_2_), channel_id=1, source_target_pairs={{0,7},{1,0},{2,1},{3,2},{4,3},{5,4},{6,5},{7,6},{8,15},{9,8},{10,9... | collective-permute-start | bytes 786440 | tf_op jit(solution)/shard_map/ppermute | solution.py:184
  45.4 17.0 %copy-start.2 = (bf16[512,256]{1,0:T(8,128)(2,1)}, bf16[512,256]{1,0:T(8,128)(2,1)S(1)}, u32[]{:S(2)}) copy-start(bf16[512,256]{1,0:T(8,128)(2,1)S(1)} %collective-permute-done.refs_1_) | copy-start | bytes 786436
  45.5 16.3 %collective-permute-start.1 = (bf16[512,256]{1,0:T(8,128)(2,1)S(1)}, bf16[512,256]{1,0:T(8,128)(2,1)S(1)}, u32[]{:S(2)}, u32[]{:S(2)}) collective-permute-start(bf16[512,256]{1,0:T(8,128)(2,1)S(1)} %collective-permute-done.refs_1_), channel_id=1, source_target_pairs={{0,1},{1,2},{2,3},{3,4},{4,5},{5,6},{6,7},{7,0},{8,9},{9,10},{10,1... | collective-permute-start | bytes 786440 | tf_op jit(solution)/shard_map/ppermute | solution.py:184
  56.7 18.0 %copy-start.4 = (bf16[512,256]{1,0:T(8,128)(2,1)}, bf16[512,256]{1,0:T(8,128)(2,1)S(1)}, u32[]{:S(2)}) copy-start(bf16[512,256]{1,0:T(8,128)(2,1)S(1)} %collective-permute-done.3.refs_4_) | copy-start | bytes 786436
  61.8 14.8 %copy-start.6 = (bf16[512,256]{1,0:T(8,128)(2,1)}, bf16[512,256]{1,0:T(8,128)(2,1)S(1)}, u32[]{:S(2)}) copy-start(bf16[512,256]{1,0:T(8,128)(2,1)S(1)} %collective-permute-done.1.refs_3_) | copy-start | bytes 786436
  63.3 11.4 %copy-start.11 = (bf16[512,128]{1,0:T(8,128)(2,1)}, bf16[512,128]{1,0:T(8,128)(2,1)S(1)}, u32[]{:S(2)}) copy-start(bf16[512,128]{1,0:T(8,128)(2,1)S(1)} %get-tuple-element.28) | copy-start | bytes 393220
  64.2 28.8 %all-to-all-start.1 = ((bf16[32,64,128]{2,1,0:T(8,128)(2,1)}), bf16[32,64,128]{2,1,0:T(8,128)(2,1)S(1)}, u32[]{:S(2)}, u32[]{:S(2)}) async-start(bf16[32,64,128]{2,1,0:T(8,128)(2,1)} %bitcast.13), calls=%async_computation.1 | async-start | bytes 1048576 | tf_op jit(solution)/shard_map/all_to_all | solution.py:217
  74.7 13.4 %collective-permute-start.5 = (bf16[512,256]{1,0:T(8,128)(2,1)S(1)}, bf16[512,256]{1,0:T(8,128)(2,1)S(1)}, u32[]{:S(2)}, u32[]{:S(2)}) collective-permute-start(bf16[512,256]{1,0:T(8,128)(2,1)S(1)} %collective-permute-done.3.refs_4_), channel_id=1, source_target_pairs={{0,7},{1,0},{2,1},{3,2},{4,3},{5,4},{6,5},{7,6},{8,15},{9,8},{10,9... | collective-permute-start | bytes 786440 | tf_op jit(solution)/shard_map/ppermute | solution.py:184
  76.6 16.3 %collective-permute-start.4 = (bf16[512,256]{1,0:T(8,128)(2,1)S(1)}, bf16[512,256]{1,0:T(8,128)(2,1)S(1)}, u32[]{:S(2)}, u32[]{:S(2)}) collective-permute-start(bf16[512,256]{1,0:T(8,128)(2,1)S(1)} %collective-permute-done.1.refs_3_), channel_id=1, source_target_pairs={{0,1},{1,2},{2,3},{3,4},{4,5},{5,6},{6,7},{7,0},{8,9},{9,10},{10,1... | collective-permute-start | bytes 786440 | tf_op jit(solution)/shard_map/ppermute | solution.py:184
  93.0 10.4 %collective-permute-start.6 = (bf16[32,64,128]{2,1,0:T(8,128)(2,1)S(1)}, bf16[32,64,128]{2,1,0:T(8,128)(2,1)S(1)}, u32[]{:S(2)}, u32[]{:S(2)}) collective-permute-start(bf16[32,64,128]{2,1,0:T(8,128)(2,1)S(1)} %all-to-all-done.1.got_ref), channel_id=1, source_target_pairs={{0,16},{16,0},{1,17},{17,1},{2,18},{18,2},{3,19},{19,3},{4,20},{20... | collective-permute-start | bytes 1572872 | tf_op jit(solution)/shard_map/ppermute | solution.py:219
  95.6 12.8 %collective-permute-start.7 = (bf16[256,256]{1,0:T(8,128)(2,1)}, bf16[256,256]{1,0:T(8,128)(2,1)S(1)}, u32[]{:S(2)}, u32[]{:S(2)}) collective-permute-start(bf16[256,256]{1,0:T(8,128)(2,1)} %slice.68), channel_id=1, source_target_pairs={{0,1},{1,2},{2,3},{3,4},{4,5},{5,6},{6,7},{7,0},{8,9},{9,10},{10,1... | collective-permute-start | bytes 393224 | tf_op jit(solution)/shard_map/ppermute | solution.py:187
  98.1 11.0 %collective-permute-start.8 = (bf16[256,256]{1,0:T(8,128)(2,1)}, bf16[256,256]{1,0:T(8,128)(2,1)S(1)}, u32[]{:S(2)}, u32[]{:S(2)}) collective-permute-start(bf16[256,256]{1,0:T(8,128)(2,1)} %slice.69), channel_id=1, source_target_pairs={{0,7},{1,0},{2,1},{3,2},{4,3},{5,4},{6,5},{7,6},{8,15},{9,8},{10,9... | collective-permute-start | bytes 393224 | tf_op jit(solution)/shard_map/ppermute | solution.py:187
  103.3 5.8 %copy-start.8 = (s32[2]{0:T(128)}, s32[2]{0:T(128)S(1)}, u32[]{:S(2)}) copy-start(s32[2]{0:T(128)S(1)} %pad_add_fusion.place_ref) | copy-start | bytes 28
  104.1 5.0 %copy-start = (bf16[8,256,256]{2,1,0:T(8,128)(2,1)}, bf16[8,256,256]{2,1,0:T(8,128)(2,1)S(1)}, u32[]{:S(2)}) copy-start(bf16[8,256,256]{2,1,0:T(8,128)(2,1)S(1)} %order_upper.1.upper_ref) | copy-start | bytes 3145732
  104.2 1.1 copy-start.3
  105.3 0.9 copy-start.5
  106.2 0.9 copy-start.7
  108.4 3.5 %copy-start.12 = (bf16[512,128]{1,0:T(8,128)(2,1)S(1)}, bf16[512,128]{1,0:T(8,128)(2,1)}, u32[]{:S(2)}) copy-start(bf16[512,128]{1,0:T(8,128)(2,1)} %copy-done.11) | copy-start | bytes 393220
  108.4 3.5 %copy-start.14 = (bf16[512,128]{1,0:T(8,128)(2,1)S(1)}, bf16[512,128]{1,0:T(8,128)(2,1)}, u32[]{:S(2)}) copy-start(bf16[512,128]{1,0:T(8,128)(2,1)} %get-tuple-element.25) | copy-start | bytes 393220
  108.4 3.5 %copy-start.15 = (bf16[512,128]{1,0:T(8,128)(2,1)S(1)}, bf16[512,128]{1,0:T(8,128)(2,1)}, u32[]{:S(2)}) copy-start(bf16[512,128]{1,0:T(8,128)(2,1)} %get-tuple-element.27) | copy-start | bytes 393220
  109.9 8.7 %collective-permute-start.9 = (bf16[512,128]{1,0:T(8,128)(2,1)S(1)}, bf16[512,128]{1,0:T(8,128)(2,1)S(1)}, u32[]{:S(2)}, u32[]{:S(2)}) collective-permute-start(bf16[512,128]{1,0:T(8,128)(2,1)S(1)} %pad_maximum_fusion.1), channel_id=1, source_target_pairs={{0,8},{8,0},{1,9},{9,1},{2,10},{10,2},{3,11},{11,3},{4,12},{12,4},... | collective-permute-start | bytes 393224 | tf_op jit(solution)/shard_map/ppermute | solution.py:233
  118.7 10.2 %copy-start.1 = (bf16[8,256,256]{2,1,0:T(8,128)(2,1)S(1)}, bf16[8,256,256]{2,1,0:T(8,128)(2,1)}, u32[]{:S(2)}) copy-start(bf16[8,256,256]{2,1,0:T(8,128)(2,1)} %copy-done) | copy-start | bytes 3145732
  118.7 10.2 %copy-start.9 = (s32[2]{0:T(128)S(1)}, s32[2]{0:T(128)}, u32[]{:S(2)}) copy-start(s32[2]{0:T(128)} %copy-done.8) | copy-start | bytes 28
  126.6 13.7 %collective-permute-start.10 = (bf16[1536,128]{1,0:T(8,128)(2,1)}, bf16[1536,128]{1,0:T(8,128)(2,1)S(1)}, u32[]{:S(2)}, u32[]{:S(2)}) collective-permute-start(bf16[1536,128]{1,0:T(8,128)(2,1)} %get-tuple-element.22), channel_id=1, source_target_pairs={{0,8},{8,0},{1,9},{9,1},{2,10},{10,2},{3,11},{11,3},{4,12},{12,4},... | collective-permute-start | bytes 1179656 | tf_op jit(solution)/shard_map/ppermute | solution.py:239
  128.8 11.5 %copy-start.10 = (f32[1536,128]{1,0:T(8,128)S(1)}, f32[1536,128]{1,0:T(8,128)}, u32[]{:S(2)}) copy-start(f32[1536,128]{1,0:T(8,128)} %get-tuple-element.19) | copy-start | bytes 2359300
Sparse Core Ops, SparseCore 0:
  9.4 107.8 all-gather.1

commit v7 on v4

--- a/solution.py
+++ b/solution.py
@@ -10,6 +10,7 @@
 CORES = 2
 PAD = 8
 TILE_M = 256
+PARTS = 2
 ROW = ("chip", "core")
 
 inv_root = 0.7071067811865476
@@ -66,9 +67,10 @@
     )(core, got, twin)
 
 
-def early_products(place, upper, stored, offsets, blocks):
-    rows, width = stored.shape
+def early_products(place, upper, stored, offsets, blocks, start, rows):
+    width = stored.shape[1]
     y_count, depth, both = upper.shape
+    bases = [start if block.shape[0] > rows else 0 for block in blocks]
 
     def body(place_ref, upper_ref, stored_ref, *refs):
         *block_refs, far_ref, rest_ref, turned = refs
@@ -77,12 +79,12 @@
         at_left = place_ref[0] == 0
 
         def one(i, carry):
-            part = pl.ds(pl.multiple_of(i * TILE_M, TILE_M), TILE_M)
-            lhs = jnp.concatenate([ref[part] for ref in block_refs], axis=1)
+            tile = lambda base: pl.ds(pl.multiple_of(base + i * TILE_M, TILE_M), TILE_M)
+            lhs = jnp.concatenate([ref[tile(base)] for ref, base in zip(block_refs, bases)], axis=1)
             total = jnp.dot(lhs, turned[...], preferred_element_type=jnp.float32)
             left, right = total[:, :width], total[:, width:]
-            far_ref[part] = jnp.where(at_left, right, left)
-            rest_ref[part] = stored_ref[part].astype(jnp.float32) - jnp.where(at_left, left, right)
+            far_ref[tile(0)] = jnp.where(at_left, right, left)
+            rest_ref[tile(0)] = stored_ref[tile(start)].astype(jnp.float32) - jnp.where(at_left, left, right)
             return carry
 
         lax.fori_loop(0, rows // TILE_M, one, 0)
@@ -93,15 +95,16 @@
         out_specs=[whole(), whole()],
         out_shape=[jax.ShapeDtypeStruct((rows, width), jnp.float32)] * 2,
         scratch_shapes=[VM((len(offsets) * depth, both), upper.dtype)],
-        compiler_params=grant(16),
+        compiler_params=grant(8),
         name="early_products",
     )(place, upper, stored, *blocks)
 
 
 def last_product(place, upper, base, halves, partner, out_dtype, sign):
     rows, width = base.shape
-    y_count, depth, both = upper.shape
+    y_count = upper.shape[0]
     half = rows // len(halves)
+    step = min(half, TILE_M)
 
     def body(place_ref, upper_ref, base_ref, *refs):
         *half_refs, out_ref = refs
@@ -109,9 +112,9 @@
         columns = upper_ref[(place_ref[1] + y_count // 2) % y_count]
         columns = jnp.where(side == 0, columns[:, :width], columns[:, width:])
         for n, ref in enumerate(half_refs):
-            for start in range(0, half, TILE_M):
-                part = slice(n * half + start, n * half + start + TILE_M)
-                term = jnp.dot(ref[start : start + TILE_M], columns, preferred_element_type=jnp.float32)
+            for start in range(0, half, step):
+                part = slice(n * half + start, n * half + start + step)
+                term = jnp.dot(ref[start : start + step], columns, preferred_element_type=jnp.float32)
                 out_ref[part] = (base_ref[part] + sign * term).astype(out_ref.dtype)
 
     return pl.pallas_call(
@@ -133,6 +136,7 @@
     share = row_count // groups
     half = row_count // 2
     quarter = row_count // 4
+    part_rows = row_count // PARTS
 
     up = [(i, (i + 1) % y_count) for i in range(y_count)]
     down = [(i, (i - 1) % y_count) for i in range(y_count)]
@@ -147,16 +151,19 @@
     )
     packed = jnp.concatenate([first.reshape(share, groups, col_width), scale_rows], axis=0)
     packed = lax.all_to_all(packed, ROW, split_axis=1, concat_axis=0, tiled=True)
-    packed = after(packed, *near)
+    joined = jnp.concatenate(near, axis=1)
+    packed = after(packed, joined)
+    far_near = tuple(lax.ppermute(block, "y", route[sign]) for block, sign in zip(near, route))
+    third, last = [], []
+    for part in range(PARTS):
+        rows = slice(part * part_rows, (part + 1) * part_rows)
+        pair = tuple(lax.ppermute(block[rows], "y", route[sign]) for block, sign in zip(far_near, route))
+        middle = part_rows // 2
+        third.append(pair)
+        last.append((lax.ppermute(pair[0][:middle], "y", up), lax.ppermute(pair[1][middle:], "y", down)))
     packed = packed.reshape(groups, share + PAD, col_width)
     cyclic = packed[:, :share].reshape(row_count, col_width)
     scale_cyclic = packed[:, share, :share].reshape(row_count)
-
-    steps, moving = [near], near
-    for distance in range(2, y_count // 2):
-        moving = tuple(lax.ppermute(block, "y", route[sign]) for block, sign in zip(moving, route))
-        steps.append(moving)
-    last = (lax.ppermute(moving[0][:half], "y", up), lax.ppermute(moving[1][half:], "y", down))
 
     level_one = butterfly(cyclic[:half], cyclic[half:])
     second = (scale_cyclic.astype(jnp.float32)[:, None] * level_one).astype(jnp.bfloat16)
@@ -173,23 +180,24 @@
     send = jnp.broadcast_to(top, (chips, X_HI, top_count, col_width)).reshape(
         chips * X_HI, top_count, col_width
     )
-    send = after(send, *steps[1])
     got = lax.all_to_all(send, ("chip", "x_hi"), split_axis=0, concat_axis=0)
+    got = after(got, *third[0])
     twin = lax.ppermute(got, "core", [(0, 1), (1, 0)])
     core = lax.axis_index("core").astype(jnp.int32).reshape(1)
     upper = order_upper(core, got, twin, y_count)
-    upper = after(upper, *steps[2])
-
     place = jnp.stack([lax.axis_index("x_hi"), lax.axis_index("y")]).astype(jnp.int32)
-    offsets, blocks = [0], [panel_lower]
-    for distance, step in enumerate(steps, 1):
-        offsets += [-distance, distance]
-        blocks += step
-    far, rest = early_products(place, upper, stored, offsets, blocks)
-    far = last_product(place, upper, far, last, True, jnp.bfloat16, 1)
-    came = lax.ppermute(far, "x_hi", [(i, X_HI - 1 - i) for i in range(X_HI)])
-    rest = last_product(place, upper, rest, last, False, jnp.float32, -1)
-    return (rest - came.astype(jnp.float32)).astype(jnp.bfloat16)
+    offsets = [0, -1, 1, -2, 2, -3, 3]
+    swap = [(i, X_HI - 1 - i) for i in range(X_HI)]
+    out = []
+    for part in range(PARTS):
+        blocks = [panel_lower, joined, *far_near, *third[part]]
+        far, rest = early_products(place, upper, stored, offsets, blocks, part * part_rows, part_rows)
+        far = last_product(place, upper, far, last[part], True, jnp.bfloat16, 1)
+        upper = after(upper, far)
+        came = lax.ppermute(far, "x_hi", swap)
+        rest = last_product(place, upper, rest, last[part], False, jnp.float32, -1)
+        out.append((rest - came.astype(jnp.float32)).astype(jnp.bfloat16))
+    return jnp.concatenate(out, axis=0)
 
 
 def solution(mesh):

time: 138 us -> 133 us (0.964)
  blocking collectives: 28.9 us -> 0 us
  starting transfers between devices: 45.9 us -> 69.9 us
  waiting for transfers between devices: 42.7 us -> 24.9 us
  local copies, waits for them, and re-layouts: 3.76 us -> 14.2 us
  other arithmetic: 5.48 us -> 9.67 us
  Pallas kernels: 9.84 us -> 12.6 us
    all_to_all x1 -> x0, blocking collectives: 28.9 us -> none  [per_device(): got = lax.all_to_all(send, ('chip', 'x_hi'), split_axis=0, concat_axis=0)]
    ppermute x3 -> x10, starting transfers between devices: 10.8 us -> 33.1 us  [the longest x4 14.1 us: per_device(): lax.ppermute(block[rows], 'y', route[sign])]
    ppermute x4 -> x2, waiting for transfers between devices: 12 us -> 0.01 us  [per_device(): lax.ppermute(block, 'y', route[sign])]
    all_to_all x0 -> x1, starting transfers between devices: none -> 9.04 us  [per_device(): got = lax.all_to_all(send, ('chip', 'x_hi'), split_axis=0, concat_axis=0)]
    ppermute x4 -> x2, starting transfers between devices: 15 us -> 7.51 us  [per_device(): lax.ppermute(block, 'y', route[sign])]
    slice x2 -> x6, local copies, waits for them, and re-layouts: 1.66 us -> 8.67 us  [the longest x2 3.31 us: per_device(): block[rows]]
    ppermute x3 -> x10, waiting for transfers between devices: 18.6 us -> 15.6 us  [the longest x4 9.27 us: per_device(): lax.ppermute(block[rows], 'y', route[sign])]
    all_to_all x1, waiting for transfers between devices: 6.91 us -> 4.29 us  [per_device(): lax.all_to_all(packed, ROW, split_axis=1, concat_axis=0, tiled=True)]
  transfers between devices with their start and end apart: 11 -> 17, of which waited for: 6 -> 5; matrix products, arithmetic and copies ran while one was open for 6% -> 17% of each run, Pallas kernels for 6% -> 10%
where the time goes in v7:
time: 133 us; the launch traced here: 132 us
  starting transfers between devices  69.9 us (53%)
  waiting for transfers between devices  24.9 us (19%)
  local copies, waits for them, and re-layouts  14.2 us (11%)
  Pallas kernels  12.6 us (9%)
  other arithmetic  9.67 us (7%)
    ppermute x4, starting transfers between devices, per_device(): lax.ppermute(block[rows], 'y', route[sign])  14.1 us
    all_to_all x1, starting transfers between devices, per_device(): lax.all_to_all(packed, ROW, split_axis=1, concat_axis=0, tiled=True)  11.8 us
    ppermute x4, waiting for transfers between devices, per_device(): lax.ppermute(block[rows], 'y', route[sign])  9.27 us
    all_to_all x1, starting transfers between devices, per_device(): got = lax.all_to_all(send, ('chip', 'x_hi'), split_axis=0, concat_axis=0)  9.04 us
    ppermute x2, starting transfers between devices, per_device(): lax.ppermute(block, 'y', route[sign])  7.51 us
    ppermute x2, starting transfers between devices, per_device(): came = lax.ppermute(far, 'x_hi', swap)  7.35 us
    ppermute x2, starting transfers between devices, per_device(): lax.ppermute(pair[1][middle:], 'y', down)  6.62 us
    ppermute x2, starting transfers between devices, per_device(): lax.ppermute(panel_lower, 'y', route[sign])  6.61 us
  transfers between devices with their start and end apart: 17, of which 5 were waited for; matrix products, arithmetic and copies ran while one was open for 17% of the time, Pallas kernels for 10%

profile of v7, /device:TPU:24, one launch (start us, length us, event | category | flops | bytes accessed | tf_op | source)
XLA Modules:
  0.0 131.6 jit_solution(2597628977478917174)
XLA Ops:
  0.0 4.7 %collective-permute-start = (bf16[2048,256]{1,0:T(8,128)(2,1)}, bf16[2048,256]{1,0:T(8,128)(2,1)}, u32[]{:S(2)}, u32[]{:S(2)}) collective-permute-start(bf16[2048,256]{1,0:T(8,128)(2,1)} %refs_0_.3), channel_id=1, source_target_pairs={{0,1},{1,2},{2,3},{3,4},{4,5},{5,6},{6,7},{7,0},{8,9},{9,10},{10,1... | collective-permute-start | bytes 3145736 | tf_op jit(solution)/shard_map/ppermute | solution.py:144
  4.7 1.9 %collective-permute-start.1 = (bf16[2048,256]{1,0:T(8,128)(2,1)}, bf16[2048,256]{1,0:T(8,128)(2,1)}, u32[]{:S(2)}, u32[]{:S(2)}) collective-permute-start(bf16[2048,256]{1,0:T(8,128)(2,1)} %refs_0_.3), channel_id=1, source_target_pairs={{0,7},{1,0},{2,1},{3,2},{4,3},{5,4},{6,5},{7,6},{8,15},{9,8},{10,9... | collective-permute-start | bytes 3145736 | tf_op jit(solution)/shard_map/ppermute | solution.py:144
  8.2 1.4 %multiply_convert_fusion = bf16[2048,128]{1,0:T(8,128)(2,1)S(1)} fusion(bf16[2048,128]{1,0:T(8,128)(2,1)} %param.4, f32[2048]{0:T(1024)S(1)} %convert_element_type.57), kind=kLoop, calls=%fused_computation.4 | loop fusion | flops 786432 | bytes 1056768 | tf_op jit(solution)/shard_map/convert_element_type | solution.py:146
  10.7 11.8 %all-to-all-start = ((bf16[72,32,128]{2,0,1:T(8,128)(2,1)}), bf16[72,32,128]{2,0,1:T(8,128)(2,1)}, u32[]{:S(2)}, u32[]{:S(2)}) async-start(bf16[72,32,128]{2,0,1:T(8,128)(2,1)} %copy.9), calls=%async_computation | async-start | bytes 1179648 | tf_op jit(solution)/shard_map/all_to_all | solution.py:153
  22.4 5.0 %collective-permute-done = bf16[2048,256]{1,0:T(8,128)(2,1)} collective-permute-done((bf16[2048,256]{1,0:T(8,128)(2,1)}, bf16[2048,256]{1,0:T(8,128)(2,1)}, u32[]{:S(2)}, u32[]{:S(2)}) %collective-permute-start) | collective-permute-done | bytes 1048608 | tf_op jit(solution)/shard_map/ppermute | solution.py:144
  27.4 5.6 %collective-permute-start.2 = (bf16[2048,256]{1,0:T(8,128)(2,1)}, bf16[2048,256]{1,0:T(8,128)(2,1)S(1)}, u32[]{:S(2)}, u32[]{:S(2)}) collective-permute-start(bf16[2048,256]{1,0:T(8,128)(2,1)} %collective-permute-done), channel_id=1, source_target_pairs={{0,1},{1,2},{2,3},{3,4},{4,5},{5,6},{6,7},{7,0},{8,9},{9,10},{10,1... | collective-permute-start | bytes 3145736 | tf_op jit(solution)/shard_map/ppermute | solution.py:156
  33.0 1.9 %collective-permute-start.4 = (bf16[2048,256]{1,0:T(8,128)(2,1)}, bf16[2048,256]{1,0:T(8,128)(2,1)}, u32[]{:S(2)}, u32[]{:S(2)}) collective-permute-start(bf16[2048,256]{1,0:T(8,128)(2,1)} %collective-permute-done.1), channel_id=1, source_target_pairs={{0,7},{1,0},{2,1},{3,2},{4,3},{5,4},{6,5},{7,6},{8,15},{9,8},{10,9... | collective-permute-start | bytes 3145736 | tf_op jit(solution)/shard_map/ppermute | solution.py:156
  34.9 1.3 constant_dynamic-update-slice_fusion.1
  36.3 1.3 constant_dynamic-update-slice_fusion.refs_1_
  37.6 4.3 %all-to-all-done = bf16[72,32,128]{2,0,1:T(8,128)(2,1)} async-done(((bf16[72,32,128]{2,0,1:T(8,128)(2,1)}), bf16[72,32,128]{2,0,1:T(8,128)(2,1)}, u32[]{:S(2)}, u32[]{:S(2)}) %all-to-all-start) | async-done | bytes 589856 | tf_op jit(solution)/shard_map/all_to_all | solution.py:153
  41.9 2.1 %fusion.3 = (f32[16,64,128]{2,1,0:T(8,128)}, f32[16,64,128]{2,1,0:T(8,128)}) fusion(bf16[32,72,128]{2,1,0:T(8,128)(2,1)} %bitcast.9), kind=kLoop, calls=%fused_computation.8 | loop fusion | flops 786432 | bytes 1572864 | tf_op jit(solution)/shard_map/mul | solution.py:22
  45.0 1.5 %fusion.1 = bf16[2048,128]{1,0:T(8,128)(2,1)S(1)} fusion(f32[1024,128]{1,0:T(8,128)} %bitcast.18, f32[1024,128]{1,0:T(8,128)} %bitcast.17, f32[2048]{0:T(1024)S(1)} %reshape.41), kind=kLoop, calls=%fused_computation.3 | loop fusion | flops 786432 | bytes 1581056 | tf_op jit(solution)/shard_map/convert_element_type | solution.py:169
  48.3 9.0 %all-to-all-start.1 = ((bf16[32,64,128]{2,1,0:T(8,128)(2,1)}), bf16[32,64,128]{2,1,0:T(8,128)(2,1)}, u32[]{:S(2)}, u32[]{:S(2)}) async-start(bf16[32,64,128]{2,1,0:T(8,128)(2,1)} %bitcast.19), calls=%async_computation.1 | async-start | bytes 1048576 | tf_op jit(solution)/shard_map/all_to_all | solution.py:183
  58.4 5.1 %collective-permute-start.3 = (bf16[1024,256]{1,0:T(8,128)(2,1)}, bf16[1024,256]{1,0:T(8,128)(2,1)}, u32[]{:S(2)}, u32[]{:S(2)}) collective-permute-start(bf16[1024,256]{1,0:T(8,128)(2,1)} %get-tuple-element.24), channel_id=1, source_target_pairs={{0,1},{1,2},{2,3},{3,4},{4,5},{5,6},{6,7},{7,0},{8,9},{9,10},{10,1... | collective-permute-start | bytes 1572872 | tf_op jit(solution)/shard_map/ppermute | solution.py:160
  63.5 2.3 %fusion.14 = (bf16[1024,256]{1,0:T(8,128)(2,1)}, bf16[1024,256]{1,0:T(8,128)(2,1)}) fusion(bf16[2048,256]{1,0:T(8,128)(2,1)} %collective-permute-done.4.refs_3_), kind=kLoop, calls=%fused_computation.31 | loop fusion | bytes 2097152 | tf_op jit(solution)/shard_map/slice | solution.py:160
  65.8 1.9 %collective-permute-start.5 = (bf16[1024,256]{1,0:T(8,128)(2,1)}, bf16[1024,256]{1,0:T(8,128)(2,1)}, u32[]{:S(2)}, u32[]{:S(2)}) collective-permute-start(bf16[1024,256]{1,0:T(8,128)(2,1)} %get-tuple-element.22), channel_id=1, source_target_pairs={{0,7},{1,0},{2,1},{3,2},{4,3},{5,4},{6,5},{7,6},{8,15},{9,8},{10,9... | collective-permute-start | bytes 1572872 | tf_op jit(solution)/shard_map/ppermute | solution.py:160
  67.7 5.1 %collective-permute-start.10 = (bf16[1024,256]{1,0:T(8,128)(2,1)}, bf16[1024,256]{1,0:T(8,128)(2,1)}, u32[]{:S(2)}, u32[]{:S(2)}) collective-permute-start(bf16[1024,256]{1,0:T(8,128)(2,1)} %get-tuple-element.23), channel_id=1, source_target_pairs={{0,1},{1,2},{2,3},{3,4},{4,5},{5,6},{6,7},{7,0},{8,9},{9,10},{10,1... | collective-permute-start | bytes 1572872 | tf_op jit(solution)/shard_map/ppermute | solution.py:160
  72.8 1.9 %collective-permute-start.11 = (bf16[1024,256]{1,0:T(8,128)(2,1)}, bf16[1024,256]{1,0:T(8,128)(2,1)}, u32[]{:S(2)}, u32[]{:S(2)}) collective-permute-start(bf16[1024,256]{1,0:T(8,128)(2,1)} %get-tuple-element.21), channel_id=1, source_target_pairs={{0,7},{1,0},{2,1},{3,2},{4,3},{5,4},{6,5},{7,6},{8,15},{9,8},{10,9... | collective-permute-start | bytes 1572872 | tf_op jit(solution)/shard_map/ppermute | solution.py:160
  75.7 8.4 %collective-permute-done.5.refs_5_ = bf16[1024,256]{1,0:T(8,128)(2,1)} collective-permute-done((bf16[1024,256]{1,0:T(8,128)(2,1)}, bf16[1024,256]{1,0:T(8,128)(2,1)}, u32[]{:S(2)}, u32[]{:S(2)}) %collective-permute-start.5) | collective-permute-done | bytes 524320 | tf_op jit(solution)/shard_map/ppermute | solution.py:160
  84.1 1.9 %collective-permute-start.6 = (bf16[32,64,128]{2,1,0:T(8,128)(2,1)}, bf16[32,64,128]{2,1,0:T(8,128)(2,1)}, u32[]{:S(2)}, u32[]{:S(2)}) collective-permute-start(bf16[32,64,128]{2,1,0:T(8,128)(2,1)} %all-to-all-done.1.got_ref), channel_id=1, source_target_pairs={{0,16},{16,0},{1,17},{17,1},{2,18},{18,2},{3,19},{19,3},{4,20},{20... | collective-permute-start | bytes 1572872 | tf_op jit(solution)/shard_map/ppermute | solution.py:185
  86.0 1.7 %slice.80 = bf16[512,256]{1,0:T(8,128)(2,1)} slice(bf16[1024,256]{1,0:T(8,128)(2,1)} %collective-permute-done.3.refs_4_), slice={[0:512], [0:256]} | slice | bytes 524288 | tf_op jit(solution)/shard_map/slice | solution.py:163
  87.7 1.9 %collective-permute-start.7 = (bf16[512,256]{1,0:T(8,128)(2,1)}, bf16[512,256]{1,0:T(8,128)(2,1)S(1)}, u32[]{:S(2)}, u32[]{:S(2)}) collective-permute-start(bf16[512,256]{1,0:T(8,128)(2,1)} %slice.80), channel_id=1, source_target_pairs={{0,1},{1,2},{2,3},{3,4},{4,5},{5,6},{6,7},{7,0},{8,9},{9,10},{10,1... | collective-permute-start | bytes 786440 | tf_op jit(solution)/shard_map/ppermute | solution.py:163
  89.6 1.7 %slice.81 = bf16[512,256]{1,0:T(8,128)(2,1)} slice(bf16[1024,256]{1,0:T(8,128)(2,1)} %collective-permute-done.5.refs_5_), slice={[512:1024], [0:256]} | slice | bytes 524288 | tf_op jit(solution)/shard_map/slice | solution.py:163
  91.2 3.9 %collective-permute-start.8 = (bf16[512,256]{1,0:T(8,128)(2,1)}, bf16[512,256]{1,0:T(8,128)(2,1)}, u32[]{:S(2)}, u32[]{:S(2)}) collective-permute-start(bf16[512,256]{1,0:T(8,128)(2,1)} %slice.81), channel_id=1, source_target_pairs={{0,7},{1,0},{2,1},{3,2},{4,3},{5,4},{6,5},{7,6},{8,15},{9,8},{10,9... | collective-permute-start | bytes 786440 | tf_op jit(solution)/shard_map/ppermute | solution.py:163
  96.3 3.1 %collective-permute-start.12 = (bf16[512,256]{1,0:T(8,128)(2,1)S(1)}, bf16[512,256]{1,0:T(8,128)(2,1)S(1)}, u32[]{:S(2)}, u32[]{:S(2)}) collective-permute-start(bf16[512,256]{1,0:T(8,128)(2,1)S(1)} %slice.84), channel_id=1, source_target_pairs={{0,1},{1,2},{2,3},{3,4},{4,5},{5,6},{6,7},{7,0},{8,9},{9,10},{10,1... | collective-permute-start | bytes 786440 | tf_op jit(solution)/shard_map/ppermute | solution.py:163
  100.4 2.7 %collective-permute-start.13 = (bf16[512,256]{1,0:T(8,128)(2,1)S(1)}, bf16[512,256]{1,0:T(8,128)(2,1)S(1)}, u32[]{:S(2)}, u32[]{:S(2)}) collective-permute-start(bf16[512,256]{1,0:T(8,128)(2,1)S(1)} %slice.85), channel_id=1, source_target_pairs={{0,7},{1,0},{2,1},{3,2},{4,3},{5,4},{6,5},{7,6},{8,15},{9,8},{10,9... | collective-permute-start | bytes 786440 | tf_op jit(solution)/shard_map/ppermute | solution.py:163
  104.2 2.0 %order_upper.1.upper_ref = bf16[8,256,256]{2,1,0:T(8,128)(2,1)S(1)} custom-call(s32[1]{0:T(128)} %bitcast.2.core_ref, bf16[32,64,128]{2,1,0:T(8,128)(2,1)} %all-to-all-done.1.got_ref, bf16[32,64,128]{2,1,0:T(8,128)(2,1)} %collective-permute-done.6.twin_ref), custom_call_target="tpu_custom_call" | custom-call | tf_op jit(solution)/shard_map/order_upper/pallas_call | solution.py:60
  106.2 3.2 %early_products.2 = (f32[1024,128]{1,0:T(8,128)S(1)}, f32[1024,128]{1,0:T(8,128)S(1)}) custom-call(s32[2]{0:T(128)S(1)} %pad_add_fusion.place_ref, bf16[8,256,256]{2,1,0:T(8,128)(2,1)S(1)} %order_upper.1.upper_ref, bf16[2048,128]{1,0:T(8,128)(2,1)S(1)} %pad_maximum_fusion.stored_ref, bf16[2048,256]{1,0:T(8,128)(2,1)S(1)} %copy-done, ...), custom_call_target="tpu_custom_call" | custom-call | tf_op jit(solution)/shard_map/early_products/pallas_call | solution.py:92
  110.7 5.1 %collective-permute-start.9 = (bf16[1024,128]{1,0:T(8,128)(2,1)S(1)}, bf16[1024,128]{1,0:T(8,128)(2,1)S(1)}, u32[]{:S(2)}, u32[]{:S(2)}) collective-permute-start(bf16[1024,128]{1,0:T(8,128)(2,1)S(1)} %last_far.2), channel_id=1, source_target_pairs={{0,8},{8,0},{1,9},{9,1},{2,10},{10,2},{3,11},{11,3},{4,12},{12,4},... | collective-permute-start | bytes 786440 | tf_op jit(solution)/shard_map/ppermute | solution.py:197
  115.8 3.2 %early_products.3 = (f32[1024,128]{1,0:T(8,128)S(1)}, f32[1024,128]{1,0:T(8,128)S(1)}) custom-call(s32[2]{0:T(128)S(1)} %pad_add_fusion.place_ref, bf16[8,256,256]{2,1,0:T(8,128)(2,1)S(1)} %order_upper.1.upper_ref, bf16[2048,128]{1,0:T(8,128)(2,1)S(1)} %pad_maximum_fusion.stored_ref, bf16[2048,256]{1,0:T(8,128)(2,1)S(1)} %copy-done, ...), custom_call_target="tpu_custom_call" | custom-call | tf_op jit(solution)/shard_map/early_products/pallas_call | solution.py:92
  120.0 2.2 %collective-permute-start.14 = (bf16[1024,128]{1,0:T(8,128)(2,1)S(1)}, bf16[1024,128]{1,0:T(8,128)(2,1)S(1)}, u32[]{:S(2)}, u32[]{:S(2)}) collective-permute-start(bf16[1024,128]{1,0:T(8,128)(2,1)S(1)} %last_far.3), channel_id=1, source_target_pairs={{0,8},{8,0},{1,9},{9,1},{2,10},{10,2},{3,11},{11,3},{4,12},{12,4},... | collective-permute-start | bytes 786440 | tf_op jit(solution)/shard_map/ppermute | solution.py:197
  124.4 6.3 %collective-permute-done.14 = bf16[1024,128]{1,0:T(8,128)(2,1)S(1)} collective-permute-done((bf16[1024,128]{1,0:T(8,128)(2,1)S(1)}, bf16[1024,128]{1,0:T(8,128)(2,1)S(1)}, u32[]{:S(2)}, u32[]{:S(2)}) %collective-permute-start.14) | collective-permute-done | bytes 262176 | tf_op jit(solution)/shard_map/ppermute | solution.py:197
  (37 shorter events, 15.6 us)
Async XLA Ops:
  0.0 27.4 %collective-permute-start = (bf16[2048,256]{1,0:T(8,128)(2,1)}, bf16[2048,256]{1,0:T(8,128)(2,1)}, u32[]{:S(2)}, u32[]{:S(2)}) collective-permute-start(bf16[2048,256]{1,0:T(8,128)(2,1)} %refs_0_.3), channel_id=1, source_target_pairs={{0,1},{1,2},{2,3},{3,4},{4,5},{5,6},{6,7},{7,0},{8,9},{9,10},{10,1... | collective-permute-start | bytes 3145736 | tf_op jit(solution)/shard_map/ppermute | solution.py:144
  4.7 28.3 %collective-permute-start.1 = (bf16[2048,256]{1,0:T(8,128)(2,1)}, bf16[2048,256]{1,0:T(8,128)(2,1)}, u32[]{:S(2)}, u32[]{:S(2)}) collective-permute-start(bf16[2048,256]{1,0:T(8,128)(2,1)} %refs_0_.3), channel_id=1, source_target_pairs={{0,7},{1,0},{2,1},{3,2},{4,3},{5,4},{6,5},{7,6},{8,15},{9,8},{10,9... | collective-permute-start | bytes 3145736 | tf_op jit(solution)/shard_map/ppermute | solution.py:144
  10.7 31.2 %all-to-all-start = ((bf16[72,32,128]{2,0,1:T(8,128)(2,1)}), bf16[72,32,128]{2,0,1:T(8,128)(2,1)}, u32[]{:S(2)}, u32[]{:S(2)}) async-start(bf16[72,32,128]{2,0,1:T(8,128)(2,1)} %copy.9), calls=%async_computation | async-start | bytes 1179648 | tf_op jit(solution)/shard_map/all_to_all | solution.py:153
  27.4 29.9 %collective-permute-start.2 = (bf16[2048,256]{1,0:T(8,128)(2,1)}, bf16[2048,256]{1,0:T(8,128)(2,1)S(1)}, u32[]{:S(2)}, u32[]{:S(2)}) collective-permute-start(bf16[2048,256]{1,0:T(8,128)(2,1)} %collective-permute-done), channel_id=1, source_target_pairs={{0,1},{1,2},{2,3},{3,4},{4,5},{5,6},{6,7},{7,0},{8,9},{9,10},{10,1... | collective-permute-start | bytes 3145736 | tf_op jit(solution)/shard_map/ppermute | solution.py:156
  33.0 30.5 %collective-permute-start.4 = (bf16[2048,256]{1,0:T(8,128)(2,1)}, bf16[2048,256]{1,0:T(8,128)(2,1)}, u32[]{:S(2)}, u32[]{:S(2)}) collective-permute-start(bf16[2048,256]{1,0:T(8,128)(2,1)} %collective-permute-done.1), channel_id=1, source_target_pairs={{0,7},{1,0},{2,1},{3,2},{4,3},{5,4},{6,5},{7,6},{8,15},{9,8},{10,9... | collective-permute-start | bytes 3145736 | tf_op jit(solution)/shard_map/ppermute | solution.py:156
  48.3 26.5 %all-to-all-start.1 = ((bf16[32,64,128]{2,1,0:T(8,128)(2,1)}), bf16[32,64,128]{2,1,0:T(8,128)(2,1)}, u32[]{:S(2)}, u32[]{:S(2)}) async-start(bf16[32,64,128]{2,1,0:T(8,128)(2,1)} %bitcast.19), calls=%async_computation.1 | async-start | bytes 1048576 | tf_op jit(solution)/shard_map/all_to_all | solution.py:183
  58.4 17.3 %collective-permute-start.3 = (bf16[1024,256]{1,0:T(8,128)(2,1)}, bf16[1024,256]{1,0:T(8,128)(2,1)}, u32[]{:S(2)}, u32[]{:S(2)}) collective-permute-start(bf16[1024,256]{1,0:T(8,128)(2,1)} %get-tuple-element.24), channel_id=1, source_target_pairs={{0,1},{1,2},{2,3},{3,4},{4,5},{5,6},{6,7},{7,0},{8,9},{9,10},{10,1... | collective-permute-start | bytes 1572872 | tf_op jit(solution)/shard_map/ppermute | solution.py:160
  65.8 18.3 %collective-permute-start.5 = (bf16[1024,256]{1,0:T(8,128)(2,1)}, bf16[1024,256]{1,0:T(8,128)(2,1)}, u32[]{:S(2)}, u32[]{:S(2)}) collective-permute-start(bf16[1024,256]{1,0:T(8,128)(2,1)} %get-tuple-element.22), channel_id=1, source_target_pairs={{0,7},{1,0},{2,1},{3,2},{4,3},{5,4},{6,5},{7,6},{8,15},{9,8},{10,9... | collective-permute-start | bytes 1572872 | tf_op jit(solution)/shard_map/ppermute | solution.py:160
  67.7 27.5 %collective-permute-start.10 = (bf16[1024,256]{1,0:T(8,128)(2,1)}, bf16[1024,256]{1,0:T(8,128)(2,1)}, u32[]{:S(2)}, u32[]{:S(2)}) collective-permute-start(bf16[1024,256]{1,0:T(8,128)(2,1)} %get-tuple-element.23), channel_id=1, source_target_pairs={{0,1},{1,2},{2,3},{3,4},{4,5},{5,6},{6,7},{7,0},{8,9},{9,10},{10,1... | collective-permute-start | bytes 1572872 | tf_op jit(solution)/shard_map/ppermute | solution.py:160
  72.8 26.6 %collective-permute-start.11 = (bf16[1024,256]{1,0:T(8,128)(2,1)}, bf16[1024,256]{1,0:T(8,128)(2,1)}, u32[]{:S(2)}, u32[]{:S(2)}) collective-permute-start(bf16[1024,256]{1,0:T(8,128)(2,1)} %get-tuple-element.21), channel_id=1, source_target_pairs={{0,7},{1,0},{2,1},{3,2},{4,3},{5,4},{6,5},{7,6},{8,15},{9,8},{10,9... | collective-permute-start | bytes 1572872 | tf_op jit(solution)/shard_map/ppermute | solution.py:160
  84.1 20.1 %collective-permute-start.6 = (bf16[32,64,128]{2,1,0:T(8,128)(2,1)}, bf16[32,64,128]{2,1,0:T(8,128)(2,1)}, u32[]{:S(2)}, u32[]{:S(2)}) collective-permute-start(bf16[32,64,128]{2,1,0:T(8,128)(2,1)} %all-to-all-done.1.got_ref), channel_id=1, source_target_pairs={{0,16},{16,0},{1,17},{17,1},{2,18},{18,2},{3,19},{19,3},{4,20},{20... | collective-permute-start | bytes 1572872 | tf_op jit(solution)/shard_map/ppermute | solution.py:185
  87.7 21.8 %collective-permute-start.7 = (bf16[512,256]{1,0:T(8,128)(2,1)}, bf16[512,256]{1,0:T(8,128)(2,1)S(1)}, u32[]{:S(2)}, u32[]{:S(2)}) collective-permute-start(bf16[512,256]{1,0:T(8,128)(2,1)} %slice.80), channel_id=1, source_target_pairs={{0,1},{1,2},{2,3},{3,4},{4,5},{5,6},{6,7},{7,0},{8,9},{9,10},{10,1... | collective-permute-start | bytes 786440 | tf_op jit(solution)/shard_map/ppermute | solution.py:163
  91.2 18.2 %collective-permute-start.8 = (bf16[512,256]{1,0:T(8,128)(2,1)}, bf16[512,256]{1,0:T(8,128)(2,1)}, u32[]{:S(2)}, u32[]{:S(2)}) collective-permute-start(bf16[512,256]{1,0:T(8,128)(2,1)} %slice.81), channel_id=1, source_target_pairs={{0,7},{1,0},{2,1},{3,2},{4,3},{5,4},{6,5},{7,6},{8,15},{9,8},{10,9... | collective-permute-start | bytes 786440 | tf_op jit(solution)/shard_map/ppermute | solution.py:163
  95.2 11.0 %copy-start = (bf16[2048,256]{1,0:T(8,128)(2,1)S(1)}, bf16[2048,256]{1,0:T(8,128)(2,1)}, u32[]{:S(2)}) copy-start(bf16[2048,256]{1,0:T(8,128)(2,1)} %refs_0_.3) | copy-start | bytes 3145732
  96.3 22.8 %collective-permute-start.12 = (bf16[512,256]{1,0:T(8,128)(2,1)S(1)}, bf16[512,256]{1,0:T(8,128)(2,1)S(1)}, u32[]{:S(2)}, u32[]{:S(2)}) collective-permute-start(bf16[512,256]{1,0:T(8,128)(2,1)S(1)} %slice.84), channel_id=1, source_target_pairs={{0,1},{1,2},{2,3},{3,4},{4,5},{5,6},{6,7},{7,0},{8,9},{9,10},{10,1... | collective-permute-start | bytes 786440 | tf_op jit(solution)/shard_map/ppermute | solution.py:163
  100.4 18.7 %collective-permute-start.13 = (bf16[512,256]{1,0:T(8,128)(2,1)S(1)}, bf16[512,256]{1,0:T(8,128)(2,1)S(1)}, u32[]{:S(2)}, u32[]{:S(2)}) collective-permute-start(bf16[512,256]{1,0:T(8,128)(2,1)S(1)} %slice.85), channel_id=1, source_target_pairs={{0,7},{1,0},{2,1},{3,2},{4,3},{5,4},{6,5},{7,6},{8,15},{9,8},{10,9... | collective-permute-start | bytes 786440 | tf_op jit(solution)/shard_map/ppermute | solution.py:163
  110.7 13.6 %collective-permute-start.9 = (bf16[1024,128]{1,0:T(8,128)(2,1)S(1)}, bf16[1024,128]{1,0:T(8,128)(2,1)S(1)}, u32[]{:S(2)}, u32[]{:S(2)}) collective-permute-start(bf16[1024,128]{1,0:T(8,128)(2,1)S(1)} %last_far.2), channel_id=1, source_target_pairs={{0,8},{8,0},{1,9},{9,1},{2,10},{10,2},{3,11},{11,3},{4,12},{12,4},... | collective-permute-start | bytes 786440 | tf_op jit(solution)/shard_map/ppermute | solution.py:197
  120.0 10.7 %collective-permute-start.14 = (bf16[1024,128]{1,0:T(8,128)(2,1)S(1)}, bf16[1024,128]{1,0:T(8,128)(2,1)S(1)}, u32[]{:S(2)}, u32[]{:S(2)}) collective-permute-start(bf16[1024,128]{1,0:T(8,128)(2,1)S(1)} %last_far.3), channel_id=1, source_target_pairs={{0,8},{8,0},{1,9},{9,1},{2,10},{10,2},{3,11},{11,3},{4,12},{12,4},... | collective-permute-start | bytes 786440 | tf_op jit(solution)/shard_map/ppermute | solution.py:197

commit v8 on v4

--- a/solution.py
+++ b/solution.py
@@ -69,39 +69,50 @@
 def early_products(place, upper, stored, offsets, blocks):
     rows, width = stored.shape
     y_count, depth, both = upper.shape
+    flat, where = [], []
+    for block in blocks:
+        where.append(len(flat))
+        flat += block
 
     def body(place_ref, upper_ref, stored_ref, *refs):
-        *block_refs, far_ref, rest_ref, turned = refs
+        block_refs, (far_ref, rest_ref, turned) = refs[: len(flat)], refs[len(flat) :]
         for n, offset in enumerate(offsets):
             turned[n * depth : (n + 1) * depth] = upper_ref[(place_ref[1] + offset + y_count) % y_count]
         at_left = place_ref[0] == 0
 
-        def one(i, carry):
-            part = pl.ds(pl.multiple_of(i * TILE_M, TILE_M), TILE_M)
-            lhs = jnp.concatenate([ref[part] for ref in block_refs], axis=1)
-            total = jnp.dot(lhs, turned[...], preferred_element_type=jnp.float32)
-            left, right = total[:, :width], total[:, width:]
-            far_ref[part] = jnp.where(at_left, right, left)
-            rest_ref[part] = stored_ref[part].astype(jnp.float32) - jnp.where(at_left, left, right)
-            return carry
-
-        lax.fori_loop(0, rows // TILE_M, one, 0)
+        for part in range(2):
+
+            def one(i, carry):
+                local = pl.ds(pl.multiple_of(i * TILE_M, TILE_M), TILE_M)
+                full = pl.ds(pl.multiple_of(part * (rows // 2) + i * TILE_M, TILE_M), TILE_M)
+                tiles = [
+                    block_refs[n][full] if len(block) == 1 else block_refs[n + part][local]
+                    for n, block in zip(where, blocks)
+                ]
+                total = jnp.dot(jnp.concatenate(tiles, axis=1), turned[...], preferred_element_type=jnp.float32)
+                left, right = total[:, :width], total[:, width:]
+                far_ref[full] = jnp.where(at_left, right, left)
+                rest_ref[full] = stored_ref[full].astype(jnp.float32) - jnp.where(at_left, left, right)
+                return carry
+
+            lax.fori_loop(0, rows // 2 // TILE_M, one, 0)
 
     return pl.pallas_call(
         body,
-        in_specs=[pl.BlockSpec(memory_space=pltpu.SMEM)] + [whole()] * (2 + len(blocks)),
+        in_specs=[pl.BlockSpec(memory_space=pltpu.SMEM)] + [whole()] * (2 + len(flat)),
         out_specs=[whole(), whole()],
         out_shape=[jax.ShapeDtypeStruct((rows, width), jnp.float32)] * 2,
         scratch_shapes=[VM((len(offsets) * depth, both), upper.dtype)],
         compiler_params=grant(16),
         name="early_products",
-    )(place, upper, stored, *blocks)
+    )(place, upper, stored, *flat)
 
 
 def last_product(place, upper, base, halves, partner, out_dtype, sign):
     rows, width = base.shape
-    y_count, depth, both = upper.shape
+    y_count = upper.shape[0]
     half = rows // len(halves)
+    step = min(half, TILE_M)
 
     def body(place_ref, upper_ref, base_ref, *refs):
         *half_refs, out_ref = refs
@@ -109,9 +120,9 @@
         columns = upper_ref[(place_ref[1] + y_count // 2) % y_count]
         columns = jnp.where(side == 0, columns[:, :width], columns[:, width:])
         for n, ref in enumerate(half_refs):
-            for start in range(0, half, TILE_M):
-                part = slice(n * half + start, n * half + start + TILE_M)
-                term = jnp.dot(ref[start : start + TILE_M], columns, preferred_element_type=jnp.float32)
+            for start in range(0, half, step):
+                part = slice(n * half + start, n * half + start + step)
+                term = jnp.dot(ref[start : start + step], columns, preferred_element_type=jnp.float32)
                 out_ref[part] = (base_ref[part] + sign * term).astype(out_ref.dtype)
 
     return pl.pallas_call(
@@ -147,16 +158,18 @@
     )
     packed = jnp.concatenate([first.reshape(share, groups, col_width), scale_rows], axis=0)
     packed = lax.all_to_all(packed, ROW, split_axis=1, concat_axis=0, tiled=True)
-    packed = after(packed, *near)
+    joined = jnp.concatenate(near, axis=1)
+    packed = after(packed, joined)
+    far_near = tuple(lax.ppermute(block, "y", route[sign]) for block, sign in zip(near, route))
+    first_keys, second_keys = ((0, -1), (1, 1)), ((1, -1), (0, 1))
+    third = {}
+    for part, sign in first_keys + second_keys:
+        block = far_near[0 if sign < 0 else 1][part * half : (part + 1) * half]
+        third[part, sign] = lax.ppermute(block, "y", route[sign])
+    last = [lax.ppermute(third[part, sign], "y", route[sign]) for part, sign in first_keys]
     packed = packed.reshape(groups, share + PAD, col_width)
     cyclic = packed[:, :share].reshape(row_count, col_width)
     scale_cyclic = packed[:, share, :share].reshape(row_count)
-
-    steps, moving = [near], near
-    for distance in range(2, y_count // 2):
-        moving = tuple(lax.ppermute(block, "y", route[sign]) for block, sign in zip(moving, route))
-        steps.append(moving)
-    last = (lax.ppermute(moving[0][:half], "y", up), lax.ppermute(moving[1][half:], "y", down))
 
     level_one = butterfly(cyclic[:half], cyclic[half:])
     second = (scale_cyclic.astype(jnp.float32)[:, None] * level_one).astype(jnp.bfloat16)
@@ -173,18 +186,16 @@
     send = jnp.broadcast_to(top, (chips, X_HI, top_count, col_width)).reshape(
         chips * X_HI, top_count, col_width
     )
-    send = after(send, *steps[1])
     got = lax.all_to_all(send, ("chip", "x_hi"), split_axis=0, concat_axis=0)
+    got = after(got, *(third[key] for key in first_keys))
     twin = lax.ppermute(got, "core", [(0, 1), (1, 0)])
+    twin = after(twin, *(third[key] for key in second_keys))
     core = lax.axis_index("core").astype(jnp.int32).reshape(1)
     upper = order_upper(core, got, twin, y_count)
-    upper = after(upper, *steps[2])
-
     place = jnp.stack([lax.axis_index("x_hi"), lax.axis_index("y")]).astype(jnp.int32)
-    offsets, blocks = [0], [panel_lower]
-    for distance, step in enumerate(steps, 1):
-        offsets += [-distance, distance]
-        blocks += step
+    offsets = [0, -1, 1, -2, 2, -3, 3]
+    blocks = [(panel_lower,), (joined,), far_near[:1], far_near[1:]]
+    blocks += [(third[0, sign], third[1, sign]) for sign in route]
     far, rest = early_products(place, upper, stored, offsets, blocks)
     far = last_product(place, upper, far, last, True, jnp.bfloat16, 1)
     came = lax.ppermute(far, "x_hi", [(i, X_HI - 1 - i) for i in range(X_HI)])

time: 138 us -> 127 us (0.920)
  the two profiles are of different devices: /device:TPU:24 before, /device:TPU:2 now
where the time goes in v8:
time: 127 us; the launch traced here: 126 us
  starting transfers between devices  63.4 us (50%)
  waiting for transfers between devices  33.3 us (26%)
  Pallas kernels  10.5 us (8%)
  other arithmetic  9.49 us (7%)
  local copies, waits for them, and re-layouts  8.8 us (7%)
    ppermute x4, starting transfers between devices, per_device(): third[part, sign] = lax.ppermute(block, 'y', route[sign])  14.1 us
    all_to_all x1, starting transfers between devices, per_device(): lax.all_to_all(packed, ROW, split_axis=1, concat_axis=0, tiled=True)  12 us
    ppermute x1, waiting for transfers between devices, per_device(): came = lax.ppermute(far, 'x_hi', [(i, X_HI - 1 - i) for i in range(X_HI)])  11 us
    all_to_all x1, starting transfers between devices, per_device(): got = lax.all_to_all(send, ('chip', 'x_hi'), split_axis=0, concat_axis=0)  9.58 us
    ppermute x2, starting transfers between devices, per_device(): lax.ppermute(third[part, sign], 'y', route[sign])  7.52 us
    ppermute x2, starting transfers between devices, per_device(): lax.ppermute(panel_lower, 'y', route[sign])  7.29 us
    ppermute x2, waiting for transfers between devices, per_device(): lax.ppermute(third[part, sign], 'y', route[sign])  7.21 us
    ppermute x2, starting transfers between devices, per_device(): lax.ppermute(block, 'y', route[sign])  7.04 us
  transfers between devices with their start and end apart: 14, of which 7 were waited for; matrix products, arithmetic and copies ran while one was open for 14% of the time, Pallas kernels for 7%

profile of v8, /device:TPU:2, one launch (start us, length us, event | category | flops | bytes accessed | tf_op | source)
XLA Modules:
  0.0 125.7 jit_solution(10955601217667022232)
XLA Ops:
  0.0 3.5 %collective-permute-start = (bf16[2048,256]{1,0:T(8,128)(2,1)}, bf16[2048,256]{1,0:T(8,128)(2,1)}, u32[]{:S(2)}, u32[]{:S(2)}) collective-permute-start(bf16[2048,256]{1,0:T(8,128)(2,1)} %refs_0_.1), channel_id=1, source_target_pairs={{0,1},{1,2},{2,3},{3,4},{4,5},{5,6},{6,7},{7,0},{8,9},{9,10},{10,1... | collective-permute-start | bytes 3145736 | tf_op jit(solution)/shard_map/ppermute | solution.py:151
  3.5 3.8 %collective-permute-start.1 = (bf16[2048,256]{1,0:T(8,128)(2,1)}, bf16[2048,256]{1,0:T(8,128)(2,1)}, u32[]{:S(2)}, u32[]{:S(2)}) collective-permute-start(bf16[2048,256]{1,0:T(8,128)(2,1)} %refs_0_.1), channel_id=1, source_target_pairs={{0,7},{1,0},{2,1},{3,2},{4,3},{5,4},{6,5},{7,6},{8,15},{9,8},{10,9... | collective-permute-start | bytes 3145736 | tf_op jit(solution)/shard_map/ppermute | solution.py:151
  8.8 1.4 %multiply_convert_fusion = bf16[2048,128]{1,0:T(8,128)(2,1)S(1)} fusion(bf16[2048,128]{1,0:T(8,128)(2,1)} %param.4, f32[2048]{0:T(1024)S(1)} %convert_element_type.51), kind=kLoop, calls=%fused_computation.5 | loop fusion | flops 786432 | bytes 1056768 | tf_op jit(solution)/shard_map/convert_element_type | solution.py:153
  11.3 12.0 %all-to-all-start = ((bf16[72,32,128]{2,0,1:T(8,128)(2,1)}), bf16[72,32,128]{2,0,1:T(8,128)(2,1)}, u32[]{:S(2)}, u32[]{:S(2)}) async-start(bf16[72,32,128]{2,0,1:T(8,128)(2,1)} %copy.9), calls=%async_computation | async-start | bytes 1179648 | tf_op jit(solution)/shard_map/all_to_all | solution.py:160
  23.3 5.5 %collective-permute-done = bf16[2048,256]{1,0:T(8,128)(2,1)} collective-permute-done((bf16[2048,256]{1,0:T(8,128)(2,1)}, bf16[2048,256]{1,0:T(8,128)(2,1)}, u32[]{:S(2)}, u32[]{:S(2)}) %collective-permute-start) | collective-permute-done | bytes 1048608 | tf_op jit(solution)/shard_map/ppermute | solution.py:151
  28.8 1.9 %collective-permute-start.2 = (bf16[2048,256]{1,0:T(8,128)(2,1)}, bf16[2048,256]{1,0:T(8,128)(2,1)S(1)}, u32[]{:S(2)}, u32[]{:S(2)}) collective-permute-start(bf16[2048,256]{1,0:T(8,128)(2,1)} %collective-permute-done), channel_id=1, source_target_pairs={{0,1},{1,2},{2,3},{3,4},{4,5},{5,6},{6,7},{7,0},{8,9},{9,10},{10,1... | collective-permute-start | bytes 3145736 | tf_op jit(solution)/shard_map/ppermute | solution.py:163
  30.8 5.1 %collective-permute-start.4 = (bf16[2048,256]{1,0:T(8,128)(2,1)}, bf16[2048,256]{1,0:T(8,128)(2,1)}, u32[]{:S(2)}, u32[]{:S(2)}) collective-permute-start(bf16[2048,256]{1,0:T(8,128)(2,1)} %collective-permute-done.1), channel_id=1, source_target_pairs={{0,7},{1,0},{2,1},{3,2},{4,3},{5,4},{6,5},{7,6},{8,15},{9,8},{10,9... | collective-permute-start | bytes 3145736 | tf_op jit(solution)/shard_map/ppermute | solution.py:163
  35.9 1.3 %constant_dynamic-update-slice_fusion.1 = bf16[2048,512]{1,0:T(8,128)(2,1)S(1)} fusion(bf16[2048,256]{1,0:T(8,128)(2,1)} %collective-permute-done), kind=kLoop, calls=%fused_computation.27 | loop fusion | bytes 2097152
  37.2 1.3 %constant_dynamic-update-slice_fusion.refs_1_ = bf16[2048,512]{1,0:T(8,128)(2,1)S(1)} fusion(bf16[2048,512]{1,0:T(8,128)(2,1)S(1)} %constant_dynamic-update-slice_fusion.1, bf16[2048,256]{1,0:T(8,128)(2,1)} %collective-permute-done.1), kind=kLoop, calls=%fused_computation.26 | loop fusion | bytes 2097152 | tf_op jit(solution)/shard_map/concatenate | solution.py:161
  38.5 4.0 %all-to-all-done = bf16[72,32,128]{2,0,1:T(8,128)(2,1)} async-done(((bf16[72,32,128]{2,0,1:T(8,128)(2,1)}), bf16[72,32,128]{2,0,1:T(8,128)(2,1)}, u32[]{:S(2)}, u32[]{:S(2)}) %all-to-all-start) | async-done | bytes 589856 | tf_op jit(solution)/shard_map/all_to_all | solution.py:160
  42.5 2.1 %fusion.3 = (f32[16,64,128]{2,1,0:T(8,128)}, f32[16,64,128]{2,1,0:T(8,128)}) fusion(bf16[32,72,128]{2,1,0:T(8,128)(2,1)} %bitcast.9), kind=kLoop, calls=%fused_computation.9 | loop fusion | flops 786432 | bytes 1572864 | tf_op jit(solution)/shard_map/mul | solution.py:21
  45.6 1.5 %fusion.1 = bf16[2048,128]{1,0:T(8,128)(2,1)S(1)} fusion(f32[1024,128]{1,0:T(8,128)} %bitcast.18, f32[1024,128]{1,0:T(8,128)} %bitcast.17, f32[2048]{0:T(1024)S(1)} %reshape.41), kind=kLoop, calls=%fused_computation.3 | loop fusion | flops 786432 | bytes 1581056 | tf_op jit(solution)/shard_map/convert_element_type | solution.py:175
  48.8 9.6 %all-to-all-start.1 = ((bf16[32,64,128]{2,1,0:T(8,128)(2,1)}), bf16[32,64,128]{2,1,0:T(8,128)(2,1)}, u32[]{:S(2)}, u32[]{:S(2)}) async-start(bf16[32,64,128]{2,1,0:T(8,128)(2,1)} %bitcast.19), calls=%async_computation.1 | async-start | bytes 1048576 | tf_op jit(solution)/shard_map/all_to_all | solution.py:189
  58.4 1.0 fusion.15
  59.5 1.9 %collective-permute-start.3 = (bf16[1024,256]{1,0:T(8,128)(2,1)}, bf16[1024,256]{1,0:T(8,128)(2,1)}, u32[]{:S(2)}, u32[]{:S(2)}) collective-permute-start(bf16[1024,256]{1,0:T(8,128)(2,1)} %get-tuple-element.18), channel_id=1, source_target_pairs={{0,1},{1,2},{2,3},{3,4},{4,5},{5,6},{6,7},{7,0},{8,9},{9,10},{10,1... | collective-permute-start | bytes 1572872 | tf_op jit(solution)/shard_map/ppermute | solution.py:168
  61.4 2.3 %fusion.14 = (bf16[1024,256]{1,0:T(8,128)(2,1)}, bf16[1024,256]{1,0:T(8,128)(2,1)}) fusion(bf16[2048,256]{1,0:T(8,128)(2,1)} %collective-permute-done.4.refs_3_), kind=kLoop, calls=%fused_computation.29 | loop fusion | bytes 2097152 | tf_op jit(solution)/shard_map/slice | solution.py:167
  63.7 5.1 %collective-permute-start.5 = (bf16[1024,256]{1,0:T(8,128)(2,1)}, bf16[1024,256]{1,0:T(8,128)(2,1)}, u32[]{:S(2)}, u32[]{:S(2)}) collective-permute-start(bf16[1024,256]{1,0:T(8,128)(2,1)} %get-tuple-element.16), channel_id=1, source_target_pairs={{0,7},{1,0},{2,1},{3,2},{4,3},{5,4},{6,5},{7,6},{8,15},{9,8},{10,9... | collective-permute-start | bytes 1572872 | tf_op jit(solution)/shard_map/ppermute | solution.py:168
  68.8 1.9 %collective-permute-start.7 = (bf16[1024,256]{1,0:T(8,128)(2,1)}, bf16[1024,256]{1,0:T(8,128)(2,1)}, u32[]{:S(2)}, u32[]{:S(2)}) collective-permute-start(bf16[1024,256]{1,0:T(8,128)(2,1)} %get-tuple-element.17), channel_id=1, source_target_pairs={{0,1},{1,2},{2,3},{3,4},{4,5},{5,6},{6,7},{7,0},{8,9},{9,10},{10,1... | collective-permute-start | bytes 1572872 | tf_op jit(solution)/shard_map/ppermute | solution.py:168
  70.7 5.1 %collective-permute-start.8 = (bf16[1024,256]{1,0:T(8,128)(2,1)}, bf16[1024,256]{1,0:T(8,128)(2,1)}, u32[]{:S(2)}, u32[]{:S(2)}) collective-permute-start(bf16[1024,256]{1,0:T(8,128)(2,1)} %get-tuple-element.15), channel_id=1, source_target_pairs={{0,7},{1,0},{2,1},{3,2},{4,3},{5,4},{6,5},{7,6},{8,15},{9,8},{10,9... | collective-permute-start | bytes 1572872 | tf_op jit(solution)/shard_map/ppermute | solution.py:168
  75.9 1.4 %collective-permute-done.3.refs_4_ = bf16[1024,256]{1,0:T(8,128)(2,1)} collective-permute-done((bf16[1024,256]{1,0:T(8,128)(2,1)}, bf16[1024,256]{1,0:T(8,128)(2,1)}, u32[]{:S(2)}, u32[]{:S(2)}) %collective-permute-start.3) | collective-permute-done | bytes 524320 | tf_op jit(solution)/shard_map/ppermute | solution.py:168
  77.3 4.2 %collective-permute-done.5.refs_7_ = bf16[1024,256]{1,0:T(8,128)(2,1)} collective-permute-done((bf16[1024,256]{1,0:T(8,128)(2,1)}, bf16[1024,256]{1,0:T(8,128)(2,1)}, u32[]{:S(2)}, u32[]{:S(2)}) %collective-permute-start.5) | collective-permute-done | bytes 524320 | tf_op jit(solution)/shard_map/ppermute | solution.py:168
  81.5 1.9 %collective-permute-start.6 = (bf16[32,64,128]{2,1,0:T(8,128)(2,1)}, bf16[32,64,128]{2,1,0:T(8,128)(2,1)}, u32[]{:S(2)}, u32[]{:S(2)}) collective-permute-start(bf16[32,64,128]{2,1,0:T(8,128)(2,1)} %all-to-all-done.1.got_ref), channel_id=1, source_target_pairs={{0,16},{16,0},{1,17},{17,1},{2,18},{18,2},{3,19},{19,3},{4,20},{20... | collective-permute-start | bytes 1572872 | tf_op jit(solution)/shard_map/ppermute | solution.py:191
  83.4 5.6 %collective-permute-start.10 = (bf16[1024,256]{1,0:T(8,128)(2,1)}, bf16[1024,256]{1,0:T(8,128)(2,1)}, u32[]{:S(2)}, u32[]{:S(2)}) collective-permute-start(bf16[1024,256]{1,0:T(8,128)(2,1)} %collective-permute-done.5.refs_7_), channel_id=1, source_target_pairs={{0,7},{1,0},{2,1},{3,2},{4,3},{5,4},{6,5},{7,6},{8,15},{9,8},{10,9... | collective-permute-start | bytes 1572872 | tf_op jit(solution)/shard_map/ppermute | solution.py:169
  89.0 1.9 %collective-permute-start.9 = (bf16[1024,256]{1,0:T(8,128)(2,1)}, bf16[1024,256]{1,0:T(8,128)(2,1)}, u32[]{:S(2)}, u32[]{:S(2)}) collective-permute-start(bf16[1024,256]{1,0:T(8,128)(2,1)} %collective-permute-done.3.refs_4_), channel_id=1, source_target_pairs={{0,1},{1,2},{2,3},{3,4},{4,5},{5,6},{6,7},{7,0},{8,9},{9,10},{10,1... | collective-permute-start | bytes 1572872 | tf_op jit(solution)/shard_map/ppermute | solution.py:169
  92.1 2.0 %order_upper.1.upper_ref = bf16[8,256,256]{2,1,0:T(8,128)(2,1)S(1)} custom-call(s32[1]{0:T(128)} %bitcast.2.core_ref, bf16[32,64,128]{2,1,0:T(8,128)(2,1)} %all-to-all-done.1.got_ref, bf16[32,64,128]{2,1,0:T(8,128)(2,1)} %collective-permute-done.6.twin_ref), custom_call_target="tpu_custom_call" | custom-call | tf_op jit(solution)/shard_map/order_upper/pallas_call | solution.py:59
  94.1 5.2 %early_products.1 = (f32[2048,128]{1,0:T(8,128)S(1)}, f32[2048,128]{1,0:T(8,128)S(1)}) custom-call(s32[2]{0:T(128)S(1)} %pad_add_fusion.place_ref, bf16[8,256,256]{2,1,0:T(8,128)(2,1)S(1)} %order_upper.1.upper_ref, bf16[2048,128]{1,0:T(8,128)(2,1)S(1)} %pad_maximum_fusion.stored_ref, bf16[2048,256]{1,0:T(8,128)(2,1)S(1)} %copy-done, ...), custom_call_target="tpu_custom_call" | custom-call | tf_op jit(solution)/shard_map/early_products/pallas_call | solution.py:100
  99.3 1.9 %collective-permute-done.10.refs_1_ = bf16[1024,256]{1,0:T(8,128)(2,1)} collective-permute-done((bf16[1024,256]{1,0:T(8,128)(2,1)}, bf16[1024,256]{1,0:T(8,128)(2,1)}, u32[]{:S(2)}, u32[]{:S(2)}) %collective-permute-start.10) | collective-permute-done | bytes 524320 | tf_op jit(solution)/shard_map/ppermute | solution.py:169
  101.1 5.3 %collective-permute-done.9.refs_0_ = bf16[1024,256]{1,0:T(8,128)(2,1)} collective-permute-done((bf16[1024,256]{1,0:T(8,128)(2,1)}, bf16[1024,256]{1,0:T(8,128)(2,1)}, u32[]{:S(2)}, u32[]{:S(2)}) %collective-permute-start.9) | collective-permute-done | bytes 524320 | tf_op jit(solution)/shard_map/ppermute | solution.py:169
  106.5 1.7 %last_far.1 = bf16[2048,128]{1,0:T(8,128)(2,1)S(1)} custom-call(s32[2]{0:T(128)S(1)} %pad_add_fusion.place_ref, bf16[8,256,256]{2,1,0:T(8,128)(2,1)S(1)} %order_upper.1.upper_ref, f32[2048,128]{1,0:T(8,128)S(1)} %get-tuple-element.14.base_ref, bf16[1024,256]{1,0:T(8,128)(2,1)} %collective-permute-done.9.refs_0_, ...), custom_call_target="tpu_custom_call" | custom-call | tf_op jit(solution)/shard_map/last_far/pallas_call | solution.py:128
  108.1 4.0 %collective-permute-start.11 = (bf16[2048,128]{1,0:T(8,128)(2,1)S(1)}, bf16[2048,128]{1,0:T(8,128)(2,1)S(1)}, u32[]{:S(2)}, u32[]{:S(2)}) collective-permute-start(bf16[2048,128]{1,0:T(8,128)(2,1)S(1)} %last_far.1), channel_id=1, source_target_pairs={{0,8},{8,0},{1,9},{9,1},{2,10},{10,2},{3,11},{11,3},{4,12},{12,4},... | collective-permute-start | bytes 1572872 | tf_op jit(solution)/shard_map/ppermute | solution.py:201
  112.1 1.6 %last_own.1 = f32[2048,128]{1,0:T(8,128)S(1)} custom-call(s32[2]{0:T(128)S(1)} %pad_add_fusion.place_ref, bf16[8,256,256]{2,1,0:T(8,128)(2,1)S(1)} %order_upper.1.upper_ref, f32[2048,128]{1,0:T(8,128)S(1)} %get-tuple-element.13.base_ref, bf16[1024,256]{1,0:T(8,128)(2,1)} %collective-permute-done.9.refs_0_, bf16[1024,256]{1,0:T(8,128)(2,1)} %collective-permute-done.10.refs_1_), custom_call_target="tpu_custom_call" | custom-call | tf_op jit(solution)/shard_map/last_own/pallas_call | solution.py:128
  113.8 11.0 %collective-permute-done.11 = bf16[2048,128]{1,0:T(8,128)(2,1)S(1)} collective-permute-done((bf16[2048,128]{1,0:T(8,128)(2,1)S(1)}, bf16[2048,128]{1,0:T(8,128)(2,1)S(1)}, u32[]{:S(2)}, u32[]{:S(2)}) %collective-permute-start.11) | collective-permute-done | bytes 524320 | tf_op jit(solution)/shard_map/ppermute | solution.py:201
  (22 shorter events, 7.3 us)
Async XLA Ops:
  0.0 28.8 %collective-permute-start = (bf16[2048,256]{1,0:T(8,128)(2,1)}, bf16[2048,256]{1,0:T(8,128)(2,1)}, u32[]{:S(2)}, u32[]{:S(2)}) collective-permute-start(bf16[2048,256]{1,0:T(8,128)(2,1)} %refs_0_.1), channel_id=1, source_target_pairs={{0,1},{1,2},{2,3},{3,4},{4,5},{5,6},{6,7},{7,0},{8,9},{9,10},{10,1... | collective-permute-start | bytes 3145736 | tf_op jit(solution)/shard_map/ppermute | solution.py:151
  3.5 27.3 %collective-permute-start.1 = (bf16[2048,256]{1,0:T(8,128)(2,1)}, bf16[2048,256]{1,0:T(8,128)(2,1)}, u32[]{:S(2)}, u32[]{:S(2)}) collective-permute-start(bf16[2048,256]{1,0:T(8,128)(2,1)} %refs_0_.1), channel_id=1, source_target_pairs={{0,7},{1,0},{2,1},{3,2},{4,3},{5,4},{6,5},{7,6},{8,15},{9,8},{10,9... | collective-permute-start | bytes 3145736 | tf_op jit(solution)/shard_map/ppermute | solution.py:151
  11.3 31.2 %all-to-all-start = ((bf16[72,32,128]{2,0,1:T(8,128)(2,1)}), bf16[72,32,128]{2,0,1:T(8,128)(2,1)}, u32[]{:S(2)}, u32[]{:S(2)}) async-start(bf16[72,32,128]{2,0,1:T(8,128)(2,1)} %copy.9), calls=%async_computation | async-start | bytes 1179648 | tf_op jit(solution)/shard_map/all_to_all | solution.py:160
  28.8 29.6 %collective-permute-start.2 = (bf16[2048,256]{1,0:T(8,128)(2,1)}, bf16[2048,256]{1,0:T(8,128)(2,1)S(1)}, u32[]{:S(2)}, u32[]{:S(2)}) collective-permute-start(bf16[2048,256]{1,0:T(8,128)(2,1)} %collective-permute-done), channel_id=1, source_target_pairs={{0,1},{1,2},{2,3},{3,4},{4,5},{5,6},{6,7},{7,0},{8,9},{9,10},{10,1... | collective-permute-start | bytes 3145736 | tf_op jit(solution)/shard_map/ppermute | solution.py:163
  30.8 30.6 %collective-permute-start.4 = (bf16[2048,256]{1,0:T(8,128)(2,1)}, bf16[2048,256]{1,0:T(8,128)(2,1)}, u32[]{:S(2)}, u32[]{:S(2)}) collective-permute-start(bf16[2048,256]{1,0:T(8,128)(2,1)} %collective-permute-done.1), channel_id=1, source_target_pairs={{0,7},{1,0},{2,1},{3,2},{4,3},{5,4},{6,5},{7,6},{8,15},{9,8},{10,9... | collective-permute-start | bytes 3145736 | tf_op jit(solution)/shard_map/ppermute | solution.py:163
  48.8 27.0 %all-to-all-start.1 = ((bf16[32,64,128]{2,1,0:T(8,128)(2,1)}), bf16[32,64,128]{2,1,0:T(8,128)(2,1)}, u32[]{:S(2)}, u32[]{:S(2)}) async-start(bf16[32,64,128]{2,1,0:T(8,128)(2,1)} %bitcast.19), calls=%async_computation.1 | async-start | bytes 1048576 | tf_op jit(solution)/shard_map/all_to_all | solution.py:189
  59.5 17.8 %collective-permute-start.3 = (bf16[1024,256]{1,0:T(8,128)(2,1)}, bf16[1024,256]{1,0:T(8,128)(2,1)}, u32[]{:S(2)}, u32[]{:S(2)}) collective-permute-start(bf16[1024,256]{1,0:T(8,128)(2,1)} %get-tuple-element.18), channel_id=1, source_target_pairs={{0,1},{1,2},{2,3},{3,4},{4,5},{5,6},{6,7},{7,0},{8,9},{9,10},{10,1... | collective-permute-start | bytes 1572872 | tf_op jit(solution)/shard_map/ppermute | solution.py:168
  63.7 17.8 %collective-permute-start.5 = (bf16[1024,256]{1,0:T(8,128)(2,1)}, bf16[1024,256]{1,0:T(8,128)(2,1)}, u32[]{:S(2)}, u32[]{:S(2)}) collective-permute-start(bf16[1024,256]{1,0:T(8,128)(2,1)} %get-tuple-element.16), channel_id=1, source_target_pairs={{0,7},{1,0},{2,1},{3,2},{4,3},{5,4},{6,5},{7,6},{8,15},{9,8},{10,9... | collective-permute-start | bytes 1572872 | tf_op jit(solution)/shard_map/ppermute | solution.py:168
  68.8 23.2 %collective-permute-start.7 = (bf16[1024,256]{1,0:T(8,128)(2,1)}, bf16[1024,256]{1,0:T(8,128)(2,1)}, u32[]{:S(2)}, u32[]{:S(2)}) collective-permute-start(bf16[1024,256]{1,0:T(8,128)(2,1)} %get-tuple-element.17), channel_id=1, source_target_pairs={{0,1},{1,2},{2,3},{3,4},{4,5},{5,6},{6,7},{7,0},{8,9},{9,10},{10,1... | collective-permute-start | bytes 1572872 | tf_op jit(solution)/shard_map/ppermute | solution.py:168
  70.7 21.3 %collective-permute-start.8 = (bf16[1024,256]{1,0:T(8,128)(2,1)}, bf16[1024,256]{1,0:T(8,128)(2,1)}, u32[]{:S(2)}, u32[]{:S(2)}) collective-permute-start(bf16[1024,256]{1,0:T(8,128)(2,1)} %get-tuple-element.15), channel_id=1, source_target_pairs={{0,7},{1,0},{2,1},{3,2},{4,3},{5,4},{6,5},{7,6},{8,15},{9,8},{10,9... | collective-permute-start | bytes 1572872 | tf_op jit(solution)/shard_map/ppermute | solution.py:168
  81.5 10.6 %collective-permute-start.6 = (bf16[32,64,128]{2,1,0:T(8,128)(2,1)}, bf16[32,64,128]{2,1,0:T(8,128)(2,1)}, u32[]{:S(2)}, u32[]{:S(2)}) collective-permute-start(bf16[32,64,128]{2,1,0:T(8,128)(2,1)} %all-to-all-done.1.got_ref), channel_id=1, source_target_pairs={{0,16},{16,0},{1,17},{17,1},{2,18},{18,2},{3,19},{19,3},{4,20},{20... | collective-permute-start | bytes 1572872 | tf_op jit(solution)/shard_map/ppermute | solution.py:191
  83.4 17.7 %collective-permute-start.10 = (bf16[1024,256]{1,0:T(8,128)(2,1)}, bf16[1024,256]{1,0:T(8,128)(2,1)}, u32[]{:S(2)}, u32[]{:S(2)}) collective-permute-start(bf16[1024,256]{1,0:T(8,128)(2,1)} %collective-permute-done.5.refs_7_), channel_id=1, source_target_pairs={{0,7},{1,0},{2,1},{3,2},{4,3},{5,4},{6,5},{7,6},{8,15},{9,8},{10,9... | collective-permute-start | bytes 1572872 | tf_op jit(solution)/shard_map/ppermute | solution.py:169
  89.0 17.5 %collective-permute-start.9 = (bf16[1024,256]{1,0:T(8,128)(2,1)}, bf16[1024,256]{1,0:T(8,128)(2,1)}, u32[]{:S(2)}, u32[]{:S(2)}) collective-permute-start(bf16[1024,256]{1,0:T(8,128)(2,1)} %collective-permute-done.3.refs_4_), channel_id=1, source_target_pairs={{0,1},{1,2},{2,3},{3,4},{4,5},{5,6},{6,7},{7,0},{8,9},{9,10},{10,1... | collective-permute-start | bytes 1572872 | tf_op jit(solution)/shard_map/ppermute | solution.py:169
  90.9 3.1 %copy-start = (bf16[2048,256]{1,0:T(8,128)(2,1)S(1)}, bf16[2048,256]{1,0:T(8,128)(2,1)}, u32[]{:S(2)}) copy-start(bf16[2048,256]{1,0:T(8,128)(2,1)} %refs_0_.1) | copy-start | bytes 3145732
  108.1 16.6 %collective-permute-start.11 = (bf16[2048,128]{1,0:T(8,128)(2,1)S(1)}, bf16[2048,128]{1,0:T(8,128)(2,1)S(1)}, u32[]{:S(2)}, u32[]{:S(2)}) collective-permute-start(bf16[2048,128]{1,0:T(8,128)(2,1)S(1)} %last_far.1), channel_id=1, source_target_pairs={{0,8},{8,0},{1,9},{9,1},{2,10},{10,2},{3,11},{11,3},{4,12},{12,4},... | collective-permute-start | bytes 1572872 | tf_op jit(solution)/shard_map/ppermute | solution.py:201

commit v9 on v8

--- a/solution.py
+++ b/solution.py
@@ -66,73 +66,73 @@
     )(core, got, twin)
 
 
-def early_products(place, upper, stored, offsets, blocks):
+def early_products(place, upper, stored, offsets, blocks, own_offsets, own_blocks):
     rows, width = stored.shape
     y_count, depth, both = upper.shape
-    flat, where = [], []
-    for block in blocks:
-        where.append(len(flat))
-        flat += block
+    parts = len(own_blocks)
+    share = rows // parts
+    common = len(offsets) * depth
 
     def body(place_ref, upper_ref, stored_ref, *refs):
-        block_refs, (far_ref, rest_ref, turned) = refs[: len(flat)], refs[len(flat) :]
+        block_refs, own_refs, out_refs = refs[: len(blocks)], refs[len(blocks) : -1 - 2 * parts], refs[-1 - 2 * parts : -1]
+        turned = refs[-1]
         for n, offset in enumerate(offsets):
             turned[n * depth : (n + 1) * depth] = upper_ref[(place_ref[1] + offset + y_count) % y_count]
         at_left = place_ref[0] == 0
 
-        for part in range(2):
+        for part in range(parts):
+            turned[common:] = upper_ref[(place_ref[1] + own_offsets[part] + y_count) % y_count]
+            far_ref, rest_ref = out_refs[2 * part : 2 * part + 2]
 
             def one(i, carry):
                 local = pl.ds(pl.multiple_of(i * TILE_M, TILE_M), TILE_M)
-                full = pl.ds(pl.multiple_of(part * (rows // 2) + i * TILE_M, TILE_M), TILE_M)
-                tiles = [
-                    block_refs[n][full] if len(block) == 1 else block_refs[n + part][local]
-                    for n, block in zip(where, blocks)
-                ]
+                full = pl.ds(pl.multiple_of(part * share + i * TILE_M, TILE_M), TILE_M)
+                tiles = [ref[full] for ref in block_refs] + [own_refs[part][local]]
                 total = jnp.dot(jnp.concatenate(tiles, axis=1), turned[...], preferred_element_type=jnp.float32)
                 left, right = total[:, :width], total[:, width:]
-                far_ref[full] = jnp.where(at_left, right, left)
-                rest_ref[full] = stored_ref[full].astype(jnp.float32) - jnp.where(at_left, left, right)
+                far_ref[local] = jnp.where(at_left, right, left)
+                rest_ref[local] = stored_ref[full].astype(jnp.float32) - jnp.where(at_left, left, right)
                 return carry
 
-            lax.fori_loop(0, rows // 2 // TILE_M, one, 0)
+            lax.fori_loop(0, share // TILE_M, one, 0)
 
     return pl.pallas_call(
         body,
-        in_specs=[pl.BlockSpec(memory_space=pltpu.SMEM)] + [whole()] * (2 + len(flat)),
-        out_specs=[whole(), whole()],
-        out_shape=[jax.ShapeDtypeStruct((rows, width), jnp.float32)] * 2,
-        scratch_shapes=[VM((len(offsets) * depth, both), upper.dtype)],
+        in_specs=[pl.BlockSpec(memory_space=pltpu.SMEM)] + [whole()] * (2 + len(blocks) + parts),
+        out_specs=[whole()] * (2 * parts),
+        out_shape=[jax.ShapeDtypeStruct((share, width), jnp.float32)] * (2 * parts),
+        scratch_shapes=[VM((common + depth, both), upper.dtype)],
         compiler_params=grant(16),
         name="early_products",
-    )(place, upper, stored, *flat)
-
-
-def last_product(place, upper, base, halves, partner, out_dtype, sign):
+    )(place, upper, stored, *blocks, *own_blocks)
+
+
+def last_product(place, upper, base, offsets, blocks, partner, out_dtype, sign):
     rows, width = base.shape
     y_count = upper.shape[0]
-    half = rows // len(halves)
-    step = min(half, TILE_M)
 
     def body(place_ref, upper_ref, base_ref, *refs):
-        *half_refs, out_ref = refs
+        *block_refs, out_ref = refs
         side = (place_ref[0] + 1) % X_HI if partner else place_ref[0]
-        columns = upper_ref[(place_ref[1] + y_count // 2) % y_count]
-        columns = jnp.where(side == 0, columns[:, :width], columns[:, width:])
-        for n, ref in enumerate(half_refs):
-            for start in range(0, half, step):
-                part = slice(n * half + start, n * half + start + step)
-                term = jnp.dot(ref[start : start + step], columns, preferred_element_type=jnp.float32)
-                out_ref[part] = (base_ref[part] + sign * term).astype(out_ref.dtype)
+        columns = []
+        for offset in offsets:
+            both = upper_ref[(place_ref[1] + offset + y_count) % y_count]
+            columns.append(jnp.where(side == 0, both[:, :width], both[:, width:]))
+        columns = jnp.concatenate(columns, axis=0)
+        for start in range(0, rows, TILE_M):
+            part = slice(start, start + TILE_M)
+            lhs = jnp.concatenate([ref[part] for ref in block_refs], axis=1)
+            term = jnp.dot(lhs, columns, preferred_element_type=jnp.float32)
+            out_ref[part] = (base_ref[part] + sign * term).astype(out_ref.dtype)
 
     return pl.pallas_call(
         body,
-        in_specs=[pl.BlockSpec(memory_space=pltpu.SMEM)] + [whole()] * (2 + len(halves)),
+        in_specs=[pl.BlockSpec(memory_space=pltpu.SMEM)] + [whole()] * (2 + len(blocks)),
         out_specs=whole(),
         out_shape=jax.ShapeDtypeStruct((rows, width), out_dtype),
         compiler_params=grant(8),
         name="last_far" if partner else "last_own",
-    )(place, upper, base, *halves)
+    )(place, upper, base, *blocks)
 
 
 def per_device(slab_block, scale_first, scale_second, panel_lower):
@@ -187,20 +187,31 @@
         chips * X_HI, top_count, col_width
     )
     got = lax.all_to_all(send, ("chip", "x_hi"), split_axis=0, concat_axis=0)
-    got = after(got, *(third[key] for key in first_keys))
+    got = after(got, third[0, -1])
     twin = lax.ppermute(got, "core", [(0, 1), (1, 0)])
     twin = after(twin, *(third[key] for key in second_keys))
     core = lax.axis_index("core").astype(jnp.int32).reshape(1)
     upper = order_upper(core, got, twin, y_count)
     place = jnp.stack([lax.axis_index("x_hi"), lax.axis_index("y")]).astype(jnp.int32)
-    offsets = [0, -1, 1, -2, 2, -3, 3]
-    blocks = [(panel_lower,), (joined,), far_near[:1], far_near[1:]]
-    blocks += [(third[0, sign], third[1, sign]) for sign in route]
-    far, rest = early_products(place, upper, stored, offsets, blocks)
-    far = last_product(place, upper, far, last, True, jnp.bfloat16, 1)
-    came = lax.ppermute(far, "x_hi", [(i, X_HI - 1 - i) for i in range(X_HI)])
-    rest = last_product(place, upper, rest, last, False, jnp.float32, -1)
-    return (rest - came.astype(jnp.float32)).astype(jnp.bfloat16)
+    swap = [(i, X_HI - 1 - i) for i in range(X_HI)]
+    sums = early_products(
+        place,
+        upper,
+        stored,
+        [0, -1, 1, -2, 2],
+        [panel_lower, joined, *far_near],
+        [sign * (y_count // 2 - 1) for _, sign in first_keys],
+        [third[key] for key in first_keys],
+    )
+    out = []
+    for part, sign in first_keys:
+        offsets = [-sign * (y_count // 2 - 1), y_count // 2]
+        blocks = [third[part, -sign], last[part]]
+        far = last_product(place, upper, sums[2 * part], offsets, blocks, True, jnp.bfloat16, 1)
+        came = lax.ppermute(far, "x_hi", swap)
+        rest = last_product(place, upper, sums[2 * part + 1], offsets, blocks, False, jnp.float32, -1)
+        out.append((rest - came.astype(jnp.float32)).astype(jnp.bfloat16))
+    return jnp.concatenate(out, axis=0)
 
 
 def solution(mesh):

time: 127 us -> 119 us (0.937)
  the two profiles are of different devices: /device:TPU:2 before, /device:TPU:472 now
where the time goes in v9:
time: 119 us; the launch traced here: 118 us
  starting transfers between devices  58.3 us (49%)
  waiting for transfers between devices  30.3 us (25%)
  Pallas kernels  13.1 us (11%)
  local copies, waits for them, and re-layouts  8.78 us (7%)
  other arithmetic  7.36 us (6%)
    ppermute x4, starting transfers between devices, per_device(): third[part, sign] = lax.ppermute(block, 'y', route[sign])  14.4 us
    ppermute x2, waiting for transfers between devices, per_device(): lax.ppermute(panel_lower, 'y', route[sign])  11 us
    ppermute x4, waiting for transfers between devices, per_device(): third[part, sign] = lax.ppermute(block, 'y', route[sign])  9.26 us
    ppermute x2, starting transfers between devices, per_device(): lax.ppermute(third[part, sign], 'y', route[sign])  7.51 us
    ppermute x2, starting transfers between devices, per_device(): lax.ppermute(block, 'y', route[sign])  7.51 us
    ppermute x2, starting transfers between devices, per_device(): came = lax.ppermute(far, 'x_hi', swap)  7.35 us
    all_to_all x1, starting transfers between devices, per_device(): got = lax.all_to_all(send, ('chip', 'x_hi'), split_axis=0, concat_axis=0)  7.26 us
    ppermute x2, starting transfers between devices, per_device(): lax.ppermute(panel_lower, 'y', route[sign])  6.62 us
  transfers between devices with their start and end apart: 15, of which 7 were waited for; matrix products, arithmetic and copies ran while one was open for 13% of the time, Pallas kernels for 11%

profile of v9, /device:TPU:472, one launch (start us, length us, event | category | flops | bytes accessed | tf_op | source)
XLA Modules:
  0.0 118.1 jit_solution(1168632540319473241)
XLA Ops:
  0.0 4.7 %collective-permute-start = (bf16[2048,256]{1,0:T(8,128)(2,1)}, bf16[2048,256]{1,0:T(8,128)(2,1)}, u32[]{:S(2)}, u32[]{:S(2)}) collective-permute-start(bf16[2048,256]{1,0:T(8,128)(2,1)} %refs_0_.1), channel_id=1, source_target_pairs={{0,1},{1,2},{2,3},{3,4},{4,5},{5,6},{6,7},{7,0},{8,9},{9,10},{10,1... | collective-permute-start | bytes 3145736 | tf_op jit(solution)/shard_map/ppermute | solution.py:151
  4.7 1.9 %collective-permute-start.1 = (bf16[2048,256]{1,0:T(8,128)(2,1)}, bf16[2048,256]{1,0:T(8,128)(2,1)}, u32[]{:S(2)}, u32[]{:S(2)}) collective-permute-start(bf16[2048,256]{1,0:T(8,128)(2,1)} %refs_0_.1), channel_id=1, source_target_pairs={{0,7},{1,0},{2,1},{3,2},{4,3},{5,4},{6,5},{7,6},{8,15},{9,8},{10,9... | collective-permute-start | bytes 3145736 | tf_op jit(solution)/shard_map/ppermute | solution.py:151
  8.2 1.4 %multiply_convert_fusion = bf16[2048,128]{1,0:T(8,128)(2,1)S(1)} fusion(bf16[2048,128]{1,0:T(8,128)(2,1)} %param.4, f32[2048]{0:T(1024)S(1)} %convert_element_type.57), kind=kLoop, calls=%fused_computation.4 | loop fusion | flops 786432 | bytes 1056768 | tf_op jit(solution)/shard_map/convert_element_type | solution.py:153
  9.6 1.0 copy.9
  10.7 5.7 %all-to-all-start = ((bf16[72,32,128]{2,0,1:T(8,128)(2,1)}), bf16[72,32,128]{2,0,1:T(8,128)(2,1)}, u32[]{:S(2)}, u32[]{:S(2)}) async-start(bf16[72,32,128]{2,0,1:T(8,128)(2,1)} %copy.9), calls=%async_computation | async-start | bytes 1179648 | tf_op jit(solution)/shard_map/all_to_all | solution.py:160
  16.4 11.0 %collective-permute-done = bf16[2048,256]{1,0:T(8,128)(2,1)} collective-permute-done((bf16[2048,256]{1,0:T(8,128)(2,1)}, bf16[2048,256]{1,0:T(8,128)(2,1)}, u32[]{:S(2)}, u32[]{:S(2)}) %collective-permute-start) | collective-permute-done | bytes 1048608 | tf_op jit(solution)/shard_map/ppermute | solution.py:151
  27.4 5.6 %collective-permute-start.2 = (bf16[2048,256]{1,0:T(8,128)(2,1)}, bf16[2048,256]{1,0:T(8,128)(2,1)S(1)}, u32[]{:S(2)}, u32[]{:S(2)}) collective-permute-start(bf16[2048,256]{1,0:T(8,128)(2,1)} %collective-permute-done), channel_id=1, source_target_pairs={{0,1},{1,2},{2,3},{3,4},{4,5},{5,6},{6,7},{7,0},{8,9},{9,10},{10,1... | collective-permute-start | bytes 3145736 | tf_op jit(solution)/shard_map/ppermute | solution.py:163
  33.0 1.9 %collective-permute-start.6 = (bf16[2048,256]{1,0:T(8,128)(2,1)}, bf16[2048,256]{1,0:T(8,128)(2,1)}, u32[]{:S(2)}, u32[]{:S(2)}) collective-permute-start(bf16[2048,256]{1,0:T(8,128)(2,1)} %collective-permute-done.1), channel_id=1, source_target_pairs={{0,7},{1,0},{2,1},{3,2},{4,3},{5,4},{6,5},{7,6},{8,15},{9,8},{10,9... | collective-permute-start | bytes 3145736 | tf_op jit(solution)/shard_map/ppermute | solution.py:163
  35.0 1.3 %constant_dynamic-update-slice_fusion.1 = bf16[2048,512]{1,0:T(8,128)(2,1)S(1)} fusion(bf16[2048,256]{1,0:T(8,128)(2,1)} %collective-permute-done), kind=kLoop, calls=%fused_computation.29 | loop fusion | bytes 2097152
  36.3 1.3 %constant_dynamic-update-slice_fusion.refs_1_ = bf16[2048,512]{1,0:T(8,128)(2,1)S(1)} fusion(bf16[2048,512]{1,0:T(8,128)(2,1)S(1)} %constant_dynamic-update-slice_fusion.1, bf16[2048,256]{1,0:T(8,128)(2,1)} %collective-permute-done.1), kind=kLoop, calls=%fused_computation.28 | loop fusion | bytes 2097152 | tf_op jit(solution)/shard_map/concatenate | solution.py:161
  38.5 1.2 fusion.3
  41.8 7.3 %all-to-all-start.1 = ((bf16[32,64,128]{2,1,0:T(8,128)(2,1)}), bf16[32,64,128]{2,1,0:T(8,128)(2,1)}, u32[]{:S(2)}, u32[]{:S(2)}) async-start(bf16[32,64,128]{2,1,0:T(8,128)(2,1)} %bitcast.19), calls=%async_computation.1 | async-start | bytes 1048576 | tf_op jit(solution)/shard_map/all_to_all | solution.py:189
  49.0 5.8 %collective-permute-done.2.refs_2_ = bf16[2048,256]{1,0:T(8,128)(2,1)S(1)} collective-permute-done((bf16[2048,256]{1,0:T(8,128)(2,1)}, bf16[2048,256]{1,0:T(8,128)(2,1)S(1)}, u32[]{:S(2)}, u32[]{:S(2)}) %collective-permute-start.2) | collective-permute-done | bytes 1048608 | tf_op jit(solution)/shard_map/ppermute | solution.py:163
  54.9 1.0 fusion.15
  55.9 5.5 %collective-permute-start.3 = (bf16[1024,256]{1,0:T(8,128)(2,1)}, bf16[1024,256]{1,0:T(8,128)(2,1)}, u32[]{:S(2)}, u32[]{:S(2)}) collective-permute-start(bf16[1024,256]{1,0:T(8,128)(2,1)} %get-tuple-element.22), channel_id=1, source_target_pairs={{0,1},{1,2},{2,3},{3,4},{4,5},{5,6},{6,7},{7,0},{8,9},{9,10},{10,1... | collective-permute-start | bytes 1572872 | tf_op jit(solution)/shard_map/ppermute | solution.py:168
  61.4 2.3 %fusion.14 = (bf16[1024,256]{1,0:T(8,128)(2,1)}, bf16[1024,256]{1,0:T(8,128)(2,1)}) fusion(bf16[2048,256]{1,0:T(8,128)(2,1)} %collective-permute-done.6.refs_3_), kind=kLoop, calls=%fused_computation.31 | loop fusion | bytes 2097152 | tf_op jit(solution)/shard_map/slice | solution.py:167
  63.7 1.9 %collective-permute-start.8 = (bf16[1024,256]{1,0:T(8,128)(2,1)}, bf16[1024,256]{1,0:T(8,128)(2,1)}, u32[]{:S(2)}, u32[]{:S(2)}) collective-permute-start(bf16[1024,256]{1,0:T(8,128)(2,1)} %get-tuple-element.19), channel_id=1, source_target_pairs={{0,7},{1,0},{2,1},{3,2},{4,3},{5,4},{6,5},{7,6},{8,15},{9,8},{10,9... | collective-permute-start | bytes 1572872 | tf_op jit(solution)/shard_map/ppermute | solution.py:168
  65.6 5.1 %collective-permute-start.5 = (bf16[1024,256]{1,0:T(8,128)(2,1)}, bf16[1024,256]{1,0:T(8,128)(2,1)}, u32[]{:S(2)}, u32[]{:S(2)}) collective-permute-start(bf16[1024,256]{1,0:T(8,128)(2,1)} %get-tuple-element.21), channel_id=1, source_target_pairs={{0,1},{1,2},{2,3},{3,4},{4,5},{5,6},{6,7},{7,0},{8,9},{9,10},{10,1... | collective-permute-start | bytes 1572872 | tf_op jit(solution)/shard_map/ppermute | solution.py:168
  70.7 1.9 %collective-permute-start.7 = (bf16[1024,256]{1,0:T(8,128)(2,1)}, bf16[1024,256]{1,0:T(8,128)(2,1)}, u32[]{:S(2)}, u32[]{:S(2)}) collective-permute-start(bf16[1024,256]{1,0:T(8,128)(2,1)} %get-tuple-element.20), channel_id=1, source_target_pairs={{0,7},{1,0},{2,1},{3,2},{4,3},{5,4},{6,5},{7,6},{8,15},{9,8},{10,9... | collective-permute-start | bytes 1572872 | tf_op jit(solution)/shard_map/ppermute | solution.py:168
  73.5 1.9 %collective-permute-start.4 = (bf16[32,64,128]{2,1,0:T(8,128)(2,1)}, bf16[32,64,128]{2,1,0:T(8,128)(2,1)}, u32[]{:S(2)}, u32[]{:S(2)}) collective-permute-start(bf16[32,64,128]{2,1,0:T(8,128)(2,1)} %all-to-all-done.1.got_ref), channel_id=1, source_target_pairs={{0,16},{16,0},{1,17},{17,1},{2,18},{18,2},{3,19},{19,3},{4,20},{20... | collective-permute-start | bytes 1572872 | tf_op jit(solution)/shard_map/ppermute | solution.py:191
  75.4 5.6 %collective-permute-start.9 = (bf16[1024,256]{1,0:T(8,128)(2,1)}, bf16[1024,256]{1,0:T(8,128)(2,1)}, u32[]{:S(2)}, u32[]{:S(2)}) collective-permute-start(bf16[1024,256]{1,0:T(8,128)(2,1)} %collective-permute-done.3.refs_4_), channel_id=1, source_target_pairs={{0,1},{1,2},{2,3},{3,4},{4,5},{5,6},{6,7},{7,0},{8,9},{9,10},{10,1... | collective-permute-start | bytes 1572872 | tf_op jit(solution)/shard_map/ppermute | solution.py:169
  81.9 1.9 %collective-permute-start.11 = (bf16[1024,256]{1,0:T(8,128)(2,1)}, bf16[1024,256]{1,0:T(8,128)(2,1)}, u32[]{:S(2)}, u32[]{:S(2)}) collective-permute-start(bf16[1024,256]{1,0:T(8,128)(2,1)} %collective-permute-done.8.refs_5_), channel_id=1, source_target_pairs={{0,7},{1,0},{2,1},{3,2},{4,3},{5,4},{6,5},{7,6},{8,15},{9,8},{10,9... | collective-permute-start | bytes 1572872 | tf_op jit(solution)/shard_map/ppermute | solution.py:169
  85.0 7.5 %collective-permute-done.7.refs_0_ = bf16[1024,256]{1,0:T(8,128)(2,1)} collective-permute-done((bf16[1024,256]{1,0:T(8,128)(2,1)}, bf16[1024,256]{1,0:T(8,128)(2,1)}, u32[]{:S(2)}, u32[]{:S(2)}) %collective-permute-start.7) | collective-permute-done | bytes 524320 | tf_op jit(solution)/shard_map/ppermute | solution.py:168
  92.5 2.0 %order_upper.1.upper_ref = bf16[8,256,256]{2,1,0:T(8,128)(2,1)S(1)} custom-call(s32[1]{0:T(128)} %bitcast.2.core_ref, bf16[32,64,128]{2,1,0:T(8,128)(2,1)} %all-to-all-done.1.got_ref, bf16[32,64,128]{2,1,0:T(8,128)(2,1)} %collective-permute-done.4.twin_ref), custom_call_target="tpu_custom_call" | custom-call | tf_op jit(solution)/shard_map/order_upper/pallas_call | solution.py:59
  94.5 4.6 %early_products.1 = (f32[1024,128]{1,0:T(8,128)S(1)}, f32[1024,128]{1,0:T(8,128)S(1)}, f32[1024,128]{1,0:T(8,128)S(1)}, f32[1024,128]{1,0:T(8,128)S(1)}) custom-call(s32[2]{0:T(128)S(1)} %pad_add_fusion.place_ref, bf16[8,256,256]{2,1,0:T(8,128)(2,1)S(1)} %order_upper.1.upper_ref, bf16[2048,128]{1,0:T(8,128)(2,1)S(1)} %pad_maximum_fusion.stored_ref, ...), custom_call_target="tpu_custom_call" | custom-call | tf_op jit(solution)/shard_map/early_products/pallas_call | solution.py:99
  99.1 1.6 %last_far.2 = bf16[1024,128]{1,0:T(8,128)(2,1)S(1)} custom-call(s32[2]{0:T(128)S(1)} %pad_add_fusion.place_ref, bf16[8,256,256]{2,1,0:T(8,128)(2,1)S(1)} %order_upper.1.upper_ref, f32[1024,128]{1,0:T(8,128)S(1)} %get-tuple-element.16.base_ref, bf16[1024,256]{1,0:T(8,128)(2,1)} %collective-permute-done.7.refs_0_, bf16[1024,256]{1,0:T(8,128)(2,1)} %collective-permute-done.9.refs_1_), custom_call_target="tpu_custom_call" | custom-call | tf_op jit(solution)/shard_map/last_far/pallas_call | solution.py:128
  100.7 5.1 %collective-permute-start.10 = (bf16[1024,128]{1,0:T(8,128)(2,1)S(1)}, bf16[1024,128]{1,0:T(8,128)(2,1)S(1)}, u32[]{:S(2)}, u32[]{:S(2)}) collective-permute-start(bf16[1024,128]{1,0:T(8,128)(2,1)S(1)} %last_far.2), channel_id=1, source_target_pairs={{0,8},{8,0},{1,9},{9,1},{2,10},{10,2},{3,11},{11,3},{4,12},{12,4},... | collective-permute-start | bytes 786440 | tf_op jit(solution)/shard_map/ppermute | solution.py:211
  105.8 1.6 %last_far.3 = bf16[1024,128]{1,0:T(8,128)(2,1)S(1)} custom-call(s32[2]{0:T(128)S(1)} %pad_add_fusion.place_ref, bf16[8,256,256]{2,1,0:T(8,128)(2,1)S(1)} %order_upper.1.upper_ref, f32[1024,128]{1,0:T(8,128)S(1)} %get-tuple-element.18.base_ref, bf16[1024,256]{1,0:T(8,128)(2,1)} %collective-permute-done.5.refs_0_, ...), custom_call_target="tpu_custom_call" | custom-call | tf_op jit(solution)/shard_map/last_far/pallas_call | solution.py:128
  107.4 2.3 %collective-permute-start.12 = (bf16[1024,128]{1,0:T(8,128)(2,1)S(1)}, bf16[1024,128]{1,0:T(8,128)(2,1)S(1)}, u32[]{:S(2)}, u32[]{:S(2)}) collective-permute-start(bf16[1024,128]{1,0:T(8,128)(2,1)S(1)} %last_far.3), channel_id=1, source_target_pairs={{0,8},{8,0},{1,9},{9,1},{2,10},{10,2},{3,11},{11,3},{4,12},{12,4},... | collective-permute-start | bytes 786440 | tf_op jit(solution)/shard_map/ppermute | solution.py:211
  109.7 1.6 %last_own.2 = f32[1024,128]{1,0:T(8,128)S(1)} custom-call(s32[2]{0:T(128)S(1)} %pad_add_fusion.place_ref, bf16[8,256,256]{2,1,0:T(8,128)(2,1)S(1)} %order_upper.1.upper_ref, f32[1024,128]{1,0:T(8,128)S(1)} %get-tuple-element.15.base_ref, bf16[1024,256]{1,0:T(8,128)(2,1)} %collective-permute-done.7.refs_0_, bf16[1024,256]{1,0:T(8,128)(2,1)} %collective-permute-done.9.refs_1_), custom_call_target="tpu_custom_call" | custom-call | tf_op jit(solution)/shard_map/last_own/pallas_call | solution.py:128
  111.4 1.6 %last_own.3 = f32[1024,128]{1,0:T(8,128)S(1)} custom-call(s32[2]{0:T(128)S(1)} %pad_add_fusion.place_ref, bf16[8,256,256]{2,1,0:T(8,128)(2,1)S(1)} %order_upper.1.upper_ref, f32[1024,128]{1,0:T(8,128)S(1)} %get-tuple-element.17.base_ref, bf16[1024,256]{1,0:T(8,128)(2,1)} %collective-permute-done.5.refs_0_, bf16[1024,256]{1,0:T(8,128)(2,1)} %collective-permute-done.11.refs_1_), custom_call_target="tpu_custom_call" | custom-call | tf_op jit(solution)/shard_map/last_own/pallas_call | solution.py:128
  113.2 4.0 %collective-permute-done.12 = bf16[1024,128]{1,0:T(8,128)(2,1)S(1)} collective-permute-done((bf16[1024,128]{1,0:T(8,128)(2,1)S(1)}, bf16[1024,128]{1,0:T(8,128)(2,1)S(1)}, u32[]{:S(2)}, u32[]{:S(2)}) %collective-permute-start.12) | collective-permute-done | bytes 262176 | tf_op jit(solution)/shard_map/ppermute | solution.py:211
  (28 shorter events, 8.5 us)
Async XLA Ops:
  0.0 27.4 %collective-permute-start = (bf16[2048,256]{1,0:T(8,128)(2,1)}, bf16[2048,256]{1,0:T(8,128)(2,1)}, u32[]{:S(2)}, u32[]{:S(2)}) collective-permute-start(bf16[2048,256]{1,0:T(8,128)(2,1)} %refs_0_.1), channel_id=1, source_target_pairs={{0,1},{1,2},{2,3},{3,4},{4,5},{5,6},{6,7},{7,0},{8,9},{9,10},{10,1... | collective-permute-start | bytes 3145736 | tf_op jit(solution)/shard_map/ppermute | solution.py:151
  4.7 28.3 %collective-permute-start.1 = (bf16[2048,256]{1,0:T(8,128)(2,1)}, bf16[2048,256]{1,0:T(8,128)(2,1)}, u32[]{:S(2)}, u32[]{:S(2)}) collective-permute-start(bf16[2048,256]{1,0:T(8,128)(2,1)} %refs_0_.1), channel_id=1, source_target_pairs={{0,7},{1,0},{2,1},{3,2},{4,3},{5,4},{6,5},{7,6},{8,15},{9,8},{10,9... | collective-permute-start | bytes 3145736 | tf_op jit(solution)/shard_map/ppermute | solution.py:151
  10.7 26.9 %all-to-all-start = ((bf16[72,32,128]{2,0,1:T(8,128)(2,1)}), bf16[72,32,128]{2,0,1:T(8,128)(2,1)}, u32[]{:S(2)}, u32[]{:S(2)}) async-start(bf16[72,32,128]{2,0,1:T(8,128)(2,1)} %copy.9), calls=%async_computation | async-start | bytes 1179648 | tf_op jit(solution)/shard_map/all_to_all | solution.py:160
  27.4 27.4 %collective-permute-start.2 = (bf16[2048,256]{1,0:T(8,128)(2,1)}, bf16[2048,256]{1,0:T(8,128)(2,1)S(1)}, u32[]{:S(2)}, u32[]{:S(2)}) collective-permute-start(bf16[2048,256]{1,0:T(8,128)(2,1)} %collective-permute-done), channel_id=1, source_target_pairs={{0,1},{1,2},{2,3},{3,4},{4,5},{5,6},{6,7},{7,0},{8,9},{9,10},{10,1... | collective-permute-start | bytes 3145736 | tf_op jit(solution)/shard_map/ppermute | solution.py:163
  33.0 28.4 %collective-permute-start.6 = (bf16[2048,256]{1,0:T(8,128)(2,1)}, bf16[2048,256]{1,0:T(8,128)(2,1)}, u32[]{:S(2)}, u32[]{:S(2)}) collective-permute-start(bf16[2048,256]{1,0:T(8,128)(2,1)} %collective-permute-done.1), channel_id=1, source_target_pairs={{0,7},{1,0},{2,1},{3,2},{4,3},{5,4},{6,5},{7,6},{8,15},{9,8},{10,9... | collective-permute-start | bytes 3145736 | tf_op jit(solution)/shard_map/ppermute | solution.py:163
  41.8 30.9 %all-to-all-start.1 = ((bf16[32,64,128]{2,1,0:T(8,128)(2,1)}), bf16[32,64,128]{2,1,0:T(8,128)(2,1)}, u32[]{:S(2)}, u32[]{:S(2)}) async-start(bf16[32,64,128]{2,1,0:T(8,128)(2,1)} %bitcast.19), calls=%async_computation.1 | async-start | bytes 1048576 | tf_op jit(solution)/shard_map/all_to_all | solution.py:189
  55.9 17.6 %collective-permute-start.3 = (bf16[1024,256]{1,0:T(8,128)(2,1)}, bf16[1024,256]{1,0:T(8,128)(2,1)}, u32[]{:S(2)}, u32[]{:S(2)}) collective-permute-start(bf16[1024,256]{1,0:T(8,128)(2,1)} %get-tuple-element.22), channel_id=1, source_target_pairs={{0,1},{1,2},{2,3},{3,4},{4,5},{5,6},{6,7},{7,0},{8,9},{9,10},{10,1... | collective-permute-start | bytes 1572872 | tf_op jit(solution)/shard_map/ppermute | solution.py:168
  63.7 18.3 %collective-permute-start.8 = (bf16[1024,256]{1,0:T(8,128)(2,1)}, bf16[1024,256]{1,0:T(8,128)(2,1)}, u32[]{:S(2)}, u32[]{:S(2)}) collective-permute-start(bf16[1024,256]{1,0:T(8,128)(2,1)} %get-tuple-element.19), channel_id=1, source_target_pairs={{0,7},{1,0},{2,1},{3,2},{4,3},{5,4},{6,5},{7,6},{8,15},{9,8},{10,9... | collective-permute-start | bytes 1572872 | tf_op jit(solution)/shard_map/ppermute | solution.py:168
  65.6 19.4 %collective-permute-start.5 = (bf16[1024,256]{1,0:T(8,128)(2,1)}, bf16[1024,256]{1,0:T(8,128)(2,1)}, u32[]{:S(2)}, u32[]{:S(2)}) collective-permute-start(bf16[1024,256]{1,0:T(8,128)(2,1)} %get-tuple-element.21), channel_id=1, source_target_pairs={{0,1},{1,2},{2,3},{3,4},{4,5},{5,6},{6,7},{7,0},{8,9},{9,10},{10,1... | collective-permute-start | bytes 1572872 | tf_op jit(solution)/shard_map/ppermute | solution.py:168
  70.7 21.8 %collective-permute-start.7 = (bf16[1024,256]{1,0:T(8,128)(2,1)}, bf16[1024,256]{1,0:T(8,128)(2,1)}, u32[]{:S(2)}, u32[]{:S(2)}) collective-permute-start(bf16[1024,256]{1,0:T(8,128)(2,1)} %get-tuple-element.20), channel_id=1, source_target_pairs={{0,7},{1,0},{2,1},{3,2},{4,3},{5,4},{6,5},{7,6},{8,15},{9,8},{10,9... | collective-permute-start | bytes 1572872 | tf_op jit(solution)/shard_map/ppermute | solution.py:168
  73.5 19.0 %collective-permute-start.4 = (bf16[32,64,128]{2,1,0:T(8,128)(2,1)}, bf16[32,64,128]{2,1,0:T(8,128)(2,1)}, u32[]{:S(2)}, u32[]{:S(2)}) collective-permute-start(bf16[32,64,128]{2,1,0:T(8,128)(2,1)} %all-to-all-done.1.got_ref), channel_id=1, source_target_pairs={{0,16},{16,0},{1,17},{17,1},{2,18},{18,2},{3,19},{19,3},{4,20},{20... | collective-permute-start | bytes 1572872 | tf_op jit(solution)/shard_map/ppermute | solution.py:191
  75.4 23.7 %collective-permute-start.9 = (bf16[1024,256]{1,0:T(8,128)(2,1)}, bf16[1024,256]{1,0:T(8,128)(2,1)}, u32[]{:S(2)}, u32[]{:S(2)}) collective-permute-start(bf16[1024,256]{1,0:T(8,128)(2,1)} %collective-permute-done.3.refs_4_), channel_id=1, source_target_pairs={{0,1},{1,2},{2,3},{3,4},{4,5},{5,6},{6,7},{7,0},{8,9},{9,10},{10,1... | collective-permute-start | bytes 1572872 | tf_op jit(solution)/shard_map/ppermute | solution.py:169
  81.9 23.8 %collective-permute-start.11 = (bf16[1024,256]{1,0:T(8,128)(2,1)}, bf16[1024,256]{1,0:T(8,128)(2,1)}, u32[]{:S(2)}, u32[]{:S(2)}) collective-permute-start(bf16[1024,256]{1,0:T(8,128)(2,1)} %collective-permute-done.8.refs_5_), channel_id=1, source_target_pairs={{0,7},{1,0},{2,1},{3,2},{4,3},{5,4},{6,5},{7,6},{8,15},{9,8},{10,9... | collective-permute-start | bytes 1572872 | tf_op jit(solution)/shard_map/ppermute | solution.py:169
  83.9 10.5 %copy-start = (bf16[2048,256]{1,0:T(8,128)(2,1)S(1)}, bf16[2048,256]{1,0:T(8,128)(2,1)}, u32[]{:S(2)}) copy-start(bf16[2048,256]{1,0:T(8,128)(2,1)} %refs_0_.1) | copy-start | bytes 3145732
  100.7 12.4 %collective-permute-start.10 = (bf16[1024,128]{1,0:T(8,128)(2,1)S(1)}, bf16[1024,128]{1,0:T(8,128)(2,1)S(1)}, u32[]{:S(2)}, u32[]{:S(2)}) collective-permute-start(bf16[1024,128]{1,0:T(8,128)(2,1)S(1)} %last_far.2), channel_id=1, source_target_pairs={{0,8},{8,0},{1,9},{9,1},{2,10},{10,2},{3,11},{11,3},{4,12},{12,4},... | collective-permute-start | bytes 786440 | tf_op jit(solution)/shard_map/ppermute | solution.py:211
  107.4 9.8 %collective-permute-start.12 = (bf16[1024,128]{1,0:T(8,128)(2,1)S(1)}, bf16[1024,128]{1,0:T(8,128)(2,1)S(1)}, u32[]{:S(2)}, u32[]{:S(2)}) collective-permute-start(bf16[1024,128]{1,0:T(8,128)(2,1)S(1)} %last_far.3), channel_id=1, source_target_pairs={{0,8},{8,0},{1,9},{9,1},{2,10},{10,2},{3,11},{11,3},{4,12},{12,4},... | collective-permute-start | bytes 786440 | tf_op jit(solution)/shard_map/ppermute | solution.py:211

commit v10 on v9

--- a/solution.py
+++ b/solution.py
@@ -10,6 +10,7 @@
 CORES = 2
 PAD = 8
 TILE_M = 256
+SPLIT = 1024
 ROW = ("chip", "core")
 
 inv_root = 0.7071067811865476
@@ -36,57 +37,44 @@
     return pl.BlockSpec(memory_space=VM)
 
 
-def order_upper(core, got, twin, y_count):
-    pairs, top, width = got.shape
-    chips = pairs // X_HI
-    low = top // y_count
-    depth = CORES * chips * low
-
-    def body(core_ref, got_ref, twin_ref, out_ref):
-        want = lax.broadcasted_iota(jnp.int32, (depth, depth), 0)
-        have = lax.broadcasted_iota(jnp.int32, (depth, depth), 1)
-        side = (want % CORES + core_ref[0]) % CORES
-        source = side * (chips * low) + want // CORES % chips * low + want // (CORES * chips)
-        move = jnp.where(source == have, 1.0, 0.0).astype(got.dtype)
-        for y in range(y_count):
-            for x in range(X_HI):
-                pick = [
-                    ref[chip * X_HI + x, y * low : (y + 1) * low] for ref in (got_ref, twin_ref) for chip in range(chips)
-                ]
-                rows = jnp.dot(move, jnp.concatenate(pick, axis=0), preferred_element_type=jnp.float32)
-                out_ref[y, :, x * width : (x + 1) * width] = rows.astype(got.dtype)
-
-    return pl.pallas_call(
-        body,
-        in_specs=[pl.BlockSpec(memory_space=pltpu.SMEM), whole(), whole()],
-        out_specs=whole(),
-        out_shape=jax.ShapeDtypeStruct((y_count, depth, X_HI * width), got.dtype),
-        compiler_params=grant(8),
-        name="order_upper",
-    )(core, got, twin)
-
-
-def early_products(place, upper, stored, offsets, blocks, own_offsets, own_blocks):
+def order_upper(core, got_ref, twin_ref, out_ref):
+    pairs, top, width = got_ref.shape
+    y_count, depth = out_ref.shape[:2]
+    chips, low = pairs // X_HI, top // y_count
+    want = lax.broadcasted_iota(jnp.int32, (depth, depth), 0)
+    have = lax.broadcasted_iota(jnp.int32, (depth, depth), 1)
+    side = (want % CORES + core) % CORES
+    source = side * (chips * low) + want // CORES % chips * low + want // (CORES * chips)
+    move = jnp.where(source == have, 1.0, 0.0).astype(out_ref.dtype)
+    for y in range(y_count):
+        for x in range(X_HI):
+            pick = [ref[chip * X_HI + x, y * low : (y + 1) * low] for ref in (got_ref, twin_ref) for chip in range(chips)]
+            rows = jnp.dot(move, jnp.concatenate(pick, axis=0), preferred_element_type=jnp.float32)
+            out_ref[y, :, x * width : (x + 1) * width] = rows.astype(out_ref.dtype)
+
+
+def early_products(place, got, twin, stored, bounds, offsets, blocks, own_offsets, own_blocks):
     rows, width = stored.shape
-    y_count, depth, both = upper.shape
+    y_count = lax.axis_size("y")
+    depth, both = blocks[0].shape[1], X_HI * width
     parts = len(own_blocks)
-    share = rows // parts
     common = len(offsets) * depth
 
-    def body(place_ref, upper_ref, stored_ref, *refs):
-        block_refs, own_refs, out_refs = refs[: len(blocks)], refs[len(blocks) : -1 - 2 * parts], refs[-1 - 2 * parts : -1]
-        turned = refs[-1]
+    def body(place_ref, got_ref, twin_ref, stored_ref, *refs):
+        block_refs, own_refs, out_refs = refs[: len(blocks)], refs[len(blocks) : -2 - 2 * parts], refs[-2 - 2 * parts : -2]
+        upper_ref, turned = refs[-2:]
+        order_upper(place_ref[2], got_ref, twin_ref, upper_ref)
         for n, offset in enumerate(offsets):
             turned[n * depth : (n + 1) * depth] = upper_ref[(place_ref[1] + offset + y_count) % y_count]
         at_left = place_ref[0] == 0
 
-        for part in range(parts):
+        for part, (start, stop) in enumerate(bounds):
             turned[common:] = upper_ref[(place_ref[1] + own_offsets[part] + y_count) % y_count]
             far_ref, rest_ref = out_refs[2 * part : 2 * part + 2]
 
             def one(i, carry):
                 local = pl.ds(pl.multiple_of(i * TILE_M, TILE_M), TILE_M)
-                full = pl.ds(pl.multiple_of(part * share + i * TILE_M, TILE_M), TILE_M)
+                full = pl.ds(pl.multiple_of(start + i * TILE_M, TILE_M), TILE_M)
                 tiles = [ref[full] for ref in block_refs] + [own_refs[part][local]]
                 total = jnp.dot(jnp.concatenate(tiles, axis=1), turned[...], preferred_element_type=jnp.float32)
                 left, right = total[:, :width], total[:, width:]
@@ -94,17 +82,18 @@
                 rest_ref[local] = stored_ref[full].astype(jnp.float32) - jnp.where(at_left, left, right)
                 return carry
 
-            lax.fori_loop(0, share // TILE_M, one, 0)
+            lax.fori_loop(0, (stop - start) // TILE_M, one, 0)
 
     return pl.pallas_call(
         body,
-        in_specs=[pl.BlockSpec(memory_space=pltpu.SMEM)] + [whole()] * (2 + len(blocks) + parts),
-        out_specs=[whole()] * (2 * parts),
-        out_shape=[jax.ShapeDtypeStruct((share, width), jnp.float32)] * (2 * parts),
-        scratch_shapes=[VM((common + depth, both), upper.dtype)],
+        in_specs=[pl.BlockSpec(memory_space=pltpu.SMEM)] + [whole()] * (3 + len(blocks) + parts),
+        out_specs=[whole()] * (2 * parts + 1),
+        out_shape=[jax.ShapeDtypeStruct((b - a, width), jnp.float32) for a, b in bounds for _ in range(2)]
+        + [jax.ShapeDtypeStruct((y_count, depth, both), stored.dtype)],
+        scratch_shapes=[VM((common + depth, both), stored.dtype)],
         compiler_params=grant(16),
         name="early_products",
-    )(place, upper, stored, *blocks, *own_blocks)
+    )(place, got, twin, stored, *blocks, *own_blocks)
 
 
 def last_product(place, upper, base, offsets, blocks, partner, out_dtype, sign):
@@ -161,10 +150,11 @@
     joined = jnp.concatenate(near, axis=1)
     packed = after(packed, joined)
     far_near = tuple(lax.ppermute(block, "y", route[sign]) for block, sign in zip(near, route))
+    bounds = ((0, SPLIT), (SPLIT, row_count))
     first_keys, second_keys = ((0, -1), (1, 1)), ((1, -1), (0, 1))
     third = {}
-    for part, sign in first_keys + second_keys:
-        block = far_near[0 if sign < 0 else 1][part * half : (part + 1) * half]
+    for part, sign in first_keys:
+        block = far_near[0 if sign < 0 else 1][slice(*bounds[part])]
         third[part, sign] = lax.ppermute(block, "y", route[sign])
     last = [lax.ppermute(third[part, sign], "y", route[sign]) for part, sign in first_keys]
     packed = packed.reshape(groups, share + PAD, col_width)
@@ -187,22 +177,24 @@
         chips * X_HI, top_count, col_width
     )
     got = lax.all_to_all(send, ("chip", "x_hi"), split_axis=0, concat_axis=0)
-    got = after(got, third[0, -1])
+    for part, sign in second_keys:
+        block = after(far_near[0 if sign < 0 else 1], got)[slice(*bounds[part])]
+        third[part, sign] = lax.ppermute(block, "y", route[sign])
     twin = lax.ppermute(got, "core", [(0, 1), (1, 0)])
-    twin = after(twin, *(third[key] for key in second_keys))
-    core = lax.axis_index("core").astype(jnp.int32).reshape(1)
-    upper = order_upper(core, got, twin, y_count)
-    place = jnp.stack([lax.axis_index("x_hi"), lax.axis_index("y")]).astype(jnp.int32)
+    place = jnp.stack([lax.axis_index(name) for name in ("x_hi", "y", "core")]).astype(jnp.int32)
     swap = [(i, X_HI - 1 - i) for i in range(X_HI)]
-    sums = early_products(
+    *sums, upper = early_products(
         place,
-        upper,
+        got,
+        twin,
         stored,
+        bounds,
         [0, -1, 1, -2, 2],
         [panel_lower, joined, *far_near],
         [sign * (y_count // 2 - 1) for _, sign in first_keys],
         [third[key] for key in first_keys],
     )
+    upper = after(upper, *(third[key] for key in second_keys))
     out = []
     for part, sign in first_keys:
         offsets = [-sign * (y_count // 2 - 1), y_count // 2]

time: 119 us -> 127 us (1.067)
  the two profiles are of different devices: /device:TPU:472 before, /device:TPU:24 now
where the time goes in v10:
time: 127 us; the launch traced here: 126 us
  starting transfers between devices  65.9 us (52%)
  waiting for transfers between devices  26.4 us (21%)
  local copies, waits for them, and re-layouts  12.1 us (10%)
  Pallas kernels  11.9 us (9%)
  other arithmetic  9.46 us (7%)
    ppermute x4, starting transfers between devices, per_device(): third[part, sign] = lax.ppermute(block, 'y', route[sign])  13.9 us
    all_to_all x1, starting transfers between devices, per_device(): lax.all_to_all(packed, ROW, split_axis=1, concat_axis=0, tiled=True)  11.8 us
    all_to_all x1, starting transfers between devices, per_device(): got = lax.all_to_all(send, ('chip', 'x_hi'), split_axis=0, concat_axis=0)  9.06 us
    ppermute x2, starting transfers between devices, per_device(): came = lax.ppermute(far, 'x_hi', swap)  8.14 us
    ppermute x2, starting transfers between devices, per_device(): lax.ppermute(block, 'y', route[sign])  7.51 us
    ppermute x2, starting transfers between devices, per_device(): lax.ppermute(third[part, sign], 'y', route[sign])  7.05 us
    all_to_all x1, waiting for transfers between devices, per_device(): got = lax.all_to_all(send, ('chip', 'x_hi'), split_axis=0, concat_axis=0)  6.89 us
    ppermute x2, starting transfers between devices, per_device(): lax.ppermute(panel_lower, 'y', route[sign])  6.61 us
  transfers between devices with their start and end apart: 15, of which 7 were waited for; matrix products, arithmetic and copies ran while one was open for 15% of the time, Pallas kernels for 9%

profile of v10, /device:TPU:24, one launch (start us, length us, event | category | flops | bytes accessed | tf_op | source)
XLA Modules:
  0.0 126.1 jit_solution(14733079430960945579)
XLA Ops:
  0.0 4.7 %collective-permute-start = (bf16[2048,256]{1,0:T(8,128)(2,1)}, bf16[2048,256]{1,0:T(8,128)(2,1)}, u32[]{:S(2)}, u32[]{:S(2)}) collective-permute-start(bf16[2048,256]{1,0:T(8,128)(2,1)} %refs_0_.1), channel_id=1, source_target_pairs={{0,1},{1,2},{2,3},{3,4},{4,5},{5,6},{6,7},{7,0},{8,9},{9,10},{10,1... | collective-permute-start | bytes 3145736 | tf_op jit(solution)/shard_map/ppermute | solution.py:140
  4.7 1.9 %collective-permute-start.1 = (bf16[2048,256]{1,0:T(8,128)(2,1)}, bf16[2048,256]{1,0:T(8,128)(2,1)}, u32[]{:S(2)}, u32[]{:S(2)}) collective-permute-start(bf16[2048,256]{1,0:T(8,128)(2,1)} %refs_0_.1), channel_id=1, source_target_pairs={{0,7},{1,0},{2,1},{3,2},{4,3},{5,4},{6,5},{7,6},{8,15},{9,8},{10,9... | collective-permute-start | bytes 3145736 | tf_op jit(solution)/shard_map/ppermute | solution.py:140
  8.2 1.4 %multiply_convert_fusion = bf16[2048,128]{1,0:T(8,128)(2,1)S(1)} fusion(bf16[2048,128]{1,0:T(8,128)(2,1)} %param.4, f32[2048]{0:T(1024)S(1)} %convert_element_type.57), kind=kLoop, calls=%fused_computation.4 | loop fusion | flops 786432 | bytes 1056768 | tf_op jit(solution)/shard_map/convert_element_type | solution.py:142
  10.6 11.8 %all-to-all-start = ((bf16[72,32,128]{2,0,1:T(8,128)(2,1)}), bf16[72,32,128]{2,0,1:T(8,128)(2,1)}, u32[]{:S(2)}, u32[]{:S(2)}) async-start(bf16[72,32,128]{2,0,1:T(8,128)(2,1)} %copy.9), calls=%async_computation | async-start | bytes 1179648 | tf_op jit(solution)/shard_map/all_to_all | solution.py:149
  22.4 5.0 %collective-permute-done = bf16[2048,256]{1,0:T(8,128)(2,1)} collective-permute-done((bf16[2048,256]{1,0:T(8,128)(2,1)}, bf16[2048,256]{1,0:T(8,128)(2,1)}, u32[]{:S(2)}, u32[]{:S(2)}) %collective-permute-start) | collective-permute-done | bytes 1048608 | tf_op jit(solution)/shard_map/ppermute | solution.py:140
  27.4 5.6 %collective-permute-start.3 = (bf16[2048,256]{1,0:T(8,128)(2,1)}, bf16[2048,256]{1,0:T(8,128)(2,1)S(1)}, u32[]{:S(2)}, u32[]{:S(2)}) collective-permute-start(bf16[2048,256]{1,0:T(8,128)(2,1)} %collective-permute-done), channel_id=1, source_target_pairs={{0,1},{1,2},{2,3},{3,4},{4,5},{5,6},{6,7},{7,0},{8,9},{9,10},{10,1... | collective-permute-start | bytes 3145736 | tf_op jit(solution)/shard_map/ppermute | solution.py:152
  33.0 1.9 %collective-permute-start.4 = (bf16[2048,256]{1,0:T(8,128)(2,1)}, bf16[2048,256]{1,0:T(8,128)(2,1)}, u32[]{:S(2)}, u32[]{:S(2)}) collective-permute-start(bf16[2048,256]{1,0:T(8,128)(2,1)} %collective-permute-done.1), channel_id=1, source_target_pairs={{0,7},{1,0},{2,1},{3,2},{4,3},{5,4},{6,5},{7,6},{8,15},{9,8},{10,9... | collective-permute-start | bytes 3145736 | tf_op jit(solution)/shard_map/ppermute | solution.py:152
  34.9 1.3 %constant_dynamic-update-slice_fusion.1 = bf16[2048,512]{1,0:T(8,128)(2,1)S(1)} fusion(bf16[2048,256]{1,0:T(8,128)(2,1)} %collective-permute-done), kind=kLoop, calls=%fused_computation.29 | loop fusion | bytes 2097152
  36.3 1.3 %constant_dynamic-update-slice_fusion.refs_1_ = bf16[2048,512]{1,0:T(8,128)(2,1)S(1)} fusion(bf16[2048,512]{1,0:T(8,128)(2,1)S(1)} %constant_dynamic-update-slice_fusion.1, bf16[2048,256]{1,0:T(8,128)(2,1)} %collective-permute-done.1), kind=kLoop, calls=%fused_computation.28 | loop fusion | bytes 2097152 | tf_op jit(solution)/shard_map/concatenate | solution.py:150
  37.6 4.3 %all-to-all-done = bf16[72,32,128]{2,0,1:T(8,128)(2,1)} async-done(((bf16[72,32,128]{2,0,1:T(8,128)(2,1)}), bf16[72,32,128]{2,0,1:T(8,128)(2,1)}, u32[]{:S(2)}, u32[]{:S(2)}) %all-to-all-start) | async-done | bytes 589856 | tf_op jit(solution)/shard_map/all_to_all | solution.py:149
  41.8 2.1 %fusion.3 = (f32[16,64,128]{2,1,0:T(8,128)}, f32[16,64,128]{2,1,0:T(8,128)}) fusion(bf16[32,72,128]{2,1,0:T(8,128)(2,1)} %bitcast.9), kind=kLoop, calls=%fused_computation.8 | loop fusion | flops 786432 | bytes 1572864 | tf_op jit(solution)/shard_map/mul | solution.py:22
  44.9 1.5 %fusion.1 = bf16[2048,128]{1,0:T(8,128)(2,1)S(1)} fusion(f32[1024,128]{1,0:T(8,128)} %bitcast.18, f32[1024,128]{1,0:T(8,128)} %bitcast.17, f32[2048]{0:T(1024)S(1)} %reshape.37), kind=kLoop, calls=%fused_computation.3 | loop fusion | flops 786432 | bytes 1581056 | tf_op jit(solution)/shard_map/convert_element_type | solution.py:165
  48.2 9.1 %all-to-all-start.1 = ((bf16[32,64,128]{2,1,0:T(8,128)(2,1)}), bf16[32,64,128]{2,1,0:T(8,128)(2,1)}, u32[]{:S(2)}, u32[]{:S(2)}) async-start(bf16[32,64,128]{2,1,0:T(8,128)(2,1)} %bitcast.19), calls=%async_computation.1 | async-start | bytes 1048576 | tf_op jit(solution)/shard_map/all_to_all | solution.py:179
  58.1 5.1 %collective-permute-start.5 = (bf16[1024,256]{1,0:T(8,128)(2,1)}, bf16[1024,256]{1,0:T(8,128)(2,1)}, u32[]{:S(2)}, u32[]{:S(2)}) collective-permute-start(bf16[1024,256]{1,0:T(8,128)(2,1)} %slice.62), channel_id=1, source_target_pairs={{0,1},{1,2},{2,3},{3,4},{4,5},{5,6},{6,7},{7,0},{8,9},{9,10},{10,1... | collective-permute-start | bytes 1572872 | tf_op jit(solution)/shard_map/ppermute | solution.py:158
  63.3 1.9 %slice.63 = bf16[1024,256]{1,0:T(8,128)(2,1)} slice(bf16[2048,256]{1,0:T(8,128)(2,1)} %collective-permute-done.4.refs_3_), slice={[1024:2048], [0:256]} | slice | bytes 1048576 | tf_op jit(solution)/shard_map/slice | solution.py:157
  65.2 1.9 %collective-permute-start.6 = (bf16[1024,256]{1,0:T(8,128)(2,1)}, bf16[1024,256]{1,0:T(8,128)(2,1)}, u32[]{:S(2)}, u32[]{:S(2)}) collective-permute-start(bf16[1024,256]{1,0:T(8,128)(2,1)} %slice.63), channel_id=1, source_target_pairs={{0,7},{1,0},{2,1},{3,2},{4,3},{5,4},{6,5},{7,6},{8,15},{9,8},{10,9... | collective-permute-start | bytes 1572872 | tf_op jit(solution)/shard_map/ppermute | solution.py:158
  67.1 6.9 %all-to-all-done.1.got_ref = bf16[32,64,128]{2,1,0:T(8,128)(2,1)} async-done(((bf16[32,64,128]{2,1,0:T(8,128)(2,1)}), bf16[32,64,128]{2,1,0:T(8,128)(2,1)}, u32[]{:S(2)}, u32[]{:S(2)}) %all-to-all-start.1) | async-done | bytes 524320 | tf_op jit(solution)/shard_map/all_to_all | solution.py:179
  74.8 4.9 %collective-permute-start.7 = (bf16[1024,256]{1,0:T(8,128)(2,1)}, bf16[1024,256]{1,0:T(8,128)(2,1)}, u32[]{:S(2)}, u32[]{:S(2)}) collective-permute-start(bf16[1024,256]{1,0:T(8,128)(2,1)} %slice.52), channel_id=1, source_target_pairs={{0,1},{1,2},{2,3},{3,4},{4,5},{5,6},{6,7},{7,0},{8,9},{9,10},{10,1... | collective-permute-start | bytes 1572872 | tf_op jit(solution)/shard_map/ppermute | solution.py:182
  79.8 1.9 %collective-permute-start.2 = (bf16[32,64,128]{2,1,0:T(8,128)(2,1)}, bf16[32,64,128]{2,1,0:T(8,128)(2,1)}, u32[]{:S(2)}, u32[]{:S(2)}) collective-permute-start(bf16[32,64,128]{2,1,0:T(8,128)(2,1)} %all-to-all-done.1.got_ref), channel_id=1, source_target_pairs={{0,16},{16,0},{1,17},{17,1},{2,18},{18,2},{3,19},{19,3},{4,20},{20... | collective-permute-start | bytes 1572872 | tf_op jit(solution)/shard_map/ppermute | solution.py:183
  81.7 1.9 %slice.53 = bf16[1024,256]{1,0:T(8,128)(2,1)} slice(bf16[2048,256]{1,0:T(8,128)(2,1)} %collective-permute-done.4.refs_3_), slice={[0:1024], [0:256]} | slice | bytes 1048576 | tf_op jit(solution)/shard_map/slice | solution.py:181
  83.6 1.9 %collective-permute-start.8 = (bf16[1024,256]{1,0:T(8,128)(2,1)}, bf16[1024,256]{1,0:T(8,128)(2,1)}, u32[]{:S(2)}, u32[]{:S(2)}) collective-permute-start(bf16[1024,256]{1,0:T(8,128)(2,1)} %slice.53), channel_id=1, source_target_pairs={{0,7},{1,0},{2,1},{3,2},{4,3},{5,4},{6,5},{7,6},{8,15},{9,8},{10,9... | collective-permute-start | bytes 1572872 | tf_op jit(solution)/shard_map/ppermute | solution.py:182
  85.5 5.1 %collective-permute-start.9 = (bf16[1024,256]{1,0:T(8,128)(2,1)}, bf16[1024,256]{1,0:T(8,128)(2,1)}, u32[]{:S(2)}, u32[]{:S(2)}) collective-permute-start(bf16[1024,256]{1,0:T(8,128)(2,1)} %collective-permute-done.5.refs_4_), channel_id=1, source_target_pairs={{0,1},{1,2},{2,3},{3,4},{4,5},{5,6},{6,7},{7,0},{8,9},{9,10},{10,1... | collective-permute-start | bytes 1572872 | tf_op jit(solution)/shard_map/ppermute | solution.py:159
  90.7 1.9 %collective-permute-start.11 = (bf16[1024,256]{1,0:T(8,128)(2,1)}, bf16[1024,256]{1,0:T(8,128)(2,1)S(1)}, u32[]{:S(2)}, u32[]{:S(2)}) collective-permute-start(bf16[1024,256]{1,0:T(8,128)(2,1)} %collective-permute-done.6.refs_5_), channel_id=1, source_target_pairs={{0,7},{1,0},{2,1},{3,2},{4,3},{5,4},{6,5},{7,6},{8,15},{9,8},{10,9... | collective-permute-start | bytes 1572872 | tf_op jit(solution)/shard_map/ppermute | solution.py:159
  94.8 5.7 %early_products.1 = (f32[1024,128]{1,0:T(8,128)S(1)}, f32[1024,128]{1,0:T(8,128)S(1)}, f32[1024,128]{1,0:T(8,128)S(1)}, f32[1024,128]{1,0:T(8,128)S(1)}, bf16[8,256,256]{2,1,0:T(8,128)(2,1)S(1)}) custom-call(s32[3]{0:T(128)S(1)} %pad_add_fusion.place_ref, bf16[32,64,128]{2,1,0:T(8,128)(2,1)} %all-to-all-done.1.got_ref, ...), custom_call_target="tpu_custom_call" | custom-call | tf_op jit(solution)/shard_map/early_products/pallas_call | solution.py:87
  102.5 1.6 %last_far.2 = bf16[1024,128]{1,0:T(8,128)(2,1)S(1)} custom-call(s32[3]{0:T(128)S(1)} %pad_add_fusion.place_ref, bf16[8,256,256]{2,1,0:T(8,128)(2,1)S(1)} %get-tuple-element.18.upper_ref, f32[1024,128]{1,0:T(8,128)S(1)} %get-tuple-element.20.base_ref, bf16[1024,256]{1,0:T(8,128)(2,1)} %collective-permute-done.8.refs_0_, ...), custom_call_target="tpu_custom_call" | custom-call | tf_op jit(solution)/shard_map/last_far/pallas_call | solution.py:117
  104.2 4.1 %collective-permute-start.10 = (bf16[1024,128]{1,0:T(8,128)(2,1)S(1)}, bf16[1024,128]{1,0:T(8,128)(2,1)S(1)}, u32[]{:S(2)}, u32[]{:S(2)}) collective-permute-start(bf16[1024,128]{1,0:T(8,128)(2,1)S(1)} %last_far.2), channel_id=1, source_target_pairs={{0,8},{8,0},{1,9},{9,1},{2,10},{10,2},{3,11},{11,3},{4,12},{12,4},... | collective-permute-start | bytes 786440 | tf_op jit(solution)/shard_map/ppermute | solution.py:203
  108.2 4.2 %collective-permute-done.11.refs_1_ = bf16[1024,256]{1,0:T(8,128)(2,1)S(1)} collective-permute-done((bf16[1024,256]{1,0:T(8,128)(2,1)}, bf16[1024,256]{1,0:T(8,128)(2,1)S(1)}, u32[]{:S(2)}, u32[]{:S(2)}) %collective-permute-start.11) | collective-permute-done | bytes 524320 | tf_op jit(solution)/shard_map/ppermute | solution.py:159
  112.4 1.5 %last_far.3 = bf16[1024,128]{1,0:T(8,128)(2,1)S(1)} custom-call(s32[3]{0:T(128)S(1)} %pad_add_fusion.place_ref, bf16[8,256,256]{2,1,0:T(8,128)(2,1)S(1)} %get-tuple-element.18.upper_ref, f32[1024,128]{1,0:T(8,128)S(1)} %get-tuple-element.22.base_ref, bf16[1024,256]{1,0:T(8,128)(2,1)} %collective-permute-done.7.refs_0_, ...), custom_call_target="tpu_custom_call" | custom-call | tf_op jit(solution)/shard_map/last_far/pallas_call | solution.py:117
  113.9 4.1 %collective-permute-start.12 = (bf16[1024,128]{1,0:T(8,128)(2,1)S(1)}, bf16[1024,128]{1,0:T(8,128)(2,1)S(1)}, u32[]{:S(2)}, u32[]{:S(2)}) collective-permute-start(bf16[1024,128]{1,0:T(8,128)(2,1)S(1)} %last_far.3), channel_id=1, source_target_pairs={{0,8},{8,0},{1,9},{9,1},{2,10},{10,2},{3,11},{11,3},{4,12},{12,4},... | collective-permute-start | bytes 786440 | tf_op jit(solution)/shard_map/ppermute | solution.py:203
  118.0 1.6 %last_own.2 = f32[1024,128]{1,0:T(8,128)S(1)} custom-call(s32[3]{0:T(128)S(1)} %pad_add_fusion.place_ref, bf16[8,256,256]{2,1,0:T(8,128)(2,1)S(1)} %get-tuple-element.18.upper_ref, f32[1024,128]{1,0:T(8,128)S(1)} %get-tuple-element.19.base_ref, bf16[1024,256]{1,0:T(8,128)(2,1)} %collective-permute-done.8.refs_0_, ...), custom_call_target="tpu_custom_call" | custom-call | tf_op jit(solution)/shard_map/last_own/pallas_call | solution.py:117
  119.7 1.5 %last_own.3 = f32[1024,128]{1,0:T(8,128)S(1)} custom-call(s32[3]{0:T(128)S(1)} %pad_add_fusion.place_ref, bf16[8,256,256]{2,1,0:T(8,128)(2,1)S(1)} %get-tuple-element.18.upper_ref, f32[1024,128]{1,0:T(8,128)S(1)} %get-tuple-element.21.base_ref, bf16[1024,256]{1,0:T(8,128)(2,1)} %collective-permute-done.7.refs_0_, ...), custom_call_target="tpu_custom_call" | custom-call | tf_op jit(solution)/shard_map/last_own/pallas_call | solution.py:117
  121.2 4.0 %collective-permute-done.12 = bf16[1024,128]{1,0:T(8,128)(2,1)S(1)} collective-permute-done((bf16[1024,128]{1,0:T(8,128)(2,1)S(1)}, bf16[1024,128]{1,0:T(8,128)(2,1)S(1)}, u32[]{:S(2)}, u32[]{:S(2)}) %collective-permute-start.12) | collective-permute-done | bytes 262176 | tf_op jit(solution)/shard_map/ppermute | solution.py:203
  (29 shorter events, 12.1 us)
Async XLA Ops:
  0.0 27.4 %collective-permute-start = (bf16[2048,256]{1,0:T(8,128)(2,1)}, bf16[2048,256]{1,0:T(8,128)(2,1)}, u32[]{:S(2)}, u32[]{:S(2)}) collective-permute-start(bf16[2048,256]{1,0:T(8,128)(2,1)} %refs_0_.1), channel_id=1, source_target_pairs={{0,1},{1,2},{2,3},{3,4},{4,5},{5,6},{6,7},{7,0},{8,9},{9,10},{10,1... | collective-permute-start | bytes 3145736 | tf_op jit(solution)/shard_map/ppermute | solution.py:140
  4.7 28.3 %collective-permute-start.1 = (bf16[2048,256]{1,0:T(8,128)(2,1)}, bf16[2048,256]{1,0:T(8,128)(2,1)}, u32[]{:S(2)}, u32[]{:S(2)}) collective-permute-start(bf16[2048,256]{1,0:T(8,128)(2,1)} %refs_0_.1), channel_id=1, source_target_pairs={{0,7},{1,0},{2,1},{3,2},{4,3},{5,4},{6,5},{7,6},{8,15},{9,8},{10,9... | collective-permute-start | bytes 3145736 | tf_op jit(solution)/shard_map/ppermute | solution.py:140
  10.6 31.2 %all-to-all-start = ((bf16[72,32,128]{2,0,1:T(8,128)(2,1)}), bf16[72,32,128]{2,0,1:T(8,128)(2,1)}, u32[]{:S(2)}, u32[]{:S(2)}) async-start(bf16[72,32,128]{2,0,1:T(8,128)(2,1)} %copy.9), calls=%async_computation | async-start | bytes 1179648 | tf_op jit(solution)/shard_map/all_to_all | solution.py:149
  27.4 29.9 %collective-permute-start.3 = (bf16[2048,256]{1,0:T(8,128)(2,1)}, bf16[2048,256]{1,0:T(8,128)(2,1)S(1)}, u32[]{:S(2)}, u32[]{:S(2)}) collective-permute-start(bf16[2048,256]{1,0:T(8,128)(2,1)} %collective-permute-done), channel_id=1, source_target_pairs={{0,1},{1,2},{2,3},{3,4},{4,5},{5,6},{6,7},{7,0},{8,9},{9,10},{10,1... | collective-permute-start | bytes 3145736 | tf_op jit(solution)/shard_map/ppermute | solution.py:152
  33.0 30.3 %collective-permute-start.4 = (bf16[2048,256]{1,0:T(8,128)(2,1)}, bf16[2048,256]{1,0:T(8,128)(2,1)}, u32[]{:S(2)}, u32[]{:S(2)}) collective-permute-start(bf16[2048,256]{1,0:T(8,128)(2,1)} %collective-permute-done.1), channel_id=1, source_target_pairs={{0,7},{1,0},{2,1},{3,2},{4,3},{5,4},{6,5},{7,6},{8,15},{9,8},{10,9... | collective-permute-start | bytes 3145736 | tf_op jit(solution)/shard_map/ppermute | solution.py:152
  48.2 25.8 %all-to-all-start.1 = ((bf16[32,64,128]{2,1,0:T(8,128)(2,1)}), bf16[32,64,128]{2,1,0:T(8,128)(2,1)}, u32[]{:S(2)}, u32[]{:S(2)}) async-start(bf16[32,64,128]{2,1,0:T(8,128)(2,1)} %bitcast.19), calls=%async_computation.1 | async-start | bytes 1048576 | tf_op jit(solution)/shard_map/all_to_all | solution.py:179
  58.1 27.4 %collective-permute-start.5 = (bf16[1024,256]{1,0:T(8,128)(2,1)}, bf16[1024,256]{1,0:T(8,128)(2,1)}, u32[]{:S(2)}, u32[]{:S(2)}) collective-permute-start(bf16[1024,256]{1,0:T(8,128)(2,1)} %slice.62), channel_id=1, source_target_pairs={{0,1},{1,2},{2,3},{3,4},{4,5},{5,6},{6,7},{7,0},{8,9},{9,10},{10,1... | collective-permute-start | bytes 1572872 | tf_op jit(solution)/shard_map/ppermute | solution.py:158
  65.2 25.5 %collective-permute-start.6 = (bf16[1024,256]{1,0:T(8,128)(2,1)}, bf16[1024,256]{1,0:T(8,128)(2,1)}, u32[]{:S(2)}, u32[]{:S(2)}) collective-permute-start(bf16[1024,256]{1,0:T(8,128)(2,1)} %slice.63), channel_id=1, source_target_pairs={{0,7},{1,0},{2,1},{3,2},{4,3},{5,4},{6,5},{7,6},{8,15},{9,8},{10,9... | collective-permute-start | bytes 1572872 | tf_op jit(solution)/shard_map/ppermute | solution.py:158
  74.8 25.7 %collective-permute-start.7 = (bf16[1024,256]{1,0:T(8,128)(2,1)}, bf16[1024,256]{1,0:T(8,128)(2,1)}, u32[]{:S(2)}, u32[]{:S(2)}) collective-permute-start(bf16[1024,256]{1,0:T(8,128)(2,1)} %slice.52), channel_id=1, source_target_pairs={{0,1},{1,2},{2,3},{3,4},{4,5},{5,6},{6,7},{7,0},{8,9},{9,10},{10,1... | collective-permute-start | bytes 1572872 | tf_op jit(solution)/shard_map/ppermute | solution.py:182
  79.8 13.8 %collective-permute-start.2 = (bf16[32,64,128]{2,1,0:T(8,128)(2,1)}, bf16[32,64,128]{2,1,0:T(8,128)(2,1)}, u32[]{:S(2)}, u32[]{:S(2)}) collective-permute-start(bf16[32,64,128]{2,1,0:T(8,128)(2,1)} %all-to-all-done.1.got_ref), channel_id=1, source_target_pairs={{0,16},{16,0},{1,17},{17,1},{2,18},{18,2},{3,19},{19,3},{4,20},{20... | collective-permute-start | bytes 1572872 | tf_op jit(solution)/shard_map/ppermute | solution.py:183
  83.6 18.1 %collective-permute-start.8 = (bf16[1024,256]{1,0:T(8,128)(2,1)}, bf16[1024,256]{1,0:T(8,128)(2,1)}, u32[]{:S(2)}, u32[]{:S(2)}) collective-permute-start(bf16[1024,256]{1,0:T(8,128)(2,1)} %slice.53), channel_id=1, source_target_pairs={{0,7},{1,0},{2,1},{3,2},{4,3},{5,4},{6,5},{7,6},{8,15},{9,8},{10,9... | collective-permute-start | bytes 1572872 | tf_op jit(solution)/shard_map/ppermute | solution.py:182
  85.5 17.0 %collective-permute-start.9 = (bf16[1024,256]{1,0:T(8,128)(2,1)}, bf16[1024,256]{1,0:T(8,128)(2,1)}, u32[]{:S(2)}, u32[]{:S(2)}) collective-permute-start(bf16[1024,256]{1,0:T(8,128)(2,1)} %collective-permute-done.5.refs_4_), channel_id=1, source_target_pairs={{0,1},{1,2},{2,3},{3,4},{4,5},{5,6},{6,7},{7,0},{8,9},{9,10},{10,1... | collective-permute-start | bytes 1572872 | tf_op jit(solution)/shard_map/ppermute | solution.py:159
  90.7 21.8 %collective-permute-start.11 = (bf16[1024,256]{1,0:T(8,128)(2,1)}, bf16[1024,256]{1,0:T(8,128)(2,1)S(1)}, u32[]{:S(2)}, u32[]{:S(2)}) collective-permute-start(bf16[1024,256]{1,0:T(8,128)(2,1)} %collective-permute-done.6.refs_5_), channel_id=1, source_target_pairs={{0,7},{1,0},{2,1},{3,2},{4,3},{5,4},{6,5},{7,6},{8,15},{9,8},{10,9... | collective-permute-start | bytes 1572872 | tf_op jit(solution)/shard_map/ppermute | solution.py:159
  93.6 1.2 copy-start
  104.2 17.0 %collective-permute-start.10 = (bf16[1024,128]{1,0:T(8,128)(2,1)S(1)}, bf16[1024,128]{1,0:T(8,128)(2,1)S(1)}, u32[]{:S(2)}, u32[]{:S(2)}) collective-permute-start(bf16[1024,128]{1,0:T(8,128)(2,1)S(1)} %last_far.2), channel_id=1, source_target_pairs={{0,8},{8,0},{1,9},{9,1},{2,10},{10,2},{3,11},{11,3},{4,12},{12,4},... | collective-permute-start | bytes 786440 | tf_op jit(solution)/shard_map/ppermute | solution.py:203
  113.9 11.3 %collective-permute-start.12 = (bf16[1024,128]{1,0:T(8,128)(2,1)S(1)}, bf16[1024,128]{1,0:T(8,128)(2,1)S(1)}, u32[]{:S(2)}, u32[]{:S(2)}) collective-permute-start(bf16[1024,128]{1,0:T(8,128)(2,1)S(1)} %last_far.3), channel_id=1, source_target_pairs={{0,8},{8,0},{1,9},{9,1},{2,10},{10,2},{3,11},{11,3},{4,12},{12,4},... | collective-permute-start | bytes 786440 | tf_op jit(solution)/shard_map/ppermute | solution.py:203

commit v11 on v10

--- a/solution.py
+++ b/solution.py
@@ -10,7 +10,6 @@
 CORES = 2
 PAD = 8
 TILE_M = 256
-SPLIT = 1024
 ROW = ("chip", "core")
 
 inv_root = 0.7071067811865476
@@ -53,11 +52,12 @@
             out_ref[y, :, x * width : (x + 1) * width] = rows.astype(out_ref.dtype)
 
 
-def early_products(place, got, twin, stored, bounds, offsets, blocks, own_offsets, own_blocks):
+def early_products(place, got, twin, stored, offsets, blocks, own_offsets, own_blocks):
     rows, width = stored.shape
     y_count = lax.axis_size("y")
     depth, both = blocks[0].shape[1], X_HI * width
     parts = len(own_blocks)
+    share = rows // parts
     common = len(offsets) * depth
 
     def body(place_ref, got_ref, twin_ref, stored_ref, *refs):
@@ -68,13 +68,13 @@
             turned[n * depth : (n + 1) * depth] = upper_ref[(place_ref[1] + offset + y_count) % y_count]
         at_left = place_ref[0] == 0
 
-        for part, (start, stop) in enumerate(bounds):
+        for part in range(parts):
             turned[common:] = upper_ref[(place_ref[1] + own_offsets[part] + y_count) % y_count]
             far_ref, rest_ref = out_refs[2 * part : 2 * part + 2]
 
             def one(i, carry):
                 local = pl.ds(pl.multiple_of(i * TILE_M, TILE_M), TILE_M)
-                full = pl.ds(pl.multiple_of(start + i * TILE_M, TILE_M), TILE_M)
+                full = pl.ds(pl.multiple_of(part * share + i * TILE_M, TILE_M), TILE_M)
                 tiles = [ref[full] for ref in block_refs] + [own_refs[part][local]]
                 total = jnp.dot(jnp.concatenate(tiles, axis=1), turned[...], preferred_element_type=jnp.float32)
                 left, right = total[:, :width], total[:, width:]
@@ -82,13 +82,13 @@
                 rest_ref[local] = stored_ref[full].astype(jnp.float32) - jnp.where(at_left, left, right)
                 return carry
 
-            lax.fori_loop(0, (stop - start) // TILE_M, one, 0)
+            lax.fori_loop(0, share // TILE_M, one, 0)
 
     return pl.pallas_call(
         body,
         in_specs=[pl.BlockSpec(memory_space=pltpu.SMEM)] + [whole()] * (3 + len(blocks) + parts),
         out_specs=[whole()] * (2 * parts + 1),
-        out_shape=[jax.ShapeDtypeStruct((b - a, width), jnp.float32) for a, b in bounds for _ in range(2)]
+        out_shape=[jax.ShapeDtypeStruct((share, width), jnp.float32)] * (2 * parts)
         + [jax.ShapeDtypeStruct((y_count, depth, both), stored.dtype)],
         scratch_shapes=[VM((common + depth, both), stored.dtype)],
         compiler_params=grant(16),
@@ -150,11 +150,10 @@
     joined = jnp.concatenate(near, axis=1)
     packed = after(packed, joined)
     far_near = tuple(lax.ppermute(block, "y", route[sign]) for block, sign in zip(near, route))
-    bounds = ((0, SPLIT), (SPLIT, row_count))
     first_keys, second_keys = ((0, -1), (1, 1)), ((1, -1), (0, 1))
     third = {}
-    for part, sign in first_keys:
-        block = far_near[0 if sign < 0 else 1][slice(*bounds[part])]
+    for part, sign in first_keys + second_keys:
+        block = far_near[0 if sign < 0 else 1][part * half : (part + 1) * half]
         third[part, sign] = lax.ppermute(block, "y", route[sign])
     last = [lax.ppermute(third[part, sign], "y", route[sign]) for part, sign in first_keys]
     packed = packed.reshape(groups, share + PAD, col_width)
@@ -177,10 +176,9 @@
         chips * X_HI, top_count, col_width
     )
     got = lax.all_to_all(send, ("chip", "x_hi"), split_axis=0, concat_axis=0)
-    for part, sign in second_keys:
-        block = after(far_near[0 if sign < 0 else 1], got)[slice(*bounds[part])]
-        third[part, sign] = lax.ppermute(block, "y", route[sign])
+    got = after(got, third[0, -1])
     twin = lax.ppermute(got, "core", [(0, 1), (1, 0)])
+    twin = after(twin, third[1, -1])
     place = jnp.stack([lax.axis_index(name) for name in ("x_hi", "y", "core")]).astype(jnp.int32)
     swap = [(i, X_HI - 1 - i) for i in range(X_HI)]
     *sums, upper = early_products(
@@ -188,13 +186,11 @@
         got,
         twin,
         stored,
-        bounds,
         [0, -1, 1, -2, 2],
         [panel_lower, joined, *far_near],
         [sign * (y_count // 2 - 1) for _, sign in first_keys],
         [third[key] for key in first_keys],
     )
-    upper = after(upper, *(third[key] for key in second_keys))
     out = []
     for part, sign in first_keys:
         offsets = [-sign * (y_count // 2 - 1), y_count // 2]

time: 127 us -> 120 us (0.945)
  the two profiles are of different devices: /device:TPU:24 before, /device:TPU:476 now
where the time goes in v11:
time: 120 us; the launch traced here: 119 us
  starting transfers between devices  55.2 us (46%)
  waiting for transfers between devices  34.4 us (29%)
  Pallas kernels  11.9 us (10%)
  local copies, waits for them, and re-layouts  9.98 us (8%)
  other arithmetic  7.27 us (6%)
    ppermute x4, starting transfers between devices, per_device(): third[part, sign] = lax.ppermute(block, 'y', route[sign])  14.4 us
    ppermute x2, waiting for transfers between devices, per_device(): lax.ppermute(panel_lower, 'y', route[sign])  11.3 us
    ppermute x2, starting transfers between devices, per_device(): lax.ppermute(third[part, sign], 'y', route[sign])  7.52 us
    ppermute x2, starting transfers between devices, per_device(): lax.ppermute(block, 'y', route[sign])  7.51 us
    all_to_all x1, starting transfers between devices, per_device(): got = lax.all_to_all(send, ('chip', 'x_hi'), split_axis=0, concat_axis=0)  7.2 us
    ppermute x2, waiting for transfers between devices, per_device(): lax.ppermute(third[part, sign], 'y', route[sign])  6.99 us
    ppermute x2, starting transfers between devices, per_device(): lax.ppermute(panel_lower, 'y', route[sign])  6.61 us
    pallas_call x4, Pallas kernels, last_product(): pl.pallas_call(body, in_specs=[pl.BlockSpec(memory_space=pltpu.SMEM)] + [...  6.26 us
  transfers between devices with their start and end apart: 15, of which 7 were waited for; matrix products, arithmetic and copies ran while one was open for 13% of the time, Pallas kernels for 10%

profile of v11, /device:TPU:476, one launch (start us, length us, event | category | flops | bytes accessed | tf_op | source)
XLA Modules:
  0.0 119.1 jit_solution(10797958248650584816)
XLA Ops:
  0.0 4.7 %collective-permute-start = (bf16[2048,256]{1,0:T(8,128)(2,1)}, bf16[2048,256]{1,0:T(8,128)(2,1)}, u32[]{:S(2)}, u32[]{:S(2)}) collective-permute-start(bf16[2048,256]{1,0:T(8,128)(2,1)} %refs_0_.1), channel_id=1, source_target_pairs={{0,1},{1,2},{2,3},{3,4},{4,5},{5,6},{6,7},{7,0},{8,9},{9,10},{10,1... | collective-permute-start | bytes 3145736 | tf_op jit(solution)/shard_map/ppermute | solution.py:140
  4.7 1.9 %collective-permute-start.1 = (bf16[2048,256]{1,0:T(8,128)(2,1)}, bf16[2048,256]{1,0:T(8,128)(2,1)}, u32[]{:S(2)}, u32[]{:S(2)}) collective-permute-start(bf16[2048,256]{1,0:T(8,128)(2,1)} %refs_0_.1), channel_id=1, source_target_pairs={{0,7},{1,0},{2,1},{3,2},{4,3},{5,4},{6,5},{7,6},{8,15},{9,8},{10,9... | collective-permute-start | bytes 3145736 | tf_op jit(solution)/shard_map/ppermute | solution.py:140
  8.2 1.4 %multiply_convert_fusion = bf16[2048,128]{1,0:T(8,128)(2,1)S(1)} fusion(bf16[2048,128]{1,0:T(8,128)(2,1)} %param.4, f32[2048]{0:T(1024)S(1)} %convert_element_type.57), kind=kLoop, calls=%fused_computation.4 | loop fusion | flops 786432 | bytes 1056768 | tf_op jit(solution)/shard_map/convert_element_type | solution.py:142
  10.6 5.4 %all-to-all-start = ((bf16[72,32,128]{2,0,1:T(8,128)(2,1)}), bf16[72,32,128]{2,0,1:T(8,128)(2,1)}, u32[]{:S(2)}, u32[]{:S(2)}) async-start(bf16[72,32,128]{2,0,1:T(8,128)(2,1)} %copy.9), calls=%async_computation | async-start | bytes 1179648 | tf_op jit(solution)/shard_map/all_to_all | solution.py:149
  16.1 11.3 %collective-permute-done = bf16[2048,256]{1,0:T(8,128)(2,1)} collective-permute-done((bf16[2048,256]{1,0:T(8,128)(2,1)}, bf16[2048,256]{1,0:T(8,128)(2,1)}, u32[]{:S(2)}, u32[]{:S(2)}) %collective-permute-start) | collective-permute-done | bytes 1048608 | tf_op jit(solution)/shard_map/ppermute | solution.py:140
  27.4 5.6 %collective-permute-start.2 = (bf16[2048,256]{1,0:T(8,128)(2,1)}, bf16[2048,256]{1,0:T(8,128)(2,1)S(1)}, u32[]{:S(2)}, u32[]{:S(2)}) collective-permute-start(bf16[2048,256]{1,0:T(8,128)(2,1)} %collective-permute-done), channel_id=1, source_target_pairs={{0,1},{1,2},{2,3},{3,4},{4,5},{5,6},{6,7},{7,0},{8,9},{9,10},{10,1... | collective-permute-start | bytes 3145736 | tf_op jit(solution)/shard_map/ppermute | solution.py:152
  33.0 1.9 %collective-permute-start.6 = (bf16[2048,256]{1,0:T(8,128)(2,1)}, bf16[2048,256]{1,0:T(8,128)(2,1)}, u32[]{:S(2)}, u32[]{:S(2)}) collective-permute-start(bf16[2048,256]{1,0:T(8,128)(2,1)} %collective-permute-done.1), channel_id=1, source_target_pairs={{0,7},{1,0},{2,1},{3,2},{4,3},{5,4},{6,5},{7,6},{8,15},{9,8},{10,9... | collective-permute-start | bytes 3145736 | tf_op jit(solution)/shard_map/ppermute | solution.py:152
  35.0 1.3 %constant_dynamic-update-slice_fusion.1 = bf16[2048,512]{1,0:T(8,128)(2,1)S(1)} fusion(bf16[2048,256]{1,0:T(8,128)(2,1)} %collective-permute-done), kind=kLoop, calls=%fused_computation.29 | loop fusion | bytes 2097152
  36.3 1.3 %constant_dynamic-update-slice_fusion.refs_1_ = bf16[2048,512]{1,0:T(8,128)(2,1)S(1)} fusion(bf16[2048,512]{1,0:T(8,128)(2,1)S(1)} %constant_dynamic-update-slice_fusion.1, bf16[2048,256]{1,0:T(8,128)(2,1)} %collective-permute-done.1), kind=kLoop, calls=%fused_computation.28 | loop fusion | bytes 2097152 | tf_op jit(solution)/shard_map/concatenate | solution.py:150
  38.5 1.2 fusion.3
  41.8 7.2 %all-to-all-start.1 = ((bf16[32,64,128]{2,1,0:T(8,128)(2,1)}), bf16[32,64,128]{2,1,0:T(8,128)(2,1)}, u32[]{:S(2)}, u32[]{:S(2)}) async-start(bf16[32,64,128]{2,1,0:T(8,128)(2,1)} %bitcast.19), calls=%async_computation.1 | async-start | bytes 1048576 | tf_op jit(solution)/shard_map/all_to_all | solution.py:178
  49.0 5.9 %collective-permute-done.2.refs_2_ = bf16[2048,256]{1,0:T(8,128)(2,1)S(1)} collective-permute-done((bf16[2048,256]{1,0:T(8,128)(2,1)}, bf16[2048,256]{1,0:T(8,128)(2,1)S(1)}, u32[]{:S(2)}, u32[]{:S(2)}) %collective-permute-start.2) | collective-permute-done | bytes 1048608 | tf_op jit(solution)/shard_map/ppermute | solution.py:152
  55.9 5.5 %collective-permute-start.3 = (bf16[1024,256]{1,0:T(8,128)(2,1)}, bf16[1024,256]{1,0:T(8,128)(2,1)}, u32[]{:S(2)}, u32[]{:S(2)}) collective-permute-start(bf16[1024,256]{1,0:T(8,128)(2,1)} %get-tuple-element.24), channel_id=1, source_target_pairs={{0,1},{1,2},{2,3},{3,4},{4,5},{5,6},{6,7},{7,0},{8,9},{9,10},{10,1... | collective-permute-start | bytes 1572872 | tf_op jit(solution)/shard_map/ppermute | solution.py:157
  61.4 2.2 %fusion.14 = (bf16[1024,256]{1,0:T(8,128)(2,1)}, bf16[1024,256]{1,0:T(8,128)(2,1)}) fusion(bf16[2048,256]{1,0:T(8,128)(2,1)} %collective-permute-done.6.refs_3_), kind=kLoop, calls=%fused_computation.31 | loop fusion | bytes 2097152 | tf_op jit(solution)/shard_map/slice | solution.py:156
  63.7 1.9 %collective-permute-start.7 = (bf16[1024,256]{1,0:T(8,128)(2,1)}, bf16[1024,256]{1,0:T(8,128)(2,1)}, u32[]{:S(2)}, u32[]{:S(2)}) collective-permute-start(bf16[1024,256]{1,0:T(8,128)(2,1)} %get-tuple-element.22), channel_id=1, source_target_pairs={{0,7},{1,0},{2,1},{3,2},{4,3},{5,4},{6,5},{7,6},{8,15},{9,8},{10,9... | collective-permute-start | bytes 1572872 | tf_op jit(solution)/shard_map/ppermute | solution.py:157
  65.6 5.1 %collective-permute-start.5 = (bf16[1024,256]{1,0:T(8,128)(2,1)}, bf16[1024,256]{1,0:T(8,128)(2,1)}, u32[]{:S(2)}, u32[]{:S(2)}) collective-permute-start(bf16[1024,256]{1,0:T(8,128)(2,1)} %get-tuple-element.23), channel_id=1, source_target_pairs={{0,1},{1,2},{2,3},{3,4},{4,5},{5,6},{6,7},{7,0},{8,9},{9,10},{10,1... | collective-permute-start | bytes 1572872 | tf_op jit(solution)/shard_map/ppermute | solution.py:157
  70.7 2.9 %collective-permute-done.3.refs_4_ = bf16[1024,256]{1,0:T(8,128)(2,1)} collective-permute-done((bf16[1024,256]{1,0:T(8,128)(2,1)}, bf16[1024,256]{1,0:T(8,128)(2,1)}, u32[]{:S(2)}, u32[]{:S(2)}) %collective-permute-start.3) | collective-permute-done | bytes 524320 | tf_op jit(solution)/shard_map/ppermute | solution.py:157
  73.6 1.9 %collective-permute-start.4 = (bf16[32,64,128]{2,1,0:T(8,128)(2,1)}, bf16[32,64,128]{2,1,0:T(8,128)(2,1)}, u32[]{:S(2)}, u32[]{:S(2)}) collective-permute-start(bf16[32,64,128]{2,1,0:T(8,128)(2,1)} %all-to-all-done.1.got_ref), channel_id=1, source_target_pairs={{0,16},{16,0},{1,17},{17,1},{2,18},{18,2},{3,19},{19,3},{4,20},{20... | collective-permute-start | bytes 1572872 | tf_op jit(solution)/shard_map/ppermute | solution.py:180
  75.5 1.9 %collective-permute-start.8 = (bf16[1024,256]{1,0:T(8,128)(2,1)}, bf16[1024,256]{1,0:T(8,128)(2,1)}, u32[]{:S(2)}, u32[]{:S(2)}) collective-permute-start(bf16[1024,256]{1,0:T(8,128)(2,1)} %get-tuple-element.21), channel_id=1, source_target_pairs={{0,7},{1,0},{2,1},{3,2},{4,3},{5,4},{6,5},{7,6},{8,15},{9,8},{10,9... | collective-permute-start | bytes 1572872 | tf_op jit(solution)/shard_map/ppermute | solution.py:157
  77.5 5.6 %collective-permute-start.9 = (bf16[1024,256]{1,0:T(8,128)(2,1)}, bf16[1024,256]{1,0:T(8,128)(2,1)}, u32[]{:S(2)}, u32[]{:S(2)}) collective-permute-start(bf16[1024,256]{1,0:T(8,128)(2,1)} %collective-permute-done.3.refs_4_), channel_id=1, source_target_pairs={{0,1},{1,2},{2,3},{3,4},{4,5},{5,6},{6,7},{7,0},{8,9},{9,10},{10,1... | collective-permute-start | bytes 1572872 | tf_op jit(solution)/shard_map/ppermute | solution.py:158
  83.1 1.9 %collective-permute-start.11 = (bf16[1024,256]{1,0:T(8,128)(2,1)}, bf16[1024,256]{1,0:T(8,128)(2,1)S(1)}, u32[]{:S(2)}, u32[]{:S(2)}) collective-permute-start(bf16[1024,256]{1,0:T(8,128)(2,1)} %collective-permute-done.7.refs_5_), channel_id=1, source_target_pairs={{0,7},{1,0},{2,1},{3,2},{4,3},{5,4},{6,5},{7,6},{8,15},{9,8},{10,9... | collective-permute-start | bytes 1572872 | tf_op jit(solution)/shard_map/ppermute | solution.py:158
  86.1 1.2 %copy-done = bf16[2048,256]{1,0:T(8,128)(2,1)S(1)} copy-done((bf16[2048,256]{1,0:T(8,128)(2,1)S(1)}, bf16[2048,256]{1,0:T(8,128)(2,1)}, u32[]{:S(2)}) %copy-start) | copy-done | bytes 1048600
  87.3 5.7 %early_products.1 = (f32[1024,128]{1,0:T(8,128)S(1)}, f32[1024,128]{1,0:T(8,128)S(1)}, f32[1024,128]{1,0:T(8,128)S(1)}, f32[1024,128]{1,0:T(8,128)S(1)}, bf16[8,256,256]{2,1,0:T(8,128)(2,1)S(1)}) custom-call(s32[3]{0:T(128)S(1)} %pad_add_fusion.place_ref, bf16[32,64,128]{2,1,0:T(8,128)(2,1)} %all-to-all-done.1.got_ref, ...), custom_call_target="tpu_custom_call" | custom-call | tf_op jit(solution)/shard_map/early_products/pallas_call | solution.py:87
  93.0 1.3 %collective-permute-done.8.refs_0_ = bf16[1024,256]{1,0:T(8,128)(2,1)} collective-permute-done((bf16[1024,256]{1,0:T(8,128)(2,1)}, bf16[1024,256]{1,0:T(8,128)(2,1)}, u32[]{:S(2)}, u32[]{:S(2)}) %collective-permute-start.8) | collective-permute-done | bytes 524320 | tf_op jit(solution)/shard_map/ppermute | solution.py:157
  95.2 1.6 %last_far.2 = bf16[1024,128]{1,0:T(8,128)(2,1)S(1)} custom-call(s32[3]{0:T(128)S(1)} %pad_add_fusion.place_ref, bf16[8,256,256]{2,1,0:T(8,128)(2,1)S(1)} %get-tuple-element.16.upper_ref, f32[1024,128]{1,0:T(8,128)S(1)} %get-tuple-element.18.base_ref, bf16[1024,256]{1,0:T(8,128)(2,1)} %collective-permute-done.8.refs_0_, ...), custom_call_target="tpu_custom_call" | custom-call | tf_op jit(solution)/shard_map/last_far/pallas_call | solution.py:117
  96.8 2.3 %collective-permute-start.10 = (bf16[1024,128]{1,0:T(8,128)(2,1)S(1)}, bf16[1024,128]{1,0:T(8,128)(2,1)S(1)}, u32[]{:S(2)}, u32[]{:S(2)}) collective-permute-start(bf16[1024,128]{1,0:T(8,128)(2,1)S(1)} %last_far.2), channel_id=1, source_target_pairs={{0,8},{8,0},{1,9},{9,1},{2,10},{10,2},{3,11},{11,3},{4,12},{12,4},... | collective-permute-start | bytes 786440 | tf_op jit(solution)/shard_map/ppermute | solution.py:199
  99.2 6.0 %collective-permute-done.11.refs_1_ = bf16[1024,256]{1,0:T(8,128)(2,1)S(1)} collective-permute-done((bf16[1024,256]{1,0:T(8,128)(2,1)}, bf16[1024,256]{1,0:T(8,128)(2,1)S(1)}, u32[]{:S(2)}, u32[]{:S(2)}) %collective-permute-start.11) | collective-permute-done | bytes 524320 | tf_op jit(solution)/shard_map/ppermute | solution.py:158
  105.2 1.5 %last_far.3 = bf16[1024,128]{1,0:T(8,128)(2,1)S(1)} custom-call(s32[3]{0:T(128)S(1)} %pad_add_fusion.place_ref, bf16[8,256,256]{2,1,0:T(8,128)(2,1)S(1)} %get-tuple-element.16.upper_ref, f32[1024,128]{1,0:T(8,128)S(1)} %get-tuple-element.20.base_ref, bf16[1024,256]{1,0:T(8,128)(2,1)} %collective-permute-done.5.refs_0_, ...), custom_call_target="tpu_custom_call" | custom-call | tf_op jit(solution)/shard_map/last_far/pallas_call | solution.py:117
  106.6 2.3 %collective-permute-start.12 = (bf16[1024,128]{1,0:T(8,128)(2,1)S(1)}, bf16[1024,128]{1,0:T(8,128)(2,1)S(1)}, u32[]{:S(2)}, u32[]{:S(2)}) collective-permute-start(bf16[1024,128]{1,0:T(8,128)(2,1)S(1)} %last_far.3), channel_id=1, source_target_pairs={{0,8},{8,0},{1,9},{9,1},{2,10},{10,2},{3,11},{11,3},{4,12},{12,4},... | collective-permute-start | bytes 786440 | tf_op jit(solution)/shard_map/ppermute | solution.py:199
  108.9 1.6 %last_own.2 = f32[1024,128]{1,0:T(8,128)S(1)} custom-call(s32[3]{0:T(128)S(1)} %pad_add_fusion.place_ref, bf16[8,256,256]{2,1,0:T(8,128)(2,1)S(1)} %get-tuple-element.16.upper_ref, f32[1024,128]{1,0:T(8,128)S(1)} %get-tuple-element.17.base_ref, bf16[1024,256]{1,0:T(8,128)(2,1)} %collective-permute-done.8.refs_0_, ...), custom_call_target="tpu_custom_call" | custom-call | tf_op jit(solution)/shard_map/last_own/pallas_call | solution.py:117
  110.6 1.5 %last_own.3 = f32[1024,128]{1,0:T(8,128)S(1)} custom-call(s32[3]{0:T(128)S(1)} %pad_add_fusion.place_ref, bf16[8,256,256]{2,1,0:T(8,128)(2,1)S(1)} %get-tuple-element.16.upper_ref, f32[1024,128]{1,0:T(8,128)S(1)} %get-tuple-element.19.base_ref, bf16[1024,256]{1,0:T(8,128)(2,1)} %collective-permute-done.5.refs_0_, ...), custom_call_target="tpu_custom_call" | custom-call | tf_op jit(solution)/shard_map/last_own/pallas_call | solution.py:117
  112.2 6.0 %collective-permute-done.12 = bf16[1024,128]{1,0:T(8,128)(2,1)S(1)} collective-permute-done((bf16[1024,128]{1,0:T(8,128)(2,1)S(1)}, bf16[1024,128]{1,0:T(8,128)(2,1)S(1)}, u32[]{:S(2)}, u32[]{:S(2)}) %collective-permute-start.12) | collective-permute-done | bytes 262176 | tf_op jit(solution)/shard_map/ppermute | solution.py:199
  (27 shorter events, 9.6 us)
Async XLA Ops:
  0.0 27.4 %collective-permute-start = (bf16[2048,256]{1,0:T(8,128)(2,1)}, bf16[2048,256]{1,0:T(8,128)(2,1)}, u32[]{:S(2)}, u32[]{:S(2)}) collective-permute-start(bf16[2048,256]{1,0:T(8,128)(2,1)} %refs_0_.1), channel_id=1, source_target_pairs={{0,1},{1,2},{2,3},{3,4},{4,5},{5,6},{6,7},{7,0},{8,9},{9,10},{10,1... | collective-permute-start | bytes 3145736 | tf_op jit(solution)/shard_map/ppermute | solution.py:140
  4.7 28.3 %collective-permute-start.1 = (bf16[2048,256]{1,0:T(8,128)(2,1)}, bf16[2048,256]{1,0:T(8,128)(2,1)}, u32[]{:S(2)}, u32[]{:S(2)}) collective-permute-start(bf16[2048,256]{1,0:T(8,128)(2,1)} %refs_0_.1), channel_id=1, source_target_pairs={{0,7},{1,0},{2,1},{3,2},{4,3},{5,4},{6,5},{7,6},{8,15},{9,8},{10,9... | collective-permute-start | bytes 3145736 | tf_op jit(solution)/shard_map/ppermute | solution.py:140
  10.6 26.9 %all-to-all-start = ((bf16[72,32,128]{2,0,1:T(8,128)(2,1)}), bf16[72,32,128]{2,0,1:T(8,128)(2,1)}, u32[]{:S(2)}, u32[]{:S(2)}) async-start(bf16[72,32,128]{2,0,1:T(8,128)(2,1)} %copy.9), calls=%async_computation | async-start | bytes 1179648 | tf_op jit(solution)/shard_map/all_to_all | solution.py:149
  27.4 27.4 %collective-permute-start.2 = (bf16[2048,256]{1,0:T(8,128)(2,1)}, bf16[2048,256]{1,0:T(8,128)(2,1)S(1)}, u32[]{:S(2)}, u32[]{:S(2)}) collective-permute-start(bf16[2048,256]{1,0:T(8,128)(2,1)} %collective-permute-done), channel_id=1, source_target_pairs={{0,1},{1,2},{2,3},{3,4},{4,5},{5,6},{6,7},{7,0},{8,9},{9,10},{10,1... | collective-permute-start | bytes 3145736 | tf_op jit(solution)/shard_map/ppermute | solution.py:152
  33.0 28.4 %collective-permute-start.6 = (bf16[2048,256]{1,0:T(8,128)(2,1)}, bf16[2048,256]{1,0:T(8,128)(2,1)}, u32[]{:S(2)}, u32[]{:S(2)}) collective-permute-start(bf16[2048,256]{1,0:T(8,128)(2,1)} %collective-permute-done.1), channel_id=1, source_target_pairs={{0,7},{1,0},{2,1},{3,2},{4,3},{5,4},{6,5},{7,6},{8,15},{9,8},{10,9... | collective-permute-start | bytes 3145736 | tf_op jit(solution)/shard_map/ppermute | solution.py:152
  41.8 28.9 %all-to-all-start.1 = ((bf16[32,64,128]{2,1,0:T(8,128)(2,1)}), bf16[32,64,128]{2,1,0:T(8,128)(2,1)}, u32[]{:S(2)}, u32[]{:S(2)}) async-start(bf16[32,64,128]{2,1,0:T(8,128)(2,1)} %bitcast.19), calls=%async_computation.1 | async-start | bytes 1048576 | tf_op jit(solution)/shard_map/all_to_all | solution.py:178
  55.9 17.7 %collective-permute-start.3 = (bf16[1024,256]{1,0:T(8,128)(2,1)}, bf16[1024,256]{1,0:T(8,128)(2,1)}, u32[]{:S(2)}, u32[]{:S(2)}) collective-permute-start(bf16[1024,256]{1,0:T(8,128)(2,1)} %get-tuple-element.24), channel_id=1, source_target_pairs={{0,1},{1,2},{2,3},{3,4},{4,5},{5,6},{6,7},{7,0},{8,9},{9,10},{10,1... | collective-permute-start | bytes 1572872 | tf_op jit(solution)/shard_map/ppermute | solution.py:157
  63.7 19.4 %collective-permute-start.7 = (bf16[1024,256]{1,0:T(8,128)(2,1)}, bf16[1024,256]{1,0:T(8,128)(2,1)}, u32[]{:S(2)}, u32[]{:S(2)}) collective-permute-start(bf16[1024,256]{1,0:T(8,128)(2,1)} %get-tuple-element.22), channel_id=1, source_target_pairs={{0,7},{1,0},{2,1},{3,2},{4,3},{5,4},{6,5},{7,6},{8,15},{9,8},{10,9... | collective-permute-start | bytes 1572872 | tf_op jit(solution)/shard_map/ppermute | solution.py:157
  65.6 20.5 %collective-permute-start.5 = (bf16[1024,256]{1,0:T(8,128)(2,1)}, bf16[1024,256]{1,0:T(8,128)(2,1)}, u32[]{:S(2)}, u32[]{:S(2)}) collective-permute-start(bf16[1024,256]{1,0:T(8,128)(2,1)} %get-tuple-element.23), channel_id=1, source_target_pairs={{0,1},{1,2},{2,3},{3,4},{4,5},{5,6},{6,7},{7,0},{8,9},{9,10},{10,1... | collective-permute-start | bytes 1572872 | tf_op jit(solution)/shard_map/ppermute | solution.py:157
  73.6 12.4 %collective-permute-start.4 = (bf16[32,64,128]{2,1,0:T(8,128)(2,1)}, bf16[32,64,128]{2,1,0:T(8,128)(2,1)}, u32[]{:S(2)}, u32[]{:S(2)}) collective-permute-start(bf16[32,64,128]{2,1,0:T(8,128)(2,1)} %all-to-all-done.1.got_ref), channel_id=1, source_target_pairs={{0,16},{16,0},{1,17},{17,1},{2,18},{18,2},{3,19},{19,3},{4,20},{20... | collective-permute-start | bytes 1572872 | tf_op jit(solution)/shard_map/ppermute | solution.py:180
  75.5 18.7 %collective-permute-start.8 = (bf16[1024,256]{1,0:T(8,128)(2,1)}, bf16[1024,256]{1,0:T(8,128)(2,1)}, u32[]{:S(2)}, u32[]{:S(2)}) collective-permute-start(bf16[1024,256]{1,0:T(8,128)(2,1)} %get-tuple-element.21), channel_id=1, source_target_pairs={{0,7},{1,0},{2,1},{3,2},{4,3},{5,4},{6,5},{7,6},{8,15},{9,8},{10,9... | collective-permute-start | bytes 1572872 | tf_op jit(solution)/shard_map/ppermute | solution.py:157
  77.5 17.7 %collective-permute-start.9 = (bf16[1024,256]{1,0:T(8,128)(2,1)}, bf16[1024,256]{1,0:T(8,128)(2,1)}, u32[]{:S(2)}, u32[]{:S(2)}) collective-permute-start(bf16[1024,256]{1,0:T(8,128)(2,1)} %collective-permute-done.3.refs_4_), channel_id=1, source_target_pairs={{0,1},{1,2},{2,3},{3,4},{4,5},{5,6},{6,7},{7,0},{8,9},{9,10},{10,1... | collective-permute-start | bytes 1572872 | tf_op jit(solution)/shard_map/ppermute | solution.py:158
  83.1 22.1 %collective-permute-start.11 = (bf16[1024,256]{1,0:T(8,128)(2,1)}, bf16[1024,256]{1,0:T(8,128)(2,1)S(1)}, u32[]{:S(2)}, u32[]{:S(2)}) collective-permute-start(bf16[1024,256]{1,0:T(8,128)(2,1)} %collective-permute-done.7.refs_5_), channel_id=1, source_target_pairs={{0,7},{1,0},{2,1},{3,2},{4,3},{5,4},{6,5},{7,6},{8,15},{9,8},{10,9... | collective-permute-start | bytes 1572872 | tf_op jit(solution)/shard_map/ppermute | solution.py:158
  86.0 1.2 %copy-start = (bf16[2048,256]{1,0:T(8,128)(2,1)S(1)}, bf16[2048,256]{1,0:T(8,128)(2,1)}, u32[]{:S(2)}) copy-start(bf16[2048,256]{1,0:T(8,128)(2,1)} %refs_0_.1) | copy-start | bytes 3145732
  96.8 15.2 %collective-permute-start.10 = (bf16[1024,128]{1,0:T(8,128)(2,1)S(1)}, bf16[1024,128]{1,0:T(8,128)(2,1)S(1)}, u32[]{:S(2)}, u32[]{:S(2)}) collective-permute-start(bf16[1024,128]{1,0:T(8,128)(2,1)S(1)} %last_far.2), channel_id=1, source_target_pairs={{0,8},{8,0},{1,9},{9,1},{2,10},{10,2},{3,11},{11,3},{4,12},{12,4},... | collective-permute-start | bytes 786440 | tf_op jit(solution)/shard_map/ppermute | solution.py:199
  106.6 11.5 %collective-permute-start.12 = (bf16[1024,128]{1,0:T(8,128)(2,1)S(1)}, bf16[1024,128]{1,0:T(8,128)(2,1)S(1)}, u32[]{:S(2)}, u32[]{:S(2)}) collective-permute-start(bf16[1024,128]{1,0:T(8,128)(2,1)S(1)} %last_far.3), channel_id=1, source_target_pairs={{0,8},{8,0},{1,9},{9,1},{2,10},{10,2},{3,11},{11,3},{4,12},{12,4},... | collective-permute-start | bytes 786440 | tf_op jit(solution)/shard_map/ppermute | solution.py:199

commit v12 on v10

--- a/solution.py
+++ b/solution.py
@@ -10,7 +10,7 @@
 CORES = 2
 PAD = 8
 TILE_M = 256
-SPLIT = 1024
+SPLIT = 1280
 ROW = ("chip", "core")
 
 inv_root = 0.7071067811865476
@@ -53,30 +53,33 @@
             out_ref[y, :, x * width : (x + 1) * width] = rows.astype(out_ref.dtype)
 
 
-def early_products(place, got, twin, stored, bounds, offsets, blocks, own_offsets, own_blocks):
+def early_products(place, got, twin, stored, bounds, offsets, blocks, own_offset, own_block):
     rows, width = stored.shape
     y_count = lax.axis_size("y")
     depth, both = blocks[0].shape[1], X_HI * width
-    parts = len(own_blocks)
+    parts = len(bounds)
     common = len(offsets) * depth
 
     def body(place_ref, got_ref, twin_ref, stored_ref, *refs):
-        block_refs, own_refs, out_refs = refs[: len(blocks)], refs[len(blocks) : -2 - 2 * parts], refs[-2 - 2 * parts : -2]
+        block_refs, own_ref, out_refs = refs[: len(blocks)], refs[len(blocks)], refs[len(blocks) + 1 : -2]
         upper_ref, turned = refs[-2:]
         order_upper(place_ref[2], got_ref, twin_ref, upper_ref)
         for n, offset in enumerate(offsets):
             turned[n * depth : (n + 1) * depth] = upper_ref[(place_ref[1] + offset + y_count) % y_count]
+        turned[common:] = upper_ref[(place_ref[1] + own_offset + y_count) % y_count]
         at_left = place_ref[0] == 0
 
         for part, (start, stop) in enumerate(bounds):
-            turned[common:] = upper_ref[(place_ref[1] + own_offsets[part] + y_count) % y_count]
             far_ref, rest_ref = out_refs[2 * part : 2 * part + 2]
 
             def one(i, carry):
                 local = pl.ds(pl.multiple_of(i * TILE_M, TILE_M), TILE_M)
                 full = pl.ds(pl.multiple_of(start + i * TILE_M, TILE_M), TILE_M)
-                tiles = [ref[full] for ref in block_refs] + [own_refs[part][local]]
-                total = jnp.dot(jnp.concatenate(tiles, axis=1), turned[...], preferred_element_type=jnp.float32)
+                tiles = [ref[full] for ref in block_refs]
+                if part == 0:
+                    tiles.append(own_ref[local])
+                depth_here = sum(tile.shape[1] for tile in tiles)
+                total = jnp.dot(jnp.concatenate(tiles, axis=1), turned[:depth_here], preferred_element_type=jnp.float32)
                 left, right = total[:, :width], total[:, width:]
                 far_ref[local] = jnp.where(at_left, right, left)
                 rest_ref[local] = stored_ref[full].astype(jnp.float32) - jnp.where(at_left, left, right)
@@ -86,17 +89,17 @@
 
     return pl.pallas_call(
         body,
-        in_specs=[pl.BlockSpec(memory_space=pltpu.SMEM)] + [whole()] * (3 + len(blocks) + parts),
+        in_specs=[pl.BlockSpec(memory_space=pltpu.SMEM)] + [whole()] * (4 + len(blocks)),
         out_specs=[whole()] * (2 * parts + 1),
         out_shape=[jax.ShapeDtypeStruct((b - a, width), jnp.float32) for a, b in bounds for _ in range(2)]
         + [jax.ShapeDtypeStruct((y_count, depth, both), stored.dtype)],
         scratch_shapes=[VM((common + depth, both), stored.dtype)],
         compiler_params=grant(16),
         name="early_products",
-    )(place, got, twin, stored, *blocks, *own_blocks)
-
-
-def last_product(place, upper, base, offsets, blocks, partner, out_dtype, sign):
+    )(place, got, twin, stored, *blocks, own_block)
+
+
+def last_product(place, upper, base, offsets, blocks, bases, partner, out_dtype, sign):
     rows, width = base.shape
     y_count = upper.shape[0]
 
@@ -110,7 +113,8 @@
         columns = jnp.concatenate(columns, axis=0)
         for start in range(0, rows, TILE_M):
             part = slice(start, start + TILE_M)
-            lhs = jnp.concatenate([ref[part] for ref in block_refs], axis=1)
+            tiles = [ref[at + start : at + start + TILE_M] for ref, at in zip(block_refs, bases)]
+            lhs = jnp.concatenate(tiles, axis=1)
             term = jnp.dot(lhs, columns, preferred_element_type=jnp.float32)
             out_ref[part] = (base_ref[part] + sign * term).astype(out_ref.dtype)
 
@@ -151,12 +155,9 @@
     packed = after(packed, joined)
     far_near = tuple(lax.ppermute(block, "y", route[sign]) for block, sign in zip(near, route))
     bounds = ((0, SPLIT), (SPLIT, row_count))
-    first_keys, second_keys = ((0, -1), (1, 1)), ((1, -1), (0, 1))
-    third = {}
-    for part, sign in first_keys:
-        block = far_near[0 if sign < 0 else 1][slice(*bounds[part])]
-        third[part, sign] = lax.ppermute(block, "y", route[sign])
-    last = [lax.ppermute(third[part, sign], "y", route[sign]) for part, sign in first_keys]
+    rising = [lax.ppermute(far_near[0][start:stop], "y", up) for start, stop in bounds]
+    falling = lax.ppermute(far_near[1], "y", down)
+    last = [lax.ppermute(rising[0], "y", up)]
     packed = packed.reshape(groups, share + PAD, col_width)
     cyclic = packed[:, :share].reshape(row_count, col_width)
     scale_cyclic = packed[:, share, :share].reshape(row_count)
@@ -177,9 +178,6 @@
         chips * X_HI, top_count, col_width
     )
     got = lax.all_to_all(send, ("chip", "x_hi"), split_axis=0, concat_axis=0)
-    for part, sign in second_keys:
-        block = after(far_near[0 if sign < 0 else 1], got)[slice(*bounds[part])]
-        third[part, sign] = lax.ppermute(block, "y", route[sign])
     twin = lax.ppermute(got, "core", [(0, 1), (1, 0)])
     place = jnp.stack([lax.axis_index(name) for name in ("x_hi", "y", "core")]).astype(jnp.int32)
     swap = [(i, X_HI - 1 - i) for i in range(X_HI)]
@@ -191,17 +189,19 @@
         bounds,
         [0, -1, 1, -2, 2],
         [panel_lower, joined, *far_near],
-        [sign * (y_count // 2 - 1) for _, sign in first_keys],
-        [third[key] for key in first_keys],
-    )
-    upper = after(upper, *(third[key] for key in second_keys))
+        1 - y_count // 2,
+        rising[0],
+    )
+    last.append(lax.ppermute(after(falling, upper)[SPLIT:], "y", down))
     out = []
-    for part, sign in first_keys:
-        offsets = [-sign * (y_count // 2 - 1), y_count // 2]
-        blocks = [third[part, -sign], last[part]]
-        far = last_product(place, upper, sums[2 * part], offsets, blocks, True, jnp.bfloat16, 1)
+    offsets = [y_count // 2 - 1, y_count // 2]
+    for part, (start, _) in enumerate(bounds):
+        blocks, bases, late = [falling, last[part]], [start, 0], []
+        if part:
+            blocks, bases, late = [*blocks, rising[part]], [*bases, 0], [1 - y_count // 2]
+        far = last_product(place, upper, sums[2 * part], offsets + late, blocks, bases, True, jnp.bfloat16, 1)
         came = lax.ppermute(far, "x_hi", swap)
-        rest = last_product(place, upper, sums[2 * part + 1], offsets, blocks, False, jnp.float32, -1)
+        rest = last_product(place, upper, sums[2 * part + 1], offsets + late, blocks, bases, False, jnp.float32, -1)
         out.append((rest - came.astype(jnp.float32)).astype(jnp.bfloat16))
     return jnp.concatenate(out, axis=0)
 

time: 127 us -> 121 us (0.953)
  local copies, waits for them, and re-layouts: 12.1 us -> 7.8 us
    all_to_all x1, waiting for transfers between devices: 6.89 us -> 0.01 us  [per_device(): got = lax.all_to_all(send, ('chip', 'x_hi'), split_axis=0, concat_axis=0)]
    ppermute x6 -> x5, waiting for transfers between devices: 6.18 us -> 12.9 us  [the longest x2 10.3 us: per_device(): lax.ppermute(far_near[0][start:stop], 'y', up)]
    slice x4 -> x3, local copies, waits for them, and re-layouts: 5.45 us -> 1.09 us  [the longest x2 1.07 us: per_device(): far_near[0][start:stop]]
    ppermute x6 -> x5, starting transfers between devices: 20.9 us -> 18.6 us  [the longest x2 7.05 us: per_device(): lax.ppermute(far_near[0][start:stop], 'y', up)]
    ppermute x2, starting transfers between devices: 8.14 us -> 9.67 us  [per_device(): came = lax.ppermute(far, 'x_hi', swap)]
  transfers between devices with their start and end apart: 15 -> 14, of which waited for: 7 -> 5; matrix products, arithmetic and copies ran while one was open for 15% -> 13% of each run, Pallas kernels for 9% -> 9%
where the time goes in v12:
time: 121 us; the launch traced here: 120 us
  starting transfers between devices  65.1 us (54%)
  waiting for transfers between devices  26.2 us (22%)
  Pallas kernels  10.7 us (9%)
  other arithmetic  9.55 us (8%)
  local copies, waits for them, and re-layouts  7.8 us (6%)
    all_to_all x1, starting transfers between devices, per_device(): lax.all_to_all(packed, ROW, split_axis=1, concat_axis=0, tiled=True)  11.8 us
    ppermute x2, waiting for transfers between devices, per_device(): lax.ppermute(far_near[0][start:stop], 'y', up)  10.3 us
    ppermute x2, starting transfers between devices, per_device(): came = lax.ppermute(far, 'x_hi', swap)  9.67 us
    all_to_all x1, starting transfers between devices, per_device(): got = lax.all_to_all(send, ('chip', 'x_hi'), split_axis=0, concat_axis=0)  9.05 us
    ppermute x2, starting transfers between devices, per_device(): lax.ppermute(block, 'y', route[sign])  7.51 us
    ppermute x2, starting transfers between devices, per_device(): lax.ppermute(far_near[0][start:stop], 'y', up)  7.05 us
    ppermute x2, starting transfers between devices, per_device(): lax.ppermute(panel_lower, 'y', route[sign])  6.61 us
    ppermute x1, starting transfers between devices, per_device(): last = [lax.ppermute(rising[0], 'y', up)]  5.69 us
  transfers between devices with their start and end apart: 14, of which 5 were waited for; matrix products, arithmetic and copies ran while one was open for 13% of the time, Pallas kernels for 9%

profile of v12, /device:TPU:24, one launch (start us, length us, event | category | flops | bytes accessed | tf_op | source)
XLA Modules:
  0.0 119.7 jit_solution(6131178203294941045)
XLA Ops:
  0.0 4.7 %collective-permute-start = (bf16[2048,256]{1,0:T(8,128)(2,1)}, bf16[2048,256]{1,0:T(8,128)(2,1)}, u32[]{:S(2)}, u32[]{:S(2)}) collective-permute-start(bf16[2048,256]{1,0:T(8,128)(2,1)} %refs_0_.1), channel_id=1, source_target_pairs={{0,1},{1,2},{2,3},{3,4},{4,5},{5,6},{6,7},{7,0},{8,9},{9,10},{10,1... | collective-permute-start | bytes 3145736 | tf_op jit(solution)/shard_map/ppermute | solution.py:144
  4.7 1.9 %collective-permute-start.1 = (bf16[2048,256]{1,0:T(8,128)(2,1)}, bf16[2048,256]{1,0:T(8,128)(2,1)}, u32[]{:S(2)}, u32[]{:S(2)}) collective-permute-start(bf16[2048,256]{1,0:T(8,128)(2,1)} %refs_0_.1), channel_id=1, source_target_pairs={{0,7},{1,0},{2,1},{3,2},{4,3},{5,4},{6,5},{7,6},{8,15},{9,8},{10,9... | collective-permute-start | bytes 3145736 | tf_op jit(solution)/shard_map/ppermute | solution.py:144
  8.2 1.4 %multiply_convert_fusion = bf16[2048,128]{1,0:T(8,128)(2,1)S(1)} fusion(bf16[2048,128]{1,0:T(8,128)(2,1)} %param.4, f32[2048]{0:T(1024)S(1)} %convert_element_type.57), kind=kLoop, calls=%fused_computation.4 | loop fusion | flops 786432 | bytes 1056768 | tf_op jit(solution)/shard_map/convert_element_type | solution.py:146
  9.6 1.0 copy.9
  10.7 11.8 %all-to-all-start = ((bf16[72,32,128]{2,0,1:T(8,128)(2,1)}), bf16[72,32,128]{2,0,1:T(8,128)(2,1)}, u32[]{:S(2)}, u32[]{:S(2)}) async-start(bf16[72,32,128]{2,0,1:T(8,128)(2,1)} %copy.9), calls=%async_computation | async-start | bytes 1179648 | tf_op jit(solution)/shard_map/all_to_all | solution.py:153
  22.4 5.0 %collective-permute-done = bf16[2048,256]{1,0:T(8,128)(2,1)} collective-permute-done((bf16[2048,256]{1,0:T(8,128)(2,1)}, bf16[2048,256]{1,0:T(8,128)(2,1)}, u32[]{:S(2)}, u32[]{:S(2)}) %collective-permute-start) | collective-permute-done | bytes 1048608 | tf_op jit(solution)/shard_map/ppermute | solution.py:144
  27.4 5.6 %collective-permute-start.3 = (bf16[2048,256]{1,0:T(8,128)(2,1)}, bf16[2048,256]{1,0:T(8,128)(2,1)S(1)}, u32[]{:S(2)}, u32[]{:S(2)}) collective-permute-start(bf16[2048,256]{1,0:T(8,128)(2,1)} %collective-permute-done), channel_id=1, source_target_pairs={{0,1},{1,2},{2,3},{3,4},{4,5},{5,6},{6,7},{7,0},{8,9},{9,10},{10,1... | collective-permute-start | bytes 3145736 | tf_op jit(solution)/shard_map/ppermute | solution.py:156
  33.0 1.9 %collective-permute-start.4 = (bf16[2048,256]{1,0:T(8,128)(2,1)}, bf16[2048,256]{1,0:T(8,128)(2,1)}, u32[]{:S(2)}, u32[]{:S(2)}) collective-permute-start(bf16[2048,256]{1,0:T(8,128)(2,1)} %collective-permute-done.1), channel_id=1, source_target_pairs={{0,7},{1,0},{2,1},{3,2},{4,3},{5,4},{6,5},{7,6},{8,15},{9,8},{10,9... | collective-permute-start | bytes 3145736 | tf_op jit(solution)/shard_map/ppermute | solution.py:156
  34.9 1.3 %constant_dynamic-update-slice_fusion.1 = bf16[2048,512]{1,0:T(8,128)(2,1)S(1)} fusion(bf16[2048,256]{1,0:T(8,128)(2,1)} %collective-permute-done), kind=kLoop, calls=%fused_computation.29 | loop fusion | bytes 2097152
  36.3 1.3 %constant_dynamic-update-slice_fusion.refs_1_ = bf16[2048,512]{1,0:T(8,128)(2,1)S(1)} fusion(bf16[2048,512]{1,0:T(8,128)(2,1)S(1)} %constant_dynamic-update-slice_fusion.1, bf16[2048,256]{1,0:T(8,128)(2,1)} %collective-permute-done.1), kind=kLoop, calls=%fused_computation.28 | loop fusion | bytes 2097152 | tf_op jit(solution)/shard_map/concatenate | solution.py:154
  37.6 4.3 %all-to-all-done = bf16[72,32,128]{2,0,1:T(8,128)(2,1)} async-done(((bf16[72,32,128]{2,0,1:T(8,128)(2,1)}), bf16[72,32,128]{2,0,1:T(8,128)(2,1)}, u32[]{:S(2)}, u32[]{:S(2)}) %all-to-all-start) | async-done | bytes 589856 | tf_op jit(solution)/shard_map/all_to_all | solution.py:153
  41.9 2.1 %fusion.3 = (f32[16,64,128]{2,1,0:T(8,128)}, f32[16,64,128]{2,1,0:T(8,128)}) fusion(bf16[32,72,128]{2,1,0:T(8,128)(2,1)} %bitcast.9), kind=kLoop, calls=%fused_computation.9 | loop fusion | flops 786432 | bytes 1572864 | tf_op jit(solution)/shard_map/mul | solution.py:22
  45.0 1.5 %fusion.1 = bf16[2048,128]{1,0:T(8,128)(2,1)S(1)} fusion(f32[1024,128]{1,0:T(8,128)} %bitcast.18, f32[1024,128]{1,0:T(8,128)} %bitcast.17, f32[2048]{0:T(1024)S(1)} %reshape.37), kind=kLoop, calls=%fused_computation.3 | loop fusion | flops 786432 | bytes 1581056 | tf_op jit(solution)/shard_map/convert_element_type | solution.py:166
  48.2 9.0 %all-to-all-start.1 = ((bf16[32,64,128]{2,1,0:T(8,128)(2,1)}), bf16[32,64,128]{2,1,0:T(8,128)(2,1)}, u32[]{:S(2)}, u32[]{:S(2)}) async-start(bf16[32,64,128]{2,1,0:T(8,128)(2,1)} %bitcast.19), calls=%async_computation.1 | async-start | bytes 1048576 | tf_op jit(solution)/shard_map/all_to_all | solution.py:180
  57.3 5.1 %collective-permute-start.5 = (bf16[1280,256]{1,0:T(8,128)(2,1)S(1)}, bf16[1280,256]{1,0:T(8,128)(2,1)}, u32[]{:S(2)}, u32[]{:S(2)}) collective-permute-start(bf16[1280,256]{1,0:T(8,128)(2,1)S(1)} %slice.58), channel_id=1, source_target_pairs={{0,1},{1,2},{2,3},{3,4},{4,5},{5,6},{6,7},{7,0},{8,9},{9,10},{10,1... | collective-permute-start | bytes 1966088 | tf_op jit(solution)/shard_map/ppermute | solution.py:158
  62.5 1.9 %collective-permute-start.6 = (bf16[2048,256]{1,0:T(8,128)(2,1)}, bf16[2048,256]{1,0:T(8,128)(2,1)S(1)}, u32[]{:S(2)}, u32[]{:S(2)}) collective-permute-start(bf16[2048,256]{1,0:T(8,128)(2,1)} %collective-permute-done.4.refs_3_), channel_id=1, source_target_pairs={{0,7},{1,0},{2,1},{3,2},{4,3},{5,4},{6,5},{7,6},{8,15},{9,8},{10,9... | collective-permute-start | bytes 3145736 | tf_op jit(solution)/shard_map/ppermute | solution.py:159
  64.4 10.3 %collective-permute-done.5.refs_4_ = bf16[1280,256]{1,0:T(8,128)(2,1)} collective-permute-done((bf16[1280,256]{1,0:T(8,128)(2,1)S(1)}, bf16[1280,256]{1,0:T(8,128)(2,1)}, u32[]{:S(2)}, u32[]{:S(2)}) %collective-permute-start.5) | collective-permute-done | bytes 655392 | tf_op jit(solution)/shard_map/ppermute | solution.py:158
  74.7 5.7 %collective-permute-start.7 = (bf16[1280,256]{1,0:T(8,128)(2,1)}, bf16[1280,256]{1,0:T(8,128)(2,1)}, u32[]{:S(2)}, u32[]{:S(2)}) collective-permute-start(bf16[1280,256]{1,0:T(8,128)(2,1)} %collective-permute-done.5.refs_4_), channel_id=1, source_target_pairs={{0,1},{1,2},{2,3},{3,4},{4,5},{5,6},{6,7},{7,0},{8,9},{9,10},{10,1... | collective-permute-start | bytes 1966088 | tf_op jit(solution)/shard_map/ppermute | solution.py:160
  80.5 1.9 %collective-permute-start.2 = (bf16[32,64,128]{2,1,0:T(8,128)(2,1)}, bf16[32,64,128]{2,1,0:T(8,128)(2,1)}, u32[]{:S(2)}, u32[]{:S(2)}) collective-permute-start(bf16[32,64,128]{2,1,0:T(8,128)(2,1)} %all-to-all-done.1.got_ref), channel_id=1, source_target_pairs={{0,16},{16,0},{1,17},{17,1},{2,18},{18,2},{3,19},{19,3},{4,20},{20... | collective-permute-start | bytes 1572872 | tf_op jit(solution)/shard_map/ppermute | solution.py:181
  82.5 1.0 pad_maximum_fusion.stored_ref
  83.5 1.0 slice.59
  84.5 1.9 %collective-permute-start.10 = (bf16[768,256]{1,0:T(8,128)(2,1)S(1)}, bf16[768,256]{1,0:T(8,128)(2,1)S(1)}, u32[]{:S(2)}, u32[]{:S(2)}) collective-permute-start(bf16[768,256]{1,0:T(8,128)(2,1)S(1)} %slice.59), channel_id=1, source_target_pairs={{0,1},{1,2},{2,3},{3,4},{4,5},{5,6},{6,7},{7,0},{8,9},{9,10},{10,1... | collective-permute-start | bytes 1179656 | tf_op jit(solution)/shard_map/ppermute | solution.py:158
  86.5 1.2 %copy-done.2 = bf16[2048,256]{1,0:T(8,128)(2,1)S(1)} copy-done((bf16[2048,256]{1,0:T(8,128)(2,1)S(1)}, bf16[2048,256]{1,0:T(8,128)(2,1)}, u32[]{:S(2)}) %copy-start.2) | copy-done | bytes 1048600
  87.7 5.5 %early_products.1 = (f32[1280,128]{1,0:T(8,128)S(1)}, f32[1280,128]{1,0:T(8,128)S(1)}, f32[768,128]{1,0:T(8,128)S(1)}, f32[768,128]{1,0:T(8,128)S(1)}, bf16[8,256,256]{2,1,0:T(8,128)(2,1)S(1)}) custom-call(s32[3]{0:T(128)S(1)} %pad_add_fusion.place_ref, bf16[32,64,128]{2,1,0:T(8,128)(2,1)} %all-to-all-done.1.got_ref, ...), custom_call_target="tpu_custom_call" | custom-call | tf_op jit(solution)/shard_map/early_products/pallas_call | solution.py:90
  93.2 3.9 %collective-permute-start.9 = (bf16[768,256]{1,0:T(8,128)(2,1)S(1)}, bf16[768,256]{1,0:T(8,128)(2,1)S(1)}, u32[]{:S(2)}, u32[]{:S(2)}) collective-permute-start(bf16[768,256]{1,0:T(8,128)(2,1)S(1)} %slice.48), channel_id=1, source_target_pairs={{0,7},{1,0},{2,1},{3,2},{4,3},{5,4},{6,5},{7,6},{8,15},{9,8},{10,9... | collective-permute-start | bytes 1179656 | tf_op jit(solution)/shard_map/ppermute | solution.py:195
  97.2 1.6 %last_far.2 = bf16[1280,128]{1,0:T(8,128)(2,1)S(1)} custom-call(s32[3]{0:T(128)S(1)} %pad_add_fusion.place_ref, bf16[8,256,256]{2,1,0:T(8,128)(2,1)S(1)} %get-tuple-element.13.upper_ref, f32[1280,128]{1,0:T(8,128)S(1)} %get-tuple-element.15.base_ref, bf16[2048,256]{1,0:T(8,128)(2,1)S(1)} %collective-permute-done.6.refs_0_, ...), custom_call_target="tpu_custom_call" | custom-call | tf_op jit(solution)/shard_map/last_far/pallas_call | solution.py:121
  98.8 4.8 %collective-permute-start.8 = (bf16[1280,128]{1,0:T(8,128)(2,1)S(1)}, bf16[1280,128]{1,0:T(8,128)(2,1)S(1)}, u32[]{:S(2)}, u32[]{:S(2)}) collective-permute-start(bf16[1280,128]{1,0:T(8,128)(2,1)S(1)} %last_far.2), channel_id=1, source_target_pairs={{0,8},{8,0},{1,9},{9,1},{2,10},{10,2},{3,11},{11,3},{4,12},{12,4},... | collective-permute-start | bytes 983048 | tf_op jit(solution)/shard_map/ppermute | solution.py:203
  103.6 1.6 %last_own.2 = f32[1280,128]{1,0:T(8,128)S(1)} custom-call(s32[3]{0:T(128)S(1)} %pad_add_fusion.place_ref, bf16[8,256,256]{2,1,0:T(8,128)(2,1)S(1)} %get-tuple-element.13.upper_ref, f32[1280,128]{1,0:T(8,128)S(1)} %get-tuple-element.14.base_ref, bf16[2048,256]{1,0:T(8,128)(2,1)S(1)} %collective-permute-done.6.refs_0_, ...), custom_call_target="tpu_custom_call" | custom-call | tf_op jit(solution)/shard_map/last_own/pallas_call | solution.py:121
  105.2 2.6 %collective-permute-done.9.refs_1_ = bf16[768,256]{1,0:T(8,128)(2,1)S(1)} collective-permute-done((bf16[768,256]{1,0:T(8,128)(2,1)S(1)}, bf16[768,256]{1,0:T(8,128)(2,1)S(1)}, u32[]{:S(2)}, u32[]{:S(2)}) %collective-permute-start.9) | collective-permute-done | bytes 393248 | tf_op jit(solution)/shard_map/ppermute | solution.py:195
  108.9 4.8 %collective-permute-start.11 = (bf16[768,128]{1,0:T(8,128)(2,1)S(1)}, bf16[768,128]{1,0:T(8,128)(2,1)S(1)}, u32[]{:S(2)}, u32[]{:S(2)}) collective-permute-start(bf16[768,128]{1,0:T(8,128)(2,1)S(1)} %last_far.3), channel_id=1, source_target_pairs={{0,8},{8,0},{1,9},{9,1},{2,10},{10,2},{3,11},{11,3},{4,12},{12,4},... | collective-permute-start | bytes 589832 | tf_op jit(solution)/shard_map/ppermute | solution.py:203
  113.7 1.0 last_own.3
  114.8 4.0 %collective-permute-done.11 = bf16[768,128]{1,0:T(8,128)(2,1)S(1)} collective-permute-done((bf16[768,128]{1,0:T(8,128)(2,1)S(1)}, bf16[768,128]{1,0:T(8,128)(2,1)S(1)}, u32[]{:S(2)}, u32[]{:S(2)}) %collective-permute-start.11) | collective-permute-done | bytes 196640 | tf_op jit(solution)/shard_map/ppermute | solution.py:203
  (30 shorter events, 6.4 us)
Async XLA Ops:
  0.0 27.4 %collective-permute-start = (bf16[2048,256]{1,0:T(8,128)(2,1)}, bf16[2048,256]{1,0:T(8,128)(2,1)}, u32[]{:S(2)}, u32[]{:S(2)}) collective-permute-start(bf16[2048,256]{1,0:T(8,128)(2,1)} %refs_0_.1), channel_id=1, source_target_pairs={{0,1},{1,2},{2,3},{3,4},{4,5},{5,6},{6,7},{7,0},{8,9},{9,10},{10,1... | collective-permute-start | bytes 3145736 | tf_op jit(solution)/shard_map/ppermute | solution.py:144
  4.7 28.3 %collective-permute-start.1 = (bf16[2048,256]{1,0:T(8,128)(2,1)}, bf16[2048,256]{1,0:T(8,128)(2,1)}, u32[]{:S(2)}, u32[]{:S(2)}) collective-permute-start(bf16[2048,256]{1,0:T(8,128)(2,1)} %refs_0_.1), channel_id=1, source_target_pairs={{0,7},{1,0},{2,1},{3,2},{4,3},{5,4},{6,5},{7,6},{8,15},{9,8},{10,9... | collective-permute-start | bytes 3145736 | tf_op jit(solution)/shard_map/ppermute | solution.py:144
  10.7 31.2 %all-to-all-start = ((bf16[72,32,128]{2,0,1:T(8,128)(2,1)}), bf16[72,32,128]{2,0,1:T(8,128)(2,1)}, u32[]{:S(2)}, u32[]{:S(2)}) async-start(bf16[72,32,128]{2,0,1:T(8,128)(2,1)} %copy.9), calls=%async_computation | async-start | bytes 1179648 | tf_op jit(solution)/shard_map/all_to_all | solution.py:153
  27.4 29.9 %collective-permute-start.3 = (bf16[2048,256]{1,0:T(8,128)(2,1)}, bf16[2048,256]{1,0:T(8,128)(2,1)S(1)}, u32[]{:S(2)}, u32[]{:S(2)}) collective-permute-start(bf16[2048,256]{1,0:T(8,128)(2,1)} %collective-permute-done), channel_id=1, source_target_pairs={{0,1},{1,2},{2,3},{3,4},{4,5},{5,6},{6,7},{7,0},{8,9},{9,10},{10,1... | collective-permute-start | bytes 3145736 | tf_op jit(solution)/shard_map/ppermute | solution.py:156
  33.0 29.5 %collective-permute-start.4 = (bf16[2048,256]{1,0:T(8,128)(2,1)}, bf16[2048,256]{1,0:T(8,128)(2,1)}, u32[]{:S(2)}, u32[]{:S(2)}) collective-permute-start(bf16[2048,256]{1,0:T(8,128)(2,1)} %collective-permute-done.1), channel_id=1, source_target_pairs={{0,7},{1,0},{2,1},{3,2},{4,3},{5,4},{6,5},{7,6},{8,15},{9,8},{10,9... | collective-permute-start | bytes 3145736 | tf_op jit(solution)/shard_map/ppermute | solution.py:156
  48.2 32.2 %all-to-all-start.1 = ((bf16[32,64,128]{2,1,0:T(8,128)(2,1)}), bf16[32,64,128]{2,1,0:T(8,128)(2,1)}, u32[]{:S(2)}, u32[]{:S(2)}) async-start(bf16[32,64,128]{2,1,0:T(8,128)(2,1)} %bitcast.19), calls=%async_computation.1 | async-start | bytes 1048576 | tf_op jit(solution)/shard_map/all_to_all | solution.py:180
  57.3 5.2 %copy-start = (bf16[2048,256]{1,0:T(8,128)(2,1)}, bf16[2048,256]{1,0:T(8,128)(2,1)S(1)}, u32[]{:S(2)}) copy-start(bf16[2048,256]{1,0:T(8,128)(2,1)S(1)} %collective-permute-done.3.refs_2_) | copy-start | bytes 3145732
  57.3 17.4 %collective-permute-start.5 = (bf16[1280,256]{1,0:T(8,128)(2,1)S(1)}, bf16[1280,256]{1,0:T(8,128)(2,1)}, u32[]{:S(2)}, u32[]{:S(2)}) collective-permute-start(bf16[1280,256]{1,0:T(8,128)(2,1)S(1)} %slice.58), channel_id=1, source_target_pairs={{0,1},{1,2},{2,3},{3,4},{4,5},{5,6},{6,7},{7,0},{8,9},{9,10},{10,1... | collective-permute-start | bytes 1966088 | tf_op jit(solution)/shard_map/ppermute | solution.py:158
  62.5 30.7 %collective-permute-start.6 = (bf16[2048,256]{1,0:T(8,128)(2,1)}, bf16[2048,256]{1,0:T(8,128)(2,1)S(1)}, u32[]{:S(2)}, u32[]{:S(2)}) collective-permute-start(bf16[2048,256]{1,0:T(8,128)(2,1)} %collective-permute-done.4.refs_3_), channel_id=1, source_target_pairs={{0,7},{1,0},{2,1},{3,2},{4,3},{5,4},{6,5},{7,6},{8,15},{9,8},{10,9... | collective-permute-start | bytes 3145736 | tf_op jit(solution)/shard_map/ppermute | solution.py:159
  74.7 22.4 %collective-permute-start.7 = (bf16[1280,256]{1,0:T(8,128)(2,1)}, bf16[1280,256]{1,0:T(8,128)(2,1)}, u32[]{:S(2)}, u32[]{:S(2)}) collective-permute-start(bf16[1280,256]{1,0:T(8,128)(2,1)} %collective-permute-done.5.refs_4_), channel_id=1, source_target_pairs={{0,1},{1,2},{2,3},{3,4},{4,5},{5,6},{6,7},{7,0},{8,9},{9,10},{10,1... | collective-permute-start | bytes 1966088 | tf_op jit(solution)/shard_map/ppermute | solution.py:160
  80.5 6.0 %collective-permute-start.2 = (bf16[32,64,128]{2,1,0:T(8,128)(2,1)}, bf16[32,64,128]{2,1,0:T(8,128)(2,1)}, u32[]{:S(2)}, u32[]{:S(2)}) collective-permute-start(bf16[32,64,128]{2,1,0:T(8,128)(2,1)} %all-to-all-done.1.got_ref), channel_id=1, source_target_pairs={{0,16},{16,0},{1,17},{17,1},{2,18},{18,2},{3,19},{19,3},{4,20},{20... | collective-permute-start | bytes 1572872 | tf_op jit(solution)/shard_map/ppermute | solution.py:181
  82.4 4.1 %copy-start.1 = (bf16[2048,256]{1,0:T(8,128)(2,1)S(1)}, bf16[2048,256]{1,0:T(8,128)(2,1)}, u32[]{:S(2)}) copy-start(bf16[2048,256]{1,0:T(8,128)(2,1)} %copy-done) | copy-start | bytes 3145732
  84.5 20.7 %collective-permute-start.10 = (bf16[768,256]{1,0:T(8,128)(2,1)S(1)}, bf16[768,256]{1,0:T(8,128)(2,1)S(1)}, u32[]{:S(2)}, u32[]{:S(2)}) collective-permute-start(bf16[768,256]{1,0:T(8,128)(2,1)S(1)} %slice.59), channel_id=1, source_target_pairs={{0,1},{1,2},{2,3},{3,4},{4,5},{5,6},{6,7},{7,0},{8,9},{9,10},{10,1... | collective-permute-start | bytes 1179656 | tf_op jit(solution)/shard_map/ppermute | solution.py:158
  86.5 1.2 %copy-start.2 = (bf16[2048,256]{1,0:T(8,128)(2,1)S(1)}, bf16[2048,256]{1,0:T(8,128)(2,1)}, u32[]{:S(2)}) copy-start(bf16[2048,256]{1,0:T(8,128)(2,1)} %refs_0_.1) | copy-start | bytes 3145732
  93.2 14.6 %collective-permute-start.9 = (bf16[768,256]{1,0:T(8,128)(2,1)S(1)}, bf16[768,256]{1,0:T(8,128)(2,1)S(1)}, u32[]{:S(2)}, u32[]{:S(2)}) collective-permute-start(bf16[768,256]{1,0:T(8,128)(2,1)S(1)} %slice.48), channel_id=1, source_target_pairs={{0,7},{1,0},{2,1},{3,2},{4,3},{5,4},{6,5},{7,6},{8,15},{9,8},{10,9... | collective-permute-start | bytes 1179656 | tf_op jit(solution)/shard_map/ppermute | solution.py:195
  98.8 15.9 %collective-permute-start.8 = (bf16[1280,128]{1,0:T(8,128)(2,1)S(1)}, bf16[1280,128]{1,0:T(8,128)(2,1)S(1)}, u32[]{:S(2)}, u32[]{:S(2)}) collective-permute-start(bf16[1280,128]{1,0:T(8,128)(2,1)S(1)} %last_far.2), channel_id=1, source_target_pairs={{0,8},{8,0},{1,9},{9,1},{2,10},{10,2},{3,11},{11,3},{4,12},{12,4},... | collective-permute-start | bytes 983048 | tf_op jit(solution)/shard_map/ppermute | solution.py:203
  108.9 9.9 %collective-permute-start.11 = (bf16[768,128]{1,0:T(8,128)(2,1)S(1)}, bf16[768,128]{1,0:T(8,128)(2,1)S(1)}, u32[]{:S(2)}, u32[]{:S(2)}) collective-permute-start(bf16[768,128]{1,0:T(8,128)(2,1)S(1)} %last_far.3), channel_id=1, source_target_pairs={{0,8},{8,0},{1,9},{9,1},{2,10},{10,2},{3,11},{11,3},{4,12},{12,4},... | collective-permute-start | bytes 589832 | tf_op jit(solution)/shard_map/ppermute | solution.py:203

commit v13 on v12

--- a/solution.py
+++ b/solution.py
@@ -16,12 +16,6 @@
 inv_root = 0.7071067811865476
 
 
-def butterfly(top, bottom):
-    top = top.astype(jnp.float32)
-    bottom = bottom.astype(jnp.float32)
-    return jnp.concatenate([(top + bottom) * inv_root, (top - bottom) * inv_root], axis=0)
-
-
 def after(value, *others):
     return lax.optimization_barrier((value, *others))[0]
 
@@ -35,6 +29,42 @@
 
 def whole():
     return pl.BlockSpec(memory_space=VM)
+
+
+def butterflies(packed, share, chips, top_count):
+    groups, _, width = packed.shape
+    quarter = groups // 4
+    rows = groups * share
+
+    def body(packed_ref, stored_ref, send_ref):
+        scale = jnp.transpose(packed_ref[:, share, :].astype(jnp.float32))
+        for d in range(quarter):
+            at = [d + n * quarter for n in range(4)]
+            one = [packed_ref[n, :share].astype(jnp.float32) for n in at]
+            two = [one[0] + one[2], one[1] + one[3], one[0] - one[2], one[1] - one[3]]
+            two = [
+                (scale[:share, n : n + 1] * (value * inv_root)).astype(packed.dtype).astype(jnp.float32)
+                for n, value in zip(at, two)
+            ]
+            out = [two[0] + two[1], two[0] - two[1], two[2] + two[3], two[2] - two[3]]
+            for n, value in zip(at, out):
+                stored_ref[n * share : (n + 1) * share] = (value * inv_root).astype(packed.dtype)
+        for x in range(X_HI):
+            top = stored_ref[x * top_count : (x + 1) * top_count]
+            for chip in range(chips):
+                send_ref[chip * X_HI + x] = top
+
+    return pl.pallas_call(
+        body,
+        in_specs=[whole()],
+        out_specs=[whole(), whole()],
+        out_shape=[
+            jax.ShapeDtypeStruct((rows, width), packed.dtype),
+            jax.ShapeDtypeStruct((chips * X_HI, top_count, width), packed.dtype),
+        ],
+        compiler_params=grant(8),
+        name="butterflies",
+    )(packed)
 
 
 def order_upper(core, got_ref, twin_ref, out_ref):
@@ -135,8 +165,6 @@
     y_count = lax.axis_size("y")
     block_width = panel_lower.shape[1]
     share = row_count // groups
-    half = row_count // 2
-    quarter = row_count // 4
 
     up = [(i, (i + 1) % y_count) for i in range(y_count)]
     down = [(i, (i - 1) % y_count) for i in range(y_count)]
@@ -159,24 +187,8 @@
     falling = lax.ppermute(far_near[1], "y", down)
     last = [lax.ppermute(rising[0], "y", up)]
     packed = packed.reshape(groups, share + PAD, col_width)
-    cyclic = packed[:, :share].reshape(row_count, col_width)
-    scale_cyclic = packed[:, share, :share].reshape(row_count)
-
-    level_one = butterfly(cyclic[:half], cyclic[half:])
-    second = (scale_cyclic.astype(jnp.float32)[:, None] * level_one).astype(jnp.bfloat16)
-    stored = jnp.concatenate(
-        [
-            butterfly(second[:quarter], second[quarter:half]),
-            butterfly(second[half : half + quarter], second[half + quarter :]),
-        ],
-        axis=0,
-    ).astype(jnp.bfloat16)
-
     top_count = PANEL_W // groups // X_HI
-    top = stored[: top_count * X_HI].reshape(1, X_HI, top_count, col_width)
-    send = jnp.broadcast_to(top, (chips, X_HI, top_count, col_width)).reshape(
-        chips * X_HI, top_count, col_width
-    )
+    stored, send = butterflies(packed, share, chips, top_count)
     got = lax.all_to_all(send, ("chip", "x_hi"), split_axis=0, concat_axis=0)
     twin = lax.ppermute(got, "core", [(0, 1), (1, 0)])
     place = jnp.stack([lax.axis_index(name) for name in ("x_hi", "y", "core")]).astype(jnp.int32)

time: 121 us -> 120 us (level)
  the two profiles are of different devices: /device:TPU:24 before, /device:TPU:472 now
where the time goes in v13:
time: 120 us; the launch traced here: 119 us
  starting transfers between devices  57.6 us (48%)
  waiting for transfers between devices  34.8 us (29%)
  Pallas kernels  12.2 us (10%)
  local copies, waits for them, and re-layouts  10.7 us (9%)
  other arithmetic  3.14 us (3%)
    ppermute x2, waiting for transfers between devices, per_device(): lax.ppermute(panel_lower, 'y', route[sign])  11 us
    ppermute x2, waiting for transfers between devices, per_device(): lax.ppermute(far_near[0][start:stop], 'y', up)  10.3 us
    ppermute x2, starting transfers between devices, per_device(): came = lax.ppermute(far, 'x_hi', swap)  9.67 us
    ppermute x2, starting transfers between devices, per_device(): lax.ppermute(block, 'y', route[sign])  7.51 us
    ppermute x2, starting transfers between devices, per_device(): lax.ppermute(far_near[0][start:stop], 'y', up)  7.42 us
    all_to_all x1, starting transfers between devices, per_device(): got = lax.all_to_all(send, ('chip', 'x_hi'), split_axis=0, concat_axis=0)  7.26 us
    ppermute x2, waiting for transfers between devices, per_device(): lax.ppermute(block, 'y', route[sign])  6.82 us
    ppermute x2, starting transfers between devices, per_device(): lax.ppermute(panel_lower, 'y', route[sign])  6.62 us
  transfers between devices with their start and end apart: 14, of which 5 were waited for; matrix products, arithmetic and copies ran while one was open for 7% of the time, Pallas kernels for 10%

profile of v13, /device:TPU:472, one launch (start us, length us, event | category | flops | bytes accessed | tf_op | source)
XLA Modules:
  0.0 118.8 jit_solution(4819531937629367154)
XLA Ops:
  0.0 4.7 %collective-permute-start = (bf16[2048,256]{1,0:T(8,128)(2,1)}, bf16[2048,256]{1,0:T(8,128)(2,1)}, u32[]{:S(2)}, u32[]{:S(2)}) collective-permute-start(bf16[2048,256]{1,0:T(8,128)(2,1)} %refs_0_.1), channel_id=1, source_target_pairs={{0,1},{1,2},{2,3},{3,4},{4,5},{5,6},{6,7},{7,0},{8,9},{9,10},{10,1... | collective-permute-start | bytes 3145736 | tf_op jit(solution)/shard_map/ppermute | solution.py:172
  4.7 1.9 %collective-permute-start.1 = (bf16[2048,256]{1,0:T(8,128)(2,1)}, bf16[2048,256]{1,0:T(8,128)(2,1)}, u32[]{:S(2)}, u32[]{:S(2)}) collective-permute-start(bf16[2048,256]{1,0:T(8,128)(2,1)} %refs_0_.1), channel_id=1, source_target_pairs={{0,7},{1,0},{2,1},{3,2},{4,3},{5,4},{6,5},{7,6},{8,15},{9,8},{10,9... | collective-permute-start | bytes 3145736 | tf_op jit(solution)/shard_map/ppermute | solution.py:172
  8.2 1.4 %multiply_convert_fusion = bf16[2048,128]{1,0:T(8,128)(2,1)S(1)} fusion(bf16[2048,128]{1,0:T(8,128)(2,1)} %param.4, f32[2048]{0:T(1024)S(1)} %convert_element_type.23), kind=kLoop, calls=%fused_computation.2 | loop fusion | flops 786432 | bytes 1056768 | tf_op jit(solution)/shard_map/convert_element_type | solution.py:174
  9.6 1.0 copy.10
  10.7 5.7 %all-to-all-start = ((bf16[72,32,128]{2,0,1:T(8,128)(2,1)}), bf16[72,32,128]{2,0,1:T(8,128)(2,1)}, u32[]{:S(2)}, u32[]{:S(2)}) async-start(bf16[72,32,128]{2,0,1:T(8,128)(2,1)} %copy.10), calls=%async_computation | async-start | bytes 1179648 | tf_op jit(solution)/shard_map/all_to_all | solution.py:181
  16.4 11.0 %collective-permute-done = bf16[2048,256]{1,0:T(8,128)(2,1)} collective-permute-done((bf16[2048,256]{1,0:T(8,128)(2,1)}, bf16[2048,256]{1,0:T(8,128)(2,1)}, u32[]{:S(2)}, u32[]{:S(2)}) %collective-permute-start) | collective-permute-done | bytes 1048608 | tf_op jit(solution)/shard_map/ppermute | solution.py:172
  27.4 5.6 %collective-permute-start.3 = (bf16[2048,256]{1,0:T(8,128)(2,1)}, bf16[2048,256]{1,0:T(8,128)(2,1)S(1)}, u32[]{:S(2)}, u32[]{:S(2)}) collective-permute-start(bf16[2048,256]{1,0:T(8,128)(2,1)} %collective-permute-done), channel_id=1, source_target_pairs={{0,1},{1,2},{2,3},{3,4},{4,5},{5,6},{6,7},{7,0},{8,9},{9,10},{10,1... | collective-permute-start | bytes 3145736 | tf_op jit(solution)/shard_map/ppermute | solution.py:184
  33.0 1.9 %collective-permute-start.4 = (bf16[2048,256]{1,0:T(8,128)(2,1)}, bf16[2048,256]{1,0:T(8,128)(2,1)}, u32[]{:S(2)}, u32[]{:S(2)}) collective-permute-start(bf16[2048,256]{1,0:T(8,128)(2,1)} %collective-permute-done.1), channel_id=1, source_target_pairs={{0,7},{1,0},{2,1},{3,2},{4,3},{5,4},{6,5},{7,6},{8,15},{9,8},{10,9... | collective-permute-start | bytes 3145736 | tf_op jit(solution)/shard_map/ppermute | solution.py:184
  35.0 1.3 %constant_dynamic-update-slice_fusion.1 = bf16[2048,512]{1,0:T(8,128)(2,1)S(1)} fusion(bf16[2048,256]{1,0:T(8,128)(2,1)} %collective-permute-done), kind=kLoop, calls=%fused_computation.8 | loop fusion | bytes 2097152
  36.3 1.3 %constant_dynamic-update-slice_fusion.refs_1_ = bf16[2048,512]{1,0:T(8,128)(2,1)S(1)} fusion(bf16[2048,512]{1,0:T(8,128)(2,1)S(1)} %constant_dynamic-update-slice_fusion.1, bf16[2048,256]{1,0:T(8,128)(2,1)} %collective-permute-done.1), kind=kLoop, calls=%fused_computation.7 | loop fusion | bytes 2097152 | tf_op jit(solution)/shard_map/concatenate | solution.py:182
  37.6 1.6 %butterflies.1 = (bf16[2048,128]{1,0:T(8,128)(2,1)S(1)}, bf16[32,64,128]{2,1,0:T(8,128)(2,1)S(1)}) custom-call(bf16[32,72,128]{2,1,0:T(8,128)(2,1)} %bitcast.9.packed_ref), custom_call_target="tpu_custom_call" | custom-call | tf_op jit(solution)/shard_map/butterflies/pallas_call | solution.py:57
  40.8 7.3 %all-to-all-start.1 = ((bf16[32,64,128]{2,1,0:T(8,128)(2,1)}), bf16[32,64,128]{2,1,0:T(8,128)(2,1)}, u32[]{:S(2)}, u32[]{:S(2)}) async-start(bf16[32,64,128]{2,1,0:T(8,128)(2,1)} %copy-done.5), calls=%async_computation.1 | async-start | bytes 1048576 | tf_op jit(solution)/shard_map/all_to_all | solution.py:192
  48.0 6.8 %collective-permute-done.3.refs_2_ = bf16[2048,256]{1,0:T(8,128)(2,1)S(1)} collective-permute-done((bf16[2048,256]{1,0:T(8,128)(2,1)}, bf16[2048,256]{1,0:T(8,128)(2,1)S(1)}, u32[]{:S(2)}, u32[]{:S(2)}) %collective-permute-start.3) | collective-permute-done | bytes 1048608 | tf_op jit(solution)/shard_map/ppermute | solution.py:184
  54.9 5.5 %collective-permute-start.5 = (bf16[1280,256]{1,0:T(8,128)(2,1)S(1)}, bf16[1280,256]{1,0:T(8,128)(2,1)}, u32[]{:S(2)}, u32[]{:S(2)}) collective-permute-start(bf16[1280,256]{1,0:T(8,128)(2,1)S(1)} %slice.12), channel_id=1, source_target_pairs={{0,1},{1,2},{2,3},{3,4},{4,5},{5,6},{6,7},{7,0},{8,9},{9,10},{10,1... | collective-permute-start | bytes 1966088 | tf_op jit(solution)/shard_map/ppermute | solution.py:186
  60.4 1.9 %collective-permute-start.6 = (bf16[2048,256]{1,0:T(8,128)(2,1)}, bf16[2048,256]{1,0:T(8,128)(2,1)S(1)}, u32[]{:S(2)}, u32[]{:S(2)}) collective-permute-start(bf16[2048,256]{1,0:T(8,128)(2,1)} %collective-permute-done.4.refs_3_), channel_id=1, source_target_pairs={{0,7},{1,0},{2,1},{3,2},{4,3},{5,4},{6,5},{7,6},{8,15},{9,8},{10,9... | collective-permute-start | bytes 3145736 | tf_op jit(solution)/shard_map/ppermute | solution.py:187
  62.4 10.3 %collective-permute-done.5.refs_4_ = bf16[1280,256]{1,0:T(8,128)(2,1)} collective-permute-done((bf16[1280,256]{1,0:T(8,128)(2,1)S(1)}, bf16[1280,256]{1,0:T(8,128)(2,1)}, u32[]{:S(2)}, u32[]{:S(2)}) %collective-permute-start.5) | collective-permute-done | bytes 655392 | tf_op jit(solution)/shard_map/ppermute | solution.py:186
  72.7 5.7 %collective-permute-start.7 = (bf16[1280,256]{1,0:T(8,128)(2,1)}, bf16[1280,256]{1,0:T(8,128)(2,1)}, u32[]{:S(2)}, u32[]{:S(2)}) collective-permute-start(bf16[1280,256]{1,0:T(8,128)(2,1)} %collective-permute-done.5.refs_4_), channel_id=1, source_target_pairs={{0,1},{1,2},{2,3},{3,4},{4,5},{5,6},{6,7},{7,0},{8,9},{9,10},{10,1... | collective-permute-start | bytes 1966088 | tf_op jit(solution)/shard_map/ppermute | solution.py:188
  78.4 1.9 %collective-permute-start.2 = (bf16[32,64,128]{2,1,0:T(8,128)(2,1)}, bf16[32,64,128]{2,1,0:T(8,128)(2,1)}, u32[]{:S(2)}, u32[]{:S(2)}) collective-permute-start(bf16[32,64,128]{2,1,0:T(8,128)(2,1)} %all-to-all-done.1.got_ref), channel_id=1, source_target_pairs={{0,16},{16,0},{1,17},{17,1},{2,18},{18,2},{3,19},{19,3},{4,20},{20... | collective-permute-start | bytes 1572872 | tf_op jit(solution)/shard_map/ppermute | solution.py:193
  80.4 1.0 slice.13
  81.5 1.9 %collective-permute-start.10 = (bf16[768,256]{1,0:T(8,128)(2,1)S(1)}, bf16[768,256]{1,0:T(8,128)(2,1)S(1)}, u32[]{:S(2)}, u32[]{:S(2)}) collective-permute-start(bf16[768,256]{1,0:T(8,128)(2,1)S(1)} %slice.13), channel_id=1, source_target_pairs={{0,1},{1,2},{2,3},{3,4},{4,5},{5,6},{6,7},{7,0},{8,9},{9,10},{10,1... | collective-permute-start | bytes 1179656 | tf_op jit(solution)/shard_map/ppermute | solution.py:186
  83.4 1.2 %copy-done.1 = bf16[2048,256]{1,0:T(8,128)(2,1)S(1)} copy-done((bf16[2048,256]{1,0:T(8,128)(2,1)S(1)}, bf16[2048,256]{1,0:T(8,128)(2,1)}, u32[]{:S(2)}) %copy-start.1) | copy-done | bytes 1048600
  84.6 1.2 %copy-done.2 = bf16[2048,256]{1,0:T(8,128)(2,1)S(1)} copy-done((bf16[2048,256]{1,0:T(8,128)(2,1)S(1)}, bf16[2048,256]{1,0:T(8,128)(2,1)}, u32[]{:S(2)}) %copy-start.2) | copy-done | bytes 1048600
  85.8 1.0 copy-done.4
  86.9 5.4 %early_products.1 = (f32[1280,128]{1,0:T(8,128)S(1)}, f32[1280,128]{1,0:T(8,128)S(1)}, f32[768,128]{1,0:T(8,128)S(1)}, f32[768,128]{1,0:T(8,128)S(1)}, bf16[8,256,256]{2,1,0:T(8,128)(2,1)S(1)}) custom-call(s32[3]{0:T(128)S(1)} %pad_add_fusion.place_ref, bf16[32,64,128]{2,1,0:T(8,128)(2,1)} %all-to-all-done.1.got_ref, ...), custom_call_target="tpu_custom_call" | custom-call | tf_op jit(solution)/shard_map/early_products/pallas_call | solution.py:120
  92.4 3.9 %collective-permute-start.9 = (bf16[768,256]{1,0:T(8,128)(2,1)S(1)}, bf16[768,256]{1,0:T(8,128)(2,1)S(1)}, u32[]{:S(2)}, u32[]{:S(2)}) collective-permute-start(bf16[768,256]{1,0:T(8,128)(2,1)S(1)} %slice.10), channel_id=1, source_target_pairs={{0,7},{1,0},{2,1},{3,2},{4,3},{5,4},{6,5},{7,6},{8,15},{9,8},{10,9... | collective-permute-start | bytes 1179656 | tf_op jit(solution)/shard_map/ppermute | solution.py:207
  96.3 1.6 %last_far.2 = bf16[1280,128]{1,0:T(8,128)(2,1)S(1)} custom-call(s32[3]{0:T(128)S(1)} %pad_add_fusion.place_ref, bf16[8,256,256]{2,1,0:T(8,128)(2,1)S(1)} %get-tuple-element.17.upper_ref, f32[1280,128]{1,0:T(8,128)S(1)} %get-tuple-element.19.base_ref, bf16[2048,256]{1,0:T(8,128)(2,1)S(1)} %collective-permute-done.6.refs_0_, ...), custom_call_target="tpu_custom_call" | custom-call | tf_op jit(solution)/shard_map/last_far/pallas_call | solution.py:151
  97.9 4.8 %collective-permute-start.8 = (bf16[1280,128]{1,0:T(8,128)(2,1)S(1)}, bf16[1280,128]{1,0:T(8,128)(2,1)S(1)}, u32[]{:S(2)}, u32[]{:S(2)}) collective-permute-start(bf16[1280,128]{1,0:T(8,128)(2,1)S(1)} %last_far.2), channel_id=1, source_target_pairs={{0,8},{8,0},{1,9},{9,1},{2,10},{10,2},{3,11},{11,3},{4,12},{12,4},... | collective-permute-start | bytes 983048 | tf_op jit(solution)/shard_map/ppermute | solution.py:215
  102.8 1.6 %last_own.2 = f32[1280,128]{1,0:T(8,128)S(1)} custom-call(s32[3]{0:T(128)S(1)} %pad_add_fusion.place_ref, bf16[8,256,256]{2,1,0:T(8,128)(2,1)S(1)} %get-tuple-element.17.upper_ref, f32[1280,128]{1,0:T(8,128)S(1)} %get-tuple-element.18.base_ref, bf16[2048,256]{1,0:T(8,128)(2,1)S(1)} %collective-permute-done.6.refs_0_, ...), custom_call_target="tpu_custom_call" | custom-call | tf_op jit(solution)/shard_map/last_own/pallas_call | solution.py:151
  104.4 2.6 %collective-permute-done.9.refs_1_ = bf16[768,256]{1,0:T(8,128)(2,1)S(1)} collective-permute-done((bf16[768,256]{1,0:T(8,128)(2,1)S(1)}, bf16[768,256]{1,0:T(8,128)(2,1)S(1)}, u32[]{:S(2)}, u32[]{:S(2)}) %collective-permute-start.9) | collective-permute-done | bytes 393248 | tf_op jit(solution)/shard_map/ppermute | solution.py:207
  108.0 4.8 %collective-permute-start.11 = (bf16[768,128]{1,0:T(8,128)(2,1)S(1)}, bf16[768,128]{1,0:T(8,128)(2,1)S(1)}, u32[]{:S(2)}, u32[]{:S(2)}) collective-permute-start(bf16[768,128]{1,0:T(8,128)(2,1)S(1)} %last_far.3), channel_id=1, source_target_pairs={{0,8},{8,0},{1,9},{9,1},{2,10},{10,2},{3,11},{11,3},{4,12},{12,4},... | collective-permute-start | bytes 589832 | tf_op jit(solution)/shard_map/ppermute | solution.py:215
  112.9 1.0 last_own.3
  114.0 4.0 %collective-permute-done.11 = bf16[768,128]{1,0:T(8,128)(2,1)S(1)} collective-permute-done((bf16[768,128]{1,0:T(8,128)(2,1)S(1)}, bf16[768,128]{1,0:T(8,128)(2,1)S(1)}, u32[]{:S(2)}, u32[]{:S(2)}) %collective-permute-start.11) | collective-permute-done | bytes 196640 | tf_op jit(solution)/shard_map/ppermute | solution.py:215
  (29 shorter events, 5.3 us)
Async XLA Ops:
  0.0 27.4 %collective-permute-start = (bf16[2048,256]{1,0:T(8,128)(2,1)}, bf16[2048,256]{1,0:T(8,128)(2,1)}, u32[]{:S(2)}, u32[]{:S(2)}) collective-permute-start(bf16[2048,256]{1,0:T(8,128)(2,1)} %refs_0_.1), channel_id=1, source_target_pairs={{0,1},{1,2},{2,3},{3,4},{4,5},{5,6},{6,7},{7,0},{8,9},{9,10},{10,1... | collective-permute-start | bytes 3145736 | tf_op jit(solution)/shard_map/ppermute | solution.py:172
  4.7 28.3 %collective-permute-start.1 = (bf16[2048,256]{1,0:T(8,128)(2,1)}, bf16[2048,256]{1,0:T(8,128)(2,1)}, u32[]{:S(2)}, u32[]{:S(2)}) collective-permute-start(bf16[2048,256]{1,0:T(8,128)(2,1)} %refs_0_.1), channel_id=1, source_target_pairs={{0,7},{1,0},{2,1},{3,2},{4,3},{5,4},{6,5},{7,6},{8,15},{9,8},{10,9... | collective-permute-start | bytes 3145736 | tf_op jit(solution)/shard_map/ppermute | solution.py:172
  10.7 26.9 %all-to-all-start = ((bf16[72,32,128]{2,0,1:T(8,128)(2,1)}), bf16[72,32,128]{2,0,1:T(8,128)(2,1)}, u32[]{:S(2)}, u32[]{:S(2)}) async-start(bf16[72,32,128]{2,0,1:T(8,128)(2,1)} %copy.10), calls=%async_computation | async-start | bytes 1179648 | tf_op jit(solution)/shard_map/all_to_all | solution.py:181
  27.4 27.4 %collective-permute-start.3 = (bf16[2048,256]{1,0:T(8,128)(2,1)}, bf16[2048,256]{1,0:T(8,128)(2,1)S(1)}, u32[]{:S(2)}, u32[]{:S(2)}) collective-permute-start(bf16[2048,256]{1,0:T(8,128)(2,1)} %collective-permute-done), channel_id=1, source_target_pairs={{0,1},{1,2},{2,3},{3,4},{4,5},{5,6},{6,7},{7,0},{8,9},{9,10},{10,1... | collective-permute-start | bytes 3145736 | tf_op jit(solution)/shard_map/ppermute | solution.py:184
  33.0 27.4 %collective-permute-start.4 = (bf16[2048,256]{1,0:T(8,128)(2,1)}, bf16[2048,256]{1,0:T(8,128)(2,1)}, u32[]{:S(2)}, u32[]{:S(2)}) collective-permute-start(bf16[2048,256]{1,0:T(8,128)(2,1)} %collective-permute-done.1), channel_id=1, source_target_pairs={{0,7},{1,0},{2,1},{3,2},{4,3},{5,4},{6,5},{7,6},{8,15},{9,8},{10,9... | collective-permute-start | bytes 3145736 | tf_op jit(solution)/shard_map/ppermute | solution.py:184
  39.2 0.8 copy-start.3
  40.0 0.8 copy-start.5
  40.8 37.6 %all-to-all-start.1 = ((bf16[32,64,128]{2,1,0:T(8,128)(2,1)}), bf16[32,64,128]{2,1,0:T(8,128)(2,1)}, u32[]{:S(2)}, u32[]{:S(2)}) async-start(bf16[32,64,128]{2,1,0:T(8,128)(2,1)} %copy-done.5), calls=%async_computation.1 | async-start | bytes 1048576 | tf_op jit(solution)/shard_map/all_to_all | solution.py:192
  54.9 5.6 %copy-start = (bf16[2048,256]{1,0:T(8,128)(2,1)}, bf16[2048,256]{1,0:T(8,128)(2,1)S(1)}, u32[]{:S(2)}) copy-start(bf16[2048,256]{1,0:T(8,128)(2,1)S(1)} %collective-permute-done.3.refs_2_) | copy-start | bytes 3145732
  54.9 17.8 %collective-permute-start.5 = (bf16[1280,256]{1,0:T(8,128)(2,1)S(1)}, bf16[1280,256]{1,0:T(8,128)(2,1)}, u32[]{:S(2)}, u32[]{:S(2)}) collective-permute-start(bf16[1280,256]{1,0:T(8,128)(2,1)S(1)} %slice.12), channel_id=1, source_target_pairs={{0,1},{1,2},{2,3},{3,4},{4,5},{5,6},{6,7},{7,0},{8,9},{9,10},{10,1... | collective-permute-start | bytes 1966088 | tf_op jit(solution)/shard_map/ppermute | solution.py:186
  60.4 31.9 %collective-permute-start.6 = (bf16[2048,256]{1,0:T(8,128)(2,1)}, bf16[2048,256]{1,0:T(8,128)(2,1)S(1)}, u32[]{:S(2)}, u32[]{:S(2)}) collective-permute-start(bf16[2048,256]{1,0:T(8,128)(2,1)} %collective-permute-done.4.refs_3_), channel_id=1, source_target_pairs={{0,7},{1,0},{2,1},{3,2},{4,3},{5,4},{6,5},{7,6},{8,15},{9,8},{10,9... | collective-permute-start | bytes 3145736 | tf_op jit(solution)/shard_map/ppermute | solution.py:187
  72.7 23.6 %collective-permute-start.7 = (bf16[1280,256]{1,0:T(8,128)(2,1)}, bf16[1280,256]{1,0:T(8,128)(2,1)}, u32[]{:S(2)}, u32[]{:S(2)}) collective-permute-start(bf16[1280,256]{1,0:T(8,128)(2,1)} %collective-permute-done.5.refs_4_), channel_id=1, source_target_pairs={{0,1},{1,2},{2,3},{3,4},{4,5},{5,6},{6,7},{7,0},{8,9},{9,10},{10,1... | collective-permute-start | bytes 1966088 | tf_op jit(solution)/shard_map/ppermute | solution.py:188
  78.4 5.0 %collective-permute-start.2 = (bf16[32,64,128]{2,1,0:T(8,128)(2,1)}, bf16[32,64,128]{2,1,0:T(8,128)(2,1)}, u32[]{:S(2)}, u32[]{:S(2)}) collective-permute-start(bf16[32,64,128]{2,1,0:T(8,128)(2,1)} %all-to-all-done.1.got_ref), channel_id=1, source_target_pairs={{0,16},{16,0},{1,17},{17,1},{2,18},{18,2},{3,19},{19,3},{4,20},{20... | collective-permute-start | bytes 1572872 | tf_op jit(solution)/shard_map/ppermute | solution.py:193
  81.5 22.9 %collective-permute-start.10 = (bf16[768,256]{1,0:T(8,128)(2,1)S(1)}, bf16[768,256]{1,0:T(8,128)(2,1)S(1)}, u32[]{:S(2)}, u32[]{:S(2)}) collective-permute-start(bf16[768,256]{1,0:T(8,128)(2,1)S(1)} %slice.13), channel_id=1, source_target_pairs={{0,1},{1,2},{2,3},{3,4},{4,5},{5,6},{6,7},{7,0},{8,9},{9,10},{10,1... | collective-permute-start | bytes 1179656 | tf_op jit(solution)/shard_map/ppermute | solution.py:186
  83.4 1.2 %copy-start.1 = (bf16[2048,256]{1,0:T(8,128)(2,1)S(1)}, bf16[2048,256]{1,0:T(8,128)(2,1)}, u32[]{:S(2)}) copy-start(bf16[2048,256]{1,0:T(8,128)(2,1)} %copy-done) | copy-start | bytes 3145732
  84.6 1.2 %copy-start.2 = (bf16[2048,256]{1,0:T(8,128)(2,1)S(1)}, bf16[2048,256]{1,0:T(8,128)(2,1)}, u32[]{:S(2)}) copy-start(bf16[2048,256]{1,0:T(8,128)(2,1)} %refs_0_.1) | copy-start | bytes 3145732
  85.8 1.0 copy-start.4
  92.4 14.6 %collective-permute-start.9 = (bf16[768,256]{1,0:T(8,128)(2,1)S(1)}, bf16[768,256]{1,0:T(8,128)(2,1)S(1)}, u32[]{:S(2)}, u32[]{:S(2)}) collective-permute-start(bf16[768,256]{1,0:T(8,128)(2,1)S(1)} %slice.10), channel_id=1, source_target_pairs={{0,7},{1,0},{2,1},{3,2},{4,3},{5,4},{6,5},{7,6},{8,15},{9,8},{10,9... | collective-permute-start | bytes 1179656 | tf_op jit(solution)/shard_map/ppermute | solution.py:207
  97.9 15.9 %collective-permute-start.8 = (bf16[1280,128]{1,0:T(8,128)(2,1)S(1)}, bf16[1280,128]{1,0:T(8,128)(2,1)S(1)}, u32[]{:S(2)}, u32[]{:S(2)}) collective-permute-start(bf16[1280,128]{1,0:T(8,128)(2,1)S(1)} %last_far.2), channel_id=1, source_target_pairs={{0,8},{8,0},{1,9},{9,1},{2,10},{10,2},{3,11},{11,3},{4,12},{12,4},... | collective-permute-start | bytes 983048 | tf_op jit(solution)/shard_map/ppermute | solution.py:215
  108.0 9.9 %collective-permute-start.11 = (bf16[768,128]{1,0:T(8,128)(2,1)S(1)}, bf16[768,128]{1,0:T(8,128)(2,1)S(1)}, u32[]{:S(2)}, u32[]{:S(2)}) collective-permute-start(bf16[768,128]{1,0:T(8,128)(2,1)S(1)} %last_far.3), channel_id=1, source_target_pairs={{0,8},{8,0},{1,9},{9,1},{2,10},{10,2},{3,11},{11,3},{4,12},{12,4},... | collective-permute-start | bytes 589832 | tf_op jit(solution)/shard_map/ppermute | solution.py:215

commit v14 on v13

--- a/solution.py
+++ b/solution.py
@@ -89,15 +89,24 @@
     depth, both = blocks[0].shape[1], X_HI * width
     parts = len(bounds)
     common = len(offsets) * depth
+    starts = [sum(block.shape[1] for block in blocks[:n]) for n in range(len(blocks))]
 
     def body(place_ref, got_ref, twin_ref, stored_ref, *refs):
-        block_refs, own_ref, out_refs = refs[: len(blocks)], refs[len(blocks)], refs[len(blocks) + 1 : -2]
-        upper_ref, turned = refs[-2:]
+        block_refs, own_ref, out_refs = refs[: len(blocks)], refs[len(blocks)], refs[len(blocks) + 1 : -4]
+        upper_ref, turned, here, arrived = refs[-4:]
+        copies = [
+            pltpu.make_async_copy(ref, here.at[:, at : at + ref.shape[1]], arrived.at[n])
+            for n, (ref, at) in enumerate(zip(block_refs, starts))
+        ]
+        for copy in copies:
+            copy.start()
         order_upper(place_ref[2], got_ref, twin_ref, upper_ref)
         for n, offset in enumerate(offsets):
             turned[n * depth : (n + 1) * depth] = upper_ref[(place_ref[1] + offset + y_count) % y_count]
         turned[common:] = upper_ref[(place_ref[1] + own_offset + y_count) % y_count]
         at_left = place_ref[0] == 0
+        for copy in copies:
+            copy.wait()
 
         for part, (start, stop) in enumerate(bounds):
             far_ref, rest_ref = out_refs[2 * part : 2 * part + 2]
@@ -105,7 +114,7 @@
             def one(i, carry):
                 local = pl.ds(pl.multiple_of(i * TILE_M, TILE_M), TILE_M)
                 full = pl.ds(pl.multiple_of(start + i * TILE_M, TILE_M), TILE_M)
-                tiles = [ref[full] for ref in block_refs]
+                tiles = [here[full]]
                 if part == 0:
                     tiles.append(own_ref[local])
                 depth_here = sum(tile.shape[1] for tile in tiles)
@@ -119,12 +128,19 @@
 
     return pl.pallas_call(
         body,
-        in_specs=[pl.BlockSpec(memory_space=pltpu.SMEM)] + [whole()] * (4 + len(blocks)),
+        in_specs=[pl.BlockSpec(memory_space=pltpu.SMEM)]
+        + [whole()] * 3
+        + [pl.BlockSpec(memory_space=pltpu.HBM)] * len(blocks)
+        + [whole()],
         out_specs=[whole()] * (2 * parts + 1),
         out_shape=[jax.ShapeDtypeStruct((b - a, width), jnp.float32) for a, b in bounds for _ in range(2)]
         + [jax.ShapeDtypeStruct((y_count, depth, both), stored.dtype)],
-        scratch_shapes=[VM((common + depth, both), stored.dtype)],
-        compiler_params=grant(16),
+        scratch_shapes=[
+            VM((common + depth, both), stored.dtype),
+            VM((rows, common), stored.dtype),
+            pltpu.SemaphoreType.DMA((len(blocks),)),
+        ],
+        compiler_params=grant(48),
         name="early_products",
     )(place, got, twin, stored, *blocks, own_block)
 

time: 120 us -> 119 us (level)
  local copies, waits for them, and re-layouts: 10.7 us -> 8.58 us
    unnamed x13 -> x3, local copies, waits for them, and re-layouts: 6.39 us -> 3.28 us
    pallas_call x1, Pallas kernels: 5.45 us -> 7.01 us  [early_products(): pl.pallas_call(body, in_specs=[pl.BlockSpec(memory_space=pltpu.SMEM)] + [...]
  transfers between devices with their start and end apart: 14 -> 14, of which waited for: 5 -> 5; matrix products, arithmetic and copies ran while one was open for 7% -> 8% of each run, Pallas kernels for 10% -> 10%
where the time goes in v14:
time: 119 us; the launch traced here: 118 us
  starting transfers between devices  57.7 us (48%)
  waiting for transfers between devices  35.8 us (30%)
  Pallas kernels  12.2 us (10%)
  local copies, waits for them, and re-layouts  8.58 us (7%)
  other arithmetic  3.14 us (3%)
    ppermute x2, waiting for transfers between devices, per_device(): lax.ppermute(panel_lower, 'y', route[sign])  11 us
    ppermute x2, waiting for transfers between devices, per_device(): lax.ppermute(far_near[0][start:stop], 'y', up)  10.2 us
    ppermute x2, starting transfers between devices, per_device(): came = lax.ppermute(far, 'x_hi', swap)  9.89 us
    ppermute x2, starting transfers between devices, per_device(): lax.ppermute(block, 'y', route[sign])  7.51 us
    ppermute x2, starting transfers between devices, per_device(): lax.ppermute(far_near[0][start:stop], 'y', up)  7.42 us
    all_to_all x1, starting transfers between devices, per_device(): got = lax.all_to_all(send, ('chip', 'x_hi'), split_axis=0, concat_axis=0)  7.2 us
    pallas_call x1, Pallas kernels, early_products(): pl.pallas_call(body, in_specs=[pl.BlockSpec(memory_space=pltpu.SMEM)] + [...  7.01 us
    ppermute x2, waiting for transfers between devices, per_device(): lax.ppermute(block, 'y', route[sign])  6.99 us
  transfers between devices with their start and end apart: 14, of which 5 were waited for; matrix products, arithmetic and copies ran while one was open for 8% of the time, Pallas kernels for 10%

profile of v14, /device:TPU:472, one launch (start us, length us, event | category | flops | bytes accessed | tf_op | source)
XLA Modules:
  0.0 117.7 jit_solution(1356963948960382304)
XLA Ops:
  0.0 4.7 %collective-permute-start = (bf16[2048,256]{1,0:T(8,128)(2,1)}, bf16[2048,256]{1,0:T(8,128)(2,1)}, u32[]{:S(2)}, u32[]{:S(2)}) collective-permute-start(bf16[2048,256]{1,0:T(8,128)(2,1)} %refs_0_.1), channel_id=1, source_target_pairs={{0,1},{1,2},{2,3},{3,4},{4,5},{5,6},{6,7},{7,0},{8,9},{9,10},{10,1... | collective-permute-start | bytes 3145736 | tf_op jit(solution)/shard_map/ppermute | solution.py:188
  4.7 1.9 %collective-permute-start.1 = (bf16[2048,256]{1,0:T(8,128)(2,1)}, bf16[2048,256]{1,0:T(8,128)(2,1)}, u32[]{:S(2)}, u32[]{:S(2)}) collective-permute-start(bf16[2048,256]{1,0:T(8,128)(2,1)} %refs_0_.1), channel_id=1, source_target_pairs={{0,7},{1,0},{2,1},{3,2},{4,3},{5,4},{6,5},{7,6},{8,15},{9,8},{10,9... | collective-permute-start | bytes 3145736 | tf_op jit(solution)/shard_map/ppermute | solution.py:188
  8.2 1.4 %multiply_convert_fusion = bf16[2048,128]{1,0:T(8,128)(2,1)S(1)} fusion(bf16[2048,128]{1,0:T(8,128)(2,1)} %param.4, f32[2048]{0:T(1024)S(1)} %convert_element_type.23), kind=kLoop, calls=%fused_computation.2 | loop fusion | flops 786432 | bytes 1056768 | tf_op jit(solution)/shard_map/convert_element_type | solution.py:190
  9.6 1.1 copy.10
  10.7 5.7 %all-to-all-start = ((bf16[72,32,128]{2,0,1:T(8,128)(2,1)}), bf16[72,32,128]{2,0,1:T(8,128)(2,1)S(1)}, u32[]{:S(2)}, u32[]{:S(2)}) async-start(bf16[72,32,128]{2,0,1:T(8,128)(2,1)} %copy.10), calls=%async_computation | async-start | bytes 1179648 | tf_op jit(solution)/shard_map/all_to_all | solution.py:197
  16.4 11.0 %collective-permute-done = bf16[2048,256]{1,0:T(8,128)(2,1)} collective-permute-done((bf16[2048,256]{1,0:T(8,128)(2,1)}, bf16[2048,256]{1,0:T(8,128)(2,1)}, u32[]{:S(2)}, u32[]{:S(2)}) %collective-permute-start) | collective-permute-done | bytes 1048608 | tf_op jit(solution)/shard_map/ppermute | solution.py:188
  27.4 5.6 %collective-permute-start.3 = (bf16[2048,256]{1,0:T(8,128)(2,1)}, bf16[2048,256]{1,0:T(8,128)(2,1)S(1)}, u32[]{:S(2)}, u32[]{:S(2)}) collective-permute-start(bf16[2048,256]{1,0:T(8,128)(2,1)} %collective-permute-done), channel_id=1, source_target_pairs={{0,1},{1,2},{2,3},{3,4},{4,5},{5,6},{6,7},{7,0},{8,9},{9,10},{10,1... | collective-permute-start | bytes 3145736 | tf_op jit(solution)/shard_map/ppermute | solution.py:200
  33.0 1.9 %collective-permute-start.4 = (bf16[2048,256]{1,0:T(8,128)(2,1)}, bf16[2048,256]{1,0:T(8,128)(2,1)}, u32[]{:S(2)}, u32[]{:S(2)}) collective-permute-start(bf16[2048,256]{1,0:T(8,128)(2,1)} %collective-permute-done.1), channel_id=1, source_target_pairs={{0,7},{1,0},{2,1},{3,2},{4,3},{5,4},{6,5},{7,6},{8,15},{9,8},{10,9... | collective-permute-start | bytes 3145736 | tf_op jit(solution)/shard_map/ppermute | solution.py:200
  35.0 2.3 %constant_dynamic-update-slice_fusion.1 = bf16[2048,512]{1,0:T(8,128)(2,1)} fusion(bf16[2048,256]{1,0:T(8,128)(2,1)} %collective-permute-done), kind=kLoop, calls=%fused_computation.8 | loop fusion | bytes 2097152
  37.3 2.3 %constant_dynamic-update-slice_fusion.refs_1_ = bf16[2048,512]{1,0:T(8,128)(2,1)} fusion(bf16[2048,512]{1,0:T(8,128)(2,1)} %constant_dynamic-update-slice_fusion.1, bf16[2048,256]{1,0:T(8,128)(2,1)} %collective-permute-done.1), kind=kLoop, calls=%fused_computation.7 | loop fusion | bytes 2097152 | tf_op jit(solution)/shard_map/concatenate | solution.py:198
  39.6 1.1 butterflies.1
  40.7 7.2 %all-to-all-start.1 = ((bf16[32,64,128]{2,1,0:T(8,128)(2,1)}), bf16[32,64,128]{2,1,0:T(8,128)(2,1)S(1)}, u32[]{:S(2)}, u32[]{:S(2)}) async-start(bf16[32,64,128]{2,1,0:T(8,128)(2,1)} %get-tuple-element.15), calls=%async_computation.1 | async-start | bytes 1048576 | tf_op jit(solution)/shard_map/all_to_all | solution.py:208
  47.9 7.0 %collective-permute-done.3.refs_2_ = bf16[2048,256]{1,0:T(8,128)(2,1)S(1)} collective-permute-done((bf16[2048,256]{1,0:T(8,128)(2,1)}, bf16[2048,256]{1,0:T(8,128)(2,1)S(1)}, u32[]{:S(2)}, u32[]{:S(2)}) %collective-permute-start.3) | collective-permute-done | bytes 1048608 | tf_op jit(solution)/shard_map/ppermute | solution.py:200
  54.9 1.0 copy-done
  55.9 5.5 %collective-permute-start.5 = (bf16[1280,256]{1,0:T(8,128)(2,1)S(1)}, bf16[1280,256]{1,0:T(8,128)(2,1)S(1)}, u32[]{:S(2)}, u32[]{:S(2)}) collective-permute-start(bf16[1280,256]{1,0:T(8,128)(2,1)S(1)} %slice.12), channel_id=1, source_target_pairs={{0,1},{1,2},{2,3},{3,4},{4,5},{5,6},{6,7},{7,0},{8,9},{9,10},{10,1... | collective-permute-start | bytes 1966088 | tf_op jit(solution)/shard_map/ppermute | solution.py:202
  61.4 1.9 %collective-permute-start.6 = (bf16[2048,256]{1,0:T(8,128)(2,1)}, bf16[2048,256]{1,0:T(8,128)(2,1)S(1)}, u32[]{:S(2)}, u32[]{:S(2)}) collective-permute-start(bf16[2048,256]{1,0:T(8,128)(2,1)} %collective-permute-done.4.refs_3_), channel_id=1, source_target_pairs={{0,7},{1,0},{2,1},{3,2},{4,3},{5,4},{6,5},{7,6},{8,15},{9,8},{10,9... | collective-permute-start | bytes 3145736 | tf_op jit(solution)/shard_map/ppermute | solution.py:203
  63.3 10.2 %collective-permute-done.5.refs_4_ = bf16[1280,256]{1,0:T(8,128)(2,1)S(1)} collective-permute-done((bf16[1280,256]{1,0:T(8,128)(2,1)S(1)}, bf16[1280,256]{1,0:T(8,128)(2,1)S(1)}, u32[]{:S(2)}, u32[]{:S(2)}) %collective-permute-start.5) | collective-permute-done | bytes 655392 | tf_op jit(solution)/shard_map/ppermute | solution.py:202
  73.6 5.6 %collective-permute-start.7 = (bf16[1280,256]{1,0:T(8,128)(2,1)S(1)}, bf16[1280,256]{1,0:T(8,128)(2,1)S(1)}, u32[]{:S(2)}, u32[]{:S(2)}) collective-permute-start(bf16[1280,256]{1,0:T(8,128)(2,1)S(1)} %collective-permute-done.5.refs_4_), channel_id=1, source_target_pairs={{0,1},{1,2},{2,3},{3,4},{4,5},{5,6},{6,7},{7,0},{8,9},{9,10},{10,1... | collective-permute-start | bytes 1966088 | tf_op jit(solution)/shard_map/ppermute | solution.py:204
  79.2 1.9 %collective-permute-start.2 = (bf16[32,64,128]{2,1,0:T(8,128)(2,1)S(1)}, bf16[32,64,128]{2,1,0:T(8,128)(2,1)}, u32[]{:S(2)}, u32[]{:S(2)}) collective-permute-start(bf16[32,64,128]{2,1,0:T(8,128)(2,1)S(1)} %all-to-all-done.1.got_ref), channel_id=1, source_target_pairs={{0,16},{16,0},{1,17},{17,1},{2,18},{18,2},{3,19},{19,3},{4,20},{20... | collective-permute-start | bytes 1572872 | tf_op jit(solution)/shard_map/ppermute | solution.py:209
  81.2 1.0 slice.13
  82.2 1.9 %collective-permute-start.10 = (bf16[768,256]{1,0:T(8,128)(2,1)S(1)}, bf16[768,256]{1,0:T(8,128)(2,1)S(1)}, u32[]{:S(2)}, u32[]{:S(2)}) collective-permute-start(bf16[768,256]{1,0:T(8,128)(2,1)S(1)} %slice.13), channel_id=1, source_target_pairs={{0,1},{1,2},{2,3},{3,4},{4,5},{5,6},{6,7},{7,0},{8,9},{9,10},{10,1... | collective-permute-start | bytes 1179656 | tf_op jit(solution)/shard_map/ppermute | solution.py:202
  84.2 7.0 %early_products.1 = (f32[1280,128]{1,0:T(8,128)S(1)}, f32[1280,128]{1,0:T(8,128)S(1)}, f32[768,128]{1,0:T(8,128)S(1)}, f32[768,128]{1,0:T(8,128)S(1)}, bf16[8,256,256]{2,1,0:T(8,128)(2,1)S(1)}) custom-call(s32[3]{0:T(128)S(1)} %pad_add_fusion.place_ref, bf16[32,64,128]{2,1,0:T(8,128)(2,1)S(1)} %all-to-all-done.1.got_ref, ...), custom_call_target="tpu_custom_call" | custom-call | tf_op jit(solution)/shard_map/early_products/pallas_call | solution.py:129
  91.2 3.9 %collective-permute-start.9 = (bf16[768,256]{1,0:T(8,128)(2,1)S(1)}, bf16[768,256]{1,0:T(8,128)(2,1)S(1)}, u32[]{:S(2)}, u32[]{:S(2)}) collective-permute-start(bf16[768,256]{1,0:T(8,128)(2,1)S(1)} %slice.10), channel_id=1, source_target_pairs={{0,7},{1,0},{2,1},{3,2},{4,3},{5,4},{6,5},{7,6},{8,15},{9,8},{10,9... | collective-permute-start | bytes 1179656 | tf_op jit(solution)/shard_map/ppermute | solution.py:223
  95.2 1.1 last_far.2
  96.2 5.0 %collective-permute-start.8 = (bf16[1280,128]{1,0:T(8,128)(2,1)S(1)}, bf16[1280,128]{1,0:T(8,128)(2,1)S(1)}, u32[]{:S(2)}, u32[]{:S(2)}) collective-permute-start(bf16[1280,128]{1,0:T(8,128)(2,1)S(1)} %last_far.2), channel_id=1, source_target_pairs={{0,8},{8,0},{1,9},{9,1},{2,10},{10,2},{3,11},{11,3},{4,12},{12,4},... | collective-permute-start | bytes 983048 | tf_op jit(solution)/shard_map/ppermute | solution.py:231
  101.2 1.0 last_own.2
  102.2 3.6 %collective-permute-done.9.refs_1_ = bf16[768,256]{1,0:T(8,128)(2,1)S(1)} collective-permute-done((bf16[768,256]{1,0:T(8,128)(2,1)S(1)}, bf16[768,256]{1,0:T(8,128)(2,1)S(1)}, u32[]{:S(2)}, u32[]{:S(2)}) %collective-permute-start.9) | collective-permute-done | bytes 393248 | tf_op jit(solution)/shard_map/ppermute | solution.py:223
  105.8 1.0 last_far.3
  106.9 4.9 %collective-permute-start.11 = (bf16[768,128]{1,0:T(8,128)(2,1)S(1)}, bf16[768,128]{1,0:T(8,128)(2,1)S(1)}, u32[]{:S(2)}, u32[]{:S(2)}) collective-permute-start(bf16[768,128]{1,0:T(8,128)(2,1)S(1)} %last_far.3), channel_id=1, source_target_pairs={{0,8},{8,0},{1,9},{9,1},{2,10},{10,2},{3,11},{11,3},{4,12},{12,4},... | collective-permute-start | bytes 589832 | tf_op jit(solution)/shard_map/ppermute | solution.py:231
  111.8 1.0 last_own.3
  112.9 3.9 %collective-permute-done.11 = bf16[768,128]{1,0:T(8,128)(2,1)S(1)} collective-permute-done((bf16[768,128]{1,0:T(8,128)(2,1)S(1)}, bf16[768,128]{1,0:T(8,128)(2,1)S(1)}, u32[]{:S(2)}, u32[]{:S(2)}) %collective-permute-start.11) | collective-permute-done | bytes 196640 | tf_op jit(solution)/shard_map/ppermute | solution.py:231
  116.8 0.8 pad_maximum_fusion
  (19 shorter events, 1.9 us)
Async XLA Ops:
  0.0 27.4 %collective-permute-start = (bf16[2048,256]{1,0:T(8,128)(2,1)}, bf16[2048,256]{1,0:T(8,128)(2,1)}, u32[]{:S(2)}, u32[]{:S(2)}) collective-permute-start(bf16[2048,256]{1,0:T(8,128)(2,1)} %refs_0_.1), channel_id=1, source_target_pairs={{0,1},{1,2},{2,3},{3,4},{4,5},{5,6},{6,7},{7,0},{8,9},{9,10},{10,1... | collective-permute-start | bytes 3145736 | tf_op jit(solution)/shard_map/ppermute | solution.py:188
  4.7 28.3 %collective-permute-start.1 = (bf16[2048,256]{1,0:T(8,128)(2,1)}, bf16[2048,256]{1,0:T(8,128)(2,1)}, u32[]{:S(2)}, u32[]{:S(2)}) collective-permute-start(bf16[2048,256]{1,0:T(8,128)(2,1)} %refs_0_.1), channel_id=1, source_target_pairs={{0,7},{1,0},{2,1},{3,2},{4,3},{5,4},{6,5},{7,6},{8,15},{9,8},{10,9... | collective-permute-start | bytes 3145736 | tf_op jit(solution)/shard_map/ppermute | solution.py:188
  10.7 28.9 %all-to-all-start = ((bf16[72,32,128]{2,0,1:T(8,128)(2,1)}), bf16[72,32,128]{2,0,1:T(8,128)(2,1)S(1)}, u32[]{:S(2)}, u32[]{:S(2)}) async-start(bf16[72,32,128]{2,0,1:T(8,128)(2,1)} %copy.10), calls=%async_computation | async-start | bytes 1179648 | tf_op jit(solution)/shard_map/all_to_all | solution.py:197
  27.4 27.4 %collective-permute-start.3 = (bf16[2048,256]{1,0:T(8,128)(2,1)}, bf16[2048,256]{1,0:T(8,128)(2,1)S(1)}, u32[]{:S(2)}, u32[]{:S(2)}) collective-permute-start(bf16[2048,256]{1,0:T(8,128)(2,1)} %collective-permute-done), channel_id=1, source_target_pairs={{0,1},{1,2},{2,3},{3,4},{4,5},{5,6},{6,7},{7,0},{8,9},{9,10},{10,1... | collective-permute-start | bytes 3145736 | tf_op jit(solution)/shard_map/ppermute | solution.py:200
  33.0 28.4 %collective-permute-start.4 = (bf16[2048,256]{1,0:T(8,128)(2,1)}, bf16[2048,256]{1,0:T(8,128)(2,1)}, u32[]{:S(2)}, u32[]{:S(2)}) collective-permute-start(bf16[2048,256]{1,0:T(8,128)(2,1)} %collective-permute-done.1), channel_id=1, source_target_pairs={{0,7},{1,0},{2,1},{3,2},{4,3},{5,4},{6,5},{7,6},{8,15},{9,8},{10,9... | collective-permute-start | bytes 3145736 | tf_op jit(solution)/shard_map/ppermute | solution.py:200
  40.7 38.5 %all-to-all-start.1 = ((bf16[32,64,128]{2,1,0:T(8,128)(2,1)}), bf16[32,64,128]{2,1,0:T(8,128)(2,1)S(1)}, u32[]{:S(2)}, u32[]{:S(2)}) async-start(bf16[32,64,128]{2,1,0:T(8,128)(2,1)} %get-tuple-element.15), calls=%async_computation.1 | async-start | bytes 1048576 | tf_op jit(solution)/shard_map/all_to_all | solution.py:208
  54.9 1.0 copy-start
  55.9 17.7 %collective-permute-start.5 = (bf16[1280,256]{1,0:T(8,128)(2,1)S(1)}, bf16[1280,256]{1,0:T(8,128)(2,1)S(1)}, u32[]{:S(2)}, u32[]{:S(2)}) collective-permute-start(bf16[1280,256]{1,0:T(8,128)(2,1)S(1)} %slice.12), channel_id=1, source_target_pairs={{0,1},{1,2},{2,3},{3,4},{4,5},{5,6},{6,7},{7,0},{8,9},{9,10},{10,1... | collective-permute-start | bytes 1966088 | tf_op jit(solution)/shard_map/ppermute | solution.py:202
  61.4 29.8 %collective-permute-start.6 = (bf16[2048,256]{1,0:T(8,128)(2,1)}, bf16[2048,256]{1,0:T(8,128)(2,1)S(1)}, u32[]{:S(2)}, u32[]{:S(2)}) collective-permute-start(bf16[2048,256]{1,0:T(8,128)(2,1)} %collective-permute-done.4.refs_3_), channel_id=1, source_target_pairs={{0,7},{1,0},{2,1},{3,2},{4,3},{5,4},{6,5},{7,6},{8,15},{9,8},{10,9... | collective-permute-start | bytes 3145736 | tf_op jit(solution)/shard_map/ppermute | solution.py:203
  73.6 21.6 %collective-permute-start.7 = (bf16[1280,256]{1,0:T(8,128)(2,1)S(1)}, bf16[1280,256]{1,0:T(8,128)(2,1)S(1)}, u32[]{:S(2)}, u32[]{:S(2)}) collective-permute-start(bf16[1280,256]{1,0:T(8,128)(2,1)S(1)} %collective-permute-done.5.refs_4_), channel_id=1, source_target_pairs={{0,1},{1,2},{2,3},{3,4},{4,5},{5,6},{6,7},{7,0},{8,9},{9,10},{10,1... | collective-permute-start | bytes 1966088 | tf_op jit(solution)/shard_map/ppermute | solution.py:204
  79.2 5.0 %collective-permute-start.2 = (bf16[32,64,128]{2,1,0:T(8,128)(2,1)S(1)}, bf16[32,64,128]{2,1,0:T(8,128)(2,1)}, u32[]{:S(2)}, u32[]{:S(2)}) collective-permute-start(bf16[32,64,128]{2,1,0:T(8,128)(2,1)S(1)} %all-to-all-done.1.got_ref), channel_id=1, source_target_pairs={{0,16},{16,0},{1,17},{17,1},{2,18},{18,2},{3,19},{19,3},{4,20},{20... | collective-permute-start | bytes 1572872 | tf_op jit(solution)/shard_map/ppermute | solution.py:209
  82.2 20.0 %collective-permute-start.10 = (bf16[768,256]{1,0:T(8,128)(2,1)S(1)}, bf16[768,256]{1,0:T(8,128)(2,1)S(1)}, u32[]{:S(2)}, u32[]{:S(2)}) collective-permute-start(bf16[768,256]{1,0:T(8,128)(2,1)S(1)} %slice.13), channel_id=1, source_target_pairs={{0,1},{1,2},{2,3},{3,4},{4,5},{5,6},{6,7},{7,0},{8,9},{9,10},{10,1... | collective-permute-start | bytes 1179656 | tf_op jit(solution)/shard_map/ppermute | solution.py:202
  91.2 14.6 %collective-permute-start.9 = (bf16[768,256]{1,0:T(8,128)(2,1)S(1)}, bf16[768,256]{1,0:T(8,128)(2,1)S(1)}, u32[]{:S(2)}, u32[]{:S(2)}) collective-permute-start(bf16[768,256]{1,0:T(8,128)(2,1)S(1)} %slice.10), channel_id=1, source_target_pairs={{0,7},{1,0},{2,1},{3,2},{4,3},{5,4},{6,5},{7,6},{8,15},{9,8},{10,9... | collective-permute-start | bytes 1179656 | tf_op jit(solution)/shard_map/ppermute | solution.py:223
  96.2 16.6 %collective-permute-start.8 = (bf16[1280,128]{1,0:T(8,128)(2,1)S(1)}, bf16[1280,128]{1,0:T(8,128)(2,1)S(1)}, u32[]{:S(2)}, u32[]{:S(2)}) collective-permute-start(bf16[1280,128]{1,0:T(8,128)(2,1)S(1)} %last_far.2), channel_id=1, source_target_pairs={{0,8},{8,0},{1,9},{9,1},{2,10},{10,2},{3,11},{11,3},{4,12},{12,4},... | collective-permute-start | bytes 983048 | tf_op jit(solution)/shard_map/ppermute | solution.py:231
  106.9 9.9 %collective-permute-start.11 = (bf16[768,128]{1,0:T(8,128)(2,1)S(1)}, bf16[768,128]{1,0:T(8,128)(2,1)S(1)}, u32[]{:S(2)}, u32[]{:S(2)}) collective-permute-start(bf16[768,128]{1,0:T(8,128)(2,1)S(1)} %last_far.3), channel_id=1, source_target_pairs={{0,8},{8,0},{1,9},{9,1},{2,10},{10,2},{3,11},{11,3},{4,12},{12,4},... | collective-permute-start | bytes 589832 | tf_op jit(solution)/shard_map/ppermute | solution.py:231

commit v15 on v14

--- a/solution.py
+++ b/solution.py
@@ -95,21 +95,26 @@
         block_refs, own_ref, out_refs = refs[: len(blocks)], refs[len(blocks)], refs[len(blocks) + 1 : -4]
         upper_ref, turned, here, arrived = refs[-4:]
         copies = [
-            pltpu.make_async_copy(ref, here.at[:, at : at + ref.shape[1]], arrived.at[n])
-            for n, (ref, at) in enumerate(zip(block_refs, starts))
+            [
+                pltpu.make_async_copy(
+                    ref.at[start:stop], here.at[start:stop, at : at + ref.shape[1]], arrived.at[part * len(blocks) + n]
+                )
+                for n, (ref, at) in enumerate(zip(block_refs, starts))
+            ]
+            for part, (start, stop) in enumerate(bounds)
         ]
-        for copy in copies:
+        for copy in sum(copies, []):
             copy.start()
         order_upper(place_ref[2], got_ref, twin_ref, upper_ref)
         for n, offset in enumerate(offsets):
             turned[n * depth : (n + 1) * depth] = upper_ref[(place_ref[1] + offset + y_count) % y_count]
         turned[common:] = upper_ref[(place_ref[1] + own_offset + y_count) % y_count]
         at_left = place_ref[0] == 0
-        for copy in copies:
-            copy.wait()
 
         for part, (start, stop) in enumerate(bounds):
             far_ref, rest_ref = out_refs[2 * part : 2 * part + 2]
+            for copy in copies[part]:
+                copy.wait()
 
             def one(i, carry):
                 local = pl.ds(pl.multiple_of(i * TILE_M, TILE_M), TILE_M)
@@ -138,7 +143,7 @@
         scratch_shapes=[
             VM((common + depth, both), stored.dtype),
             VM((rows, common), stored.dtype),
-            pltpu.SemaphoreType.DMA((len(blocks),)),
+            pltpu.SemaphoreType.DMA((parts * len(blocks),)),
         ],
         compiler_params=grant(48),
         name="early_products",

time: 119 us -> 118 us (level)
  no operation moved by 1% of the time
where the time goes in v15:
time: 118 us; the launch traced here: 117 us
  starting transfers between devices  57.7 us (49%)
  waiting for transfers between devices  35.8 us (30%)
  Pallas kernels  11.7 us (10%)
  local copies, waits for them, and re-layouts  8.58 us (7%)
  other arithmetic  3.14 us (3%)
    ppermute x2, waiting for transfers between devices, per_device(): lax.ppermute(panel_lower, 'y', route[sign])  11 us
    ppermute x2, waiting for transfers between devices, per_device(): lax.ppermute(far_near[0][start:stop], 'y', up)  10.2 us
    ppermute x2, starting transfers between devices, per_device(): came = lax.ppermute(far, 'x_hi', swap)  9.9 us
    ppermute x2, starting transfers between devices, per_device(): lax.ppermute(block, 'y', route[sign])  7.51 us
    ppermute x2, starting transfers between devices, per_device(): lax.ppermute(far_near[0][start:stop], 'y', up)  7.42 us
    all_to_all x1, starting transfers between devices, per_device(): got = lax.all_to_all(send, ('chip', 'x_hi'), split_axis=0, concat_axis=0)  7.2 us
    ppermute x2, waiting for transfers between devices, per_device(): lax.ppermute(block, 'y', route[sign])  6.99 us
    ppermute x2, starting transfers between devices, per_device(): lax.ppermute(panel_lower, 'y', route[sign])  6.62 us
  transfers between devices with their start and end apart: 14, of which 5 were waited for; matrix products, arithmetic and copies ran while one was open for 8% of the time, Pallas kernels for 10%

profile of v15, /device:TPU:472, one launch (start us, length us, event | category | flops | bytes accessed | tf_op | source)
XLA Modules:
  0.0 117.1 jit_solution(8736931249594157015)
XLA Ops:
  0.0 4.7 %collective-permute-start = (bf16[2048,256]{1,0:T(8,128)(2,1)}, bf16[2048,256]{1,0:T(8,128)(2,1)}, u32[]{:S(2)}, u32[]{:S(2)}) collective-permute-start(bf16[2048,256]{1,0:T(8,128)(2,1)} %refs_0_.1), channel_id=1, source_target_pairs={{0,1},{1,2},{2,3},{3,4},{4,5},{5,6},{6,7},{7,0},{8,9},{9,10},{10,1... | collective-permute-start | bytes 3145736 | tf_op jit(solution)/shard_map/ppermute | solution.py:193
  4.7 1.9 %collective-permute-start.1 = (bf16[2048,256]{1,0:T(8,128)(2,1)}, bf16[2048,256]{1,0:T(8,128)(2,1)}, u32[]{:S(2)}, u32[]{:S(2)}) collective-permute-start(bf16[2048,256]{1,0:T(8,128)(2,1)} %refs_0_.1), channel_id=1, source_target_pairs={{0,7},{1,0},{2,1},{3,2},{4,3},{5,4},{6,5},{7,6},{8,15},{9,8},{10,9... | collective-permute-start | bytes 3145736 | tf_op jit(solution)/shard_map/ppermute | solution.py:193
  8.2 1.4 %multiply_convert_fusion = bf16[2048,128]{1,0:T(8,128)(2,1)S(1)} fusion(bf16[2048,128]{1,0:T(8,128)(2,1)} %param.4, f32[2048]{0:T(1024)S(1)} %convert_element_type.23), kind=kLoop, calls=%fused_computation.2 | loop fusion | flops 786432 | bytes 1056768 | tf_op jit(solution)/shard_map/convert_element_type | solution.py:195
  9.6 1.1 copy.10
  10.7 5.7 %all-to-all-start = ((bf16[72,32,128]{2,0,1:T(8,128)(2,1)}), bf16[72,32,128]{2,0,1:T(8,128)(2,1)S(1)}, u32[]{:S(2)}, u32[]{:S(2)}) async-start(bf16[72,32,128]{2,0,1:T(8,128)(2,1)} %copy.10), calls=%async_computation | async-start | bytes 1179648 | tf_op jit(solution)/shard_map/all_to_all | solution.py:202
  16.4 11.0 %collective-permute-done = bf16[2048,256]{1,0:T(8,128)(2,1)} collective-permute-done((bf16[2048,256]{1,0:T(8,128)(2,1)}, bf16[2048,256]{1,0:T(8,128)(2,1)}, u32[]{:S(2)}, u32[]{:S(2)}) %collective-permute-start) | collective-permute-done | bytes 1048608 | tf_op jit(solution)/shard_map/ppermute | solution.py:193
  27.4 5.6 %collective-permute-start.3 = (bf16[2048,256]{1,0:T(8,128)(2,1)}, bf16[2048,256]{1,0:T(8,128)(2,1)S(1)}, u32[]{:S(2)}, u32[]{:S(2)}) collective-permute-start(bf16[2048,256]{1,0:T(8,128)(2,1)} %collective-permute-done), channel_id=1, source_target_pairs={{0,1},{1,2},{2,3},{3,4},{4,5},{5,6},{6,7},{7,0},{8,9},{9,10},{10,1... | collective-permute-start | bytes 3145736 | tf_op jit(solution)/shard_map/ppermute | solution.py:205
  33.0 1.9 %collective-permute-start.4 = (bf16[2048,256]{1,0:T(8,128)(2,1)}, bf16[2048,256]{1,0:T(8,128)(2,1)}, u32[]{:S(2)}, u32[]{:S(2)}) collective-permute-start(bf16[2048,256]{1,0:T(8,128)(2,1)} %collective-permute-done.1), channel_id=1, source_target_pairs={{0,7},{1,0},{2,1},{3,2},{4,3},{5,4},{6,5},{7,6},{8,15},{9,8},{10,9... | collective-permute-start | bytes 3145736 | tf_op jit(solution)/shard_map/ppermute | solution.py:205
  35.0 2.3 %constant_dynamic-update-slice_fusion.1 = bf16[2048,512]{1,0:T(8,128)(2,1)} fusion(bf16[2048,256]{1,0:T(8,128)(2,1)} %collective-permute-done), kind=kLoop, calls=%fused_computation.8 | loop fusion | bytes 2097152
  37.3 2.3 %constant_dynamic-update-slice_fusion.refs_1_ = bf16[2048,512]{1,0:T(8,128)(2,1)} fusion(bf16[2048,512]{1,0:T(8,128)(2,1)} %constant_dynamic-update-slice_fusion.1, bf16[2048,256]{1,0:T(8,128)(2,1)} %collective-permute-done.1), kind=kLoop, calls=%fused_computation.7 | loop fusion | bytes 2097152 | tf_op jit(solution)/shard_map/concatenate | solution.py:203
  39.6 1.1 butterflies.1
  40.7 7.2 %all-to-all-start.1 = ((bf16[32,64,128]{2,1,0:T(8,128)(2,1)}), bf16[32,64,128]{2,1,0:T(8,128)(2,1)S(1)}, u32[]{:S(2)}, u32[]{:S(2)}) async-start(bf16[32,64,128]{2,1,0:T(8,128)(2,1)} %get-tuple-element.15), calls=%async_computation.1 | async-start | bytes 1048576 | tf_op jit(solution)/shard_map/all_to_all | solution.py:213
  47.9 7.0 %collective-permute-done.3.refs_2_ = bf16[2048,256]{1,0:T(8,128)(2,1)S(1)} collective-permute-done((bf16[2048,256]{1,0:T(8,128)(2,1)}, bf16[2048,256]{1,0:T(8,128)(2,1)S(1)}, u32[]{:S(2)}, u32[]{:S(2)}) %collective-permute-start.3) | collective-permute-done | bytes 1048608 | tf_op jit(solution)/shard_map/ppermute | solution.py:205
  54.9 1.0 copy-done
  55.9 5.5 %collective-permute-start.5 = (bf16[1280,256]{1,0:T(8,128)(2,1)S(1)}, bf16[1280,256]{1,0:T(8,128)(2,1)S(1)}, u32[]{:S(2)}, u32[]{:S(2)}) collective-permute-start(bf16[1280,256]{1,0:T(8,128)(2,1)S(1)} %slice.12), channel_id=1, source_target_pairs={{0,1},{1,2},{2,3},{3,4},{4,5},{5,6},{6,7},{7,0},{8,9},{9,10},{10,1... | collective-permute-start | bytes 1966088 | tf_op jit(solution)/shard_map/ppermute | solution.py:207
  61.4 1.9 %collective-permute-start.6 = (bf16[2048,256]{1,0:T(8,128)(2,1)}, bf16[2048,256]{1,0:T(8,128)(2,1)S(1)}, u32[]{:S(2)}, u32[]{:S(2)}) collective-permute-start(bf16[2048,256]{1,0:T(8,128)(2,1)} %collective-permute-done.4.refs_3_), channel_id=1, source_target_pairs={{0,7},{1,0},{2,1},{3,2},{4,3},{5,4},{6,5},{7,6},{8,15},{9,8},{10,9... | collective-permute-start | bytes 3145736 | tf_op jit(solution)/shard_map/ppermute | solution.py:208
  63.3 10.2 %collective-permute-done.5.refs_4_ = bf16[1280,256]{1,0:T(8,128)(2,1)S(1)} collective-permute-done((bf16[1280,256]{1,0:T(8,128)(2,1)S(1)}, bf16[1280,256]{1,0:T(8,128)(2,1)S(1)}, u32[]{:S(2)}, u32[]{:S(2)}) %collective-permute-start.5) | collective-permute-done | bytes 655392 | tf_op jit(solution)/shard_map/ppermute | solution.py:207
  73.6 5.6 %collective-permute-start.7 = (bf16[1280,256]{1,0:T(8,128)(2,1)S(1)}, bf16[1280,256]{1,0:T(8,128)(2,1)S(1)}, u32[]{:S(2)}, u32[]{:S(2)}) collective-permute-start(bf16[1280,256]{1,0:T(8,128)(2,1)S(1)} %collective-permute-done.5.refs_4_), channel_id=1, source_target_pairs={{0,1},{1,2},{2,3},{3,4},{4,5},{5,6},{6,7},{7,0},{8,9},{9,10},{10,1... | collective-permute-start | bytes 1966088 | tf_op jit(solution)/shard_map/ppermute | solution.py:209
  79.2 1.9 %collective-permute-start.2 = (bf16[32,64,128]{2,1,0:T(8,128)(2,1)S(1)}, bf16[32,64,128]{2,1,0:T(8,128)(2,1)}, u32[]{:S(2)}, u32[]{:S(2)}) collective-permute-start(bf16[32,64,128]{2,1,0:T(8,128)(2,1)S(1)} %all-to-all-done.1.got_ref), channel_id=1, source_target_pairs={{0,16},{16,0},{1,17},{17,1},{2,18},{18,2},{3,19},{19,3},{4,20},{20... | collective-permute-start | bytes 1572872 | tf_op jit(solution)/shard_map/ppermute | solution.py:214
  81.2 1.0 slice.13
  82.2 1.9 %collective-permute-start.10 = (bf16[768,256]{1,0:T(8,128)(2,1)S(1)}, bf16[768,256]{1,0:T(8,128)(2,1)S(1)}, u32[]{:S(2)}, u32[]{:S(2)}) collective-permute-start(bf16[768,256]{1,0:T(8,128)(2,1)S(1)} %slice.13), channel_id=1, source_target_pairs={{0,1},{1,2},{2,3},{3,4},{4,5},{5,6},{6,7},{7,0},{8,9},{9,10},{10,1... | collective-permute-start | bytes 1179656 | tf_op jit(solution)/shard_map/ppermute | solution.py:207
  84.2 6.4 %early_products.1 = (f32[1280,128]{1,0:T(8,128)S(1)}, f32[1280,128]{1,0:T(8,128)S(1)}, f32[768,128]{1,0:T(8,128)S(1)}, f32[768,128]{1,0:T(8,128)S(1)}, bf16[8,256,256]{2,1,0:T(8,128)(2,1)S(1)}) custom-call(s32[3]{0:T(128)S(1)} %pad_add_fusion.place_ref, bf16[32,64,128]{2,1,0:T(8,128)(2,1)S(1)} %all-to-all-done.1.got_ref, ...), custom_call_target="tpu_custom_call" | custom-call | tf_op jit(solution)/shard_map/early_products/pallas_call | solution.py:134
  90.6 3.9 %collective-permute-start.9 = (bf16[768,256]{1,0:T(8,128)(2,1)S(1)}, bf16[768,256]{1,0:T(8,128)(2,1)S(1)}, u32[]{:S(2)}, u32[]{:S(2)}) collective-permute-start(bf16[768,256]{1,0:T(8,128)(2,1)S(1)} %slice.10), channel_id=1, source_target_pairs={{0,7},{1,0},{2,1},{3,2},{4,3},{5,4},{6,5},{7,6},{8,15},{9,8},{10,9... | collective-permute-start | bytes 1179656 | tf_op jit(solution)/shard_map/ppermute | solution.py:228
  94.6 1.0 last_far.2
  95.6 5.0 %collective-permute-start.8 = (bf16[1280,128]{1,0:T(8,128)(2,1)S(1)}, bf16[1280,128]{1,0:T(8,128)(2,1)S(1)}, u32[]{:S(2)}, u32[]{:S(2)}) collective-permute-start(bf16[1280,128]{1,0:T(8,128)(2,1)S(1)} %last_far.2), channel_id=1, source_target_pairs={{0,8},{8,0},{1,9},{9,1},{2,10},{10,2},{3,11},{11,3},{4,12},{12,4},... | collective-permute-start | bytes 983048 | tf_op jit(solution)/shard_map/ppermute | solution.py:236
  100.6 1.0 last_own.2
  101.7 3.6 %collective-permute-done.9.refs_1_ = bf16[768,256]{1,0:T(8,128)(2,1)S(1)} collective-permute-done((bf16[768,256]{1,0:T(8,128)(2,1)S(1)}, bf16[768,256]{1,0:T(8,128)(2,1)S(1)}, u32[]{:S(2)}, u32[]{:S(2)}) %collective-permute-start.9) | collective-permute-done | bytes 393248 | tf_op jit(solution)/shard_map/ppermute | solution.py:228
  105.3 1.0 last_far.3
  106.3 4.9 %collective-permute-start.11 = (bf16[768,128]{1,0:T(8,128)(2,1)S(1)}, bf16[768,128]{1,0:T(8,128)(2,1)S(1)}, u32[]{:S(2)}, u32[]{:S(2)}) collective-permute-start(bf16[768,128]{1,0:T(8,128)(2,1)S(1)} %last_far.3), channel_id=1, source_target_pairs={{0,8},{8,0},{1,9},{9,1},{2,10},{10,2},{3,11},{11,3},{4,12},{12,4},... | collective-permute-start | bytes 589832 | tf_op jit(solution)/shard_map/ppermute | solution.py:236
  111.2 1.0 last_own.3
  112.3 3.9 %collective-permute-done.11 = bf16[768,128]{1,0:T(8,128)(2,1)S(1)} collective-permute-done((bf16[768,128]{1,0:T(8,128)(2,1)S(1)}, bf16[768,128]{1,0:T(8,128)(2,1)S(1)}, u32[]{:S(2)}, u32[]{:S(2)}) %collective-permute-start.11) | collective-permute-done | bytes 196640 | tf_op jit(solution)/shard_map/ppermute | solution.py:236
  116.3 0.8 pad_maximum_fusion
  (19 shorter events, 1.9 us)
Async XLA Ops:
  0.0 27.4 %collective-permute-start = (bf16[2048,256]{1,0:T(8,128)(2,1)}, bf16[2048,256]{1,0:T(8,128)(2,1)}, u32[]{:S(2)}, u32[]{:S(2)}) collective-permute-start(bf16[2048,256]{1,0:T(8,128)(2,1)} %refs_0_.1), channel_id=1, source_target_pairs={{0,1},{1,2},{2,3},{3,4},{4,5},{5,6},{6,7},{7,0},{8,9},{9,10},{10,1... | collective-permute-start | bytes 3145736 | tf_op jit(solution)/shard_map/ppermute | solution.py:193
  4.7 28.3 %collective-permute-start.1 = (bf16[2048,256]{1,0:T(8,128)(2,1)}, bf16[2048,256]{1,0:T(8,128)(2,1)}, u32[]{:S(2)}, u32[]{:S(2)}) collective-permute-start(bf16[2048,256]{1,0:T(8,128)(2,1)} %refs_0_.1), channel_id=1, source_target_pairs={{0,7},{1,0},{2,1},{3,2},{4,3},{5,4},{6,5},{7,6},{8,15},{9,8},{10,9... | collective-permute-start | bytes 3145736 | tf_op jit(solution)/shard_map/ppermute | solution.py:193
  10.7 28.9 %all-to-all-start = ((bf16[72,32,128]{2,0,1:T(8,128)(2,1)}), bf16[72,32,128]{2,0,1:T(8,128)(2,1)S(1)}, u32[]{:S(2)}, u32[]{:S(2)}) async-start(bf16[72,32,128]{2,0,1:T(8,128)(2,1)} %copy.10), calls=%async_computation | async-start | bytes 1179648 | tf_op jit(solution)/shard_map/all_to_all | solution.py:202
  27.4 27.4 %collective-permute-start.3 = (bf16[2048,256]{1,0:T(8,128)(2,1)}, bf16[2048,256]{1,0:T(8,128)(2,1)S(1)}, u32[]{:S(2)}, u32[]{:S(2)}) collective-permute-start(bf16[2048,256]{1,0:T(8,128)(2,1)} %collective-permute-done), channel_id=1, source_target_pairs={{0,1},{1,2},{2,3},{3,4},{4,5},{5,6},{6,7},{7,0},{8,9},{9,10},{10,1... | collective-permute-start | bytes 3145736 | tf_op jit(solution)/shard_map/ppermute | solution.py:205
  33.0 28.4 %collective-permute-start.4 = (bf16[2048,256]{1,0:T(8,128)(2,1)}, bf16[2048,256]{1,0:T(8,128)(2,1)}, u32[]{:S(2)}, u32[]{:S(2)}) collective-permute-start(bf16[2048,256]{1,0:T(8,128)(2,1)} %collective-permute-done.1), channel_id=1, source_target_pairs={{0,7},{1,0},{2,1},{3,2},{4,3},{5,4},{6,5},{7,6},{8,15},{9,8},{10,9... | collective-permute-start | bytes 3145736 | tf_op jit(solution)/shard_map/ppermute | solution.py:205
  40.7 38.5 %all-to-all-start.1 = ((bf16[32,64,128]{2,1,0:T(8,128)(2,1)}), bf16[32,64,128]{2,1,0:T(8,128)(2,1)S(1)}, u32[]{:S(2)}, u32[]{:S(2)}) async-start(bf16[32,64,128]{2,1,0:T(8,128)(2,1)} %get-tuple-element.15), calls=%async_computation.1 | async-start | bytes 1048576 | tf_op jit(solution)/shard_map/all_to_all | solution.py:213
  54.9 1.0 copy-start
  55.9 17.7 %collective-permute-start.5 = (bf16[1280,256]{1,0:T(8,128)(2,1)S(1)}, bf16[1280,256]{1,0:T(8,128)(2,1)S(1)}, u32[]{:S(2)}, u32[]{:S(2)}) collective-permute-start(bf16[1280,256]{1,0:T(8,128)(2,1)S(1)} %slice.12), channel_id=1, source_target_pairs={{0,1},{1,2},{2,3},{3,4},{4,5},{5,6},{6,7},{7,0},{8,9},{9,10},{10,1... | collective-permute-start | bytes 1966088 | tf_op jit(solution)/shard_map/ppermute | solution.py:207
  61.4 29.2 %collective-permute-start.6 = (bf16[2048,256]{1,0:T(8,128)(2,1)}, bf16[2048,256]{1,0:T(8,128)(2,1)S(1)}, u32[]{:S(2)}, u32[]{:S(2)}) collective-permute-start(bf16[2048,256]{1,0:T(8,128)(2,1)} %collective-permute-done.4.refs_3_), channel_id=1, source_target_pairs={{0,7},{1,0},{2,1},{3,2},{4,3},{5,4},{6,5},{7,6},{8,15},{9,8},{10,9... | collective-permute-start | bytes 3145736 | tf_op jit(solution)/shard_map/ppermute | solution.py:208
  73.6 21.0 %collective-permute-start.7 = (bf16[1280,256]{1,0:T(8,128)(2,1)S(1)}, bf16[1280,256]{1,0:T(8,128)(2,1)S(1)}, u32[]{:S(2)}, u32[]{:S(2)}) collective-permute-start(bf16[1280,256]{1,0:T(8,128)(2,1)S(1)} %collective-permute-done.5.refs_4_), channel_id=1, source_target_pairs={{0,1},{1,2},{2,3},{3,4},{4,5},{5,6},{6,7},{7,0},{8,9},{9,10},{10,1... | collective-permute-start | bytes 1966088 | tf_op jit(solution)/shard_map/ppermute | solution.py:209
  79.2 5.0 %collective-permute-start.2 = (bf16[32,64,128]{2,1,0:T(8,128)(2,1)S(1)}, bf16[32,64,128]{2,1,0:T(8,128)(2,1)}, u32[]{:S(2)}, u32[]{:S(2)}) collective-permute-start(bf16[32,64,128]{2,1,0:T(8,128)(2,1)S(1)} %all-to-all-done.1.got_ref), channel_id=1, source_target_pairs={{0,16},{16,0},{1,17},{17,1},{2,18},{18,2},{3,19},{19,3},{4,20},{20... | collective-permute-start | bytes 1572872 | tf_op jit(solution)/shard_map/ppermute | solution.py:214
  82.2 19.4 %collective-permute-start.10 = (bf16[768,256]{1,0:T(8,128)(2,1)S(1)}, bf16[768,256]{1,0:T(8,128)(2,1)S(1)}, u32[]{:S(2)}, u32[]{:S(2)}) collective-permute-start(bf16[768,256]{1,0:T(8,128)(2,1)S(1)} %slice.13), channel_id=1, source_target_pairs={{0,1},{1,2},{2,3},{3,4},{4,5},{5,6},{6,7},{7,0},{8,9},{9,10},{10,1... | collective-permute-start | bytes 1179656 | tf_op jit(solution)/shard_map/ppermute | solution.py:207
  90.6 14.6 %collective-permute-start.9 = (bf16[768,256]{1,0:T(8,128)(2,1)S(1)}, bf16[768,256]{1,0:T(8,128)(2,1)S(1)}, u32[]{:S(2)}, u32[]{:S(2)}) collective-permute-start(bf16[768,256]{1,0:T(8,128)(2,1)S(1)} %slice.10), channel_id=1, source_target_pairs={{0,7},{1,0},{2,1},{3,2},{4,3},{5,4},{6,5},{7,6},{8,15},{9,8},{10,9... | collective-permute-start | bytes 1179656 | tf_op jit(solution)/shard_map/ppermute | solution.py:228
  95.6 16.6 %collective-permute-start.8 = (bf16[1280,128]{1,0:T(8,128)(2,1)S(1)}, bf16[1280,128]{1,0:T(8,128)(2,1)S(1)}, u32[]{:S(2)}, u32[]{:S(2)}) collective-permute-start(bf16[1280,128]{1,0:T(8,128)(2,1)S(1)} %last_far.2), channel_id=1, source_target_pairs={{0,8},{8,0},{1,9},{9,1},{2,10},{10,2},{3,11},{11,3},{4,12},{12,4},... | collective-permute-start | bytes 983048 | tf_op jit(solution)/shard_map/ppermute | solution.py:236
  106.3 9.9 %collective-permute-start.11 = (bf16[768,128]{1,0:T(8,128)(2,1)S(1)}, bf16[768,128]{1,0:T(8,128)(2,1)S(1)}, u32[]{:S(2)}, u32[]{:S(2)}) collective-permute-start(bf16[768,128]{1,0:T(8,128)(2,1)S(1)} %last_far.3), channel_id=1, source_target_pairs={{0,8},{8,0},{1,9},{9,1},{2,10},{10,2},{3,11},{11,3},{4,12},{12,4},... | collective-permute-start | bytes 589832 | tf_op jit(solution)/shard_map/ppermute | solution.py:236

commit v16 on v15

--- a/solution.py
+++ b/solution.py
@@ -204,9 +204,10 @@
     packed = after(packed, joined)
     far_near = tuple(lax.ppermute(block, "y", route[sign]) for block, sign in zip(near, route))
     bounds = ((0, SPLIT), (SPLIT, row_count))
-    rising = [lax.ppermute(far_near[0][start:stop], "y", up) for start, stop in bounds]
+    pieces = [far_near[0][start:stop] for start, stop in bounds]
+    rising = [lax.ppermute(piece, "y", up) for piece in pieces]
     falling = lax.ppermute(far_near[1], "y", down)
-    last = [lax.ppermute(rising[0], "y", up)]
+    last = [lax.ppermute(after(rising[0], pieces[1]), "y", up)]
     packed = packed.reshape(groups, share + PAD, col_width)
     top_count = PANEL_W // groups // X_HI
     stored, send = butterflies(packed, share, chips, top_count)
@@ -226,15 +227,17 @@
         rising[0],
     )
     last.append(lax.ppermute(after(falling, upper)[SPLIT:], "y", down))
+    offsets = [y_count // 2 - 1, y_count // 2]
+    late = [(offsets, [falling, last[0]], [0, 0])]
+    late.append(([*offsets, 1 - y_count // 2], [falling, last[1], rising[1]], [SPLIT, 0, 0]))
+    fars = [
+        last_product(place, upper, sums[2 * part], *args, True, jnp.bfloat16, 1) for part, args in enumerate(late)
+    ]
     out = []
-    offsets = [y_count // 2 - 1, y_count // 2]
-    for part, (start, _) in enumerate(bounds):
-        blocks, bases, late = [falling, last[part]], [start, 0], []
-        if part:
-            blocks, bases, late = [*blocks, rising[part]], [*bases, 0], [1 - y_count // 2]
-        far = last_product(place, upper, sums[2 * part], offsets + late, blocks, bases, True, jnp.bfloat16, 1)
-        came = lax.ppermute(far, "x_hi", swap)
-        rest = last_product(place, upper, sums[2 * part + 1], offsets + late, blocks, bases, False, jnp.float32, -1)
+    for part, args in enumerate(late):
+        came = lax.ppermute(fars[part], "x_hi", swap)
+        base = after(sums[2 * part + 1], fars[-1])
+        rest = last_product(place, upper, base, *args, False, jnp.float32, -1)
         out.append((rest - came.astype(jnp.float32)).astype(jnp.bfloat16))
     return jnp.concatenate(out, axis=0)
 

time: 118 us -> 117 us (level)
  waiting for transfers between devices: 35.8 us -> 34.1 us
    ppermute x5, waiting for transfers between devices: 14.1 us -> 12.1 us  [the longest x2 8.48 us: per_device(): rising = [lax.ppermute(piece, 'y', up) for piece in pieces]]
    slice x2, local copies, waits for them, and re-layouts: 1.07 us -> 2.89 us  [per_device(): pieces = [far_near[0][start:stop] for start, stop in bounds]]
    unnamed x3 -> x1, local copies, waits for them, and re-layouts: 3.28 us -> 2.3 us
  transfers between devices with their start and end apart: 14 -> 14, of which waited for: 5 -> 6; matrix products, arithmetic and copies ran while one was open for 8% -> 10% of each run, Pallas kernels for 10% -> 10%
where the time goes in v16:
time: 117 us; the launch traced here: 116 us
  starting transfers between devices  57.8 us (49%)
  waiting for transfers between devices  34.1 us (29%)
  Pallas kernels  11.7 us (10%)
  local copies, waits for them, and re-layouts  9.41 us (8%)
  other arithmetic  3.15 us (3%)
    ppermute x2, waiting for transfers between devices, per_device(): lax.ppermute(panel_lower, 'y', route[sign])  11.1 us
    ppermute x2, starting transfers between devices, per_device(): came = lax.ppermute(fars[part], 'x_hi', swap)  9.89 us
    ppermute x2, waiting for transfers between devices, per_device(): rising = [lax.ppermute(piece, 'y', up) for piece in pieces]  8.48 us
    ppermute x2, starting transfers between devices, per_device(): lax.ppermute(block, 'y', route[sign])  7.51 us
    ppermute x2, starting transfers between devices, per_device(): rising = [lax.ppermute(piece, 'y', up) for piece in pieces]  7.51 us
    all_to_all x1, starting transfers between devices, per_device(): got = lax.all_to_all(send, ('chip', 'x_hi'), split_axis=0, concat_axis=0)  7.2 us
    ppermute x2, waiting for transfers between devices, per_device(): lax.ppermute(block, 'y', route[sign])  6.98 us
    ppermute x2, starting transfers between devices, per_device(): lax.ppermute(panel_lower, 'y', route[sign])  6.62 us
  transfers between devices with their start and end apart: 14, of which 6 were waited for; matrix products, arithmetic and copies ran while one was open for 10% of the time, Pallas kernels for 10%

profile of v16, /device:TPU:472, one launch (start us, length us, event | category | flops | bytes accessed | tf_op | source)
XLA Modules:
  0.0 116.3 jit_solution(16103200432943915965)
XLA Ops:
  0.0 4.7 %collective-permute-start = (bf16[2048,256]{1,0:T(8,128)(2,1)}, bf16[2048,256]{1,0:T(8,128)(2,1)}, u32[]{:S(2)}, u32[]{:S(2)}) collective-permute-start(bf16[2048,256]{1,0:T(8,128)(2,1)} %refs_0_.1), channel_id=1, source_target_pairs={{0,1},{1,2},{2,3},{3,4},{4,5},{5,6},{6,7},{7,0},{8,9},{9,10},{10,1... | collective-permute-start | bytes 3145736 | tf_op jit(solution)/shard_map/ppermute | solution.py:193
  4.7 1.9 %collective-permute-start.1 = (bf16[2048,256]{1,0:T(8,128)(2,1)}, bf16[2048,256]{1,0:T(8,128)(2,1)}, u32[]{:S(2)}, u32[]{:S(2)}) collective-permute-start(bf16[2048,256]{1,0:T(8,128)(2,1)} %refs_0_.1), channel_id=1, source_target_pairs={{0,7},{1,0},{2,1},{3,2},{4,3},{5,4},{6,5},{7,6},{8,15},{9,8},{10,9... | collective-permute-start | bytes 3145736 | tf_op jit(solution)/shard_map/ppermute | solution.py:193
  8.2 1.4 %multiply_convert_fusion = bf16[2048,128]{1,0:T(8,128)(2,1)S(1)} fusion(bf16[2048,128]{1,0:T(8,128)(2,1)} %param.4, f32[2048]{0:T(1024)S(1)} %convert_element_type.23), kind=kLoop, calls=%fused_computation.2 | loop fusion | flops 786432 | bytes 1056768 | tf_op jit(solution)/shard_map/convert_element_type | solution.py:195
  9.6 1.0 copy.10
  10.7 5.7 %all-to-all-start = ((bf16[72,32,128]{2,0,1:T(8,128)(2,1)}), bf16[72,32,128]{2,0,1:T(8,128)(2,1)S(1)}, u32[]{:S(2)}, u32[]{:S(2)}) async-start(bf16[72,32,128]{2,0,1:T(8,128)(2,1)} %copy.10), calls=%async_computation | async-start | bytes 1179648 | tf_op jit(solution)/shard_map/all_to_all | solution.py:202
  16.3 11.1 %collective-permute-done = bf16[2048,256]{1,0:T(8,128)(2,1)} collective-permute-done((bf16[2048,256]{1,0:T(8,128)(2,1)}, bf16[2048,256]{1,0:T(8,128)(2,1)}, u32[]{:S(2)}, u32[]{:S(2)}) %collective-permute-start) | collective-permute-done | bytes 1048608 | tf_op jit(solution)/shard_map/ppermute | solution.py:193
  27.4 5.6 %collective-permute-start.3 = (bf16[2048,256]{1,0:T(8,128)(2,1)}, bf16[2048,256]{1,0:T(8,128)(2,1)}, u32[]{:S(2)}, u32[]{:S(2)}) collective-permute-start(bf16[2048,256]{1,0:T(8,128)(2,1)} %collective-permute-done), channel_id=1, source_target_pairs={{0,1},{1,2},{2,3},{3,4},{4,5},{5,6},{6,7},{7,0},{8,9},{9,10},{10,1... | collective-permute-start | bytes 3145736 | tf_op jit(solution)/shard_map/ppermute | solution.py:205
  33.0 1.9 %collective-permute-start.4 = (bf16[2048,256]{1,0:T(8,128)(2,1)}, bf16[2048,256]{1,0:T(8,128)(2,1)}, u32[]{:S(2)}, u32[]{:S(2)}) collective-permute-start(bf16[2048,256]{1,0:T(8,128)(2,1)} %collective-permute-done.1), channel_id=1, source_target_pairs={{0,7},{1,0},{2,1},{3,2},{4,3},{5,4},{6,5},{7,6},{8,15},{9,8},{10,9... | collective-permute-start | bytes 3145736 | tf_op jit(solution)/shard_map/ppermute | solution.py:205
  35.0 2.3 %constant_dynamic-update-slice_fusion.1 = bf16[2048,512]{1,0:T(8,128)(2,1)} fusion(bf16[2048,256]{1,0:T(8,128)(2,1)} %collective-permute-done), kind=kLoop, calls=%fused_computation.8 | loop fusion | bytes 2097152
  37.3 2.3 %constant_dynamic-update-slice_fusion.refs_1_ = bf16[2048,512]{1,0:T(8,128)(2,1)} fusion(bf16[2048,512]{1,0:T(8,128)(2,1)} %constant_dynamic-update-slice_fusion.1, bf16[2048,256]{1,0:T(8,128)(2,1)} %collective-permute-done.1), kind=kLoop, calls=%fused_computation.7 | loop fusion | bytes 2097152 | tf_op jit(solution)/shard_map/concatenate | solution.py:203
  39.6 1.1 butterflies.1
  40.7 7.2 %all-to-all-start.1 = ((bf16[32,64,128]{2,1,0:T(8,128)(2,1)}), bf16[32,64,128]{2,1,0:T(8,128)(2,1)S(1)}, u32[]{:S(2)}, u32[]{:S(2)}) async-start(bf16[32,64,128]{2,1,0:T(8,128)(2,1)} %get-tuple-element.18), calls=%async_computation.1 | async-start | bytes 1048576 | tf_op jit(solution)/shard_map/all_to_all | solution.py:214
  47.9 7.0 %collective-permute-done.3.refs_2_ = bf16[2048,256]{1,0:T(8,128)(2,1)} collective-permute-done((bf16[2048,256]{1,0:T(8,128)(2,1)}, bf16[2048,256]{1,0:T(8,128)(2,1)}, u32[]{:S(2)}, u32[]{:S(2)}) %collective-permute-start.3) | collective-permute-done | bytes 1048608 | tf_op jit(solution)/shard_map/ppermute | solution.py:205
  54.9 1.1 slice.12
  56.0 5.6 %collective-permute-start.5 = (bf16[1280,256]{1,0:T(8,128)(2,1)S(1)}, bf16[1280,256]{1,0:T(8,128)(2,1)S(1)}, u32[]{:S(2)}, u32[]{:S(2)}) collective-permute-start(bf16[1280,256]{1,0:T(8,128)(2,1)S(1)} %slice.12), channel_id=1, source_target_pairs={{0,1},{1,2},{2,3},{3,4},{4,5},{5,6},{6,7},{7,0},{8,9},{9,10},{10,1... | collective-permute-start | bytes 1966088 | tf_op jit(solution)/shard_map/ppermute | solution.py:208
  61.6 1.9 %collective-permute-start.6 = (bf16[2048,256]{1,0:T(8,128)(2,1)}, bf16[2048,256]{1,0:T(8,128)(2,1)S(1)}, u32[]{:S(2)}, u32[]{:S(2)}) collective-permute-start(bf16[2048,256]{1,0:T(8,128)(2,1)} %collective-permute-done.4.refs_3_), channel_id=1, source_target_pairs={{0,7},{1,0},{2,1},{3,2},{4,3},{5,4},{6,5},{7,6},{8,15},{9,8},{10,9... | collective-permute-start | bytes 3145736 | tf_op jit(solution)/shard_map/ppermute | solution.py:209
  63.5 1.8 %slice.13 = bf16[768,256]{1,0:T(8,128)(2,1)} slice(bf16[2048,256]{1,0:T(8,128)(2,1)} %collective-permute-done.3.refs_2_), slice={[1280:2048], [0:256]} | slice | bytes 786432 | tf_op jit(solution)/shard_map/slice | solution.py:207
  65.3 8.5 %collective-permute-done.5.refs_4_ = bf16[1280,256]{1,0:T(8,128)(2,1)S(1)} collective-permute-done((bf16[1280,256]{1,0:T(8,128)(2,1)S(1)}, bf16[1280,256]{1,0:T(8,128)(2,1)S(1)}, u32[]{:S(2)}, u32[]{:S(2)}) %collective-permute-start.5) | collective-permute-done | bytes 655392 | tf_op jit(solution)/shard_map/ppermute | solution.py:208
  73.8 5.6 %collective-permute-start.9 = (bf16[1280,256]{1,0:T(8,128)(2,1)S(1)}, bf16[1280,256]{1,0:T(8,128)(2,1)S(1)}, u32[]{:S(2)}, u32[]{:S(2)}) collective-permute-start(bf16[1280,256]{1,0:T(8,128)(2,1)S(1)} %collective-permute-done.5.refs_4_), channel_id=1, source_target_pairs={{0,1},{1,2},{2,3},{3,4},{4,5},{5,6},{6,7},{7,0},{8,9},{9,10},{10,1... | collective-permute-start | bytes 1966088 | tf_op jit(solution)/shard_map/ppermute | solution.py:210
  79.4 1.9 %collective-permute-start.2 = (bf16[32,64,128]{2,1,0:T(8,128)(2,1)S(1)}, bf16[32,64,128]{2,1,0:T(8,128)(2,1)}, u32[]{:S(2)}, u32[]{:S(2)}) collective-permute-start(bf16[32,64,128]{2,1,0:T(8,128)(2,1)S(1)} %all-to-all-done.1.got_ref), channel_id=1, source_target_pairs={{0,16},{16,0},{1,17},{17,1},{2,18},{18,2},{3,19},{19,3},{4,20},{20... | collective-permute-start | bytes 1572872 | tf_op jit(solution)/shard_map/ppermute | solution.py:215
  81.4 1.9 %collective-permute-start.8 = (bf16[768,256]{1,0:T(8,128)(2,1)}, bf16[768,256]{1,0:T(8,128)(2,1)S(1)}, u32[]{:S(2)}, u32[]{:S(2)}) collective-permute-start(bf16[768,256]{1,0:T(8,128)(2,1)} %slice.13), channel_id=1, source_target_pairs={{0,1},{1,2},{2,3},{3,4},{4,5},{5,6},{6,7},{7,0},{8,9},{9,10},{10,1... | collective-permute-start | bytes 1179656 | tf_op jit(solution)/shard_map/ppermute | solution.py:208
  83.3 6.4 %early_products.1 = (f32[1280,128]{1,0:T(8,128)S(1)}, f32[1280,128]{1,0:T(8,128)S(1)}, f32[768,128]{1,0:T(8,128)S(1)}, f32[768,128]{1,0:T(8,128)S(1)}, bf16[8,256,256]{2,1,0:T(8,128)(2,1)S(1)}) custom-call(s32[3]{0:T(128)S(1)} %pad_add_fusion.place_ref, bf16[32,64,128]{2,1,0:T(8,128)(2,1)S(1)} %all-to-all-done.1.got_ref, ...), custom_call_target="tpu_custom_call" | custom-call | tf_op jit(solution)/shard_map/early_products/pallas_call | solution.py:134
  89.8 3.9 %collective-permute-start.7 = (bf16[768,256]{1,0:T(8,128)(2,1)S(1)}, bf16[768,256]{1,0:T(8,128)(2,1)S(1)}, u32[]{:S(2)}, u32[]{:S(2)}) collective-permute-start(bf16[768,256]{1,0:T(8,128)(2,1)S(1)} %slice.10), channel_id=1, source_target_pairs={{0,7},{1,0},{2,1},{3,2},{4,3},{5,4},{6,5},{7,6},{8,15},{9,8},{10,9... | collective-permute-start | bytes 1179656 | tf_op jit(solution)/shard_map/ppermute | solution.py:229
  94.5 1.0 last_far.3
  95.6 5.0 %collective-permute-start.10 = (bf16[1280,128]{1,0:T(8,128)(2,1)S(1)}, bf16[1280,128]{1,0:T(8,128)(2,1)S(1)}, u32[]{:S(2)}, u32[]{:S(2)}) collective-permute-start(bf16[1280,128]{1,0:T(8,128)(2,1)S(1)} %last_far.3), channel_id=1, source_target_pairs={{0,8},{8,0},{1,9},{9,1},{2,10},{10,2},{3,11},{11,3},{4,12},{12,4},... | collective-permute-start | bytes 983048 | tf_op jit(solution)/shard_map/ppermute | solution.py:238
  100.6 3.9 %collective-permute-done.7.refs_1_ = bf16[768,256]{1,0:T(8,128)(2,1)S(1)} collective-permute-done((bf16[768,256]{1,0:T(8,128)(2,1)S(1)}, bf16[768,256]{1,0:T(8,128)(2,1)S(1)}, u32[]{:S(2)}, u32[]{:S(2)}) %collective-permute-start.7) | collective-permute-done | bytes 393248 | tf_op jit(solution)/shard_map/ppermute | solution.py:229
  104.5 1.0 last_far.2
  105.5 4.9 %collective-permute-start.11 = (bf16[768,128]{1,0:T(8,128)(2,1)S(1)}, bf16[768,128]{1,0:T(8,128)(2,1)S(1)}, u32[]{:S(2)}, u32[]{:S(2)}) collective-permute-start(bf16[768,128]{1,0:T(8,128)(2,1)S(1)} %last_far.2), channel_id=1, source_target_pairs={{0,8},{8,0},{1,9},{9,1},{2,10},{10,2},{3,11},{11,3},{4,12},{12,4},... | collective-permute-start | bytes 589832 | tf_op jit(solution)/shard_map/ppermute | solution.py:238
  110.4 1.0 last_own.2
  111.5 1.0 last_own.3
  112.6 2.8 %collective-permute-done.11 = bf16[768,128]{1,0:T(8,128)(2,1)S(1)} collective-permute-done((bf16[768,128]{1,0:T(8,128)(2,1)S(1)}, bf16[768,128]{1,0:T(8,128)(2,1)S(1)}, u32[]{:S(2)}, u32[]{:S(2)}) %collective-permute-start.11) | collective-permute-done | bytes 196640 | tf_op jit(solution)/shard_map/ppermute | solution.py:238
  115.5 0.8 pad_maximum_fusion
  (17 shorter events, 2.6 us)
Async XLA Ops:
  0.0 27.4 %collective-permute-start = (bf16[2048,256]{1,0:T(8,128)(2,1)}, bf16[2048,256]{1,0:T(8,128)(2,1)}, u32[]{:S(2)}, u32[]{:S(2)}) collective-permute-start(bf16[2048,256]{1,0:T(8,128)(2,1)} %refs_0_.1), channel_id=1, source_target_pairs={{0,1},{1,2},{2,3},{3,4},{4,5},{5,6},{6,7},{7,0},{8,9},{9,10},{10,1... | collective-permute-start | bytes 3145736 | tf_op jit(solution)/shard_map/ppermute | solution.py:193
  4.7 28.3 %collective-permute-start.1 = (bf16[2048,256]{1,0:T(8,128)(2,1)}, bf16[2048,256]{1,0:T(8,128)(2,1)}, u32[]{:S(2)}, u32[]{:S(2)}) collective-permute-start(bf16[2048,256]{1,0:T(8,128)(2,1)} %refs_0_.1), channel_id=1, source_target_pairs={{0,7},{1,0},{2,1},{3,2},{4,3},{5,4},{6,5},{7,6},{8,15},{9,8},{10,9... | collective-permute-start | bytes 3145736 | tf_op jit(solution)/shard_map/ppermute | solution.py:193
  10.7 28.9 %all-to-all-start = ((bf16[72,32,128]{2,0,1:T(8,128)(2,1)}), bf16[72,32,128]{2,0,1:T(8,128)(2,1)S(1)}, u32[]{:S(2)}, u32[]{:S(2)}) async-start(bf16[72,32,128]{2,0,1:T(8,128)(2,1)} %copy.10), calls=%async_computation | async-start | bytes 1179648 | tf_op jit(solution)/shard_map/all_to_all | solution.py:202
  27.4 27.4 %collective-permute-start.3 = (bf16[2048,256]{1,0:T(8,128)(2,1)}, bf16[2048,256]{1,0:T(8,128)(2,1)}, u32[]{:S(2)}, u32[]{:S(2)}) collective-permute-start(bf16[2048,256]{1,0:T(8,128)(2,1)} %collective-permute-done), channel_id=1, source_target_pairs={{0,1},{1,2},{2,3},{3,4},{4,5},{5,6},{6,7},{7,0},{8,9},{9,10},{10,1... | collective-permute-start | bytes 3145736 | tf_op jit(solution)/shard_map/ppermute | solution.py:205
  33.0 28.6 %collective-permute-start.4 = (bf16[2048,256]{1,0:T(8,128)(2,1)}, bf16[2048,256]{1,0:T(8,128)(2,1)}, u32[]{:S(2)}, u32[]{:S(2)}) collective-permute-start(bf16[2048,256]{1,0:T(8,128)(2,1)} %collective-permute-done.1), channel_id=1, source_target_pairs={{0,7},{1,0},{2,1},{3,2},{4,3},{5,4},{6,5},{7,6},{8,15},{9,8},{10,9... | collective-permute-start | bytes 3145736 | tf_op jit(solution)/shard_map/ppermute | solution.py:205
  40.7 38.7 %all-to-all-start.1 = ((bf16[32,64,128]{2,1,0:T(8,128)(2,1)}), bf16[32,64,128]{2,1,0:T(8,128)(2,1)S(1)}, u32[]{:S(2)}, u32[]{:S(2)}) async-start(bf16[32,64,128]{2,1,0:T(8,128)(2,1)} %get-tuple-element.18), calls=%async_computation.1 | async-start | bytes 1048576 | tf_op jit(solution)/shard_map/all_to_all | solution.py:214
  56.0 17.8 %collective-permute-start.5 = (bf16[1280,256]{1,0:T(8,128)(2,1)S(1)}, bf16[1280,256]{1,0:T(8,128)(2,1)S(1)}, u32[]{:S(2)}, u32[]{:S(2)}) collective-permute-start(bf16[1280,256]{1,0:T(8,128)(2,1)S(1)} %slice.12), channel_id=1, source_target_pairs={{0,1},{1,2},{2,3},{3,4},{4,5},{5,6},{6,7},{7,0},{8,9},{9,10},{10,1... | collective-permute-start | bytes 1966088 | tf_op jit(solution)/shard_map/ppermute | solution.py:208
  61.6 28.2 %collective-permute-start.6 = (bf16[2048,256]{1,0:T(8,128)(2,1)}, bf16[2048,256]{1,0:T(8,128)(2,1)S(1)}, u32[]{:S(2)}, u32[]{:S(2)}) collective-permute-start(bf16[2048,256]{1,0:T(8,128)(2,1)} %collective-permute-done.4.refs_3_), channel_id=1, source_target_pairs={{0,7},{1,0},{2,1},{3,2},{4,3},{5,4},{6,5},{7,6},{8,15},{9,8},{10,9... | collective-permute-start | bytes 3145736 | tf_op jit(solution)/shard_map/ppermute | solution.py:209
  73.8 20.8 %collective-permute-start.9 = (bf16[1280,256]{1,0:T(8,128)(2,1)S(1)}, bf16[1280,256]{1,0:T(8,128)(2,1)S(1)}, u32[]{:S(2)}, u32[]{:S(2)}) collective-permute-start(bf16[1280,256]{1,0:T(8,128)(2,1)S(1)} %collective-permute-done.5.refs_4_), channel_id=1, source_target_pairs={{0,1},{1,2},{2,3},{3,4},{4,5},{5,6},{6,7},{7,0},{8,9},{9,10},{10,1... | collective-permute-start | bytes 1966088 | tf_op jit(solution)/shard_map/ppermute | solution.py:210
  79.4 3.9 %collective-permute-start.2 = (bf16[32,64,128]{2,1,0:T(8,128)(2,1)S(1)}, bf16[32,64,128]{2,1,0:T(8,128)(2,1)}, u32[]{:S(2)}, u32[]{:S(2)}) collective-permute-start(bf16[32,64,128]{2,1,0:T(8,128)(2,1)S(1)} %all-to-all-done.1.got_ref), channel_id=1, source_target_pairs={{0,16},{16,0},{1,17},{17,1},{2,18},{18,2},{3,19},{19,3},{4,20},{20... | collective-permute-start | bytes 1572872 | tf_op jit(solution)/shard_map/ppermute | solution.py:215
  81.4 19.2 %collective-permute-start.8 = (bf16[768,256]{1,0:T(8,128)(2,1)}, bf16[768,256]{1,0:T(8,128)(2,1)S(1)}, u32[]{:S(2)}, u32[]{:S(2)}) collective-permute-start(bf16[768,256]{1,0:T(8,128)(2,1)} %slice.13), channel_id=1, source_target_pairs={{0,1},{1,2},{2,3},{3,4},{4,5},{5,6},{6,7},{7,0},{8,9},{9,10},{10,1... | collective-permute-start | bytes 1179656 | tf_op jit(solution)/shard_map/ppermute | solution.py:208
  89.8 14.6 %collective-permute-start.7 = (bf16[768,256]{1,0:T(8,128)(2,1)S(1)}, bf16[768,256]{1,0:T(8,128)(2,1)S(1)}, u32[]{:S(2)}, u32[]{:S(2)}) collective-permute-start(bf16[768,256]{1,0:T(8,128)(2,1)S(1)} %slice.10), channel_id=1, source_target_pairs={{0,7},{1,0},{2,1},{3,2},{4,3},{5,4},{6,5},{7,6},{8,15},{9,8},{10,9... | collective-permute-start | bytes 1179656 | tf_op jit(solution)/shard_map/ppermute | solution.py:229
  95.6 16.9 %collective-permute-start.10 = (bf16[1280,128]{1,0:T(8,128)(2,1)S(1)}, bf16[1280,128]{1,0:T(8,128)(2,1)S(1)}, u32[]{:S(2)}, u32[]{:S(2)}) collective-permute-start(bf16[1280,128]{1,0:T(8,128)(2,1)S(1)} %last_far.3), channel_id=1, source_target_pairs={{0,8},{8,0},{1,9},{9,1},{2,10},{10,2},{3,11},{11,3},{4,12},{12,4},... | collective-permute-start | bytes 983048 | tf_op jit(solution)/shard_map/ppermute | solution.py:238
  105.5 9.9 %collective-permute-start.11 = (bf16[768,128]{1,0:T(8,128)(2,1)S(1)}, bf16[768,128]{1,0:T(8,128)(2,1)S(1)}, u32[]{:S(2)}, u32[]{:S(2)}) collective-permute-start(bf16[768,128]{1,0:T(8,128)(2,1)S(1)} %last_far.2), channel_id=1, source_target_pairs={{0,8},{8,0},{1,9},{9,1},{2,10},{10,2},{3,11},{11,3},{4,12},{12,4},... | collective-permute-start | bytes 589832 | tf_op jit(solution)/shard_map/ppermute | solution.py:238

commit v17 on v16

--- a/solution.py
+++ b/solution.py
@@ -129,7 +129,7 @@
                 rest_ref[local] = stored_ref[full].astype(jnp.float32) - jnp.where(at_left, left, right)
                 return carry
 
-            lax.fori_loop(0, (stop - start) // TILE_M, one, 0)
+            lax.fori_loop(0, (stop - start) // TILE_M, one, 0, unroll=True)
 
     return pl.pallas_call(
         body,

time: 117 us -> 117 us (level)
  the two profiles are of different devices: /device:TPU:472 before, /device:TPU:476 now
where the time goes in v17:
time: 117 us; the launch traced here: 116 us
  starting transfers between devices  52.3 us (45%)
  waiting for transfers between devices  39.5 us (34%)
  Pallas kernels  11 us (9%)
  local copies, waits for them, and re-layouts  9.41 us (8%)
  other arithmetic  3.15 us (3%)
    ppermute x2, waiting for transfers between devices, per_device(): lax.ppermute(panel_lower, 'y', route[sign])  11.4 us
    ppermute x2, waiting for transfers between devices, per_device(): rising = [lax.ppermute(piece, 'y', up) for piece in pieces]  9.67 us
    ppermute x2, starting transfers between devices, per_device(): lax.ppermute(block, 'y', route[sign])  7.51 us
    ppermute x2, starting transfers between devices, per_device(): rising = [lax.ppermute(piece, 'y', up) for piece in pieces]  7.51 us
    all_to_all x1, starting transfers between devices, per_device(): got = lax.all_to_all(send, ('chip', 'x_hi'), split_axis=0, concat_axis=0)  7.15 us
    ppermute x2, waiting for transfers between devices, per_device(): lax.ppermute(block, 'y', route[sign])  7.04 us
    ppermute x2, starting transfers between devices, per_device(): lax.ppermute(panel_lower, 'y', route[sign])  6.61 us
    pallas_call x1, Pallas kernels, early_products(): pl.pallas_call(body, in_specs=[pl.BlockSpec(memory_space=pltpu.SMEM)] + [...  5.77 us
  transfers between devices with their start and end apart: 14, of which 7 were waited for; matrix products, arithmetic and copies ran while one was open for 10% of the time, Pallas kernels for 10%

profile of v17, /device:TPU:476, one launch (start us, length us, event | category | flops | bytes accessed | tf_op | source)
XLA Modules:
  0.0 115.6 jit_solution(12380086115118487036)
XLA Ops:
  0.0 4.7 %collective-permute-start = (bf16[2048,256]{1,0:T(8,128)(2,1)}, bf16[2048,256]{1,0:T(8,128)(2,1)}, u32[]{:S(2)}, u32[]{:S(2)}) collective-permute-start(bf16[2048,256]{1,0:T(8,128)(2,1)} %refs_0_.1), channel_id=1, source_target_pairs={{0,1},{1,2},{2,3},{3,4},{4,5},{5,6},{6,7},{7,0},{8,9},{9,10},{10,1... | collective-permute-start | bytes 3145736 | tf_op jit(solution)/shard_map/ppermute | solution.py:193
  4.7 1.9 %collective-permute-start.1 = (bf16[2048,256]{1,0:T(8,128)(2,1)}, bf16[2048,256]{1,0:T(8,128)(2,1)}, u32[]{:S(2)}, u32[]{:S(2)}) collective-permute-start(bf16[2048,256]{1,0:T(8,128)(2,1)} %refs_0_.1), channel_id=1, source_target_pairs={{0,7},{1,0},{2,1},{3,2},{4,3},{5,4},{6,5},{7,6},{8,15},{9,8},{10,9... | collective-permute-start | bytes 3145736 | tf_op jit(solution)/shard_map/ppermute | solution.py:193
  8.2 1.4 %multiply_convert_fusion = bf16[2048,128]{1,0:T(8,128)(2,1)S(1)} fusion(bf16[2048,128]{1,0:T(8,128)(2,1)} %param.4, f32[2048]{0:T(1024)S(1)} %convert_element_type.23), kind=kLoop, calls=%fused_computation.2 | loop fusion | flops 786432 | bytes 1056768 | tf_op jit(solution)/shard_map/convert_element_type | solution.py:195
  9.6 1.0 copy.10
  10.7 5.4 %all-to-all-start = ((bf16[72,32,128]{2,0,1:T(8,128)(2,1)}), bf16[72,32,128]{2,0,1:T(8,128)(2,1)S(1)}, u32[]{:S(2)}, u32[]{:S(2)}) async-start(bf16[72,32,128]{2,0,1:T(8,128)(2,1)} %copy.10), calls=%async_computation | async-start | bytes 1179648 | tf_op jit(solution)/shard_map/all_to_all | solution.py:202
  16.0 11.4 %collective-permute-done = bf16[2048,256]{1,0:T(8,128)(2,1)} collective-permute-done((bf16[2048,256]{1,0:T(8,128)(2,1)}, bf16[2048,256]{1,0:T(8,128)(2,1)}, u32[]{:S(2)}, u32[]{:S(2)}) %collective-permute-start) | collective-permute-done | bytes 1048608 | tf_op jit(solution)/shard_map/ppermute | solution.py:193
  27.4 5.6 %collective-permute-start.3 = (bf16[2048,256]{1,0:T(8,128)(2,1)}, bf16[2048,256]{1,0:T(8,128)(2,1)}, u32[]{:S(2)}, u32[]{:S(2)}) collective-permute-start(bf16[2048,256]{1,0:T(8,128)(2,1)} %collective-permute-done), channel_id=1, source_target_pairs={{0,1},{1,2},{2,3},{3,4},{4,5},{5,6},{6,7},{7,0},{8,9},{9,10},{10,1... | collective-permute-start | bytes 3145736 | tf_op jit(solution)/shard_map/ppermute | solution.py:205
  33.0 1.9 %collective-permute-start.4 = (bf16[2048,256]{1,0:T(8,128)(2,1)}, bf16[2048,256]{1,0:T(8,128)(2,1)}, u32[]{:S(2)}, u32[]{:S(2)}) collective-permute-start(bf16[2048,256]{1,0:T(8,128)(2,1)} %collective-permute-done.1), channel_id=1, source_target_pairs={{0,7},{1,0},{2,1},{3,2},{4,3},{5,4},{6,5},{7,6},{8,15},{9,8},{10,9... | collective-permute-start | bytes 3145736 | tf_op jit(solution)/shard_map/ppermute | solution.py:205
  35.0 2.3 %constant_dynamic-update-slice_fusion.1 = bf16[2048,512]{1,0:T(8,128)(2,1)} fusion(bf16[2048,256]{1,0:T(8,128)(2,1)} %collective-permute-done), kind=kLoop, calls=%fused_computation.8 | loop fusion | bytes 2097152
  37.3 2.3 %constant_dynamic-update-slice_fusion.refs_1_ = bf16[2048,512]{1,0:T(8,128)(2,1)} fusion(bf16[2048,512]{1,0:T(8,128)(2,1)} %constant_dynamic-update-slice_fusion.1, bf16[2048,256]{1,0:T(8,128)(2,1)} %collective-permute-done.1), kind=kLoop, calls=%fused_computation.7 | loop fusion | bytes 2097152 | tf_op jit(solution)/shard_map/concatenate | solution.py:203
  39.6 1.1 butterflies.1
  40.7 7.1 %all-to-all-start.1 = ((bf16[32,64,128]{2,1,0:T(8,128)(2,1)}), bf16[32,64,128]{2,1,0:T(8,128)(2,1)S(1)}, u32[]{:S(2)}, u32[]{:S(2)}) async-start(bf16[32,64,128]{2,1,0:T(8,128)(2,1)} %get-tuple-element.18), calls=%async_computation.1 | async-start | bytes 1048576 | tf_op jit(solution)/shard_map/all_to_all | solution.py:214
  47.8 7.0 %collective-permute-done.3.refs_2_ = bf16[2048,256]{1,0:T(8,128)(2,1)} collective-permute-done((bf16[2048,256]{1,0:T(8,128)(2,1)}, bf16[2048,256]{1,0:T(8,128)(2,1)}, u32[]{:S(2)}, u32[]{:S(2)}) %collective-permute-start.3) | collective-permute-done | bytes 1048608 | tf_op jit(solution)/shard_map/ppermute | solution.py:205
  54.9 1.1 slice.12
  56.0 5.6 %collective-permute-start.5 = (bf16[1280,256]{1,0:T(8,128)(2,1)S(1)}, bf16[1280,256]{1,0:T(8,128)(2,1)S(1)}, u32[]{:S(2)}, u32[]{:S(2)}) collective-permute-start(bf16[1280,256]{1,0:T(8,128)(2,1)S(1)} %slice.12), channel_id=1, source_target_pairs={{0,1},{1,2},{2,3},{3,4},{4,5},{5,6},{6,7},{7,0},{8,9},{9,10},{10,1... | collective-permute-start | bytes 1966088 | tf_op jit(solution)/shard_map/ppermute | solution.py:208
  61.6 1.9 %collective-permute-start.6 = (bf16[2048,256]{1,0:T(8,128)(2,1)}, bf16[2048,256]{1,0:T(8,128)(2,1)S(1)}, u32[]{:S(2)}, u32[]{:S(2)}) collective-permute-start(bf16[2048,256]{1,0:T(8,128)(2,1)} %collective-permute-done.4.refs_3_), channel_id=1, source_target_pairs={{0,7},{1,0},{2,1},{3,2},{4,3},{5,4},{6,5},{7,6},{8,15},{9,8},{10,9... | collective-permute-start | bytes 3145736 | tf_op jit(solution)/shard_map/ppermute | solution.py:209
  63.5 1.8 %slice.13 = bf16[768,256]{1,0:T(8,128)(2,1)} slice(bf16[2048,256]{1,0:T(8,128)(2,1)} %collective-permute-done.3.refs_2_), slice={[1280:2048], [0:256]} | slice | bytes 786432 | tf_op jit(solution)/shard_map/slice | solution.py:207
  65.3 8.5 %collective-permute-done.5.refs_4_ = bf16[1280,256]{1,0:T(8,128)(2,1)S(1)} collective-permute-done((bf16[1280,256]{1,0:T(8,128)(2,1)S(1)}, bf16[1280,256]{1,0:T(8,128)(2,1)S(1)}, u32[]{:S(2)}, u32[]{:S(2)}) %collective-permute-start.5) | collective-permute-done | bytes 655392 | tf_op jit(solution)/shard_map/ppermute | solution.py:208
  73.8 5.6 %collective-permute-start.9 = (bf16[1280,256]{1,0:T(8,128)(2,1)S(1)}, bf16[1280,256]{1,0:T(8,128)(2,1)S(1)}, u32[]{:S(2)}, u32[]{:S(2)}) collective-permute-start(bf16[1280,256]{1,0:T(8,128)(2,1)S(1)} %collective-permute-done.5.refs_4_), channel_id=1, source_target_pairs={{0,1},{1,2},{2,3},{3,4},{4,5},{5,6},{6,7},{7,0},{8,9},{9,10},{10,1... | collective-permute-start | bytes 1966088 | tf_op jit(solution)/shard_map/ppermute | solution.py:210
  79.4 1.9 %collective-permute-start.2 = (bf16[32,64,128]{2,1,0:T(8,128)(2,1)S(1)}, bf16[32,64,128]{2,1,0:T(8,128)(2,1)}, u32[]{:S(2)}, u32[]{:S(2)}) collective-permute-start(bf16[32,64,128]{2,1,0:T(8,128)(2,1)S(1)} %all-to-all-done.1.got_ref), channel_id=1, source_target_pairs={{0,16},{16,0},{1,17},{17,1},{2,18},{18,2},{3,19},{19,3},{4,20},{20... | collective-permute-start | bytes 1572872 | tf_op jit(solution)/shard_map/ppermute | solution.py:215
  81.4 1.9 %collective-permute-start.8 = (bf16[768,256]{1,0:T(8,128)(2,1)}, bf16[768,256]{1,0:T(8,128)(2,1)S(1)}, u32[]{:S(2)}, u32[]{:S(2)}) collective-permute-start(bf16[768,256]{1,0:T(8,128)(2,1)} %slice.13), channel_id=1, source_target_pairs={{0,1},{1,2},{2,3},{3,4},{4,5},{5,6},{6,7},{7,0},{8,9},{9,10},{10,1... | collective-permute-start | bytes 1179656 | tf_op jit(solution)/shard_map/ppermute | solution.py:208
  83.3 5.8 %early_products.1 = (f32[1280,128]{1,0:T(8,128)S(1)}, f32[1280,128]{1,0:T(8,128)S(1)}, f32[768,128]{1,0:T(8,128)S(1)}, f32[768,128]{1,0:T(8,128)S(1)}, bf16[8,256,256]{2,1,0:T(8,128)(2,1)S(1)}) custom-call(s32[3]{0:T(128)S(1)} %pad_add_fusion.place_ref, bf16[32,64,128]{2,1,0:T(8,128)(2,1)S(1)} %all-to-all-done.1.got_ref, ...), custom_call_target="tpu_custom_call" | custom-call | tf_op jit(solution)/shard_map/early_products/pallas_call | solution.py:134
  89.2 3.9 %collective-permute-start.7 = (bf16[768,256]{1,0:T(8,128)(2,1)S(1)}, bf16[768,256]{1,0:T(8,128)(2,1)S(1)}, u32[]{:S(2)}, u32[]{:S(2)}) collective-permute-start(bf16[768,256]{1,0:T(8,128)(2,1)S(1)} %slice.10), channel_id=1, source_target_pairs={{0,7},{1,0},{2,1},{3,2},{4,3},{5,4},{6,5},{7,6},{8,15},{9,8},{10,9... | collective-permute-start | bytes 1179656 | tf_op jit(solution)/shard_map/ppermute | solution.py:229
  93.1 1.5 %collective-permute-done.9.refs_1_ = bf16[1280,256]{1,0:T(8,128)(2,1)S(1)} collective-permute-done((bf16[1280,256]{1,0:T(8,128)(2,1)S(1)}, bf16[1280,256]{1,0:T(8,128)(2,1)S(1)}, u32[]{:S(2)}, u32[]{:S(2)}) %collective-permute-start.9) | collective-permute-done | bytes 655392 | tf_op jit(solution)/shard_map/ppermute | solution.py:210
  94.6 1.0 last_far.3
  95.6 2.4 %collective-permute-start.10 = (bf16[1280,128]{1,0:T(8,128)(2,1)S(1)}, bf16[1280,128]{1,0:T(8,128)(2,1)S(1)}, u32[]{:S(2)}, u32[]{:S(2)}) collective-permute-start(bf16[1280,128]{1,0:T(8,128)(2,1)S(1)} %last_far.3), channel_id=1, source_target_pairs={{0,8},{8,0},{1,9},{9,1},{2,10},{10,2},{3,11},{11,3},{4,12},{12,4},... | collective-permute-start | bytes 983048 | tf_op jit(solution)/shard_map/ppermute | solution.py:238
  98.0 1.2 %collective-permute-done.8.refs_2_ = bf16[768,256]{1,0:T(8,128)(2,1)S(1)} collective-permute-done((bf16[768,256]{1,0:T(8,128)(2,1)}, bf16[768,256]{1,0:T(8,128)(2,1)S(1)}, u32[]{:S(2)}, u32[]{:S(2)}) %collective-permute-start.8) | collective-permute-done | bytes 393248 | tf_op jit(solution)/shard_map/ppermute | solution.py:208
  99.2 4.6 %collective-permute-done.7.refs_1_ = bf16[768,256]{1,0:T(8,128)(2,1)S(1)} collective-permute-done((bf16[768,256]{1,0:T(8,128)(2,1)S(1)}, bf16[768,256]{1,0:T(8,128)(2,1)S(1)}, u32[]{:S(2)}, u32[]{:S(2)}) %collective-permute-start.7) | collective-permute-done | bytes 393248 | tf_op jit(solution)/shard_map/ppermute | solution.py:229
  103.8 1.0 last_far.2
  104.8 2.4 %collective-permute-start.11 = (bf16[768,128]{1,0:T(8,128)(2,1)S(1)}, bf16[768,128]{1,0:T(8,128)(2,1)S(1)}, u32[]{:S(2)}, u32[]{:S(2)}) collective-permute-start(bf16[768,128]{1,0:T(8,128)(2,1)S(1)} %last_far.2), channel_id=1, source_target_pairs={{0,8},{8,0},{1,9},{9,1},{2,10},{10,2},{3,11},{11,3},{4,12},{12,4},... | collective-permute-start | bytes 589832 | tf_op jit(solution)/shard_map/ppermute | solution.py:238
  107.2 1.0 last_own.2
  109.4 5.4 %collective-permute-done.11 = bf16[768,128]{1,0:T(8,128)(2,1)S(1)} collective-permute-done((bf16[768,128]{1,0:T(8,128)(2,1)S(1)}, bf16[768,128]{1,0:T(8,128)(2,1)S(1)}, u32[]{:S(2)}, u32[]{:S(2)}) %collective-permute-start.11) | collective-permute-done | bytes 196640 | tf_op jit(solution)/shard_map/ppermute | solution.py:238
  (17 shorter events, 3.7 us)
Async XLA Ops:
  0.0 27.4 %collective-permute-start = (bf16[2048,256]{1,0:T(8,128)(2,1)}, bf16[2048,256]{1,0:T(8,128)(2,1)}, u32[]{:S(2)}, u32[]{:S(2)}) collective-permute-start(bf16[2048,256]{1,0:T(8,128)(2,1)} %refs_0_.1), channel_id=1, source_target_pairs={{0,1},{1,2},{2,3},{3,4},{4,5},{5,6},{6,7},{7,0},{8,9},{9,10},{10,1... | collective-permute-start | bytes 3145736 | tf_op jit(solution)/shard_map/ppermute | solution.py:193
  4.7 28.3 %collective-permute-start.1 = (bf16[2048,256]{1,0:T(8,128)(2,1)}, bf16[2048,256]{1,0:T(8,128)(2,1)}, u32[]{:S(2)}, u32[]{:S(2)}) collective-permute-start(bf16[2048,256]{1,0:T(8,128)(2,1)} %refs_0_.1), channel_id=1, source_target_pairs={{0,7},{1,0},{2,1},{3,2},{4,3},{5,4},{6,5},{7,6},{8,15},{9,8},{10,9... | collective-permute-start | bytes 3145736 | tf_op jit(solution)/shard_map/ppermute | solution.py:193
  10.7 28.9 %all-to-all-start = ((bf16[72,32,128]{2,0,1:T(8,128)(2,1)}), bf16[72,32,128]{2,0,1:T(8,128)(2,1)S(1)}, u32[]{:S(2)}, u32[]{:S(2)}) async-start(bf16[72,32,128]{2,0,1:T(8,128)(2,1)} %copy.10), calls=%async_computation | async-start | bytes 1179648 | tf_op jit(solution)/shard_map/all_to_all | solution.py:202
  27.4 27.4 %collective-permute-start.3 = (bf16[2048,256]{1,0:T(8,128)(2,1)}, bf16[2048,256]{1,0:T(8,128)(2,1)}, u32[]{:S(2)}, u32[]{:S(2)}) collective-permute-start(bf16[2048,256]{1,0:T(8,128)(2,1)} %collective-permute-done), channel_id=1, source_target_pairs={{0,1},{1,2},{2,3},{3,4},{4,5},{5,6},{6,7},{7,0},{8,9},{9,10},{10,1... | collective-permute-start | bytes 3145736 | tf_op jit(solution)/shard_map/ppermute | solution.py:205
  33.0 28.6 %collective-permute-start.4 = (bf16[2048,256]{1,0:T(8,128)(2,1)}, bf16[2048,256]{1,0:T(8,128)(2,1)}, u32[]{:S(2)}, u32[]{:S(2)}) collective-permute-start(bf16[2048,256]{1,0:T(8,128)(2,1)} %collective-permute-done.1), channel_id=1, source_target_pairs={{0,7},{1,0},{2,1},{3,2},{4,3},{5,4},{6,5},{7,6},{8,15},{9,8},{10,9... | collective-permute-start | bytes 3145736 | tf_op jit(solution)/shard_map/ppermute | solution.py:205
  40.7 38.7 %all-to-all-start.1 = ((bf16[32,64,128]{2,1,0:T(8,128)(2,1)}), bf16[32,64,128]{2,1,0:T(8,128)(2,1)S(1)}, u32[]{:S(2)}, u32[]{:S(2)}) async-start(bf16[32,64,128]{2,1,0:T(8,128)(2,1)} %get-tuple-element.18), calls=%async_computation.1 | async-start | bytes 1048576 | tf_op jit(solution)/shard_map/all_to_all | solution.py:214
  56.0 17.8 %collective-permute-start.5 = (bf16[1280,256]{1,0:T(8,128)(2,1)S(1)}, bf16[1280,256]{1,0:T(8,128)(2,1)S(1)}, u32[]{:S(2)}, u32[]{:S(2)}) collective-permute-start(bf16[1280,256]{1,0:T(8,128)(2,1)S(1)} %slice.12), channel_id=1, source_target_pairs={{0,1},{1,2},{2,3},{3,4},{4,5},{5,6},{6,7},{7,0},{8,9},{9,10},{10,1... | collective-permute-start | bytes 1966088 | tf_op jit(solution)/shard_map/ppermute | solution.py:208
  61.6 27.5 %collective-permute-start.6 = (bf16[2048,256]{1,0:T(8,128)(2,1)}, bf16[2048,256]{1,0:T(8,128)(2,1)S(1)}, u32[]{:S(2)}, u32[]{:S(2)}) collective-permute-start(bf16[2048,256]{1,0:T(8,128)(2,1)} %collective-permute-done.4.refs_3_), channel_id=1, source_target_pairs={{0,7},{1,0},{2,1},{3,2},{4,3},{5,4},{6,5},{7,6},{8,15},{9,8},{10,9... | collective-permute-start | bytes 3145736 | tf_op jit(solution)/shard_map/ppermute | solution.py:209
  73.8 20.8 %collective-permute-start.9 = (bf16[1280,256]{1,0:T(8,128)(2,1)S(1)}, bf16[1280,256]{1,0:T(8,128)(2,1)S(1)}, u32[]{:S(2)}, u32[]{:S(2)}) collective-permute-start(bf16[1280,256]{1,0:T(8,128)(2,1)S(1)} %collective-permute-done.5.refs_4_), channel_id=1, source_target_pairs={{0,1},{1,2},{2,3},{3,4},{4,5},{5,6},{6,7},{7,0},{8,9},{9,10},{10,1... | collective-permute-start | bytes 1966088 | tf_op jit(solution)/shard_map/ppermute | solution.py:210
  79.4 3.9 %collective-permute-start.2 = (bf16[32,64,128]{2,1,0:T(8,128)(2,1)S(1)}, bf16[32,64,128]{2,1,0:T(8,128)(2,1)}, u32[]{:S(2)}, u32[]{:S(2)}) collective-permute-start(bf16[32,64,128]{2,1,0:T(8,128)(2,1)S(1)} %all-to-all-done.1.got_ref), channel_id=1, source_target_pairs={{0,16},{16,0},{1,17},{17,1},{2,18},{18,2},{3,19},{19,3},{4,20},{20... | collective-permute-start | bytes 1572872 | tf_op jit(solution)/shard_map/ppermute | solution.py:215
  81.4 17.8 %collective-permute-start.8 = (bf16[768,256]{1,0:T(8,128)(2,1)}, bf16[768,256]{1,0:T(8,128)(2,1)S(1)}, u32[]{:S(2)}, u32[]{:S(2)}) collective-permute-start(bf16[768,256]{1,0:T(8,128)(2,1)} %slice.13), channel_id=1, source_target_pairs={{0,1},{1,2},{2,3},{3,4},{4,5},{5,6},{6,7},{7,0},{8,9},{9,10},{10,1... | collective-permute-start | bytes 1179656 | tf_op jit(solution)/shard_map/ppermute | solution.py:208
  89.2 14.6 %collective-permute-start.7 = (bf16[768,256]{1,0:T(8,128)(2,1)S(1)}, bf16[768,256]{1,0:T(8,128)(2,1)S(1)}, u32[]{:S(2)}, u32[]{:S(2)}) collective-permute-start(bf16[768,256]{1,0:T(8,128)(2,1)S(1)} %slice.10), channel_id=1, source_target_pairs={{0,7},{1,0},{2,1},{3,2},{4,3},{5,4},{6,5},{7,6},{8,15},{9,8},{10,9... | collective-permute-start | bytes 1179656 | tf_op jit(solution)/shard_map/ppermute | solution.py:229
  95.6 13.7 %collective-permute-start.10 = (bf16[1280,128]{1,0:T(8,128)(2,1)S(1)}, bf16[1280,128]{1,0:T(8,128)(2,1)S(1)}, u32[]{:S(2)}, u32[]{:S(2)}) collective-permute-start(bf16[1280,128]{1,0:T(8,128)(2,1)S(1)} %last_far.3), channel_id=1, source_target_pairs={{0,8},{8,0},{1,9},{9,1},{2,10},{10,2},{3,11},{11,3},{4,12},{12,4},... | collective-permute-start | bytes 983048 | tf_op jit(solution)/shard_map/ppermute | solution.py:238
  104.8 9.9 %collective-permute-start.11 = (bf16[768,128]{1,0:T(8,128)(2,1)S(1)}, bf16[768,128]{1,0:T(8,128)(2,1)S(1)}, u32[]{:S(2)}, u32[]{:S(2)}) collective-permute-start(bf16[768,128]{1,0:T(8,128)(2,1)S(1)} %last_far.2), channel_id=1, source_target_pairs={{0,8},{8,0},{1,9},{9,1},{2,10},{10,2},{3,11},{11,3},{4,12},{12,4},... | collective-permute-start | bytes 589832 | tf_op jit(solution)/shard_map/ppermute | solution.py:238

commit v18 on v17

--- a/solution.py
+++ b/solution.py
@@ -9,7 +9,7 @@
 X_HI = 2
 CORES = 2
 PAD = 8
-TILE_M = 256
+TILE_M = 128
 SPLIT = 1280
 ROW = ("chip", "core")
 

time: 117 us -> 116 us (level)
  the two profiles are of different devices: /device:TPU:476 before, /device:TPU:472 now
where the time goes in v18:
time: 116 us; the launch traced here: 115 us
  starting transfers between devices  57.8 us (50%)
  waiting for transfers between devices  34.1 us (29%)
  Pallas kernels  10.7 us (9%)
  local copies, waits for them, and re-layouts  9.41 us (8%)
  other arithmetic  3.15 us (3%)
    ppermute x2, waiting for transfers between devices, per_device(): lax.ppermute(panel_lower, 'y', route[sign])  11.1 us
    ppermute x2, starting transfers between devices, per_device(): came = lax.ppermute(fars[part], 'x_hi', swap)  9.88 us
    ppermute x2, waiting for transfers between devices, per_device(): rising = [lax.ppermute(piece, 'y', up) for piece in pieces]  8.48 us
    ppermute x2, starting transfers between devices, per_device(): lax.ppermute(block, 'y', route[sign])  7.51 us
    ppermute x2, starting transfers between devices, per_device(): rising = [lax.ppermute(piece, 'y', up) for piece in pieces]  7.51 us
    all_to_all x1, starting transfers between devices, per_device(): got = lax.all_to_all(send, ('chip', 'x_hi'), split_axis=0, concat_axis=0)  7.2 us
    ppermute x2, waiting for transfers between devices, per_device(): lax.ppermute(block, 'y', route[sign])  6.98 us
    ppermute x2, starting transfers between devices, per_device(): lax.ppermute(panel_lower, 'y', route[sign])  6.62 us
  transfers between devices with their start and end apart: 14, of which 6 were waited for; matrix products, arithmetic and copies ran while one was open for 10% of the time, Pallas kernels for 9%

profile of v18, /device:TPU:472, one launch (start us, length us, event | category | flops | bytes accessed | tf_op | source)
XLA Modules:
  0.0 115.3 jit_solution(531353914067651395)
XLA Ops:
  0.0 4.7 %collective-permute-start = (bf16[2048,256]{1,0:T(8,128)(2,1)}, bf16[2048,256]{1,0:T(8,128)(2,1)}, u32[]{:S(2)}, u32[]{:S(2)}) collective-permute-start(bf16[2048,256]{1,0:T(8,128)(2,1)} %refs_0_.1), channel_id=1, source_target_pairs={{0,1},{1,2},{2,3},{3,4},{4,5},{5,6},{6,7},{7,0},{8,9},{9,10},{10,1... | collective-permute-start | bytes 3145736 | tf_op jit(solution)/shard_map/ppermute | solution.py:193
  4.7 1.9 %collective-permute-start.1 = (bf16[2048,256]{1,0:T(8,128)(2,1)}, bf16[2048,256]{1,0:T(8,128)(2,1)}, u32[]{:S(2)}, u32[]{:S(2)}) collective-permute-start(bf16[2048,256]{1,0:T(8,128)(2,1)} %refs_0_.1), channel_id=1, source_target_pairs={{0,7},{1,0},{2,1},{3,2},{4,3},{5,4},{6,5},{7,6},{8,15},{9,8},{10,9... | collective-permute-start | bytes 3145736 | tf_op jit(solution)/shard_map/ppermute | solution.py:193
  8.2 1.4 %multiply_convert_fusion = bf16[2048,128]{1,0:T(8,128)(2,1)S(1)} fusion(bf16[2048,128]{1,0:T(8,128)(2,1)} %param.4, f32[2048]{0:T(1024)S(1)} %convert_element_type.23), kind=kLoop, calls=%fused_computation.2 | loop fusion | flops 786432 | bytes 1056768 | tf_op jit(solution)/shard_map/convert_element_type | solution.py:195
  9.6 1.0 copy.10
  10.7 5.7 %all-to-all-start = ((bf16[72,32,128]{2,0,1:T(8,128)(2,1)}), bf16[72,32,128]{2,0,1:T(8,128)(2,1)S(1)}, u32[]{:S(2)}, u32[]{:S(2)}) async-start(bf16[72,32,128]{2,0,1:T(8,128)(2,1)} %copy.10), calls=%async_computation | async-start | bytes 1179648 | tf_op jit(solution)/shard_map/all_to_all | solution.py:202
  16.3 11.1 %collective-permute-done = bf16[2048,256]{1,0:T(8,128)(2,1)} collective-permute-done((bf16[2048,256]{1,0:T(8,128)(2,1)}, bf16[2048,256]{1,0:T(8,128)(2,1)}, u32[]{:S(2)}, u32[]{:S(2)}) %collective-permute-start) | collective-permute-done | bytes 1048608 | tf_op jit(solution)/shard_map/ppermute | solution.py:193
  27.4 5.6 %collective-permute-start.3 = (bf16[2048,256]{1,0:T(8,128)(2,1)}, bf16[2048,256]{1,0:T(8,128)(2,1)}, u32[]{:S(2)}, u32[]{:S(2)}) collective-permute-start(bf16[2048,256]{1,0:T(8,128)(2,1)} %collective-permute-done), channel_id=1, source_target_pairs={{0,1},{1,2},{2,3},{3,4},{4,5},{5,6},{6,7},{7,0},{8,9},{9,10},{10,1... | collective-permute-start | bytes 3145736 | tf_op jit(solution)/shard_map/ppermute | solution.py:205
  33.0 1.9 %collective-permute-start.4 = (bf16[2048,256]{1,0:T(8,128)(2,1)}, bf16[2048,256]{1,0:T(8,128)(2,1)}, u32[]{:S(2)}, u32[]{:S(2)}) collective-permute-start(bf16[2048,256]{1,0:T(8,128)(2,1)} %collective-permute-done.1), channel_id=1, source_target_pairs={{0,7},{1,0},{2,1},{3,2},{4,3},{5,4},{6,5},{7,6},{8,15},{9,8},{10,9... | collective-permute-start | bytes 3145736 | tf_op jit(solution)/shard_map/ppermute | solution.py:205
  35.0 2.3 %constant_dynamic-update-slice_fusion.1 = bf16[2048,512]{1,0:T(8,128)(2,1)} fusion(bf16[2048,256]{1,0:T(8,128)(2,1)} %collective-permute-done), kind=kLoop, calls=%fused_computation.8 | loop fusion | bytes 2097152
  37.3 2.3 %constant_dynamic-update-slice_fusion.refs_1_ = bf16[2048,512]{1,0:T(8,128)(2,1)} fusion(bf16[2048,512]{1,0:T(8,128)(2,1)} %constant_dynamic-update-slice_fusion.1, bf16[2048,256]{1,0:T(8,128)(2,1)} %collective-permute-done.1), kind=kLoop, calls=%fused_computation.7 | loop fusion | bytes 2097152 | tf_op jit(solution)/shard_map/concatenate | solution.py:203
  39.6 1.1 butterflies.1
  40.7 7.2 %all-to-all-start.1 = ((bf16[32,64,128]{2,1,0:T(8,128)(2,1)}), bf16[32,64,128]{2,1,0:T(8,128)(2,1)S(1)}, u32[]{:S(2)}, u32[]{:S(2)}) async-start(bf16[32,64,128]{2,1,0:T(8,128)(2,1)} %get-tuple-element.18), calls=%async_computation.1 | async-start | bytes 1048576 | tf_op jit(solution)/shard_map/all_to_all | solution.py:214
  47.9 7.0 %collective-permute-done.3.refs_2_ = bf16[2048,256]{1,0:T(8,128)(2,1)} collective-permute-done((bf16[2048,256]{1,0:T(8,128)(2,1)}, bf16[2048,256]{1,0:T(8,128)(2,1)}, u32[]{:S(2)}, u32[]{:S(2)}) %collective-permute-start.3) | collective-permute-done | bytes 1048608 | tf_op jit(solution)/shard_map/ppermute | solution.py:205
  54.9 1.1 slice.12
  56.0 5.6 %collective-permute-start.5 = (bf16[1280,256]{1,0:T(8,128)(2,1)S(1)}, bf16[1280,256]{1,0:T(8,128)(2,1)S(1)}, u32[]{:S(2)}, u32[]{:S(2)}) collective-permute-start(bf16[1280,256]{1,0:T(8,128)(2,1)S(1)} %slice.12), channel_id=1, source_target_pairs={{0,1},{1,2},{2,3},{3,4},{4,5},{5,6},{6,7},{7,0},{8,9},{9,10},{10,1... | collective-permute-start | bytes 1966088 | tf_op jit(solution)/shard_map/ppermute | solution.py:208
  61.6 1.9 %collective-permute-start.6 = (bf16[2048,256]{1,0:T(8,128)(2,1)}, bf16[2048,256]{1,0:T(8,128)(2,1)S(1)}, u32[]{:S(2)}, u32[]{:S(2)}) collective-permute-start(bf16[2048,256]{1,0:T(8,128)(2,1)} %collective-permute-done.4.refs_3_), channel_id=1, source_target_pairs={{0,7},{1,0},{2,1},{3,2},{4,3},{5,4},{6,5},{7,6},{8,15},{9,8},{10,9... | collective-permute-start | bytes 3145736 | tf_op jit(solution)/shard_map/ppermute | solution.py:209
  63.5 1.8 %slice.13 = bf16[768,256]{1,0:T(8,128)(2,1)} slice(bf16[2048,256]{1,0:T(8,128)(2,1)} %collective-permute-done.3.refs_2_), slice={[1280:2048], [0:256]} | slice | bytes 786432 | tf_op jit(solution)/shard_map/slice | solution.py:207
  65.3 8.5 %collective-permute-done.5.refs_4_ = bf16[1280,256]{1,0:T(8,128)(2,1)S(1)} collective-permute-done((bf16[1280,256]{1,0:T(8,128)(2,1)S(1)}, bf16[1280,256]{1,0:T(8,128)(2,1)S(1)}, u32[]{:S(2)}, u32[]{:S(2)}) %collective-permute-start.5) | collective-permute-done | bytes 655392 | tf_op jit(solution)/shard_map/ppermute | solution.py:208
  73.8 5.6 %collective-permute-start.9 = (bf16[1280,256]{1,0:T(8,128)(2,1)S(1)}, bf16[1280,256]{1,0:T(8,128)(2,1)S(1)}, u32[]{:S(2)}, u32[]{:S(2)}) collective-permute-start(bf16[1280,256]{1,0:T(8,128)(2,1)S(1)} %collective-permute-done.5.refs_4_), channel_id=1, source_target_pairs={{0,1},{1,2},{2,3},{3,4},{4,5},{5,6},{6,7},{7,0},{8,9},{9,10},{10,1... | collective-permute-start | bytes 1966088 | tf_op jit(solution)/shard_map/ppermute | solution.py:210
  79.4 1.9 %collective-permute-start.2 = (bf16[32,64,128]{2,1,0:T(8,128)(2,1)S(1)}, bf16[32,64,128]{2,1,0:T(8,128)(2,1)}, u32[]{:S(2)}, u32[]{:S(2)}) collective-permute-start(bf16[32,64,128]{2,1,0:T(8,128)(2,1)S(1)} %all-to-all-done.1.got_ref), channel_id=1, source_target_pairs={{0,16},{16,0},{1,17},{17,1},{2,18},{18,2},{3,19},{19,3},{4,20},{20... | collective-permute-start | bytes 1572872 | tf_op jit(solution)/shard_map/ppermute | solution.py:215
  81.4 1.9 %collective-permute-start.8 = (bf16[768,256]{1,0:T(8,128)(2,1)}, bf16[768,256]{1,0:T(8,128)(2,1)S(1)}, u32[]{:S(2)}, u32[]{:S(2)}) collective-permute-start(bf16[768,256]{1,0:T(8,128)(2,1)} %slice.13), channel_id=1, source_target_pairs={{0,1},{1,2},{2,3},{3,4},{4,5},{5,6},{6,7},{7,0},{8,9},{9,10},{10,1... | collective-permute-start | bytes 1179656 | tf_op jit(solution)/shard_map/ppermute | solution.py:208
  83.3 5.4 %early_products.1 = (f32[1280,128]{1,0:T(8,128)S(1)}, f32[1280,128]{1,0:T(8,128)S(1)}, f32[768,128]{1,0:T(8,128)S(1)}, f32[768,128]{1,0:T(8,128)S(1)}, bf16[8,256,256]{2,1,0:T(8,128)(2,1)S(1)}) custom-call(s32[3]{0:T(128)S(1)} %pad_add_fusion.place_ref, bf16[32,64,128]{2,1,0:T(8,128)(2,1)S(1)} %all-to-all-done.1.got_ref, ...), custom_call_target="tpu_custom_call" | custom-call | tf_op jit(solution)/shard_map/early_products/pallas_call | solution.py:134
  88.8 3.9 %collective-permute-start.7 = (bf16[768,256]{1,0:T(8,128)(2,1)S(1)}, bf16[768,256]{1,0:T(8,128)(2,1)S(1)}, u32[]{:S(2)}, u32[]{:S(2)}) collective-permute-start(bf16[768,256]{1,0:T(8,128)(2,1)S(1)} %slice.10), channel_id=1, source_target_pairs={{0,7},{1,0},{2,1},{3,2},{4,3},{5,4},{6,5},{7,6},{8,15},{9,8},{10,9... | collective-permute-start | bytes 1179656 | tf_op jit(solution)/shard_map/ppermute | solution.py:229
  92.7 1.8 %collective-permute-done.9.refs_1_ = bf16[1280,256]{1,0:T(8,128)(2,1)S(1)} collective-permute-done((bf16[1280,256]{1,0:T(8,128)(2,1)S(1)}, bf16[1280,256]{1,0:T(8,128)(2,1)S(1)}, u32[]{:S(2)}, u32[]{:S(2)}) %collective-permute-start.9) | collective-permute-done | bytes 655392 | tf_op jit(solution)/shard_map/ppermute | solution.py:210
  94.5 1.0 last_far.3
  95.6 4.9 %collective-permute-start.10 = (bf16[1280,128]{1,0:T(8,128)(2,1)S(1)}, bf16[1280,128]{1,0:T(8,128)(2,1)S(1)}, u32[]{:S(2)}, u32[]{:S(2)}) collective-permute-start(bf16[1280,128]{1,0:T(8,128)(2,1)S(1)} %last_far.3), channel_id=1, source_target_pairs={{0,8},{8,0},{1,9},{9,1},{2,10},{10,2},{3,11},{11,3},{4,12},{12,4},... | collective-permute-start | bytes 983048 | tf_op jit(solution)/shard_map/ppermute | solution.py:238
  100.6 2.9 %collective-permute-done.7.refs_1_ = bf16[768,256]{1,0:T(8,128)(2,1)S(1)} collective-permute-done((bf16[768,256]{1,0:T(8,128)(2,1)S(1)}, bf16[768,256]{1,0:T(8,128)(2,1)S(1)}, u32[]{:S(2)}, u32[]{:S(2)}) %collective-permute-start.7) | collective-permute-done | bytes 393248 | tf_op jit(solution)/shard_map/ppermute | solution.py:229
  103.5 1.0 last_far.2
  104.5 4.9 %collective-permute-start.11 = (bf16[768,128]{1,0:T(8,128)(2,1)S(1)}, bf16[768,128]{1,0:T(8,128)(2,1)S(1)}, u32[]{:S(2)}, u32[]{:S(2)}) collective-permute-start(bf16[768,128]{1,0:T(8,128)(2,1)S(1)} %last_far.2), channel_id=1, source_target_pairs={{0,8},{8,0},{1,9},{9,1},{2,10},{10,2},{3,11},{11,3},{4,12},{12,4},... | collective-permute-start | bytes 589832 | tf_op jit(solution)/shard_map/ppermute | solution.py:238
  109.4 1.0 last_own.2
  110.5 1.0 last_own.3
  111.6 2.8 %collective-permute-done.11 = bf16[768,128]{1,0:T(8,128)(2,1)S(1)} collective-permute-done((bf16[768,128]{1,0:T(8,128)(2,1)S(1)}, bf16[768,128]{1,0:T(8,128)(2,1)S(1)}, u32[]{:S(2)}, u32[]{:S(2)}) %collective-permute-start.11) | collective-permute-done | bytes 196640 | tf_op jit(solution)/shard_map/ppermute | solution.py:238
  (17 shorter events, 2.7 us)
Async XLA Ops:
  0.0 27.4 %collective-permute-start = (bf16[2048,256]{1,0:T(8,128)(2,1)}, bf16[2048,256]{1,0:T(8,128)(2,1)}, u32[]{:S(2)}, u32[]{:S(2)}) collective-permute-start(bf16[2048,256]{1,0:T(8,128)(2,1)} %refs_0_.1), channel_id=1, source_target_pairs={{0,1},{1,2},{2,3},{3,4},{4,5},{5,6},{6,7},{7,0},{8,9},{9,10},{10,1... | collective-permute-start | bytes 3145736 | tf_op jit(solution)/shard_map/ppermute | solution.py:193
  4.7 28.3 %collective-permute-start.1 = (bf16[2048,256]{1,0:T(8,128)(2,1)}, bf16[2048,256]{1,0:T(8,128)(2,1)}, u32[]{:S(2)}, u32[]{:S(2)}) collective-permute-start(bf16[2048,256]{1,0:T(8,128)(2,1)} %refs_0_.1), channel_id=1, source_target_pairs={{0,7},{1,0},{2,1},{3,2},{4,3},{5,4},{6,5},{7,6},{8,15},{9,8},{10,9... | collective-permute-start | bytes 3145736 | tf_op jit(solution)/shard_map/ppermute | solution.py:193
  10.7 28.9 %all-to-all-start = ((bf16[72,32,128]{2,0,1:T(8,128)(2,1)}), bf16[72,32,128]{2,0,1:T(8,128)(2,1)S(1)}, u32[]{:S(2)}, u32[]{:S(2)}) async-start(bf16[72,32,128]{2,0,1:T(8,128)(2,1)} %copy.10), calls=%async_computation | async-start | bytes 1179648 | tf_op jit(solution)/shard_map/all_to_all | solution.py:202
  27.4 27.4 %collective-permute-start.3 = (bf16[2048,256]{1,0:T(8,128)(2,1)}, bf16[2048,256]{1,0:T(8,128)(2,1)}, u32[]{:S(2)}, u32[]{:S(2)}) collective-permute-start(bf16[2048,256]{1,0:T(8,128)(2,1)} %collective-permute-done), channel_id=1, source_target_pairs={{0,1},{1,2},{2,3},{3,4},{4,5},{5,6},{6,7},{7,0},{8,9},{9,10},{10,1... | collective-permute-start | bytes 3145736 | tf_op jit(solution)/shard_map/ppermute | solution.py:205
  33.0 28.6 %collective-permute-start.4 = (bf16[2048,256]{1,0:T(8,128)(2,1)}, bf16[2048,256]{1,0:T(8,128)(2,1)}, u32[]{:S(2)}, u32[]{:S(2)}) collective-permute-start(bf16[2048,256]{1,0:T(8,128)(2,1)} %collective-permute-done.1), channel_id=1, source_target_pairs={{0,7},{1,0},{2,1},{3,2},{4,3},{5,4},{6,5},{7,6},{8,15},{9,8},{10,9... | collective-permute-start | bytes 3145736 | tf_op jit(solution)/shard_map/ppermute | solution.py:205
  40.7 38.7 %all-to-all-start.1 = ((bf16[32,64,128]{2,1,0:T(8,128)(2,1)}), bf16[32,64,128]{2,1,0:T(8,128)(2,1)S(1)}, u32[]{:S(2)}, u32[]{:S(2)}) async-start(bf16[32,64,128]{2,1,0:T(8,128)(2,1)} %get-tuple-element.18), calls=%async_computation.1 | async-start | bytes 1048576 | tf_op jit(solution)/shard_map/all_to_all | solution.py:214
  56.0 17.8 %collective-permute-start.5 = (bf16[1280,256]{1,0:T(8,128)(2,1)S(1)}, bf16[1280,256]{1,0:T(8,128)(2,1)S(1)}, u32[]{:S(2)}, u32[]{:S(2)}) collective-permute-start(bf16[1280,256]{1,0:T(8,128)(2,1)S(1)} %slice.12), channel_id=1, source_target_pairs={{0,1},{1,2},{2,3},{3,4},{4,5},{5,6},{6,7},{7,0},{8,9},{9,10},{10,1... | collective-permute-start | bytes 1966088 | tf_op jit(solution)/shard_map/ppermute | solution.py:208
  61.6 27.2 %collective-permute-start.6 = (bf16[2048,256]{1,0:T(8,128)(2,1)}, bf16[2048,256]{1,0:T(8,128)(2,1)S(1)}, u32[]{:S(2)}, u32[]{:S(2)}) collective-permute-start(bf16[2048,256]{1,0:T(8,128)(2,1)} %collective-permute-done.4.refs_3_), channel_id=1, source_target_pairs={{0,7},{1,0},{2,1},{3,2},{4,3},{5,4},{6,5},{7,6},{8,15},{9,8},{10,9... | collective-permute-start | bytes 3145736 | tf_op jit(solution)/shard_map/ppermute | solution.py:209
  73.8 20.8 %collective-permute-start.9 = (bf16[1280,256]{1,0:T(8,128)(2,1)S(1)}, bf16[1280,256]{1,0:T(8,128)(2,1)S(1)}, u32[]{:S(2)}, u32[]{:S(2)}) collective-permute-start(bf16[1280,256]{1,0:T(8,128)(2,1)S(1)} %collective-permute-done.5.refs_4_), channel_id=1, source_target_pairs={{0,1},{1,2},{2,3},{3,4},{4,5},{5,6},{6,7},{7,0},{8,9},{9,10},{10,1... | collective-permute-start | bytes 1966088 | tf_op jit(solution)/shard_map/ppermute | solution.py:210
  79.4 3.9 %collective-permute-start.2 = (bf16[32,64,128]{2,1,0:T(8,128)(2,1)S(1)}, bf16[32,64,128]{2,1,0:T(8,128)(2,1)}, u32[]{:S(2)}, u32[]{:S(2)}) collective-permute-start(bf16[32,64,128]{2,1,0:T(8,128)(2,1)S(1)} %all-to-all-done.1.got_ref), channel_id=1, source_target_pairs={{0,16},{16,0},{1,17},{17,1},{2,18},{18,2},{3,19},{19,3},{4,20},{20... | collective-permute-start | bytes 1572872 | tf_op jit(solution)/shard_map/ppermute | solution.py:215
  81.4 19.2 %collective-permute-start.8 = (bf16[768,256]{1,0:T(8,128)(2,1)}, bf16[768,256]{1,0:T(8,128)(2,1)S(1)}, u32[]{:S(2)}, u32[]{:S(2)}) collective-permute-start(bf16[768,256]{1,0:T(8,128)(2,1)} %slice.13), channel_id=1, source_target_pairs={{0,1},{1,2},{2,3},{3,4},{4,5},{5,6},{6,7},{7,0},{8,9},{9,10},{10,1... | collective-permute-start | bytes 1179656 | tf_op jit(solution)/shard_map/ppermute | solution.py:208
  88.8 14.6 %collective-permute-start.7 = (bf16[768,256]{1,0:T(8,128)(2,1)S(1)}, bf16[768,256]{1,0:T(8,128)(2,1)S(1)}, u32[]{:S(2)}, u32[]{:S(2)}) collective-permute-start(bf16[768,256]{1,0:T(8,128)(2,1)S(1)} %slice.10), channel_id=1, source_target_pairs={{0,7},{1,0},{2,1},{3,2},{4,3},{5,4},{6,5},{7,6},{8,15},{9,8},{10,9... | collective-permute-start | bytes 1179656 | tf_op jit(solution)/shard_map/ppermute | solution.py:229
  95.6 15.9 %collective-permute-start.10 = (bf16[1280,128]{1,0:T(8,128)(2,1)S(1)}, bf16[1280,128]{1,0:T(8,128)(2,1)S(1)}, u32[]{:S(2)}, u32[]{:S(2)}) collective-permute-start(bf16[1280,128]{1,0:T(8,128)(2,1)S(1)} %last_far.3), channel_id=1, source_target_pairs={{0,8},{8,0},{1,9},{9,1},{2,10},{10,2},{3,11},{11,3},{4,12},{12,4},... | collective-permute-start | bytes 983048 | tf_op jit(solution)/shard_map/ppermute | solution.py:238
  104.5 9.9 %collective-permute-start.11 = (bf16[768,128]{1,0:T(8,128)(2,1)S(1)}, bf16[768,128]{1,0:T(8,128)(2,1)S(1)}, u32[]{:S(2)}, u32[]{:S(2)}) collective-permute-start(bf16[768,128]{1,0:T(8,128)(2,1)S(1)} %last_far.2), channel_id=1, source_target_pairs={{0,8},{8,0},{1,9},{9,1},{2,10},{10,2},{3,11},{11,3},{4,12},{12,4},... | collective-permute-start | bytes 589832 | tf_op jit(solution)/shard_map/ppermute | solution.py:238
